TPU v7x, 128 devices: a whole 4x4x4 slice. The times are simulated.
128 devices in a mesh: rows: 2 (over core), waves: 64 (over z, y, x).
Axes of the slice: x: 4, y: 4, z: 4, core: 2. Of those that a mesh axis runs over, the one named last changes fastest.
Arguments:
- feats: float32 [32768, 256], P(('rows', 'waves')), may hold values from -6 to 6
- positions: float32 [3, 32768], P(None, ('rows', 'waves')), may hold values from 0 to 6
- cell_counts: int32 [256], P(('rows', 'waves')), may hold values from 1 to 128
- neighbours: int32 [256, 5], P(('rows', 'waves')), may hold values from 0 to 255, as said below
- nbr_count: int32 [256], P(('rows', 'waves')), may hold values from 3 to 5
- kvec: float32 [3, 3072], P(None, 'waves'), may hold values from -4 to 4
- filters: float32 [3072, 256], P('waves'), may hold values from -5 to 5
- w_msg: float32 [256, 256], replicated, may hold values from -0.375 to 0.375
- w_val: float32 [256, 256], replicated, may hold values from -0.375 to 0.375
- w_one: float32 [256, 256], replicated, may hold values from -0.375 to 0.375
- w_two: float32 [256, 256], replicated, may hold values from -0.375 to 0.375
Outputs:
- updated: float32 [32768, 256], P(('rows', 'waves'))
Inputs may be any that keep to these rules, and one draw needn't show every extreme that they name: `neighbours`: column 0 of each cell's list is the cell itself, column 1 the cell (c - 2) mod 256, column 2 the cell (c + 2) mod 256; the 5 entries of a list are distinct cells, and every listed cell c' of cell c satisfies (c' - c) mod 256 <= 2 or (c - c') mod 256 <= 2; entries at or beyond nbr_count are in range and unused.
All inputs are finite; a program needn't handle non-finite values.
Results may differ from a plain program's by a relative error of at most 0.0003.
Values sent between devices are 32-bit elements; how exact they have to be, the bound alone decides.
No kernel may reach another device: no remote copies, remote signals or barrier semaphores. Data moves between devices by JAX's collectives and lax.ppermute only.
A program may use at most 128 MiB of HBM per device.

v0:
```python
import math

import jax
import jax.numpy as jnp
from jax import lax
from jax.sharding import Mesh
from jax.sharding import PartitionSpec as P

WAVES = ("waves_0", "waves_1", "waves_2")
ROWS_WAVES = ("rows", "waves_0", "waves_1", "waves_2")


HIGH = lax.Precision.HIGHEST


def extended(x, sides, width):
    edges = {}
    for axis, dim in sides:
        size, length = (lax.axis_size(axis), x.shape[dim])
        up = [(i, (i + 1) % size) for i in range(size)]
        last = lax.slice_in_dim(x, length - width, length, axis=dim)
        first = lax.slice_in_dim(x, 0, width, axis=dim)
        edges[dim] = (
            lax.ppermute(last, axis, up),
            lax.ppermute(first, axis, [(b, a) for a, b in up]),
        )
    done = []
    for _, dim in sides:
        low, high = edges[dim]
        around = [(width, width) if d in done else (0, 0) for d in range(x.ndim)]
        x = jnp.concatenate([jnp.pad(low, around), x, jnp.pad(high, around)], axis=dim)
        done.append(dim)
    return x


def in_order(tiles, dim):
    tiles = jnp.moveaxis(tiles, 0, dim)
    dims = tiles.shape
    return tiles.reshape(*dims[:dim], dims[dim] * dims[dim + 1], *dims[dim + 2 :])


def from_everyone(x, axis):
    length = lax.axis_size(axis)
    return lax.all_to_all(jnp.broadcast_to(x[None], (length, *x.shape)), axis, 0, 0, tiled=True)


def gathered_copies(x, axis, dim):
    return in_order(from_everyone(x, axis), dim)


def over_copies(x, axis):
    return from_everyone(x, axis).sum(axis=0)


def packed_total(arrays, axis):
    vector, at, outs = (jnp.concatenate([a.reshape(-1) for a in arrays]), 0, [])
    subtotal = over_copies(vector, axis)
    for a in arrays:
        outs.append(subtotal[at : at + a.size].reshape(a.shape))
        at += a.size
    return tuple(outs)


def cut_along(x, dim, length):
    dims = x.shape
    tiles = x.reshape(*dims[:dim], length, dims[dim] // length, *dims[dim + 1 :])
    return jnp.moveaxis(tiles, dim, 0)


def edges_of(length, count):
    unit = 8 if length >= 8 * count else 1
    return [length // unit * k // count * unit for k in range(1, count)]


def reduced_to_own(tiles, axes, order):
    dims = [lax.axis_size(a) for a in axes]
    tiles = tiles.reshape(*dims, *tiles.shape[1:])
    tiles = tiles.transpose(*order, *range(len(axes), tiles.ndim))
    tiles = tiles.reshape(-1, *tiles.shape[len(axes) :])
    for k in order:
        tiles = lax.psum_scatter(tiles, axes[k], scatter_dimension=0, tiled=True)
    return tiles[0]


def sum_at_once(x, axes, dim):
    tiles = cut_along(x, dim, lax.axis_size(axes))
    widest = max(range(1, max(2, tiles.ndim - 1)), key=lambda d: tiles.shape[d])
    count, outs = (len(axes), [])
    for first, section in enumerate(
        jnp.split(tiles, edges_of(tiles.shape[widest], count), axis=widest)
    ):
        if section.size:
            order = [(first + k) % count for k in range(count)]
            outs.append(reduced_to_own(section, axes, order))
    return jnp.concatenate(outs, axis=widest - 1)


def shards(
    feats, positions, cell_counts, neighbours, nbr_count, kvec, filters, w_msg, w_val, w_one, w_two
):
    cells = cell_counts.shape[0]
    slots = feats.shape[0]
    cell = slots // cells
    width = feats.shape[1]
    kcol = kvec.shape[1]
    devices = lax.axis_size("rows") * lax.axis_size(WAVES)
    slot_ids = jnp.arange(cell, dtype=jnp.int32)
    valid2 = (slot_ids[None, :] < cell_counts[:, None]).astype(jnp.float32)
    valid = valid2.reshape(-1)
    hw_cols = jnp.einsum("fg,sf->gs", w_msg, feats, precision=HIGH)
    payload = jnp.concatenate([hw_cols, positions, valid[None, :]], axis=0)
    widened = extended(payload, ((ROWS_WAVES, 1),), slots)
    widened = widened.reshape(width + 4, 3 * cells, cell)
    first = lax.axis_index(ROWS_WAVES) * cells
    total_cells = cells * devices
    own_ids = first + jnp.arange(cells, dtype=jnp.int32)
    own_pos = positions.reshape(3, cells, cell)
    same_slot = jnp.eye(cell, dtype=jnp.bool_)

    def pair_step(index, acc):
        listed = lax.dynamic_index_in_dim(neighbours, index, 1, keepdims=False)
        local = (listed - first + cells) % total_cells
        blocks = jnp.take(widened, local, axis=1)
        near_hw = blocks[:width]
        near_pos = blocks[width : width + 3]
        near_valid = blocks[width + 3]
        dist = jnp.sum((own_pos[:, :, :, None] - near_pos[:, :, None, :]) ** 2, axis=0)
        live = (index < nbr_count).astype(jnp.float32)
        keep = valid2[:, :, None] * near_valid[:, None, :] * live[:, None, None]
        same = (listed == own_ids)[:, None, None] & same_slot[None]
        weight = jnp.where(same, 0.0, jnp.exp(-0.125 * dist) * keep)
        return acc + jnp.einsum("cij,gcj->cig", weight, near_hw, precision=HIGH)

    msg0 = jnp.zeros((cells, cell, width), jnp.float32)
    msg = lax.fori_loop(0, jnp.max(nbr_count), pair_step, msg0)
    msg = 0.125 * msg.reshape(slots, width)
    row_pos = gathered_copies(positions, WAVES, 1)
    val_cols = jnp.einsum("fg,sf->gs", w_val, feats, precision=HIGH) * valid[None, :]
    piece = lax.all_gather(val_cols, WAVES, axis=1, tiled=True)
    part_pos = row_pos
    phase = jnp.dot(kvec.T, part_pos, precision=HIGH)
    dims = (((1,), (1,)), ((), ()))
    sum_cos = lax.dot_general(jnp.cos(phase), piece, dims, precision=HIGH)
    sum_sin = lax.dot_general(jnp.sin(phase), piece, dims, precision=HIGH)
    whole_cos, whole_sin = packed_total((sum_cos, sum_sin), "rows")
    filt_cos = filters * whole_cos
    filt_sin = filters * whole_sin
    scale_factor = 1.0 / math.sqrt(float(slots * devices) * float(kcol * lax.axis_size(WAVES)))
    part_pos = row_pos
    phase = jnp.dot(part_pos.T, kvec, precision=HIGH)
    ewald = (
        sum_at_once(
            jnp.dot(jnp.cos(phase), filt_cos, precision=HIGH)
            + jnp.dot(jnp.sin(phase), filt_sin, precision=HIGH),
            WAVES,
            0,
        )
        * scale_factor
    )
    summed = feats + msg + ewald
    normed = summed / jnp.sqrt(jnp.mean(summed * summed, axis=1, keepdims=True) + 1e-06)
    hidden = jax.nn.silu(jnp.dot(normed, w_one, precision=HIGH))
    return (summed + jnp.dot(hidden, w_two, precision=HIGH)) * valid[:, None]


def solution(mesh):
    torus = Mesh(
        mesh.devices.reshape(mesh.shape["rows"], 4, 4, 4), ("rows", "waves_0", "waves_1", "waves_2")
    )
    return jax.shard_map(
        shards,
        mesh=torus,
        in_specs=(
            P(ROWS_WAVES, None),
            P(None, ROWS_WAVES),
            P(ROWS_WAVES),
            P(ROWS_WAVES, None),
            P(ROWS_WAVES),
            P(None, WAVES),
            P(WAVES, None),
            P(),
            P(),
            P(),
            P(),
        ),
        out_specs=P(ROWS_WAVES, None),
        check_vma=False,
    )
```

profile of v0, /device:TPU:1, one launch (start us, length us, event | category | flops | bytes accessed | tf_op | source)
XLA Modules:
  0.0 578.9 jit_solution(914687151199923344)
XLA Ops:
  6.5 0.8 compare_convert_fusion.2
  7.3 0.2 copy-done
  7.5 2.2 convolution_multiply_fusion
  9.8 0.7 broadcast_in_dim.47
  10.5 21.3 %all_to_all.11 = f32[64,3,256]{2,1,0:T(4,128)S(1)} all-to-all(f32[64,3,256]{2,1,0:T(4,128)S(1)} %broadcast_in_dim.47), channel_id=1, replica_groups=mesh['rows'=2,'waves_0'=4,'waves_1'=4,'waves_2'=4] {'waves_0','waves_1',..., dimensions={0} | all-to-all | bytes 393216 | tf_op jit(solution)/shard_map/all_to_all | solution.py:44
  31.8 3.3 fusion.57
  35.2 4.3 fusion.56
  39.5 93.8 %all-gather.2.cloned.1.call-done = f32[256,16384]{1,0:T(8,128)} async-done(((f32[256,256]{1,0:T(8,128)}), f32[256,16384]{1,0:T(8,128)}) %all-gather.2.cloned.1.call-update) | async-done | bytes 16777232 | tf_op jit(solution)/shard_map/all_gather | solution.py:139
  133.3 25.0 %fusion.32 = f32[6,2,8,128]{3,2,1,0:T(8,128)S(1)} fusion(f32[256,16384]{1,0:T(8,128)} %all-gather.2.cloned.1.call-done, f32[48,16384]{1,0:T(8,128)S(1)} %fusion.57), kind=kOutput, calls=%fused_computation.47 | convolution fusion | flops 2415919104 | bytes 19972096 | tf_op jit(solution)/shard_map/dot_general | solution.py:143
  158.3 24.5 %fusion.35 = f32[6,2,8,128]{3,2,1,0:T(8,128)S(1)} fusion(f32[256,16384]{1,0:T(8,128)S(1)} %copy-done.2, f32[48,16384]{1,0:T(8,128)S(1)} %fusion.57), kind=kOutput, calls=%fused_computation.48 | convolution fusion | flops 2415919104 | bytes 19972096 | tf_op jit(solution)/shard_map/dot_general | solution.py:144
  183.0 5.1 all_to_all.12
  188.1 0.3 reduce_sum.30
  188.5 24.2 %fusion.29 = f32[16384,256]{1,0:T(8,128)S(1)} fusion(f32[16384,48]{0,1:T(8,128)} %fusion.56, f32[48,256]{1,0:T(8,128)S(1)} %copy-done.6, f32[48,256]{1,0:T(8,128)S(1)} %slice.45), kind=kOutput, calls=%fused_computation.42 | convolution fusion | flops 2415931392 | bytes 20021248 | tf_op jit(solution)/shard_map/dot_general | solution.py:153
  212.7 25.2 %convolution_add_fusion.1 = f32[16384,256]{1,0:T(8,128)} fusion(f32[16384,256]{1,0:T(8,128)S(1)} %fusion.29, f32[16384,48]{0,1:T(8,128)S(1)} %copy-done.3, f32[48,256]{1,0:T(8,128)S(1)} %copy-done.6, f32[48,256]{1,0:T(8,128)S(1)} %slice.47), kind=kOutput, calls=%fused_computation.36 | convolution fusion | flops 2420125696 | bytes 36798464 | tf_op jit(solution)/shard_map/dot_general | solution.py:154
  237.9 5.2 split.12
  243.2 7.6 %fusion.53 = (f32[64,88,256]{2,1,0:T(8,128)}, f32[64,88,256]{2,1,0:T(8,128)S(1)}) fusion(f32[64,256,256]{2,1,0:T(8,128)} %bitcast.62), kind=kLoop, calls=%fused_computation.72 | loop fusion | bytes 23068672 | tf_op jit(solution)/shard_map/split | solution.py:90
  250.8 3.1 copy.31
  253.9 5.9 %copy.30 = f32[4,4,4,88,256]{4,3,0,2,1:T(8,128)} copy(f32[4,4,4,88,256]{4,3,2,1,0:T(8,128)} %bitcast.65) | data formatting | bytes 11534336 | tf_op jit(solution)/shard_map/reshape | solution.py:77
  260.0 37.9 %reduce-scatter.10.cloned.1.call-done = f32[16,80,256]{2,1,0:T(8,128)} async-done(((f32[64,80,256]{2,1,0:T(8,128)}), f32[16,80,256]{2,1,0:T(8,128)}) %reduce-scatter.10.cloned.1.call-update) | async-done | bytes 1310736 | tf_op jit(solution)/shard_map/reduce_scatter | solution.py:81
  297.9 61.6 %reduce-scatter.22.cloned.1.call-done = f32[16,88,256]{2,1,0:T(8,128)} async-done(((f32[64,88,256]{2,1,0:T(8,128)}), f32[16,88,256]{2,1,0:T(8,128)}) %reduce-scatter.22.cloned.1.call-update) | async-done | bytes 1441808 | tf_op jit(solution)/shard_map/reduce_scatter | solution.py:81
  359.6 61.7 %reduce-scatter.16.cloned.1.call-done = f32[16,88,256]{2,1,0:T(8,128)} async-done(((f32[64,88,256]{2,1,0:T(8,128)}), f32[16,88,256]{2,1,0:T(8,128)}) %reduce-scatter.16.cloned.1.call-update) | async-done | bytes 1441808 | tf_op jit(solution)/shard_map/reduce_scatter | solution.py:81
  421.3 25.1 %reduce-scatter.12.cloned.1.call-done = f32[4,80,256]{2,1,0:T(8,128)} async-done(((f32[16,80,256]{2,1,0:T(8,128)}), f32[4,80,256]{2,1,0:T(8,128)}) %reduce-scatter.12.cloned.1.call-update) | async-done | bytes 327696 | tf_op jit(solution)/shard_map/reduce_scatter | solution.py:81
  446.5 27.0 %reduce-scatter.24.cloned.1.call-done = f32[4,88,256]{2,1,0:T(8,128)} async-done(((f32[16,88,256]{2,1,0:T(8,128)}), f32[4,88,256]{2,1,0:T(8,128)}) %reduce-scatter.24.cloned.1.call-update) | async-done | bytes 360464 | tf_op jit(solution)/shard_map/reduce_scatter | solution.py:81
  473.6 0.6 fusion.55
  474.2 7.5 %collective-permute-start.1 = (f32[260,256]{1,0:T(8,128)S(1)}, f32[260,256]{1,0:T(8,128)S(1)}, u32[]{:S(2)}, u32[]{:S(2)}) collective-permute-start(f32[260,256]{1,0:T(8,128)S(1)} %pad_maximum_fusion.1), channel_id=1, source_target_pairs={{1,0},{2,1},{3,2},{4,3},{5,4},{6,5},{7,6},{8,7},{9,8},{10,9},{11,1... | collective-permute-start | bytes 798728 | tf_op jit(solution)/shard_map/ppermute | solution.py:25
  481.8 0.7 reduce_max.9
  482.5 7.5 %collective-permute-done.1 = f32[260,256]{1,0:T(8,128)S(1)} collective-permute-done((f32[260,256]{1,0:T(8,128)S(1)}, f32[260,256]{1,0:T(8,128)S(1)}, u32[]{:S(2)}, u32[]{:S(2)}) %collective-permute-start.1) | collective-permute-done | bytes 266272 | tf_op jit(solution)/shard_map/ppermute | solution.py:25
  490.0 7.3 %collective-permute-done = f32[260,256]{1,0:T(8,128)S(1)} collective-permute-done((f32[260,256]{1,0:T(8,128)S(1)}, f32[260,256]{1,0:T(8,128)S(1)}, u32[]{:S(2)}, u32[]{:S(2)}) %collective-permute-start) | collective-permute-done | bytes 266272 | tf_op jit(solution)/shard_map/ppermute | solution.py:24
  497.6 4.4 reduce-scatter.18.cloned.1.call-done
  502.1 11.4 %while.15 = (s32[]{:T(128)}, f32[2,128,256]{2,1,0:T(8,128)S(1)}, s32[]{:T(128)}, s32[2,5]{0,1:T(8,128)S(1)}, f32[3,256]{1,0:T(4,128)}, /*index=5*/s32[]{:T(128)}...) while((s32[]{:T(128)}, f32[2,128,256]{2,1,0:T(8,128)S(1)}, ...), condition=%wide.wide.region_3.4_spmd.clone.clone, body=%wide.wide.region_1.3_spmd.clone.clone.sunk | while | flops 101272112 | bytes 2175233 | solution.py:135
  502.9 0.6 gather_fusion
  503.8 0.5 convolution_add_fusion.5
  505.1 0.6 gather_fusion
  505.8 0.2 multiply_reduce_fusion.4
  506.0 0.5 convolution_add_fusion.5
  507.2 0.6 gather_fusion
  508.1 0.5 convolution_add_fusion.5
  509.4 0.6 gather_fusion
  510.1 0.2 multiply_reduce_fusion.4
  510.3 0.5 convolution_add_fusion.5
  511.6 0.6 gather_fusion
  512.4 0.5 convolution_add_fusion.5
  513.6 9.8 %reduce-scatter.14.cloned.1.call-done = f32[1,80,256]{2,1,0:T(8,128)} async-done(((f32[4,80,256]{2,1,0:T(8,128)}), f32[1,80,256]{2,1,0:T(8,128)}) %reduce-scatter.14.cloned.1.call-update) | async-done | bytes 81936 | tf_op jit(solution)/shard_map/reduce_scatter | solution.py:81
  523.4 23.0 %reduce-scatter.26.cloned.1.call-done = f32[1,88,256]{2,1,0:T(8,128)} async-done(((f32[4,88,256]{2,1,0:T(8,128)}), f32[1,88,256]{2,1,0:T(8,128)}) %reduce-scatter.26.cloned.1.call-update) | async-done | bytes 90128 | tf_op jit(solution)/shard_map/reduce_scatter | solution.py:81
  546.4 23.0 %reduce-scatter.20.cloned.1.call-done = f32[1,88,256]{2,1,0:T(8,128)} async-done(((f32[4,88,256]{2,1,0:T(8,128)}), f32[1,88,256]{2,1,0:T(8,128)}) %reduce-scatter.20.cloned.1.call-update) | async-done | bytes 90128 | tf_op jit(solution)/shard_map/reduce_scatter | solution.py:81
  569.4 1.1 multiply_reduce_fusion.1
  570.5 0.4 fusion.44
  570.9 1.1 fusion.31
  (112 shorter events, 3.0 us)
Async XLA Ops:
  6.5 1.0 copy-start
  6.5 28.6 %copy-start.9 = (f32[3,48]{1,0:T(4,128)S(1)}, f32[3,48]{1,0:T(4,128)}, u32[]{:S(2)}) copy-start(f32[3,48]{1,0:T(4,128)} %param.18) | copy-start | bytes 1732
  6.5 126.7 %all-gather.2.cloned.1.call-start = ((), (), s32[]{:S(2)}) async-start(), calls=%async_computation.11 | async-start | bytes 17039360 | tf_op jit(solution)/shard_map/all_gather | solution.py:139
  9.8 288.1 %reduce-scatter.10.cloned.1.call-start = ((), (), s32[]{:S(2)}) async-start(), calls=%async_computation.12 | async-start | bytes 6553600 | tf_op jit(solution)/shard_map/reduce_scatter | solution.py:81
  133.3 25.0 %copy-start.2 = (f32[256,16384]{1,0:T(8,128)S(1)}, f32[256,16384]{1,0:T(8,128)}, u32[]{:S(2)}) copy-start(f32[256,16384]{1,0:T(8,128)} %all-gather.2.cloned.1.call-done) | copy-start | bytes 50331652
  158.3 30.1 %copy-start.6 = (f32[48,256]{1,0:T(8,128)S(1)}, f32[48,256]{1,0:T(8,128)}, u32[]{:S(2)}) copy-start(f32[48,256]{1,0:T(8,128)} %param.19) | copy-start | bytes 147460
  188.5 24.2 %copy-start.3 = (f32[16384,48]{0,1:T(8,128)S(1)}, f32[16384,48]{0,1:T(8,128)}, u32[]{:S(2)}) copy-start(f32[16384,48]{0,1:T(8,128)} %fusion.56) | copy-start | bytes 9437188
  243.1 116.4 %reduce-scatter.22.cloned.1.call-start = ((), (), s32[]{:S(2)}) async-start(), calls=%async_computation.18 | async-start | bytes 7208960 | tf_op jit(solution)/shard_map/reduce_scatter | solution.py:81
  253.9 167.4 %reduce-scatter.16.cloned.1.call-start = ((), (), s32[]{:S(2)}) async-start(), calls=%async_computation.15 | async-start | bytes 7208960 | tf_op jit(solution)/shard_map/reduce_scatter | solution.py:81
  259.9 213.6 %copy-start.4 = (f32[256,256]{1,0:T(8,128)S(1)}, f32[256,256]{1,0:T(8,128)}, u32[]{:S(2)}) copy-start(f32[256,256]{1,0:T(8,128)} %param.13) | copy-start | bytes 786436
  259.9 213.6 %copy-start.5 = (f32[256,256]{1,0:T(8,128)S(1)}, f32[256,256]{1,0:T(8,128)}, u32[]{:S(2)}) copy-start(f32[256,256]{1,0:T(8,128)} %param.20) | copy-start | bytes 786436
  259.9 214.2 %copy-start.7 = (f32[3,256]{1,0:T(4,128)S(1)}, f32[3,256]{1,0:T(4,128)}, u32[]{:S(2)}) copy-start(f32[3,256]{1,0:T(4,128)} %param.14) | copy-start | bytes 9220
  259.9 221.8 %copy-start.10 = (s32[2,5]{1,0:T(2,128)S(1)}, s32[2,5]{1,0:T(2,128)}, u32[]{:S(2)}) copy-start(s32[2,5]{1,0:T(2,128)} %param.16) | copy-start | bytes 124
  260.0 221.9 %copy-start.8 = (s32[2]{0:T(128)S(1)}, s32[2]{0:T(128)}, u32[]{:S(2)}) copy-start(s32[2]{0:T(128)} %param.17) | copy-start | bytes 28
  260.0 186.4 %reduce-scatter.12.cloned.1.call-start = ((), (), s32[]{:S(2)}) async-start(), calls=%async_computation.13 | async-start | bytes 1638400 | tf_op jit(solution)/shard_map/reduce_scatter | solution.py:81
  297.9 175.6 %reduce-scatter.24.cloned.1.call-start = ((), (), s32[]{:S(2)}) async-start(), calls=%async_computation.19 | async-start | bytes 1802240 | tf_op jit(solution)/shard_map/reduce_scatter | solution.py:81
  359.6 142.5 %reduce-scatter.18.cloned.1.call-start = ((), (), s32[]{:S(2)}) async-start(), calls=%async_computation.16 | async-start | bytes 1802240 | tf_op jit(solution)/shard_map/reduce_scatter | solution.py:81
  421.3 102.1 %reduce-scatter.14.cloned.1.call-start = ((), (), s32[]{:S(2)}) async-start(), calls=%async_computation.14 | async-start | bytes 409600 | tf_op jit(solution)/shard_map/reduce_scatter | solution.py:81
  446.4 99.9 %reduce-scatter.26.cloned.1.call-start = ((), (), s32[]{:S(2)}) async-start(), calls=%async_computation.20 | async-start | bytes 450560 | tf_op jit(solution)/shard_map/reduce_scatter | solution.py:81
  473.5 95.9 %reduce-scatter.20.cloned.1.call-start = ((), (), s32[]{:S(2)}) async-start(), calls=%async_computation.17 | async-start | bytes 450560 | tf_op jit(solution)/shard_map/reduce_scatter | solution.py:81
  474.2 27.9 %copy-start.11 = (s32[2]{0:T(128)S(1)}, s32[2]{0:T(128)}, u32[]{:S(2)}) copy-start(s32[2]{0:T(128)} %param.15) | copy-start | bytes 28
  474.2 15.8 %collective-permute-start.1 = (f32[260,256]{1,0:T(8,128)S(1)}, f32[260,256]{1,0:T(8,128)S(1)}, u32[]{:S(2)}, u32[]{:S(2)}) collective-permute-start(f32[260,256]{1,0:T(8,128)S(1)} %pad_maximum_fusion.1), channel_id=1, source_target_pairs={{1,0},{2,1},{3,2},{4,3},{5,4},{6,5},{7,6},{8,7},{9,8},{10,9},{11,1... | collective-permute-start | bytes 798728 | tf_op jit(solution)/shard_map/ppermute | solution.py:25
  481.7 15.6 %collective-permute-start = (f32[260,256]{1,0:T(8,128)S(1)}, f32[260,256]{1,0:T(8,128)S(1)}, u32[]{:S(2)}, u32[]{:S(2)}) collective-permute-start(f32[260,256]{1,0:T(8,128)S(1)} %pad_maximum_fusion.1), channel_id=1, source_target_pairs={{0,1},{1,2},{2,3},{3,4},{4,5},{5,6},{6,7},{7,8},{8,9},{9,10},{10,1... | collective-permute-start | bytes 798728 | tf_op jit(solution)/shard_map/ppermute | solution.py:24
  502.1 68.4 %copy-start.12 = (f32[256,256]{1,0:T(8,128)S(1)}, f32[256,256]{1,0:T(8,128)}, u32[]{:S(2)}) copy-start(f32[256,256]{1,0:T(8,128)} %param.22) | copy-start | bytes 786436
  502.1 68.8 %copy-start.13 = (f32[256,256]{1,0:T(8,128)S(1)}, f32[256,256]{1,0:T(8,128)}, u32[]{:S(2)}) copy-start(f32[256,256]{1,0:T(8,128)} %param.23) | copy-start | bytes 786436
  513.5 58.5 %copy-start.1 = (f32[256,256]{1,0:T(8,128)S(1)}, f32[256,256]{1,0:T(8,128)}, u32[]{:S(2)}) copy-start(f32[256,256]{1,0:T(8,128)} %param.21) | copy-start | bytes 786436
Sparse Core Ops, SparseCore 0:
  10.1 123.1 all-gather.1
  243.3 54.5 reduce-scatter.9
  300.3 59.1 reduce-scatter.21
  361.8 59.4 reduce-scatter.15
  423.5 22.8 reduce-scatter.11
  448.7 24.7 reduce-scatter.23
  475.9 26.0 reduce-scatter.17
  504.4 18.9 reduce-scatter.13
  525.8 20.5 reduce-scatter.25
  548.6 20.7 reduce-scatter.19
where the time goes:
time: 581 us; the launch traced here: 579 us
  waiting for transfers between devices  382 us (66%)
  matrix products  113 us (19%)
  blocking collectives  26.4 us (5%)
  local copies, waits for them, and re-layouts  26.3 us (5%)
  between operations  13.9 us (2%)
  starting transfers between devices  7.86 us (1%)
    reduce_scatter x9, waiting for transfers between devices, reduced_to_own(): tiles = lax.psum_scatter(tiles, axes[k], scatter_dimension=0, tiled=True)  273 us
    all_gather x1, waiting for transfers between devices, shards(): piece = lax.all_gather(val_cols, WAVES, axis=1, tiled=True)  93.8 us
    all_to_all x2, blocking collectives, from_everyone(): lax.all_to_all(jnp.broadcast_to(x[None], (length, *x.shape)), axis, 0, 0,...  26.4 us
    dot_general x1, matrix products, shards(): jnp.dot(jnp.sin(phase), filt_sin, precision=HIGH)  25.2 us
    dot_general x1, matrix products, shards(): sum_cos = lax.dot_general(jnp.cos(phase), piece, dims, precision=HIGH)  25 us
    dot_general x1, matrix products, shards(): sum_sin = lax.dot_general(jnp.sin(phase), piece, dims, precision=HIGH)  24.5 us
    dot_general x1, matrix products, shards(): jnp.dot(jnp.cos(phase), filt_cos, precision=HIGH)  24.2 us
    split x2, local copies, waits for them, and re-layouts, sum_at_once(): jnp.split(tiles, edges_of(tiles.shape[widest], count), axis=widest)  12.8 us
  transfers between devices with their start and end apart: 12, of which 12 were waited for; matrix products, arithmetic and copies ran while one was open for 6% of the time, Pallas kernels for 0%

commit v1 on v0

v1 whole, which is shorter than its diff:
```python
import math

import jax
import jax.numpy as jnp
from jax import lax
from jax.experimental import pallas as pl
from jax.experimental.pallas import tpu as pltpu
from jax.sharding import Mesh
from jax.sharding import PartitionSpec as P

Z, Y, X = "waves_0", "waves_1", "waves_2"
WAVES = (Z, Y, X)
ROWS_WAVES = ("rows", Z, Y, X)
F32 = jnp.float32
BF16 = jnp.bfloat16

SIN_POLY = (6.283185280154403, -10.33542015333633, 5.100154773052372, -1.1965808225334407, 0.15531182448662934)
COS_POLY = (0.9999999997791529, -4.934802136928833, 4.058709154760502, -1.335211949366169, 0.23493706849740192, -0.0243959319559508)


def horner(coeffs, u):
    out = coeffs[-1]
    for c in coeffs[-2::-1]:
        out = out * u + c
    return out


def split(a):
    high = a.astype(BF16)
    return high, (a - high.astype(F32)).astype(BF16)


def dot(a, b):
    return jnp.dot(a, b, preferred_element_type=F32)


def dot3(a, b):
    return dot(a[0], b[0]) + (dot(a[1], b[0]) + dot(a[0], b[1]))


def call(kernel, outs, scratch=(), smem=(), n_in=0, limit=40 << 20):
    return pl.pallas_call(
        kernel,
        out_shape=outs,
        in_specs=[
            pl.BlockSpec(memory_space=pltpu.SMEM if i in smem else pltpu.VMEM) for i in range(n_in)
        ],
        out_specs=jax.tree.map(lambda _: pl.BlockSpec(memory_space=pltpu.VMEM), outs),
        scratch_shapes=scratch,
        compiler_params=pltpu.CompilerParams(vmem_limit_bytes=limit),
    )


def live_rows(counts, cells, cell):
    row = lax.broadcasted_iota(jnp.int32, (cells * cell, 1), 0)
    limit = jnp.full(row.shape, counts[0])
    for c in range(1, cells):
        limit = jnp.where(row >= c * cell, c * cell + counts[c], limit)
    return row < limit


def prepare(cells, cell):
    slots = cells * cell

    def kernel(counts, feats, positions, out):
        out[:slots] = jnp.where(live_rows(counts, cells, cell), feats[...], 0.0)
        out[slots:] = jnp.zeros((8, out.shape[1]), F32)
        out[slots : slots + 3] = positions[...]

    return kernel


def forward(slots, count, waves, first):
    block = 48

    def kernel(kt, w_val, *refs):
        chunks, refs = refs[:count], refs[count:]
        if not first:
            before, refs = refs[0], refs[1:]
        out, ch, cl, sh, sl, acc_c, acc_s = refs
        w = split(w_val[...])
        for j, chunk in enumerate(chunks):
            v = split(dot3(split(chunk[:slots]), w))
            px = chunk[slots : slots + 1]
            py = chunk[slots + 1 : slots + 2]
            pz = chunk[slots + 2 : slots + 3]

            def body(i, carry, j=j, px=px, py=py, pz=pz):
                rows = pl.ds(pl.multiple_of(i * block, block), block)
                k = kt[rows, :]
                t = k[:, 0:1] * px + k[:, 1:2] * py + k[:, 2:3] * pz
                f = t - jnp.round(t)
                u = f * f
                s = f * horner(SIN_POLY, u)
                c = horner(COS_POLY, u)
                ch[j, rows, :], cl[j, rows, :] = split(1.0 - 0.5 * (s * s))
                sh[j, rows, :], sl[j, rows, :] = split(s * c)
                return carry

            lax.fori_loop(0, waves // block, body, 0)
            part_c = dot3((ch[j], cl[j]), v)
            part_s = dot3((sh[j], sl[j]), v)
            if j == 0:
                acc_c[...] = part_c
                acc_s[...] = part_s
            else:
                acc_c[...] += part_c
                acc_s[...] += part_s
        own = out.shape[2]
        total_c = acc_c[...].reshape(-1, own, out.shape[3])
        total_s = acc_s[...].reshape(-1, own, out.shape[3])
        if first:
            out[:, 0] = total_c
            out[:, 1] = total_s
        else:
            out[:, 0] = before[:, 0] + total_c
            out[:, 1] = before[:, 1] + total_s

    return kernel


def filtered(scale):
    def kernel(half, parts, filters, out):
        groups, _, own, _ = parts.shape
        f = filters[pl.ds(pl.multiple_of(half[0] * own, 8), own), :] * scale
        for i in range(2):
            total = parts[0, i]
            for g in range(1, groups):
                total = total + parts[g, i]
            total = total * f
            for g in range(groups):
                out[g, i] = total

    return kernel


def backward(count, waves):
    def kernel(f, ch, cl, sh, sl, out):
        fc = split(f[:, 0].reshape(waves, -1).T)
        fs = split(f[:, 1].reshape(waves, -1).T)
        for j in range(count):
            out[j] = dot3(fc, (ch[j], cl[j])) + dot3(fs, (sh[j], sl[j]))

    return kernel


def messages(cells, cell, cells_all, nb):
    slots = cells * cell

    def kernel(place, neighbours, nbr_count, own, low, high, edge, w_msg, out):
        x, last, first = place[0], place[1], place[2]
        lo = jnp.where(x == 0, edge[...], low[...])
        hi = jnp.where(x == last, edge[...], high[...])
        blocks = (lo, own[...], hi)
        parts = [split(b[:slots]) for b in blocks]
        wide = [tuple(p[k][c * cell : (c + 1) * cell] for k in range(2)) for p in parts for c in range(cells)]
        pos = [
            b[slots : slots + 3, c * cell : (c + 1) * cell] for b in blocks for c in range(cells)
        ]
        cols = own[slots : slots + 8].T
        eye = lax.broadcasted_iota(jnp.int32, (cell, cell), 0) == lax.broadcasted_iota(jnp.int32, (cell, cell), 1)
        gathered = []
        for c in range(cells):
            mine = cols[c * cell : (c + 1) * cell]
            acc = None
            for step in range(2 * cells + 1):
                other = c + step
                local = other - cells
                target = lax.rem(first + local + cells_all, cells_all)
                listed = jnp.float32(0.0)
                for b in range(nb):
                    hit = (neighbours[c, b] == target) & (b < nbr_count[c])
                    listed = listed + jnp.where(hit, jnp.float32(1.0), jnp.float32(0.0))
                near = pos[other]
                d0 = mine[:, 0:1] - near[0:1]
                d1 = mine[:, 1:2] - near[1:2]
                d2 = mine[:, 2:3] - near[2:3]
                weight = jnp.exp(-0.125 * (d0 * d0 + d1 * d1 + d2 * d2)) * listed
                if step == cells:
                    weight = jnp.where(eye, 0.0, weight)
                part = dot3(split(weight), wide[other])
                acc = part if acc is None else acc + part
            gathered.append(acc)
        total = jnp.concatenate(gathered, axis=0)
        out[...] = 0.125 * dot3(split(total), split(w_msg[...]))

    return kernel


def finish(cells, cell):
    def kernel(counts, feats, msg, own, swap, a, b, c, w_one, w_two, out):
        live = live_rows(counts, cells, cell)
        spectral = ((own[...] + swap[...]) + (a[...] + b[...])) + c[...]
        u = feats[...] + jnp.where(live, msg[...], 0.0) + spectral.T
        normed = u / jnp.sqrt(jnp.mean(u * u, axis=1, keepdims=True) + 1e-06)
        v = dot3(split(normed), split(w_one[...]))
        hidden = v / (1.0 + jnp.exp(-v))
        res = u + dot3(split(hidden), split(w_two[...]))
        out[...] = jnp.where(live, res, 0.0)

    return kernel


def shift(axis, by):
    size = lax.axis_size(axis)
    return [(i, (i + by) % size) for i in range(size)]


def shards(
    feats, positions, cell_counts, neighbours, nbr_count, kvec, filters, w_msg, w_val, w_one, w_two
):
    cells = cell_counts.shape[0]
    slots, width = feats.shape
    cell = slots // cells
    devices = lax.axis_size(ROWS_WAVES)
    nx = lax.axis_size(X)
    rows = lax.axis_size("rows")
    group = lax.axis_size((Z, Y))
    own_waves = kvec.shape[1] // rows
    waves = own_waves * group
    half = lax.axis_index("rows").astype(jnp.int32)
    x = lax.axis_index(X).astype(jnp.int32)
    first = lax.axis_index(ROWS_WAVES).astype(jnp.int32) * cells

    tall = slots + 8
    payload = call(prepare(cells, cell), jax.ShapeDtypeStruct((tall, width), F32), smem=(0,), n_in=3)(
        cell_counts, feats, positions
    )
    near2 = lax.ppermute(payload, X, shift(X, 2))
    above = lax.ppermute(payload, X, shift(X, -1))
    below = lax.ppermute(payload, X, shift(X, 1))
    ends = [(d, (d + 1) % devices) for d in range(devices) if d % nx == nx - 1]
    ends = ends + [(b, a) for a, b in ends]
    edge = lax.ppermute(payload, ROWS_WAVES, ends)

    kt = lax.dynamic_slice_in_dim(kvec.T, half * own_waves, own_waves, 0) * (0.5 / math.pi)
    kt = jnp.pad(kt, ((0, 0), (0, 128 - kt.shape[1])))
    kt = lax.all_to_all(jnp.broadcast_to(kt[None], (group, *kt.shape)), (Z, Y), 0, 0, tiled=True)
    kt = kt.reshape(waves, 128)

    line = (payload, above, below, near2)
    other = tuple(lax.ppermute(c, "rows", shift("rows", 1)) for c in line)
    count = len(line)
    wide = jax.ShapeDtypeStruct((count, waves, slots), BF16)
    sums = jax.ShapeDtypeStruct((group, 2, own_waves, width), F32)
    acc = [pltpu.VMEM((waves, width), F32)] * 2
    part, *mine = call(forward(slots, count, waves, True), (sums,) + (wide,) * 4, acc, n_in=2 + count)(
        kt, w_val, *line
    )
    part, *theirs = call(forward(slots, count, waves, False), (sums,) + (wide,) * 4, acc, n_in=3 + count)(
        kt, w_val, *other, part
    )
    parts = lax.all_to_all(part, (Z, Y), 0, 0, tiled=True)
    scale = 1.0 / math.sqrt(float(slots * devices) * float(waves * rows * nx))
    spread = call(filtered(scale), sums, smem=(0,), n_in=3)(half.reshape(1), parts, filters)
    f = lax.all_to_all(spread, (Z, Y), 0, 0, tiled=True)

    back = call(backward(count, waves), jax.ShapeDtypeStruct((count, width, slots), F32), n_in=5)
    swap = lax.ppermute(back(f, *theirs), "rows", shift("rows", 1))
    own = back(f, *mine)
    e1 = lax.ppermute(own[1] + swap[1], X, shift(X, 1))
    e2 = lax.ppermute(own[2] + swap[2], X, shift(X, -1))
    e3 = lax.ppermute(own[3] + swap[3], X, shift(X, 2))

    place = jnp.stack([x, jnp.int32(nx - 1), first])
    msg = call(
        messages(cells, cell, cells * devices, neighbours.shape[1]),
        jax.ShapeDtypeStruct((slots, width), F32),
        smem=(0, 1, 2),
        n_in=8,
    )(place, neighbours, nbr_count, payload, below, above, edge, w_msg)
    return call(finish(cells, cell), jax.ShapeDtypeStruct((slots, width), F32), smem=(0,), n_in=10)(
        cell_counts, feats, msg, own[0], swap[0], e1, e2, e3, w_one, w_two
    )


def solution(mesh):
    torus = Mesh(mesh.devices.reshape(mesh.shape["rows"], 4, 4, 4), ROWS_WAVES)
    return jax.shard_map(
        shards,
        mesh=torus,
        in_specs=(
            P(ROWS_WAVES, None),
            P(None, ROWS_WAVES),
            P(ROWS_WAVES),
            P(ROWS_WAVES, None),
            P(ROWS_WAVES),
            P(None, WAVES),
            P(WAVES, None),
            P(),
            P(),
            P(),
            P(),
        ),
        out_specs=P(ROWS_WAVES, None),
        check_vma=False,
    )
```

time: 581 us -> 112 us (0.19)
  waiting for transfers between devices: 382 us -> 19.1 us
  matrix products: 113 us -> 0 us
  local copies, waits for them, and re-layouts: 26.3 us -> 3.06 us
  Pallas kernels: 0 us -> 22.7 us
  blocking collectives: 26.4 us -> 44.7 us
  starting transfers between devices: 7.86 us -> 21.6 us
  between operations: 13.9 us -> 0.23 us
    reduce_scatter x9 -> x0, waiting for transfers between devices: 273 us -> none  [reduced_to_own(): tiles = lax.psum_scatter(tiles, axes[k], scatter_dimension=0, tiled=True)]
    dot_general x15 -> x0, matrix products: 113 us -> none  [the longest x1 25.2 us: shards(): jnp.dot(jnp.sin(phase), filt_sin, precision=HIGH)]
    all_gather x1 -> x0, waiting for transfers between devices: 93.8 us -> none  [shards(): piece = lax.all_gather(val_cols, WAVES, axis=1, tiled=True)]
    pallas_call x0 -> x8, Pallas kernels: none -> 22.7 us  [the longest x1 7.28 us: shards(): call(forward(slots, count, waves, False), (sums,) + (wide,) * 4, acc, n_i...]
    all_to_all x2 -> x3, blocking collectives: 26.4 us -> 44.7 us  [the longest x1 15.4 us: shards(): parts = lax.all_to_all(part, (Z, Y), 0, 0, tiled=True)]
    ppermute x2 -> x12, starting transfers between devices: 7.5 us -> 21.6 us  [the longest x4 6.08 us: shards(): other = tuple((lax.ppermute(c, 'rows', shift('rows', 1)) for c in line))]
    split x2 -> x0, local copies, waits for them, and re-layouts: 12.8 us -> none  [sum_at_once(): jnp.split(tiles, edges_of(tiles.shape[widest], count), axis=widest)]
    reshape x3 -> x0, local copies, waits for them, and re-layouts: 9.16 us -> none  [the longest x2 9.04 us: reduced_to_own(): tiles = tiles.reshape(*dims, *tiles.shape[1:])]
  transfers between devices with their start and end apart: 12 -> 12, of which waited for: 12 -> 3; matrix products, arithmetic and copies ran while one was open for 6% -> 0% of each run, Pallas kernels for 0% -> 10%
where the time goes in v1:
time: 112 us
  blocking collectives  44.7 us (40%)
  Pallas kernels  22.7 us (20%)
  starting transfers between devices  21.6 us (19%)
  waiting for transfers between devices  19.1 us (17%)
  local copies, waits for them, and re-layouts  3.06 us (3%)
    all_to_all x1, blocking collectives, shards(): parts = lax.all_to_all(part, (Z, Y), 0, 0, tiled=True)  15.4 us
    all_to_all x1, blocking collectives, shards(): lax.all_to_all(jnp.broadcast_to(kt[None], (group, *kt.shape)), (Z, Y), 0,...  14.9 us
    all_to_all x1, blocking collectives, shards(): f = lax.all_to_all(spread, (Z, Y), 0, 0, tiled=True)  14.4 us
    ppermute x1, waiting for transfers between devices, shards(): edge = lax.ppermute(payload, ROWS_WAVES, ends)  13 us
    pallas_call x1, Pallas kernels, shards(): call(forward(slots, count, waves, False), (sums,) + (wide,) * 4, acc, n_i...  7.28 us
    pallas_call x1, Pallas kernels, shards(): call(forward(slots, count, waves, True), (sums,) + (wide,) * 4, acc, n_in...  7.27 us
    ppermute x4, starting transfers between devices, shards(): other = tuple((lax.ppermute(c, 'rows', shift('rows', 1)) for c in line))  6.08 us
    ppermute x1, starting transfers between devices, shards(): edge = lax.ppermute(payload, ROWS_WAVES, ends)  4.89 us
  transfers between devices with their start and end apart: 12, of which 3 were waited for; matrix products, arithmetic and copies ran while one was open for 0% of the time, Pallas kernels for 10%

profile of v1, /device:TPU:1, one launch (start us, length us, event | category | flops | bytes accessed | tf_op | source)
XLA Modules:
  0.0 111.7 jit_solution(14003531139461885367)
XLA Ops:
  0.0 0.9 copy-done.1
  1.0 0.7 copy-done.7
  1.6 0.7 copy-done.8
  2.3 0.6 shard_map.109.own.refs_0_
  2.9 3.7 %collective-permute-start.6 = (f32[264,256]{1,0:T(8,128)S(1)}, f32[264,256]{1,0:T(8,128)S(1)}, u32[]{:S(2)}, u32[]{:S(2)}) collective-permute-start(f32[264,256]{1,0:T(8,128)S(1)} %shard_map.109.own.refs_0_), channel_id=1, source_target_pairs={{0,2},{1,3},{2,0},{3,1},{4,6},{5,7},{6,4},{7,5},{8,10},{9,11},{10,... | collective-permute-start | bytes 811016 | tf_op jit(solution)/shard_map/ppermute | solution.py:229
  6.5 0.9 collective-permute-start.1
  7.4 0.6 collective-permute-start
  8.0 1.5 %collective-permute-start.3 = (f32[264,256]{1,0:T(8,128)S(1)}, f32[264,256]{1,0:T(8,128)S(1)}, u32[]{:S(2)}, u32[]{:S(2)}) collective-permute-start(f32[264,256]{1,0:T(8,128)S(1)} %shard_map.109.own.refs_0_), channel_id=1, source_target_pairs={{0,64},{64,0},{1,65},{65,1},{2,66},{66,2},{3,67},{67,3},{4,68},{68... | collective-permute-start | bytes 811016 | tf_op jit(solution)/shard_map/ppermute | solution.py:242
  9.5 2.7 %collective-permute-done.6.refs_3_ = f32[264,256]{1,0:T(8,128)S(1)} collective-permute-done((f32[264,256]{1,0:T(8,128)S(1)}, f32[264,256]{1,0:T(8,128)S(1)}, u32[]{:S(2)}, u32[]{:S(2)}) %collective-permute-start.6) | collective-permute-done | bytes 270368 | tf_op jit(solution)/shard_map/ppermute | solution.py:229
  12.2 3.0 %collective-permute-start.7 = (f32[264,256]{1,0:T(8,128)S(1)}, f32[264,256]{1,0:T(8,128)S(1)}, u32[]{:S(2)}, u32[]{:S(2)}) collective-permute-start(f32[264,256]{1,0:T(8,128)S(1)} %collective-permute-done.6.refs_3_), channel_id=1, source_target_pairs={{0,64},{64,0},{1,65},{65,1},{2,66},{66,2},{3,67},{67,3},{4,68},{68... | collective-permute-start | bytes 811016 | tf_op jit(solution)/shard_map/ppermute | solution.py:242
  15.3 3.3 %collective-permute-done.1.high.refs_1_ = f32[264,256]{1,0:T(8,128)S(1)} collective-permute-done((f32[264,256]{1,0:T(8,128)S(1)}, f32[264,256]{1,0:T(8,128)S(1)}, u32[]{:S(2)}, u32[]{:S(2)}) %collective-permute-start.1) | collective-permute-done | bytes 270368 | tf_op jit(solution)/shard_map/ppermute | solution.py:230
  18.6 1.5 %collective-permute-start.4 = (f32[264,256]{1,0:T(8,128)S(1)}, f32[264,256]{1,0:T(8,128)S(1)}, u32[]{:S(2)}, u32[]{:S(2)}) collective-permute-start(f32[264,256]{1,0:T(8,128)S(1)} %collective-permute-done.1.high.refs_1_), channel_id=1, source_target_pairs={{0,64},{64,0},{1,65},{65,1},{2,66},{66,2},{3,67},{67,3},{4,68},{68... | collective-permute-start | bytes 811016 | tf_op jit(solution)/shard_map/ppermute | solution.py:242
  20.1 0.0 collective-permute-done.low.refs_2_
  20.1 0.0 collective-permute-start.5
  20.1 0.0 copy-done.12
  20.1 0.1 multiply_bitcast_fusion
  20.2 0.1 copy.13
  20.3 14.9 %all_to_all.15 = f32[16,24,128]{2,1,0:T(8,128)S(1)} all-to-all(f32[16,24,128]{2,1,0:T(8,128)S(1)} %broadcast_in_dim.2), channel_id=1, replica_groups=mesh['rows'=2,'waves_0'=4,'waves_1'=4,'waves_2'=4] {'waves_0','waves_1'}, dimensions={0} | all-to-all | bytes 393216 | tf_op jit(solution)/shard_map/all_to_all | solution.py:238
  35.2 7.3 %shard_map.111 = (f32[16,2,24,256]{3,2,1,0:T(8,128)S(1)}, bf16[4,384,256]{2,1,0:T(8,128)(2,1)S(1)}, bf16[4,384,256]{2,1,0:T(8,128)(2,1)S(1)}, bf16[4,384,256]{2,1,0:T(8,128)(2,1)S(1)}, bf16[4,384,256]{2,1,0:T(8,128)(2,1)S(1)}) custom-call(f32[384,128]{1,0:T(8,128)S(1)} %bitcast.16, f32[256,256]{1,0:T(8,128)S(1)} %copy-done, ...), custom_call_target="tpu_custom_call" | custom-call | tf_op jit(solution)/shard_map/pallas_call | solution.py:247
  42.5 0.0 collective-permute-done.3.refs_0_
  42.5 0.0 collective-permute-done.7.refs_3_
  42.5 0.0 collective-permute-done.4.refs_1_
  42.5 0.0 collective-permute-done.5.refs_2_
  42.5 7.3 %shard_map.112 = (f32[16,2,24,256]{3,2,1,0:T(8,128)S(1)}, bf16[4,384,256]{2,1,0:T(8,128)(2,1)S(1)}, bf16[4,384,256]{2,1,0:T(8,128)(2,1)S(1)}, bf16[4,384,256]{2,1,0:T(8,128)(2,1)S(1)}, bf16[4,384,256]{2,1,0:T(8,128)(2,1)S(1)}) custom-call(f32[384,128]{1,0:T(8,128)S(1)} %bitcast.17, f32[256,256]{1,0:T(8,128)S(1)} %copy-done, ...), custom_call_target="tpu_custom_call" | custom-call | tf_op jit(solution)/shard_map/pallas_call | solution.py:250
  49.8 0.0 copy-start.6
  49.8 15.4 %all_to_all.16.parts = f32[16,2,24,256]{3,2,1,0:T(8,128)S(1)} all-to-all(f32[16,2,24,256]{3,2,1,0:T(8,128)S(1)} %get-tuple-element.16), channel_id=1, replica_groups=mesh['rows'=2,'waves_0'=4,'waves_1'=4,'waves_2'=4] {'waves_0','waves_1'}, dimensions={0} | all-to-all | bytes 1572864 | tf_op jit(solution)/shard_map/all_to_all | solution.py:253
  65.2 0.1 shard_map.113
  65.3 14.4 %all_to_all.17.f = f32[16,2,24,256]{3,2,1,0:T(8,128)S(1)} all-to-all(f32[16,2,24,256]{3,2,1,0:T(8,128)S(1)} %shard_map.113), channel_id=1, replica_groups=mesh['rows'=2,'waves_0'=4,'waves_1'=4,'waves_2'=4] {'waves_0','waves_1'}, dimensions={0} | all-to-all | bytes 1572864 | tf_op jit(solution)/shard_map/all_to_all | solution.py:256
  79.7 1.8 %shard_map.115 = f32[4,256,256]{2,1,0:T(8,128)S(1)} custom-call(f32[16,2,24,256]{3,2,1,0:T(8,128)S(1)} %all_to_all.17.f, bf16[4,384,256]{2,1,0:T(8,128)(2,1)S(1)} %get-tuple-element.21.ch, bf16[4,384,256]{2,1,0:T(8,128)(2,1)S(1)} %get-tuple-element.22.cl, bf16[4,384,256]{2,1,0:T(8,128)(2,1)S(1)} %get-tuple-element.23.sh, ...), custom_call_target="tpu_custom_call" | custom-call | tf_op jit(solution)/shard_map/pallas_call | solution.py:259
  81.6 3.9 %collective-permute-start.8 = (f32[4,256,256]{2,1,0:T(8,128)S(1)}, f32[4,256,256]{2,1,0:T(8,128)S(1)}, u32[]{:S(2)}, u32[]{:S(2)}) collective-permute-start(f32[4,256,256]{2,1,0:T(8,128)S(1)} %shard_map.115), channel_id=1, source_target_pairs={{0,64},{64,0},{1,65},{65,1},{2,66},{66,2},{3,67},{67,3},{4,68},{68... | collective-permute-start | bytes 3145736 | tf_op jit(solution)/shard_map/ppermute | solution.py:259
  85.5 4.9 %collective-permute-start.2 = (f32[264,256]{1,0:T(8,128)S(1)}, f32[264,256]{1,0:T(8,128)S(1)}, u32[]{:S(2)}, u32[]{:S(2)}) collective-permute-start(f32[264,256]{1,0:T(8,128)S(1)} %shard_map.109.own.refs_0_), channel_id=1, source_target_pairs={{3,4},{7,8},{11,12},{15,16},{19,20},{23,24},{27,28},{31,32},{35,36... | collective-permute-start | bytes 811016 | tf_op jit(solution)/shard_map/ppermute | solution.py:234
  90.4 1.8 %shard_map.114 = f32[4,256,256]{2,1,0:T(8,128)S(1)} custom-call(f32[16,2,24,256]{3,2,1,0:T(8,128)S(1)} %all_to_all.17.f, bf16[4,384,256]{2,1,0:T(8,128)(2,1)S(1)} %get-tuple-element.17.ch, bf16[4,384,256]{2,1,0:T(8,128)(2,1)S(1)} %get-tuple-element.18.cl, bf16[4,384,256]{2,1,0:T(8,128)(2,1)S(1)} %get-tuple-element.19.sh, ...), custom_call_target="tpu_custom_call" | custom-call | tf_op jit(solution)/shard_map/pallas_call | solution.py:260
  92.2 0.0 copy-start.3
  92.2 0.0 collective-permute-done.8
  92.2 0.2 fusion
  92.4 0.1 collective-permute-start.11
  92.5 0.1 collective-permute-start.10
  92.6 1.5 %collective-permute-start.9 = (f32[256,256]{1,0:T(8,128)S(1)}, f32[256,256]{1,0:T(8,128)S(1)}, u32[]{:S(2)}, u32[]{:S(2)}) collective-permute-start(f32[256,256]{1,0:T(8,128)S(1)} %get-tuple-element.27), channel_id=1, source_target_pairs={{0,1},{1,2},{2,3},{3,0},{4,5},{5,6},{6,7},{7,4},{8,9},{9,10},{10,1... | collective-permute-start | bytes 786440 | tf_op jit(solution)/shard_map/ppermute | solution.py:261
  94.0 0.1 pad_add_fusion.place
  94.1 13.0 %collective-permute-done.2.edge = f32[264,256]{1,0:T(8,128)S(1)} collective-permute-done((f32[264,256]{1,0:T(8,128)S(1)}, f32[264,256]{1,0:T(8,128)S(1)}, u32[]{:S(2)}, u32[]{:S(2)}) %collective-permute-start.2) | collective-permute-done | bytes 270368 | tf_op jit(solution)/shard_map/ppermute | solution.py:234
  107.1 0.0 copy-done.10
  107.1 1.7 %shard_map.110.msg = f32[256,256]{1,0:T(8,128)S(1)} custom-call(s32[3]{0:T(128)S(1)} %pad_add_fusion.place, s32[2,5]{1,0:T(2,128)S(1)} %copy-done.10, s32[2]{0:T(128)S(1)} %copy-done.11, f32[264,256]{1,0:T(8,128)S(1)} %shard_map.109.own.refs_0_, f32[264,256]{1,0:T(8,128)S(1)} %collective-permute-done.low.refs_2_, ...), custom_call_target="tpu_custom_call" | custom-call | tf_op jit(solution)/shard_map/pallas_call | solution.py:266
  108.9 0.0 collective-permute-done.11.c
  108.9 0.0 collective-permute-done.10.b
  108.9 0.0 collective-permute-done.9.a
  108.9 0.0 copy-start.9
  109.0 0.6 copy-done.9
  109.6 2.1 %shard_map.116 = f32[256,256]{1,0:T(8,128)} custom-call(s32[2]{0:T(128)S(1)} %copy-done.9, f32[256,256]{1,0:T(8,128)S(1)} %copy-done.2, f32[256,256]{1,0:T(8,128)S(1)} %shard_map.110.msg, f32[256,256]{1,0:T(8,128)S(1)} %get-tuple-element.28.own, f32[256,256]{1,0:T(8,128)S(1)} %get-tuple-element.29.swap, f32[256,256]{1,0:T(8,128)S(1)} %collective-permute-done.9.a, ...), custom_call_target="tpu_custom_call" | custom-call | tf_op jit(solution)/shard_map/pallas_call | solution.py:272
  (19 shorter events, 0.1 us)
Async XLA Ops:
  0.0 0.9 copy-start.1
  1.0 0.7 copy-start.7
  1.6 0.7 copy-start.8
  2.9 9.4 %collective-permute-start.6 = (f32[264,256]{1,0:T(8,128)S(1)}, f32[264,256]{1,0:T(8,128)S(1)}, u32[]{:S(2)}, u32[]{:S(2)}) collective-permute-start(f32[264,256]{1,0:T(8,128)S(1)} %shard_map.109.own.refs_0_), channel_id=1, source_target_pairs={{0,2},{1,3},{2,0},{3,1},{4,6},{5,7},{6,4},{7,5},{8,10},{9,11},{10,... | collective-permute-start | bytes 811016 | tf_op jit(solution)/shard_map/ppermute | solution.py:229
  6.5 12.0 %collective-permute-start.1 = (f32[264,256]{1,0:T(8,128)S(1)}, f32[264,256]{1,0:T(8,128)S(1)}, u32[]{:S(2)}, u32[]{:S(2)}) collective-permute-start(f32[264,256]{1,0:T(8,128)S(1)} %shard_map.109.own.refs_0_), channel_id=1, source_target_pairs={{0,3},{1,0},{2,1},{3,2},{4,7},{5,4},{6,5},{7,6},{8,11},{9,8},{10,9... | collective-permute-start | bytes 811016 | tf_op jit(solution)/shard_map/ppermute | solution.py:230
  7.4 12.7 %collective-permute-start = (f32[264,256]{1,0:T(8,128)S(1)}, f32[264,256]{1,0:T(8,128)S(1)}, u32[]{:S(2)}, u32[]{:S(2)}) collective-permute-start(f32[264,256]{1,0:T(8,128)S(1)} %shard_map.109.own.refs_0_), channel_id=1, source_target_pairs={{0,1},{1,2},{2,3},{3,0},{4,5},{5,6},{6,7},{7,4},{8,9},{9,10},{10,1... | collective-permute-start | bytes 811016 | tf_op jit(solution)/shard_map/ppermute | solution.py:231
  8.0 34.5 %collective-permute-start.3 = (f32[264,256]{1,0:T(8,128)S(1)}, f32[264,256]{1,0:T(8,128)S(1)}, u32[]{:S(2)}, u32[]{:S(2)}) collective-permute-start(f32[264,256]{1,0:T(8,128)S(1)} %shard_map.109.own.refs_0_), channel_id=1, source_target_pairs={{0,64},{64,0},{1,65},{65,1},{2,66},{66,2},{3,67},{67,3},{4,68},{68... | collective-permute-start | bytes 811016 | tf_op jit(solution)/shard_map/ppermute | solution.py:242
  9.5 10.6 %copy-start.12 = (f32[3,48]{1,0:T(4,128)S(1)}, f32[3,48]{1,0:T(4,128)}, u32[]{:S(2)}) copy-start(f32[3,48]{1,0:T(4,128)} %param.16) | copy-start | bytes 1732
  12.2 30.2 %collective-permute-start.7 = (f32[264,256]{1,0:T(8,128)S(1)}, f32[264,256]{1,0:T(8,128)S(1)}, u32[]{:S(2)}, u32[]{:S(2)}) collective-permute-start(f32[264,256]{1,0:T(8,128)S(1)} %collective-permute-done.6.refs_3_), channel_id=1, source_target_pairs={{0,64},{64,0},{1,65},{65,1},{2,66},{66,2},{3,67},{67,3},{4,68},{68... | collective-permute-start | bytes 811016 | tf_op jit(solution)/shard_map/ppermute | solution.py:242
  18.6 24.0 %collective-permute-start.4 = (f32[264,256]{1,0:T(8,128)S(1)}, f32[264,256]{1,0:T(8,128)S(1)}, u32[]{:S(2)}, u32[]{:S(2)}) collective-permute-start(f32[264,256]{1,0:T(8,128)S(1)} %collective-permute-done.1.high.refs_1_), channel_id=1, source_target_pairs={{0,64},{64,0},{1,65},{65,1},{2,66},{66,2},{3,67},{67,3},{4,68},{68... | collective-permute-start | bytes 811016 | tf_op jit(solution)/shard_map/ppermute | solution.py:242
  20.1 22.4 %collective-permute-start.5 = (f32[264,256]{1,0:T(8,128)S(1)}, f32[264,256]{1,0:T(8,128)S(1)}, u32[]{:S(2)}, u32[]{:S(2)}) collective-permute-start(f32[264,256]{1,0:T(8,128)S(1)} %collective-permute-done.low.refs_2_), channel_id=1, source_target_pairs={{0,64},{64,0},{1,65},{65,1},{2,66},{66,2},{3,67},{67,3},{4,68},{68... | collective-permute-start | bytes 811016 | tf_op jit(solution)/shard_map/ppermute | solution.py:242
  20.3 14.9 %copy-start = (f32[256,256]{1,0:T(8,128)S(1)}, f32[256,256]{1,0:T(8,128)}, u32[]{:S(2)}) copy-start(f32[256,256]{1,0:T(8,128)} %w_val.3) | copy-start | bytes 786436
  49.8 15.4 %copy-start.6 = (f32[48,256]{1,0:T(8,128)S(1)}, f32[48,256]{1,0:T(8,128)}, u32[]{:S(2)}) copy-start(f32[48,256]{1,0:T(8,128)} %filters.1) | copy-start | bytes 147460
  81.6 10.7 %collective-permute-start.8 = (f32[4,256,256]{2,1,0:T(8,128)S(1)}, f32[4,256,256]{2,1,0:T(8,128)S(1)}, u32[]{:S(2)}, u32[]{:S(2)}) collective-permute-start(f32[4,256,256]{2,1,0:T(8,128)S(1)} %shard_map.115), channel_id=1, source_target_pairs={{0,64},{64,0},{1,65},{65,1},{2,66},{66,2},{3,67},{67,3},{4,68},{68... | collective-permute-start | bytes 3145736 | tf_op jit(solution)/shard_map/ppermute | solution.py:259
  85.5 21.7 %collective-permute-start.2 = (f32[264,256]{1,0:T(8,128)S(1)}, f32[264,256]{1,0:T(8,128)S(1)}, u32[]{:S(2)}, u32[]{:S(2)}) collective-permute-start(f32[264,256]{1,0:T(8,128)S(1)} %shard_map.109.own.refs_0_), channel_id=1, source_target_pairs={{3,4},{7,8},{11,12},{15,16},{19,20},{23,24},{27,28},{31,32},{35,36... | collective-permute-start | bytes 811016 | tf_op jit(solution)/shard_map/ppermute | solution.py:234
  92.2 14.9 %copy-start.3 = (f32[256,256]{1,0:T(8,128)S(1)}, f32[256,256]{1,0:T(8,128)}, u32[]{:S(2)}) copy-start(f32[256,256]{1,0:T(8,128)} %w_msg.1) | copy-start | bytes 786436
  92.4 16.5 %collective-permute-start.11 = (f32[256,256]{1,0:T(8,128)S(1)}, f32[256,256]{1,0:T(8,128)S(1)}, u32[]{:S(2)}, u32[]{:S(2)}) collective-permute-start(f32[256,256]{1,0:T(8,128)S(1)} %get-tuple-element.25), channel_id=1, source_target_pairs={{0,2},{1,3},{2,0},{3,1},{4,6},{5,7},{6,4},{7,5},{8,10},{9,11},{10,... | collective-permute-start | bytes 786440 | tf_op jit(solution)/shard_map/ppermute | solution.py:263
  92.5 16.4 %collective-permute-start.10 = (f32[256,256]{1,0:T(8,128)S(1)}, f32[256,256]{1,0:T(8,128)S(1)}, u32[]{:S(2)}, u32[]{:S(2)}) collective-permute-start(f32[256,256]{1,0:T(8,128)S(1)} %get-tuple-element.26), channel_id=1, source_target_pairs={{0,3},{1,0},{2,1},{3,2},{4,7},{5,4},{6,5},{7,6},{8,11},{9,8},{10,9... | collective-permute-start | bytes 786440 | tf_op jit(solution)/shard_map/ppermute | solution.py:262
  92.6 16.3 %collective-permute-start.9 = (f32[256,256]{1,0:T(8,128)S(1)}, f32[256,256]{1,0:T(8,128)S(1)}, u32[]{:S(2)}, u32[]{:S(2)}) collective-permute-start(f32[256,256]{1,0:T(8,128)S(1)} %get-tuple-element.27), channel_id=1, source_target_pairs={{0,1},{1,2},{2,3},{3,0},{4,5},{5,6},{6,7},{7,4},{8,9},{9,10},{10,1... | collective-permute-start | bytes 786440 | tf_op jit(solution)/shard_map/ppermute | solution.py:261
  94.0 13.1 %copy-start.10 = (s32[2,5]{1,0:T(2,128)S(1)}, s32[2,5]{1,0:T(2,128)}, u32[]{:S(2)}) copy-start(s32[2,5]{1,0:T(2,128)} %neighbours.1) | copy-start | bytes 124
  94.0 13.1 %copy-start.11 = (s32[2]{0:T(128)S(1)}, s32[2]{0:T(128)}, u32[]{:S(2)}) copy-start(s32[2]{0:T(128)} %nbr_count.1) | copy-start | bytes 28
  94.1 14.8 %copy-start.2 = (f32[256,256]{1,0:T(8,128)S(1)}, f32[256,256]{1,0:T(8,128)}, u32[]{:S(2)}) copy-start(f32[256,256]{1,0:T(8,128)} %feats.3) | copy-start | bytes 786436
  94.1 14.8 %copy-start.4 = (f32[256,256]{1,0:T(8,128)S(1)}, f32[256,256]{1,0:T(8,128)}, u32[]{:S(2)}) copy-start(f32[256,256]{1,0:T(8,128)} %w_one.1) | copy-start | bytes 786436
  94.1 14.9 %copy-start.5 = (f32[256,256]{1,0:T(8,128)S(1)}, f32[256,256]{1,0:T(8,128)}, u32[]{:S(2)}) copy-start(f32[256,256]{1,0:T(8,128)} %w_two.1) | copy-start | bytes 786436
  108.9 0.7 copy-start.9

commit v2 on v1

v2 whole, which is shorter than its diff:
```python
import math

import jax
import jax.numpy as jnp
from jax import lax
from jax.experimental import pallas as pl
from jax.experimental.pallas import tpu as pltpu
from jax.sharding import Mesh
from jax.sharding import PartitionSpec as P

Z, Y, X = "waves_0", "waves_1", "waves_2"
WAVES = (Z, Y, X)
ROWS_WAVES = ("rows", Z, Y, X)
F32 = jnp.float32
BF16 = jnp.bfloat16

SIN_POLY = (6.283185280154403, -10.33542015333633, 5.100154773052372, -1.1965808225334407, 0.15531182448662934)
COS_POLY = (0.9999999997791529, -4.934802136928833, 4.058709154760502, -1.335211949366169, 0.23493706849740192, -0.0243959319559508)
ROUNDER = 12582912.0


def horner(coeffs, u):
    out = coeffs[-1]
    for c in coeffs[-2::-1]:
        out = out * u + c
    return out


def split(a):
    high = a.astype(BF16)
    return high, (a - high.astype(F32)).astype(BF16)


def thirds(a):
    high = a.astype(BF16).astype(F32)
    rest = a - high
    middle = rest.astype(BF16).astype(F32)
    return high, middle, rest - middle


def dot(a, b):
    return jnp.dot(a, b, preferred_element_type=F32)


def dot3(a, b):
    return dot(a[0], b[0]) + (dot(a[1], b[0]) + dot(a[0], b[1]))


def call(kernel, outs, n_in, scratch=(), smem=(), hbm=(), limit=40 << 20):
    def space(i):
        return pltpu.SMEM if i in smem else pltpu.HBM if i in hbm else pltpu.VMEM

    return pl.pallas_call(
        kernel,
        out_shape=outs,
        in_specs=[pl.BlockSpec(memory_space=space(i)) for i in range(n_in)],
        out_specs=jax.tree.map(lambda _: pl.BlockSpec(memory_space=pltpu.VMEM), outs),
        scratch_shapes=scratch,
        compiler_params=pltpu.CompilerParams(vmem_limit_bytes=limit),
    )


def live_rows(counts, cells, cell):
    row = lax.broadcasted_iota(jnp.int32, (cells * cell, 1), 0)
    limit = jnp.full(row.shape, counts[0])
    for c in range(1, cells):
        limit = jnp.where(row >= c * cell, c * cell + counts[c], limit)
    return row < limit


def prepare(cells, cell):
    slots = cells * cell

    def kernel(counts, feats, positions, out, counts_s, pos_s, sems):
        copies = [
            pltpu.make_async_copy(counts, counts_s, sems.at[0]),
            pltpu.make_async_copy(positions, pos_s, sems.at[1]),
            pltpu.make_async_copy(feats, out.at[pl.ds(0, slots)], sems.at[2]),
        ]
        for c in copies:
            c.start()
        for c in copies:
            c.wait()
        out[:slots] = jnp.where(live_rows(counts_s, cells, cell), out[:slots], 0.0)
        out[slots:] = jnp.zeros((8, out.shape[1]), F32)
        out[slots : slots + 3] = pos_s[...]

    return kernel


def forward(slots, count, own, groups, first):
    def kernel(kt, w_val, *refs):
        chunks, refs = refs[:count], refs[count:]
        if not first:
            before, refs = refs[0], refs[1:]
        out, mh, ml = refs
        w = split(w_val[...])
        kh, km, kl = thirds(kt[...])
        lhs = kh
        for at, part in enumerate((kh, km, kh, km, kl)):
            lhs = lhs + pltpu.roll(part, 8 * (at + 1), 1)
        lhs = lhs[:, :48].astype(BF16)
        for j, chunk in enumerate(chunks):
            v = split(dot3(split(chunk[:slots]), w))
            ph, pm, pl_ = thirds(chunk[slots : slots + 8])
            turns = dot(lhs, jnp.concatenate([ph, pm, ph, pl_, pm, ph], axis=0).astype(BF16))
            for g in range(groups):
                t = turns[g * own : (g + 1) * own]
                f = t - ((t + ROUNDER) - ROUNDER)
                u = f * f
                s = f * horner(SIN_POLY, u)
                c = horner(COS_POLY, u)
                both = jnp.concatenate([1.0 - 0.5 * (s * s), s * c], axis=0)
                rows = slice(2 * own * g, 2 * own * (g + 1))
                mh[j, rows], ml[j, rows] = split(both)
            part = dot3((mh[j], ml[j]), v)
            if j:
                out[...] += part
            elif first:
                out[...] = part
            else:
                out[...] = before[...] + part

    return kernel


def filtered(scale):
    def kernel(half, parts, filters, out):
        groups, double, _ = parts.shape
        own = double // 2
        f = filters[pl.ds(pl.multiple_of(half[0] * own, 8), own), :] * scale
        total = parts[0]
        for g in range(1, groups):
            total = total + parts[g]
        total = total * jnp.concatenate([f, f], axis=0)
        for g in range(groups):
            out[g] = total

    return kernel


def backward(count):
    def kernel(f, mh, ml, out):
        ft = split(f[...].T)
        for j in range(count):
            out[j] = dot3(ft, (mh[j], ml[j]))

    return kernel


def messages(cells, cell, cells_all, nb):
    slots = cells * cell

    def kernel(place, neighbours, nbr_count, counts, feats, own, low, high, edge, w_msg, out, mask):
        x, last, first = place[0], place[1], place[2]
        lo = jnp.where(x == 0, edge[...], low[...])
        hi = jnp.where(x == last, edge[...], high[...])
        blocks = (lo, own[...], hi)
        parts = [split(b[:slots]) for b in blocks]
        wide = [tuple(p[k][c * cell : (c + 1) * cell] for k in range(2)) for p in parts for c in range(cells)]
        pos = [
            b[slots : slots + 3, c * cell : (c + 1) * cell] for b in blocks for c in range(cells)
        ]
        cols = own[slots : slots + 8].T
        eye = lax.broadcasted_iota(jnp.int32, (cell, cell), 0) == lax.broadcasted_iota(jnp.int32, (cell, cell), 1)
        gathered = []
        for c in range(cells):
            mine = cols[c * cell : (c + 1) * cell]
            acc = None
            for step in range(2 * cells + 1):
                other = c + step
                local = other - cells
                target = lax.rem(first + local + cells_all, cells_all)
                listed = jnp.float32(0.0)
                for b in range(nb):
                    hit = (neighbours[c, b] == target) & (b < nbr_count[c])
                    listed = listed + jnp.where(hit, jnp.float32(1.0), jnp.float32(0.0))
                near = pos[other]
                d0 = mine[:, 0:1] - near[0:1]
                d1 = mine[:, 1:2] - near[1:2]
                d2 = mine[:, 2:3] - near[2:3]
                weight = jnp.exp(-0.125 * (d0 * d0 + d1 * d1 + d2 * d2)) * listed
                if step == cells:
                    weight = jnp.where(eye, 0.0, weight)
                part = dot3(split(weight), wide[other])
                acc = part if acc is None else acc + part
            gathered.append(acc)
        total = jnp.concatenate(gathered, axis=0)
        live = live_rows(counts, cells, cell)
        msg = 0.125 * dot3(split(total), split(w_msg[...]))
        out[...] = feats[...] + jnp.where(live, msg, 0.0)
        mask[...] = jnp.broadcast_to(jnp.where(live, 1.0, 0.0), mask.shape)

    return kernel


def finish():
    def kernel(base, mask, own, swap, a, b, c, w_one, w_two, out):
        spectral = ((own[...] + swap[...]) + (a[...] + b[...])) + c[...]
        u = base[...] + spectral.T
        normed = u / jnp.sqrt(jnp.mean(u * u, axis=1, keepdims=True) + 1e-06)
        v = dot3(split(normed), split(w_one[...]))
        hidden = v / (1.0 + jnp.exp(-v))
        out[...] = (u + dot3(split(hidden), split(w_two[...]))) * mask[:, 0:1]

    return kernel


def shift(axis, by):
    size = lax.axis_size(axis)
    return [(i, (i + by) % size) for i in range(size)]


def shards(
    feats, positions, cell_counts, neighbours, nbr_count, kvec, filters, w_msg, w_val, w_one, w_two
):
    cells = cell_counts.shape[0]
    slots, width = feats.shape
    cell = slots // cells
    devices = lax.axis_size(ROWS_WAVES)
    nx = lax.axis_size(X)
    rows = lax.axis_size("rows")
    group = lax.axis_size((Z, Y))
    own_waves = kvec.shape[1] // rows
    waves = own_waves * group
    half = lax.axis_index("rows").astype(jnp.int32)
    x = lax.axis_index(X).astype(jnp.int32)
    first = lax.axis_index(ROWS_WAVES).astype(jnp.int32) * cells

    tall = slots + 8
    payload = call(
        prepare(cells, cell),
        jax.ShapeDtypeStruct((tall, width), F32),
        3,
        [pltpu.SMEM((cells,), jnp.int32), pltpu.VMEM((3, slots), F32), pltpu.SemaphoreType.DMA((3,))],
        hbm=(0, 1, 2),
    )(cell_counts, feats, positions)
    near2 = lax.ppermute(payload, X, shift(X, 2))
    above = lax.ppermute(payload, X, shift(X, -1))
    below = lax.ppermute(payload, X, shift(X, 1))
    ends = [(d, (d + 1) % devices) for d in range(devices) if d % nx == nx - 1]
    ends = ends + [(b, a) for a, b in ends]
    edge = lax.ppermute(payload, ROWS_WAVES, ends)
    other = [lax.ppermute(payload, "rows", shift("rows", 1))]

    kt = lax.dynamic_slice_in_dim(kvec.T, half * own_waves, own_waves, 0) * (0.5 / math.pi)
    kt = jnp.pad(kt, ((0, 0), (0, 128 - kt.shape[1])))
    kt = lax.all_to_all(jnp.broadcast_to(kt[None], (group, *kt.shape)), (Z, Y), 0, 0, tiled=True)
    kt, near2, above, below, edge = lax.optimization_barrier((kt, near2, above, below, edge))
    kt = kt.reshape(waves, 128)

    line = (payload, above, below, near2)
    other += [lax.ppermute(c, "rows", shift("rows", 1)) for c in line[1:]]
    count = len(line)
    wide = jax.ShapeDtypeStruct((count, 2 * waves, slots), BF16)
    sums = jax.ShapeDtypeStruct((2 * waves, width), F32)
    part, *mine = call(forward(slots, count, own_waves, group, True), (sums, wide, wide), 2 + count)(
        kt, w_val, *line
    )
    part, *theirs = call(forward(slots, count, own_waves, group, False), (sums, wide, wide), 3 + count)(
        kt, w_val, *other, part
    )
    parts = lax.all_to_all(part.reshape(group, 2 * own_waves, width), (Z, Y), 0, 0, tiled=True)
    scale = 1.0 / math.sqrt(float(slots * devices) * float(waves * rows * nx))
    spread = call(filtered(scale), jax.ShapeDtypeStruct(parts.shape, F32), 3, smem=(0,))(
        half.reshape(1), parts, filters
    )
    f = lax.all_to_all(spread, (Z, Y), 0, 0, tiled=True).reshape(2 * waves, width)

    back = call(backward(count), jax.ShapeDtypeStruct((count, width, slots), F32), 3)
    swap = lax.ppermute(back(f, *theirs), "rows", shift("rows", 1))
    own = back(f, *mine)
    e3 = lax.ppermute(own[3] + swap[3], X, shift(X, 2))
    e1 = lax.ppermute(own[1] + swap[1], X, shift(X, 1))
    e2 = lax.ppermute(own[2] + swap[2], X, shift(X, -1))

    place = jnp.stack([x, jnp.int32(nx - 1), first])
    base, mask = call(
        messages(cells, cell, cells * devices, neighbours.shape[1]),
        (jax.ShapeDtypeStruct((slots, width), F32), jax.ShapeDtypeStruct((slots, 128), F32)),
        10,
        smem=(0, 1, 2, 3),
    )(place, neighbours, nbr_count, cell_counts, feats, payload, below, above, edge, w_msg)
    return call(finish(), jax.ShapeDtypeStruct((slots, width), F32), 9)(
        base, mask, own[0], swap[0], e1, e2, e3, w_one, w_two
    )


def solution(mesh):
    torus = Mesh(mesh.devices.reshape(mesh.shape["rows"], 4, 4, 4), ROWS_WAVES)
    return jax.shard_map(
        shards,
        mesh=torus,
        in_specs=(
            P(ROWS_WAVES, None),
            P(None, ROWS_WAVES),
            P(ROWS_WAVES),
            P(ROWS_WAVES, None),
            P(ROWS_WAVES),
            P(None, WAVES),
            P(WAVES, None),
            P(),
            P(),
            P(),
            P(),
        ),
        out_specs=P(ROWS_WAVES, None),
        check_vma=False,
    )
```

time: 112 us -> 100 us (0.89)
  blocking collectives: 44.7 us -> 32.9 us
  Pallas kernels: 22.7 us -> 14.9 us
  starting transfers between devices: 21.6 us -> 25.6 us
  local copies, waits for them, and re-layouts: 3.06 us -> 5.01 us
  other arithmetic: 0.31 us -> 1.77 us
    ppermute x1, waiting for transfers between devices: 13 us -> 0.01 us  [shards(): edge = lax.ppermute(payload, ROWS_WAVES, ends)]
    all_to_all x3 -> x2, blocking collectives: 44.7 us -> 32.9 us  [the longest x1 16.9 us: shards(): lax.all_to_all(part.reshape(group, 2 * own_waves, width), (Z, Y), 0, 0, t...]
    all_to_all x0 -> x1, waiting for transfers between devices: none -> 7.27 us  [shards(): lax.all_to_all(jnp.broadcast_to(kt[None], (group, *kt.shape)), (Z, Y), 0,...]
    pallas_call x6, Pallas kernels: 19.1 us -> 12 us  [the longest x1 4.01 us: shards(): call(forward(slots, count, own_waves, group, False), (sums, wide, wide),...]
    ppermute x1, starting transfers between devices: 4.89 us -> 11.7 us  [shards(): edge = lax.ppermute(payload, ROWS_WAVES, ends)]
    ppermute x1, waiting for transfers between devices: 0.01 us -> 6.53 us  [shards(): e2 = lax.ppermute(own[2] + swap[2], X, shift(X, -1))]
    ppermute x4, starting transfers between devices: 6.08 us -> 1.37 us  [the longest x3 0.93 us: shards(): other += [lax.ppermute(c, 'rows', shift('rows', 1)) for c in line[1:]]]
    ppermute x1, starting transfers between devices: 3.65 us -> 0.01 us  [shards(): near2 = lax.ppermute(payload, X, shift(X, 2))]
  transfers between devices with their start and end apart: 12 -> 13, of which waited for: 3 -> 5; matrix products, arithmetic and copies ran while one was open for 0% -> 2% of each run, Pallas kernels for 10% -> 7%
where the time goes in v2:
time: 100 us; the launch traced here: 99.8 us
  blocking collectives  32.9 us (33%)
  starting transfers between devices  25.6 us (26%)
  waiting for transfers between devices  19.5 us (20%)
  Pallas kernels  14.9 us (15%)
  local copies, waits for them, and re-layouts  5.01 us (5%)
  other arithmetic  1.77 us (2%)
    all_to_all x1, blocking collectives, shards(): lax.all_to_all(part.reshape(group, 2 * own_waves, width), (Z, Y), 0, 0, t...  16.9 us
    all_to_all x1, blocking collectives, shards(): lax.all_to_all(spread, (Z, Y), 0, 0, tiled=True).reshape(2 * waves, width)  16 us
    ppermute x1, starting transfers between devices, shards(): edge = lax.ppermute(payload, ROWS_WAVES, ends)  11.7 us
    all_to_all x1, waiting for transfers between devices, shards(): lax.all_to_all(jnp.broadcast_to(kt[None], (group, *kt.shape)), (Z, Y), 0,...  7.27 us
    ppermute x1, waiting for transfers between devices, shards(): e2 = lax.ppermute(own[2] + swap[2], X, shift(X, -1))  6.53 us
    unnamed x25, local copies, waits for them, and re-layouts  4.31 us
    pallas_call x1, Pallas kernels, shards(): call(forward(slots, count, own_waves, group, False), (sums, wide, wide),...  4.01 us
    pallas_call x1, Pallas kernels, shards(): call(forward(slots, count, own_waves, group, True), (sums, wide, wide), 2...  4 us
  transfers between devices with their start and end apart: 13, of which 5 were waited for; matrix products, arithmetic and copies ran while one was open for 2% of the time, Pallas kernels for 7%

profile of v2, /device:TPU:1, one launch (start us, length us, event | category | flops | bytes accessed | tf_op | source)
XLA Modules:
  0.0 99.8 jit_solution(935250975952817494)
XLA Ops:
  0.0 0.9 copy-done.1
  1.0 0.7 copy-done.7
  1.6 0.7 copy-done.8
  2.3 0.6 shard_map.109.own.refs_0_
  2.9 11.7 %collective-permute-start.3 = (f32[264,256]{1,0:T(8,128)S(1)}, f32[264,256]{1,0:T(8,128)S(1)}, u32[]{:S(2)}, u32[]{:S(2)}) collective-permute-start(f32[264,256]{1,0:T(8,128)S(1)} %shard_map.109.own.refs_0_), channel_id=1, source_target_pairs={{3,4},{7,8},{11,12},{15,16},{19,20},{23,24},{27,28},{31,32},{35,36... | collective-permute-start | bytes 811016 | tf_op jit(solution)/shard_map/ppermute | solution.py:243
  14.6 0.1 collective-permute-start.2
  14.7 2.7 %collective-permute-start.1 = (f32[264,256]{1,0:T(8,128)S(1)}, f32[264,256]{1,0:T(8,128)S(1)}, u32[]{:S(2)}, u32[]{:S(2)}) collective-permute-start(f32[264,256]{1,0:T(8,128)S(1)} %shard_map.109.own.refs_0_), channel_id=1, source_target_pairs={{0,3},{1,0},{2,1},{3,2},{4,7},{5,4},{6,5},{7,6},{8,11},{9,8},{10,9... | collective-permute-start | bytes 811016 | tf_op jit(solution)/shard_map/ppermute | solution.py:239
  17.4 0.0 collective-permute-start
  17.4 0.8 multiply_bitcast_fusion
  18.1 0.1 copy.13
  18.2 0.7 broadcast_in_dim.2
  18.9 3.5 %all-to-all-start = ((f32[16,24,128]{2,1,0:T(8,128)}), f32[16,24,128]{2,1,0:T(8,128)S(1)}, u32[]{:S(2)}, u32[]{:S(2)}) async-start(f32[16,24,128]{2,1,0:T(8,128)} %broadcast_in_dim.2), calls=%async_computation | async-start | bytes 393216 | tf_op jit(solution)/shard_map/all_to_all | solution.py:248
  22.5 0.4 collective-permute-start.4
  22.9 7.3 %all-to-all-done = f32[16,24,128]{2,1,0:T(8,128)S(1)} async-done(((f32[16,24,128]{2,1,0:T(8,128)}), f32[16,24,128]{2,1,0:T(8,128)S(1)}, u32[]{:S(2)}, u32[]{:S(2)}) %all-to-all-start) | async-done | bytes 196640 | tf_op jit(solution)/shard_map/all_to_all | solution.py:248
  30.2 0.0 collective-permute-done.2.low.refs_2_
  30.2 2.3 %collective-permute-done.1.high.refs_1_ = f32[264,256]{1,0:T(8,128)S(1)} collective-permute-done((f32[264,256]{1,0:T(8,128)S(1)}, f32[264,256]{1,0:T(8,128)S(1)}, u32[]{:S(2)}, u32[]{:S(2)}) %collective-permute-start.1) | collective-permute-done | bytes 270368 | tf_op jit(solution)/shard_map/ppermute | solution.py:239
  32.5 0.0 collective-permute-done.refs_3_
  32.5 0.4 collective-permute-start.7
  32.9 0.1 collective-permute-start.6
  33.0 0.4 collective-permute-start.5
  33.4 0.9 copy-done
  34.3 4.0 %shard_map.111 = (f32[768,256]{1,0:T(8,128)S(1)}, bf16[4,768,256]{2,1,0:T(8,128)(2,1)S(1)}, bf16[4,768,256]{2,1,0:T(8,128)(2,1)S(1)}) custom-call(f32[384,128]{1,0:T(8,128)S(1)} %bitcast.20, f32[256,256]{1,0:T(8,128)S(1)} %copy-done, f32[264,256]{1,0:T(8,128)S(1)} %shard_map.109.own.refs_0_, f32[264,256]{1,0:T(8,128)S(1)} %collective-permute-done.1.high.refs_1_, ...), custom_call_target="tpu_custom_call" | custom-call | tf_op jit(solution)/shard_map/pallas_call | solution.py:257
  38.3 0.0 collective-permute-done.4.refs_0_
  38.4 0.0 collective-permute-done.5.refs_1_
  38.4 0.0 copy-start.6
  38.4 4.0 %shard_map.112 = (f32[768,256]{1,0:T(8,128)S(1)}, bf16[4,768,256]{2,1,0:T(8,128)(2,1)S(1)}, bf16[4,768,256]{2,1,0:T(8,128)(2,1)S(1)}) custom-call(f32[384,128]{1,0:T(8,128)S(1)} %bitcast.21, f32[256,256]{1,0:T(8,128)S(1)} %copy-done, f32[264,256]{1,0:T(8,128)S(1)} %collective-permute-done.4.refs_0_, f32[264,256]{1,0:T(8,128)S(1)} %collective-permute-done.5.refs_1_, ...), custom_call_target="tpu_custom_call" | custom-call | tf_op jit(solution)/shard_map/pallas_call | solution.py:260
  42.4 16.9 %all_to_all.15.parts = f32[16,48,256]{2,1,0:T(8,128)S(1)} all-to-all(f32[16,48,256]{2,1,0:T(8,128)S(1)} %bitcast.22), channel_id=1, replica_groups=mesh['rows'=2,'waves_0'=4,'waves_1'=4,'waves_2'=4] {'waves_0','waves_1'}, dimensions={0} | all-to-all | bytes 1572864 | tf_op jit(solution)/shard_map/all_to_all | solution.py:263
  59.3 0.1 shard_map.113
  59.4 16.0 %all_to_all.16 = f32[16,48,256]{2,1,0:T(8,128)S(1)} all-to-all(f32[16,48,256]{2,1,0:T(8,128)S(1)} %shard_map.113), channel_id=1, replica_groups=mesh['rows'=2,'waves_0'=4,'waves_1'=4,'waves_2'=4] {'waves_0','waves_1'}, dimensions={0} | all-to-all | bytes 1572864 | tf_op jit(solution)/shard_map/all_to_all | solution.py:268
  75.4 1.4 %shard_map.115 = f32[4,256,256]{2,1,0:T(8,128)S(1)} custom-call(f32[768,256]{1,0:T(8,128)S(1)} %bitcast.18, bf16[4,768,256]{2,1,0:T(8,128)(2,1)S(1)} %get-tuple-element.29.mh, bf16[4,768,256]{2,1,0:T(8,128)(2,1)S(1)} %get-tuple-element.30.ml), custom_call_target="tpu_custom_call" | custom-call | tf_op jit(solution)/shard_map/pallas_call | solution.py:271
  76.9 2.4 %collective-permute-start.8 = (f32[4,256,256]{2,1,0:T(8,128)S(1)}, f32[4,256,256]{2,1,0:T(8,128)S(1)}, u32[]{:S(2)}, u32[]{:S(2)}) collective-permute-start(f32[4,256,256]{2,1,0:T(8,128)S(1)} %shard_map.115), channel_id=1, source_target_pairs={{0,64},{64,0},{1,65},{65,1},{2,66},{66,2},{3,67},{67,3},{4,68},{68... | collective-permute-start | bytes 3145736 | tf_op jit(solution)/shard_map/ppermute | solution.py:271
  79.2 1.4 %shard_map.114 = f32[4,256,256]{2,1,0:T(8,128)S(1)} custom-call(f32[768,256]{1,0:T(8,128)S(1)} %bitcast.19, bf16[4,768,256]{2,1,0:T(8,128)(2,1)S(1)} %get-tuple-element.27.mh, bf16[4,768,256]{2,1,0:T(8,128)(2,1)S(1)} %get-tuple-element.28.ml), custom_call_target="tpu_custom_call" | custom-call | tf_op jit(solution)/shard_map/pallas_call | solution.py:272
  80.6 0.0 copy-start.2
  80.7 0.0 copy-start.9
  80.7 0.0 copy-start.10
  80.7 0.0 copy-start.11
  80.7 0.8 collective-permute-done.8
  81.5 0.9 fusion
  82.5 1.6 %collective-permute-start.11 = (f32[256,256]{1,0:T(8,128)}, f32[256,256]{1,0:T(8,128)S(1)}, u32[]{:S(2)}, u32[]{:S(2)}) collective-permute-start(f32[256,256]{1,0:T(8,128)} %get-tuple-element.31), channel_id=1, source_target_pairs={{0,2},{1,3},{2,0},{3,1},{4,6},{5,7},{6,4},{7,5},{8,10},{9,11},{10,... | collective-permute-start | bytes 786440 | tf_op jit(solution)/shard_map/ppermute | solution.py:273
  84.0 1.8 %collective-permute-start.10 = (f32[256,256]{1,0:T(8,128)}, f32[256,256]{1,0:T(8,128)S(1)}, u32[]{:S(2)}, u32[]{:S(2)}) collective-permute-start(f32[256,256]{1,0:T(8,128)} %get-tuple-element.32), channel_id=1, source_target_pairs={{0,3},{1,0},{2,1},{3,2},{4,7},{5,4},{6,5},{7,6},{8,11},{9,8},{10,9... | collective-permute-start | bytes 786440 | tf_op jit(solution)/shard_map/ppermute | solution.py:275
  85.8 0.5 collective-permute-start.9
  86.3 0.1 pad_add_fusion.place
  86.4 0.0 copy-start.5
  86.4 0.9 copy-done.5
  87.4 1.8 %shard_map.110 = (f32[256,256]{1,0:T(8,128)S(1)}, f32[256,128]{1,0:T(8,128)S(1)}) custom-call(s32[3]{0:T(128)S(1)} %pad_add_fusion.place, s32[2,5]{1,0:T(2,128)S(1)} %copy-done.10, s32[2]{0:T(128)S(1)} %copy-done.11, s32[2]{0:T(128)S(1)} %copy-done.9, f32[256,256]{1,0:T(8,128)S(1)} %copy-done.2, f32[264,256]{1,0:T(8,128)S(1)} %shard_map.109.own.refs_0_, ...), custom_call_target="tpu_custom_call" | custom-call | tf_op jit(solution)/shard_map/pallas_call | solution.py:278
  89.1 2.6 %collective-permute-done.11.c = f32[256,256]{1,0:T(8,128)S(1)} collective-permute-done((f32[256,256]{1,0:T(8,128)}, f32[256,256]{1,0:T(8,128)S(1)}, u32[]{:S(2)}, u32[]{:S(2)}) %collective-permute-start.11) | collective-permute-done | bytes 262176 | tf_op jit(solution)/shard_map/ppermute | solution.py:273
  91.7 6.5 %collective-permute-done.10.b = f32[256,256]{1,0:T(8,128)S(1)} collective-permute-done((f32[256,256]{1,0:T(8,128)}, f32[256,256]{1,0:T(8,128)S(1)}, u32[]{:S(2)}, u32[]{:S(2)}) %collective-permute-start.10) | collective-permute-done | bytes 262176 | tf_op jit(solution)/shard_map/ppermute | solution.py:275
  98.3 1.6 %shard_map.116 = f32[256,256]{1,0:T(8,128)} custom-call(f32[256,256]{1,0:T(8,128)S(1)} %get-tuple-element.21.base, f32[256,128]{1,0:T(8,128)S(1)} %get-tuple-element.22.mask, f32[256,256]{1,0:T(8,128)S(1)} %get-tuple-element.34.own, f32[256,256]{1,0:T(8,128)S(1)} %get-tuple-element.35.swap, f32[256,256]{1,0:T(8,128)S(1)} %collective-permute-done.9.a, ...), custom_call_target="tpu_custom_call" | custom-call | tf_op jit(solution)/shard_map/pallas_call | solution.py:284
  (18 shorter events, 0.0 us)
Async XLA Ops:
  0.0 0.9 copy-start.1
  1.0 0.7 copy-start.7
  1.6 0.7 copy-start.8
  2.9 27.3 %collective-permute-start.3 = (f32[264,256]{1,0:T(8,128)S(1)}, f32[264,256]{1,0:T(8,128)S(1)}, u32[]{:S(2)}, u32[]{:S(2)}) collective-permute-start(f32[264,256]{1,0:T(8,128)S(1)} %shard_map.109.own.refs_0_), channel_id=1, source_target_pairs={{3,4},{7,8},{11,12},{15,16},{19,20},{23,24},{27,28},{31,32},{35,36... | collective-permute-start | bytes 811016 | tf_op jit(solution)/shard_map/ppermute | solution.py:243
  14.6 15.6 %collective-permute-start.2 = (f32[264,256]{1,0:T(8,128)S(1)}, f32[264,256]{1,0:T(8,128)S(1)}, u32[]{:S(2)}, u32[]{:S(2)}) collective-permute-start(f32[264,256]{1,0:T(8,128)S(1)} %shard_map.109.own.refs_0_), channel_id=1, source_target_pairs={{0,1},{1,2},{2,3},{3,0},{4,5},{5,6},{6,7},{7,4},{8,9},{9,10},{10,1... | collective-permute-start | bytes 811016 | tf_op jit(solution)/shard_map/ppermute | solution.py:240
  14.7 17.8 %collective-permute-start.1 = (f32[264,256]{1,0:T(8,128)S(1)}, f32[264,256]{1,0:T(8,128)S(1)}, u32[]{:S(2)}, u32[]{:S(2)}) collective-permute-start(f32[264,256]{1,0:T(8,128)S(1)} %shard_map.109.own.refs_0_), channel_id=1, source_target_pairs={{0,3},{1,0},{2,1},{3,2},{4,7},{5,4},{6,5},{7,6},{8,11},{9,8},{10,9... | collective-permute-start | bytes 811016 | tf_op jit(solution)/shard_map/ppermute | solution.py:239
  17.4 15.1 %collective-permute-start = (f32[264,256]{1,0:T(8,128)S(1)}, f32[264,256]{1,0:T(8,128)S(1)}, u32[]{:S(2)}, u32[]{:S(2)}) collective-permute-start(f32[264,256]{1,0:T(8,128)S(1)} %shard_map.109.own.refs_0_), channel_id=1, source_target_pairs={{0,2},{1,3},{2,0},{3,1},{4,6},{5,7},{6,4},{7,5},{8,10},{9,11},{10,... | collective-permute-start | bytes 811016 | tf_op jit(solution)/shard_map/ppermute | solution.py:238
  18.9 11.2 %all-to-all-start = ((f32[16,24,128]{2,1,0:T(8,128)}), f32[16,24,128]{2,1,0:T(8,128)S(1)}, u32[]{:S(2)}, u32[]{:S(2)}) async-start(f32[16,24,128]{2,1,0:T(8,128)} %broadcast_in_dim.2), calls=%async_computation | async-start | bytes 393216 | tf_op jit(solution)/shard_map/all_to_all | solution.py:248
  22.5 15.9 %collective-permute-start.4 = (f32[264,256]{1,0:T(8,128)S(1)}, f32[264,256]{1,0:T(8,128)S(1)}, u32[]{:S(2)}, u32[]{:S(2)}) collective-permute-start(f32[264,256]{1,0:T(8,128)S(1)} %shard_map.109.own.refs_0_), channel_id=1, source_target_pairs={{0,64},{64,0},{1,65},{65,1},{2,66},{66,2},{3,67},{67,3},{4,68},{68... | collective-permute-start | bytes 811016 | tf_op jit(solution)/shard_map/ppermute | solution.py:244
  32.5 5.9 %collective-permute-start.7 = (f32[264,256]{1,0:T(8,128)S(1)}, f32[264,256]{1,0:T(8,128)S(1)}, u32[]{:S(2)}, u32[]{:S(2)}) collective-permute-start(f32[264,256]{1,0:T(8,128)S(1)} %collective-permute-done.refs_3_), channel_id=1, source_target_pairs={{0,64},{64,0},{1,65},{65,1},{2,66},{66,2},{3,67},{67,3},{4,68},{68... | collective-permute-start | bytes 811016 | tf_op jit(solution)/shard_map/ppermute | solution.py:253
  32.9 5.5 %collective-permute-start.6 = (f32[264,256]{1,0:T(8,128)S(1)}, f32[264,256]{1,0:T(8,128)S(1)}, u32[]{:S(2)}, u32[]{:S(2)}) collective-permute-start(f32[264,256]{1,0:T(8,128)S(1)} %collective-permute-done.2.low.refs_2_), channel_id=1, source_target_pairs={{0,64},{64,0},{1,65},{65,1},{2,66},{66,2},{3,67},{67,3},{4,68},{68... | collective-permute-start | bytes 811016 | tf_op jit(solution)/shard_map/ppermute | solution.py:253
  33.0 5.4 %collective-permute-start.5 = (f32[264,256]{1,0:T(8,128)S(1)}, f32[264,256]{1,0:T(8,128)S(1)}, u32[]{:S(2)}, u32[]{:S(2)}) collective-permute-start(f32[264,256]{1,0:T(8,128)S(1)} %collective-permute-done.1.high.refs_1_), channel_id=1, source_target_pairs={{0,64},{64,0},{1,65},{65,1},{2,66},{66,2},{3,67},{67,3},{4,68},{68... | collective-permute-start | bytes 811016 | tf_op jit(solution)/shard_map/ppermute | solution.py:253
  33.4 0.9 copy-start
  38.4 20.9 %copy-start.6 = (f32[48,256]{1,0:T(8,128)S(1)}, f32[48,256]{1,0:T(8,128)}, u32[]{:S(2)}) copy-start(f32[48,256]{1,0:T(8,128)} %filters.1) | copy-start | bytes 147460
  76.9 4.7 %collective-permute-start.8 = (f32[4,256,256]{2,1,0:T(8,128)S(1)}, f32[4,256,256]{2,1,0:T(8,128)S(1)}, u32[]{:S(2)}, u32[]{:S(2)}) collective-permute-start(f32[4,256,256]{2,1,0:T(8,128)S(1)} %shard_map.115), channel_id=1, source_target_pairs={{0,64},{64,0},{1,65},{65,1},{2,66},{66,2},{3,67},{67,3},{4,68},{68... | collective-permute-start | bytes 3145736 | tf_op jit(solution)/shard_map/ppermute | solution.py:271
  80.6 5.8 %copy-start.2 = (f32[256,256]{1,0:T(8,128)S(1)}, f32[256,256]{1,0:T(8,128)}, u32[]{:S(2)}) copy-start(f32[256,256]{1,0:T(8,128)} %feats.3) | copy-start | bytes 786436
  80.7 5.7 %copy-start.9 = (s32[2]{0:T(128)S(1)}, s32[2]{0:T(128)}, u32[]{:S(2)}) copy-start(s32[2]{0:T(128)} %counts.3) | copy-start | bytes 28
  80.7 5.7 %copy-start.10 = (s32[2,5]{1,0:T(2,128)S(1)}, s32[2,5]{1,0:T(2,128)}, u32[]{:S(2)}) copy-start(s32[2,5]{1,0:T(2,128)} %neighbours.1) | copy-start | bytes 124
  80.7 5.7 %copy-start.11 = (s32[2]{0:T(128)S(1)}, s32[2]{0:T(128)}, u32[]{:S(2)}) copy-start(s32[2]{0:T(128)} %nbr_count.1) | copy-start | bytes 28
  82.5 15.8 %copy-start.3 = (f32[256,256]{1,0:T(8,128)S(1)}, f32[256,256]{1,0:T(8,128)}, u32[]{:S(2)}) copy-start(f32[256,256]{1,0:T(8,128)} %w_one.1) | copy-start | bytes 786436
  82.5 15.8 %copy-start.4 = (f32[256,256]{1,0:T(8,128)S(1)}, f32[256,256]{1,0:T(8,128)}, u32[]{:S(2)}) copy-start(f32[256,256]{1,0:T(8,128)} %w_two.1) | copy-start | bytes 786436
  82.5 9.3 %collective-permute-start.11 = (f32[256,256]{1,0:T(8,128)}, f32[256,256]{1,0:T(8,128)S(1)}, u32[]{:S(2)}, u32[]{:S(2)}) collective-permute-start(f32[256,256]{1,0:T(8,128)} %get-tuple-element.31), channel_id=1, source_target_pairs={{0,2},{1,3},{2,0},{3,1},{4,6},{5,7},{6,4},{7,5},{8,10},{9,11},{10,... | collective-permute-start | bytes 786440 | tf_op jit(solution)/shard_map/ppermute | solution.py:273
  84.0 14.2 %collective-permute-start.10 = (f32[256,256]{1,0:T(8,128)}, f32[256,256]{1,0:T(8,128)S(1)}, u32[]{:S(2)}, u32[]{:S(2)}) collective-permute-start(f32[256,256]{1,0:T(8,128)} %get-tuple-element.32), channel_id=1, source_target_pairs={{0,3},{1,0},{2,1},{3,2},{4,7},{5,4},{6,5},{7,6},{8,11},{9,8},{10,9... | collective-permute-start | bytes 786440 | tf_op jit(solution)/shard_map/ppermute | solution.py:275
  85.8 12.4 %collective-permute-start.9 = (f32[256,256]{1,0:T(8,128)}, f32[256,256]{1,0:T(8,128)S(1)}, u32[]{:S(2)}, u32[]{:S(2)}) collective-permute-start(f32[256,256]{1,0:T(8,128)} %get-tuple-element.33), channel_id=1, source_target_pairs={{0,1},{1,2},{2,3},{3,0},{4,5},{5,6},{6,7},{7,4},{8,9},{9,10},{10,1... | collective-permute-start | bytes 786440 | tf_op jit(solution)/shard_map/ppermute | solution.py:274
  86.4 1.0 copy-start.5

commit v3 on v2

v3 whole, which is shorter than its diff:
```python
import math

import jax
import jax.numpy as jnp
from jax import lax
from jax.experimental import pallas as pl
from jax.experimental.pallas import tpu as pltpu
from jax.sharding import Mesh
from jax.sharding import PartitionSpec as P

Z, Y, X = "waves_0", "waves_1", "waves_2"
WAVES = (Z, Y, X)
ROWS_WAVES = ("rows", Z, Y, X)
F32 = jnp.float32
BF16 = jnp.bfloat16

SIN_POLY = (6.283185280154403, -10.33542015333633, 5.100154773052372, -1.1965808225334407, 0.15531182448662934)
COS_POLY = (0.9999999997791529, -4.934802136928833, 4.058709154760502, -1.335211949366169, 0.23493706849740192, -0.0243959319559508)
ROUNDER = 12582912.0


def horner(coeffs, u):
    out = coeffs[-1]
    for c in coeffs[-2::-1]:
        out = out * u + c
    return out


def split(a):
    high = a.astype(BF16)
    return high, (a - high.astype(F32)).astype(BF16)


def thirds(a):
    high = a.astype(BF16).astype(F32)
    rest = a - high
    middle = rest.astype(BF16).astype(F32)
    return high, middle, rest - middle


def dot(a, b):
    return jnp.dot(a, b, preferred_element_type=F32)


def dot3(a, b):
    return dot(a[0], b[0]) + (dot(a[1], b[0]) + dot(a[0], b[1]))


def call(kernel, outs, n_in, scratch=(), smem=(), hbm=(), limit=40 << 20):
    def space(i):
        return pltpu.SMEM if i in smem else pltpu.HBM if i in hbm else pltpu.VMEM

    return pl.pallas_call(
        kernel,
        out_shape=outs,
        in_specs=[pl.BlockSpec(memory_space=space(i)) for i in range(n_in)],
        out_specs=jax.tree.map(lambda _: pl.BlockSpec(memory_space=pltpu.VMEM), outs),
        scratch_shapes=scratch,
        compiler_params=pltpu.CompilerParams(vmem_limit_bytes=limit),
    )


def live_rows(counts, cells, cell):
    row = lax.broadcasted_iota(jnp.int32, (cells * cell, 1), 0)
    limit = jnp.full(row.shape, counts[0])
    for c in range(1, cells):
        limit = jnp.where(row >= c * cell, c * cell + counts[c], limit)
    return row < limit


def assemble(own):
    def kernel(z, a, b, c, d, kt, filters, kv):
        kv[...] = jnp.zeros(kv.shape, F32)
        for j, ref in enumerate((a, b, c, d)):
            home = lax.rem(z[0] + j, 4)
            filters[pl.ds(pl.multiple_of(home * own, 8), own), :] = ref[:own]
            kv[...] += pltpu.roll(ref[own : own + 8, :128], home * own, 1)
        kt[...] = jnp.zeros(kt.shape, F32)
        kt[:, 0:8] = kv[...].T[: 4 * own]

    return kernel


def values(slots):
    def kernel(w_val, *refs):
        chunks, (vh, vl, where) = refs[:4], refs[4:]
        w = split(w_val[...])
        for j, chunk in enumerate(chunks):
            vh[j], vl[j] = split(dot3(split(chunk[:slots]), w))
            ph, pm, pl_ = thirds(chunk[slots : slots + 8])
            where[j] = jnp.concatenate([ph, pm, ph, pl_, pm, ph], axis=0).astype(BF16)

    return kernel


def forward(own):
    def kernel(ka, kb, vh0, vl0, at0, vh1, vl1, at1, sa, sb, mh0, ml0, mh1, ml1, acc):
        half = ka.shape[0]
        kh, km, kl = thirds(jnp.concatenate([ka[...], kb[...]], axis=0))
        lhs = kh
        for at, part in enumerate((kh, km, kh, km, kl)):
            lhs = lhs + pltpu.roll(part, 8 * (at + 1), 1)
        lhs = lhs[:, :48].astype(BF16)
        sides = ((vh0, vl0, at0, mh0, ml0), (vh1, vl1, at1, mh1, ml1))
        for side, (vh, vl, where, mh, ml) in enumerate(sides):
            for j in range(4):
                turns = dot(lhs, where[j])
                for g in range(2 * half // own):
                    t = turns[g * own : (g + 1) * own]
                    f = t - ((t + ROUNDER) - ROUNDER)
                    u = f * f
                    s = f * horner(SIN_POLY, u)
                    c = horner(COS_POLY, u)
                    both = jnp.concatenate([1.0 - 0.5 * (s * s), s * c], axis=0)
                    rows = slice(2 * own * g, 2 * own * (g + 1))
                    mh[j, rows], ml[j, rows] = split(both)
                part = dot3((mh[j], ml[j]), (vh[j], vl[j]))
                if side or j:
                    acc[...] += part
                else:
                    acc[...] = part
        sa[...] = acc[: 2 * half]
        sb[...] = acc[2 * half :]

    return kernel


def four(a, b, c, d, out):
    out[...] = (a[...] + b[...]) + (c[...] + d[...])


def filtered(own):
    def kernel(a, b, c, d, filters, out):
        total = (a[...] + b[...]) + (c[...] + d[...])
        for g in range(total.shape[0] // (2 * own)):
            f = filters[g * own : (g + 1) * own]
            for k in range(2):
                rows = slice((2 * g + k) * own, (2 * g + k + 1) * own)
                out[rows] = total[rows] * f

    return kernel


def backward(fa, fb, fc, fd, mha, mla, mhb, mlb, out):
    ft = split(jnp.concatenate([fa[...], fb[...], fc[...], fd[...]], axis=0).T)
    for j in range(out.shape[0]):
        mh = jnp.concatenate([mha[j], mhb[j]], axis=0)
        ml = jnp.concatenate([mla[j], mlb[j]], axis=0)
        out[j] = dot3(ft, (mh, ml))


def pairs(a, b, *outs):
    for j, out in enumerate(outs):
        out[...] = a[j] + b[j]


def messages(cells, cell, cells_all, nb):
    slots = cells * cell

    def kernel(place, neighbours, nbr_count, counts, feats, own, low, high, edge, w_msg, out, mask):
        x, last, first = place[0], place[1], place[2]
        lo = jnp.where(x == 0, edge[...], low[...])
        hi = jnp.where(x == last, edge[...], high[...])
        blocks = (lo, own[...], hi)
        parts = [split(b[:slots]) for b in blocks]
        wide = [tuple(p[k][c * cell : (c + 1) * cell] for k in range(2)) for p in parts for c in range(cells)]
        pos = [
            b[slots : slots + 3, c * cell : (c + 1) * cell] for b in blocks for c in range(cells)
        ]
        cols = own[slots : slots + 8].T
        eye = lax.broadcasted_iota(jnp.int32, (cell, cell), 0) == lax.broadcasted_iota(jnp.int32, (cell, cell), 1)
        gathered = []
        for c in range(cells):
            mine = cols[c * cell : (c + 1) * cell]
            acc = None
            for step in range(2 * cells + 1):
                other = c + step
                local = other - cells
                target = lax.rem(first + local + cells_all, cells_all)
                listed = jnp.float32(0.0)
                for b in range(nb):
                    hit = (neighbours[c, b] == target) & (b < nbr_count[c])
                    listed = listed + jnp.where(hit, jnp.float32(1.0), jnp.float32(0.0))
                near = pos[other]
                d0 = mine[:, 0:1] - near[0:1]
                d1 = mine[:, 1:2] - near[1:2]
                d2 = mine[:, 2:3] - near[2:3]
                weight = jnp.exp(-0.125 * (d0 * d0 + d1 * d1 + d2 * d2)) * listed
                if step == cells:
                    weight = jnp.where(eye, 0.0, weight)
                part = dot3(split(weight), wide[other])
                acc = part if acc is None else acc + part
            gathered.append(acc)
        total = jnp.concatenate(gathered, axis=0)
        live = live_rows(counts, cells, cell)
        msg = 0.125 * dot3(split(total), split(w_msg[...]))
        out[...] = feats[...] + jnp.where(live, msg, 0.0)
        mask[...] = jnp.broadcast_to(jnp.where(live, 1.0, 0.0), mask.shape)

    return kernel


def finish():
    def kernel(base, mask, own, a, b, c, w_one, w_two, out):
        spectral = (own[...] + a[...]) + (b[...] + c[...])
        u = base[...] + spectral.T
        normed = u / jnp.sqrt(jnp.mean(u * u, axis=1, keepdims=True) + 1e-06)
        v = dot3(split(normed), split(w_one[...]))
        hidden = v / (1.0 + jnp.exp(-v))
        out[...] = (u + dot3(split(hidden), split(w_two[...]))) * mask[:, 0:1]

    return kernel


def shift(axis, by):
    size = lax.axis_size(axis)
    return [(i, (i + by) % size) for i in range(size)]


def from_others(x, axis):
    return tuple(lax.ppermute(x, axis, shift(axis, by)) for by in (-1, 2, 1))


def shards(
    feats, positions, cell_counts, neighbours, nbr_count, kvec, filters, w_msg, w_val, w_one, w_two
):
    cells = cell_counts.shape[0]
    slots, width = feats.shape
    cell = slots // cells
    devices = lax.axis_size(ROWS_WAVES)
    nx = lax.axis_size(X)
    rows = lax.axis_size("rows")
    own = kvec.shape[1] // rows
    total_waves = kvec.shape[1] * lax.axis_size(WAVES)
    half = lax.axis_index("rows").astype(jnp.int32)
    x = lax.axis_index(X).astype(jnp.int32)
    z = lax.axis_index(Z).astype(jnp.int32)
    first = lax.axis_index(ROWS_WAVES).astype(jnp.int32) * cells

    def floats(*dims):
        return jax.ShapeDtypeStruct(dims, F32)

    def halves(*dims):
        return jax.ShapeDtypeStruct(dims, BF16)

    live = jnp.arange(cell, dtype=jnp.int32)[None, :] < cell_counts[:, None]
    masked = jnp.where(live.reshape(slots, 1), feats, 0.0)
    payload = jnp.pad(masked, ((0, 8), (0, 0))) + jnp.pad(positions, ((slots, 5), (0, 0)))
    above, near2, below = from_others(payload, X)
    ends = [(d, (d + 1) % devices) for d in range(devices) if d % nx == nx - 1]
    ends = ends + [(b, a) for a, b in ends]

    scale = 1.0 / math.sqrt(float(slots * devices) * float(total_waves))
    mine_k = lax.dynamic_slice_in_dim(kvec * (0.5 / math.pi), half * own, own, 1)
    mine_f = lax.dynamic_slice_in_dim(filters * scale, half * own, own, 0)
    home = jnp.pad(mine_f, ((0, 8), (0, 0))) + jnp.pad(mine_k, ((own, 5), (0, width - own)))
    k0, filt = call(
        assemble(own),
        (floats(4 * own, 128), floats(4 * own, width)),
        5,
        [pltpu.VMEM((8, 128), F32)],
        smem=(0,),
    )(z.reshape(1), home, *from_others(home, Z))
    k1, k2, k3 = from_others(k0, Y)

    line = (payload, above, near2, below)
    after = lax.optimization_barrier((k1, k2, k3, *line))[3:]
    other = tuple(lax.ppermute(c, "rows", shift("rows", 1)) for c in after)
    lists = (halves(4, slots, width), halves(4, slots, width), halves(4, 48, slots))
    v_mine = call(values(slots), lists, 5)(w_val, *line)
    v_theirs = call(values(slots), lists, 5)(w_val, *other)
    wide = (halves(4, 16 * own, slots),) * 4
    fwd = call(
        forward(own), (floats(8 * own, width),) * 2 + wide, 8, [pltpu.VMEM((16 * own, width), F32)]
    )
    s2, s1, *m_a = fwd(k2, k1, *v_mine, *v_theirs)
    t2 = lax.ppermute(s2, Y, shift(Y, 2))
    t1 = lax.ppermute(s1, Y, shift(Y, 1))
    edge = lax.ppermute(lax.optimization_barrier((s1, payload))[1], ROWS_WAVES, ends)
    s3, s0, *m_b = fwd(k3, k0, *v_mine, *v_theirs)
    t3 = lax.ppermute(s3, Y, shift(Y, -1))
    s0, edge = lax.optimization_barrier((s0, edge))
    plane = call(four, floats(8 * own, width), 4)(s0, t1, t2, t3)
    f0 = call(filtered(own), floats(8 * own, width), 5)(plane, *from_others(plane, Z), filt)
    f1, f2, f3 = from_others(f0, Y)

    back = call(backward, floats(4, width, slots), 8)
    swap = lax.ppermute(back(f2, f1, f3, f0, *m_a[2:], *m_b[2:]), "rows", shift("rows", 1))
    part = back(f2, f1, f3, f0, *m_a[:2], *m_b[:2])
    e0, e1, e2, e3 = call(pairs, (floats(width, slots),) * 4, 2)(part, swap)
    e2 = lax.ppermute(e2, X, shift(X, 2))
    e1 = lax.ppermute(e1, X, shift(X, 1))
    e3 = lax.ppermute(e3, X, shift(X, -1))

    place = jnp.stack([x, jnp.int32(nx - 1), first])
    base, mask = call(
        messages(cells, cell, cells * devices, neighbours.shape[1]),
        (floats(slots, width), floats(slots, 128)),
        10,
        smem=(0, 1, 2, 3),
    )(place, neighbours, nbr_count, cell_counts, feats, payload, below, above, edge, w_msg)
    return call(finish(), floats(slots, width), 8)(base, mask, e0, e1, e2, e3, w_one, w_two)


def solution(mesh):
    torus = Mesh(mesh.devices.reshape(mesh.shape["rows"], 4, 4, 4), ROWS_WAVES)
    return jax.shard_map(
        shards,
        mesh=torus,
        in_specs=(
            P(ROWS_WAVES, None),
            P(None, ROWS_WAVES),
            P(ROWS_WAVES),
            P(ROWS_WAVES, None),
            P(ROWS_WAVES),
            P(None, WAVES),
            P(WAVES, None),
            P(),
            P(),
            P(),
            P(),
        ),
        out_specs=P(ROWS_WAVES, None),
        check_vma=False,
    )
```

time: 100 us -> 107 us (1.070)
  blocking collectives: 32.9 us -> 0 us
  waiting for transfers between devices: 19.5 us -> 45.2 us
  starting transfers between devices: 25.6 us -> 42.5 us
  local copies, waits for them, and re-layouts: 5.01 us -> 0.71 us
  Pallas kernels: 14.9 us -> 16 us
    ppermute x12 -> x27, waiting for transfers between devices: 12.2 us -> 45.2 us  [the longest x15 27.4 us: from_others(): return tuple((lax.ppermute(x, axis, shift(axis, by)) for by in (-1, 2, 1)))]
    all_to_all x2 -> x0, blocking collectives: 32.9 us -> none  [the longest x1 16.9 us: shards(): lax.all_to_all(part.reshape(group, 2 * own_waves, width), (Z, Y), 0, 0, t...]
    ppermute x12 -> x27, starting transfers between devices: 22.1 us -> 42.5 us  [the longest x15 21.8 us: from_others(): return tuple((lax.ppermute(x, axis, shift(axis, by)) for by in (-1, 2, 1)))]
    all_to_all x1 -> x0, waiting for transfers between devices: 7.27 us -> none  [shards(): lax.all_to_all(jnp.broadcast_to(kt[None], (group, *kt.shape)), (Z, Y), 0,...]
    unnamed x25 -> x22, local copies, waits for them, and re-layouts: 4.31 us -> 0.64 us
    all_to_all x1 -> x0, starting transfers between devices: 3.52 us -> none  [shards(): lax.all_to_all(jnp.broadcast_to(kt[None], (group, *kt.shape)), (Z, Y), 0,...]
    pallas_call x8 -> x12, Pallas kernels: 14.9 us -> 16 us  [the longest x1 4.15 us: shards(): s3, s0, *m_b = fwd(k3, k0, *v_mine, *v_theirs)]
  transfers between devices with their start and end apart: 13 -> 27, of which waited for: 5 -> 20; matrix products, arithmetic and copies ran while one was open for 2% -> 0% of each run, Pallas kernels for 7% -> 8%
where the time goes in v3:
time: 107 us
  waiting for transfers between devices  45.2 us (42%)
  starting transfers between devices  42.5 us (40%)
  Pallas kernels  16 us (15%)
  other arithmetic  1.9 us (2%)
    ppermute x15, waiting for transfers between devices, from_others(): return tuple((lax.ppermute(x, axis, shift(axis, by)) for by in (-1, 2, 1)))  27.4 us
    ppermute x15, starting transfers between devices, from_others(): return tuple((lax.ppermute(x, axis, shift(axis, by)) for by in (-1, 2, 1)))  21.8 us
    ppermute x1, waiting for transfers between devices, shards(): e2 = lax.ppermute(e2, X, shift(X, 2))  6.48 us
    ppermute x1, starting transfers between devices, shards(): lax.ppermute(lax.optimization_barrier((s1, payload))[1], ROWS_WAVES, ends)  6.25 us
    ppermute x4, starting transfers between devices, shards(): other = tuple((lax.ppermute(c, 'rows', shift('rows', 1)) for c in after))  5.47 us
    ppermute x1, starting transfers between devices, shards(): e2 = lax.ppermute(e2, X, shift(X, 2))  4.6 us
    pallas_call x1, Pallas kernels, shards(): s3, s0, *m_b = fwd(k3, k0, *v_mine, *v_theirs)  4.15 us
    pallas_call x1, Pallas kernels, shards(): s2, s1, *m_a = fwd(k2, k1, *v_mine, *v_theirs)  4.15 us
  transfers between devices with their start and end apart: 27, of which 20 were waited for; matrix products, arithmetic and copies ran while one was open for 0% of the time, Pallas kernels for 8%

profile of v3, /device:TPU:1, one launch (start us, length us, event | category | flops | bytes accessed | tf_op | source)
XLA Modules:
  0.0 106.6 jit_solution(16408472410422446005)
XLA Ops:
  0.0 0.7 compare_bitcast_fusion
  0.7 1.1 broadcast_select_fusion
  1.9 2.1 %collective-permute-start = (f32[264,256]{1,0:T(8,128)S(1)}, f32[264,256]{1,0:T(8,128)S(1)}, u32[]{:S(2)}, u32[]{:S(2)}) collective-permute-start(f32[264,256]{1,0:T(8,128)S(1)} %pad_add_fusion.refs_0_.own), channel_id=1, source_target_pairs={{0,1},{1,2},{2,3},{3,0},{4,5},{5,6},{6,7},{7,4},{8,9},{9,10},{10,1... | collective-permute-start | bytes 811016 | tf_op jit(solution)/shard_map/ppermute | solution.py:221
  4.0 1.3 %collective-permute-start.1 = (f32[264,256]{1,0:T(8,128)S(1)}, f32[264,256]{1,0:T(8,128)S(1)}, u32[]{:S(2)}, u32[]{:S(2)}) collective-permute-start(f32[264,256]{1,0:T(8,128)S(1)} %pad_add_fusion.refs_0_.own), channel_id=1, source_target_pairs={{0,3},{1,0},{2,1},{3,2},{4,7},{5,4},{6,5},{7,6},{8,11},{9,8},{10,9... | collective-permute-start | bytes 811016 | tf_op jit(solution)/shard_map/ppermute | solution.py:221
  5.3 1.6 %collective-permute-start.6 = (f32[264,256]{1,0:T(8,128)S(1)}, f32[264,256]{1,0:T(8,128)S(1)}, u32[]{:S(2)}, u32[]{:S(2)}) collective-permute-start(f32[264,256]{1,0:T(8,128)S(1)} %pad_add_fusion.refs_0_.own), channel_id=1, source_target_pairs={{0,2},{1,3},{2,0},{3,1},{4,6},{5,7},{6,4},{7,5},{8,10},{9,11},{10,... | collective-permute-start | bytes 811016 | tf_op jit(solution)/shard_map/ppermute | solution.py:221
  7.1 3.8 %collective-permute-start.2 = (f32[32,256]{1,0:T(8,128)S(1)}, f32[32,256]{1,0:T(8,128)S(1)}, u32[]{:S(2)}, u32[]{:S(2)}) collective-permute-start(f32[32,256]{1,0:T(8,128)S(1)} %pad_add_fusion.1.a), channel_id=1, source_target_pairs={{0,48},{16,0},{32,16},{48,32},{1,49},{17,1},{33,17},{49,33},{2,50}... | collective-permute-start | bytes 98312 | tf_op jit(solution)/shard_map/ppermute | solution.py:221
  10.9 1.0 collective-permute-done.2.b
  12.0 3.4 %collective-permute-done.3.c = f32[32,256]{1,0:T(8,128)S(1)} collective-permute-done((f32[32,256]{1,0:T(8,128)S(1)}, f32[32,256]{1,0:T(8,128)S(1)}, u32[]{:S(2)}, u32[]{:S(2)}) %collective-permute-start.3) | collective-permute-done | bytes 32800 | tf_op jit(solution)/shard_map/ppermute | solution.py:221
  15.5 1.3 %collective-permute-done.4.d = f32[32,256]{1,0:T(8,128)S(1)} collective-permute-done((f32[32,256]{1,0:T(8,128)S(1)}, f32[32,256]{1,0:T(8,128)S(1)}, u32[]{:S(2)}, u32[]{:S(2)}) %collective-permute-start.4) | collective-permute-done | bytes 32800 | tf_op jit(solution)/shard_map/ppermute | solution.py:221
  16.9 1.4 %collective-permute-start.5 = (f32[96,128]{1,0:T(8,128)S(1)}, f32[96,128]{1,0:T(8,128)S(1)}, u32[]{:S(2)}, u32[]{:S(2)}) collective-permute-start(f32[96,128]{1,0:T(8,128)S(1)} %get-tuple-element.38.kb), channel_id=1, source_target_pairs={{0,4},{4,8},{8,12},{12,0},{1,5},{5,9},{9,13},{13,1},{2,6},{6,10},{... | collective-permute-start | bytes 147464 | tf_op jit(solution)/shard_map/ppermute | solution.py:221
  18.3 1.5 %collective-permute-start.7 = (f32[96,128]{1,0:T(8,128)S(1)}, f32[96,128]{1,0:T(8,128)S(1)}, u32[]{:S(2)}, u32[]{:S(2)}) collective-permute-start(f32[96,128]{1,0:T(8,128)S(1)} %get-tuple-element.38.kb), channel_id=1, source_target_pairs={{0,12},{4,0},{8,4},{12,8},{1,13},{5,1},{9,5},{13,9},{2,14},{6,2},{... | collective-permute-start | bytes 147464 | tf_op jit(solution)/shard_map/ppermute | solution.py:221
  19.8 1.4 %collective-permute-done.5.ka = f32[96,128]{1,0:T(8,128)S(1)} collective-permute-done((f32[96,128]{1,0:T(8,128)S(1)}, f32[96,128]{1,0:T(8,128)S(1)}, u32[]{:S(2)}, u32[]{:S(2)}) %collective-permute-start.5) | collective-permute-done | bytes 49184 | tf_op jit(solution)/shard_map/ppermute | solution.py:221
  21.2 1.6 %collective-permute-start.8 = (f32[96,128]{1,0:T(8,128)S(1)}, f32[96,128]{1,0:T(8,128)S(1)}, u32[]{:S(2)}, u32[]{:S(2)}) collective-permute-start(f32[96,128]{1,0:T(8,128)S(1)} %get-tuple-element.38.kb), channel_id=1, source_target_pairs={{0,8},{4,12},{8,0},{12,4},{1,9},{5,13},{9,1},{13,5},{2,10},{6,14},... | collective-permute-start | bytes 147464 | tf_op jit(solution)/shard_map/ppermute | solution.py:221
  22.9 3.2 %collective-permute-done.8.ka = f32[96,128]{1,0:T(8,128)S(1)} collective-permute-done((f32[96,128]{1,0:T(8,128)S(1)}, f32[96,128]{1,0:T(8,128)S(1)}, u32[]{:S(2)}, u32[]{:S(2)}) %collective-permute-start.8) | collective-permute-done | bytes 49184 | tf_op jit(solution)/shard_map/ppermute | solution.py:221
  26.1 4.9 %collective-permute-start.9 = (f32[264,256]{1,0:T(8,128)S(1)}, f32[264,256]{1,0:T(8,128)S(1)}, u32[]{:S(2)}, u32[]{:S(2)}) collective-permute-start(f32[264,256]{1,0:T(8,128)S(1)} %pad_add_fusion.refs_0_.own), channel_id=1, source_target_pairs={{0,64},{64,0},{1,65},{65,1},{2,66},{66,2},{3,67},{67,3},{4,68},{68... | collective-permute-start | bytes 811016 | tf_op jit(solution)/shard_map/ppermute | solution.py:268
  31.0 0.4 collective-permute-start.11
  31.6 0.6 shard_map.110
  32.2 0.3 collective-permute-done.10.refs_1_
  32.5 0.4 collective-permute-done.11.refs_2_
  32.9 0.4 collective-permute-done.12.refs_3_
  33.3 0.6 shard_map.111
  33.9 4.2 %shard_map.113 = (f32[192,256]{1,0:T(8,128)S(1)}, f32[192,256]{1,0:T(8,128)S(1)}, bf16[4,384,256]{2,1,0:T(8,128)(2,1)S(1)}, bf16[4,384,256]{2,1,0:T(8,128)(2,1)S...) custom-call(f32[96,128]{1,0:T(8,128)S(1)} %collective-permute-done.8.ka, ...), custom_call_target="tpu_custom_call" | custom-call | tf_op jit(solution)/shard_map/pallas_call | solution.py:276
  38.1 6.2 %collective-permute-start.13 = (f32[264,256]{1,0:T(8,128)S(1)}, f32[264,256]{1,0:T(8,128)S(1)}, u32[]{:S(2)}, u32[]{:S(2)}) collective-permute-start(f32[264,256]{1,0:T(8,128)S(1)} %pad_add_fusion.refs_0_.own), channel_id=1, source_target_pairs={{3,4},{7,8},{11,12},{15,16},{19,20},{23,24},{27,28},{31,32},{35,36... | collective-permute-start | bytes 811016 | tf_op jit(solution)/shard_map/ppermute | solution.py:279
  44.5 4.2 %shard_map.112 = (f32[192,256]{1,0:T(8,128)S(1)}, f32[192,256]{1,0:T(8,128)S(1)}, bf16[4,384,256]{2,1,0:T(8,128)(2,1)S(1)}, bf16[4,384,256]{2,1,0:T(8,128)(2,1)S...) custom-call(f32[96,128]{1,0:T(8,128)S(1)} %collective-permute-done.5.ka, ...), custom_call_target="tpu_custom_call" | custom-call | tf_op jit(solution)/shard_map/pallas_call | solution.py:280
  48.7 2.8 %collective-permute-start.16 = (f32[192,256]{1,0:T(8,128)S(1)}, f32[192,256]{1,0:T(8,128)S(1)}, u32[]{:S(2)}, u32[]{:S(2)}) collective-permute-start(f32[192,256]{1,0:T(8,128)S(1)} %get-tuple-element.57), channel_id=1, source_target_pairs={{0,12},{4,0},{8,4},{12,8},{1,13},{5,1},{9,5},{13,9},{2,14},{6,2},{... | collective-permute-start | bytes 589832 | tf_op jit(solution)/shard_map/ppermute | solution.py:281
  51.5 2.5 %collective-permute-done.13.edge = f32[264,256]{1,0:T(8,128)S(1)} collective-permute-done((f32[264,256]{1,0:T(8,128)S(1)}, f32[264,256]{1,0:T(8,128)S(1)}, u32[]{:S(2)}, u32[]{:S(2)}) %collective-permute-start.13) | collective-permute-done | bytes 270368 | tf_op jit(solution)/shard_map/ppermute | solution.py:279
  54.0 0.4 collective-permute-done.14.b
  54.4 3.8 %collective-permute-done.15.c = f32[192,256]{1,0:T(8,128)S(1)} collective-permute-done((f32[192,256]{1,0:T(8,128)S(1)}, f32[192,256]{1,0:T(8,128)S(1)}, u32[]{:S(2)}, u32[]{:S(2)}) %collective-permute-start.15) | collective-permute-done | bytes 196640 | tf_op jit(solution)/shard_map/ppermute | solution.py:277
  58.2 1.8 %collective-permute-start.17 = (f32[192,256]{1,0:T(8,128)S(1)}, f32[192,256]{1,0:T(8,128)S(1)}, u32[]{:S(2)}, u32[]{:S(2)}) collective-permute-start(f32[192,256]{1,0:T(8,128)S(1)} %shard_map.115.a), channel_id=1, source_target_pairs={{0,48},{16,0},{32,16},{48,32},{1,49},{17,1},{33,17},{49,33},{2,50}... | collective-permute-start | bytes 589832 | tf_op jit(solution)/shard_map/ppermute | solution.py:221
  60.0 2.3 %collective-permute-start.18 = (f32[192,256]{1,0:T(8,128)S(1)}, f32[192,256]{1,0:T(8,128)S(1)}, u32[]{:S(2)}, u32[]{:S(2)}) collective-permute-start(f32[192,256]{1,0:T(8,128)S(1)} %shard_map.115.a), channel_id=1, source_target_pairs={{0,32},{16,48},{32,0},{48,16},{1,33},{17,49},{33,1},{49,17},{2,34}... | collective-permute-start | bytes 589832 | tf_op jit(solution)/shard_map/ppermute | solution.py:221
  62.3 2.5 %collective-permute-done.17.b = f32[192,256]{1,0:T(8,128)S(1)} collective-permute-done((f32[192,256]{1,0:T(8,128)S(1)}, f32[192,256]{1,0:T(8,128)S(1)}, u32[]{:S(2)}, u32[]{:S(2)}) %collective-permute-start.17) | collective-permute-done | bytes 196640 | tf_op jit(solution)/shard_map/ppermute | solution.py:221
  64.8 1.3 %collective-permute-done.18.c = f32[192,256]{1,0:T(8,128)S(1)} collective-permute-done((f32[192,256]{1,0:T(8,128)S(1)}, f32[192,256]{1,0:T(8,128)S(1)}, u32[]{:S(2)}, u32[]{:S(2)}) %collective-permute-start.18) | collective-permute-done | bytes 196640 | tf_op jit(solution)/shard_map/ppermute | solution.py:221
  66.1 5.5 %collective-permute-done.19.d = f32[192,256]{1,0:T(8,128)S(1)} collective-permute-done((f32[192,256]{1,0:T(8,128)S(1)}, f32[192,256]{1,0:T(8,128)S(1)}, u32[]{:S(2)}, u32[]{:S(2)}) %collective-permute-start.19) | collective-permute-done | bytes 196640 | tf_op jit(solution)/shard_map/ppermute | solution.py:221
  71.6 2.7 %collective-permute-start.20 = (f32[192,256]{1,0:T(8,128)S(1)}, f32[192,256]{1,0:T(8,128)S(1)}, u32[]{:S(2)}, u32[]{:S(2)}) collective-permute-start(f32[192,256]{1,0:T(8,128)S(1)} %shard_map.116.fd), channel_id=1, source_target_pairs={{0,8},{4,12},{8,0},{12,4},{1,9},{5,13},{9,1},{13,5},{2,10},{6,14},... | collective-permute-start | bytes 589832 | tf_op jit(solution)/shard_map/ppermute | solution.py:221
  74.3 1.5 %collective-permute-start.22 = (f32[192,256]{1,0:T(8,128)S(1)}, f32[192,256]{1,0:T(8,128)S(1)}, u32[]{:S(2)}, u32[]{:S(2)}) collective-permute-start(f32[192,256]{1,0:T(8,128)S(1)} %shard_map.116.fd), channel_id=1, source_target_pairs={{0,4},{4,8},{8,12},{12,0},{1,5},{5,9},{9,13},{13,1},{2,6},{6,10},{... | collective-permute-start | bytes 589832 | tf_op jit(solution)/shard_map/ppermute | solution.py:221
  75.7 2.3 %collective-permute-done.20.fa = f32[192,256]{1,0:T(8,128)S(1)} collective-permute-done((f32[192,256]{1,0:T(8,128)S(1)}, f32[192,256]{1,0:T(8,128)S(1)}, u32[]{:S(2)}, u32[]{:S(2)}) %collective-permute-start.20) | collective-permute-done | bytes 196640 | tf_op jit(solution)/shard_map/ppermute | solution.py:221
  78.0 1.6 %collective-permute-done.21.fb = f32[192,256]{1,0:T(8,128)S(1)} collective-permute-done((f32[192,256]{1,0:T(8,128)S(1)}, f32[192,256]{1,0:T(8,128)S(1)}, u32[]{:S(2)}, u32[]{:S(2)}) %collective-permute-start.21) | collective-permute-done | bytes 196640 | tf_op jit(solution)/shard_map/ppermute | solution.py:221
  79.6 4.0 %collective-permute-done.22.fc = f32[192,256]{1,0:T(8,128)S(1)} collective-permute-done((f32[192,256]{1,0:T(8,128)S(1)}, f32[192,256]{1,0:T(8,128)S(1)}, u32[]{:S(2)}, u32[]{:S(2)}) %collective-permute-start.22) | collective-permute-done | bytes 196640 | tf_op jit(solution)/shard_map/ppermute | solution.py:221
  83.5 1.4 %shard_map.118 = f32[4,256,256]{2,1,0:T(8,128)S(1)} custom-call(f32[192,256]{1,0:T(8,128)S(1)} %collective-permute-done.20.fa, f32[192,256]{1,0:T(8,128)S(1)} %collective-permute-done.21.fb, f32[192,256]{1,0:T(8,128)S(1)} %collective-permute-done.22.fc, f32[192,256]{1,0:T(8,128)S(1)} %shard_map.116.fd, bf16[4,384,256]{2,1,0:T(8,128)(2,1)S(1)} %get-tuple-element.63.mha, ...), custom_call_target="tpu_custom_call" | custom-call | tf_op jit(solution)/shard_map/pallas_call | solution.py:288
  85.0 1.3 %collective-permute-start.23 = (f32[4,256,256]{2,1,0:T(8,128)S(1)}, f32[4,256,256]{2,1,0:T(8,128)S(1)}, u32[]{:S(2)}, u32[]{:S(2)}) collective-permute-start(f32[4,256,256]{2,1,0:T(8,128)S(1)} %shard_map.118), channel_id=1, source_target_pairs={{0,64},{64,0},{1,65},{65,1},{2,66},{66,2},{3,67},{67,3},{4,68},{68... | collective-permute-start | bytes 3145736 | tf_op jit(solution)/shard_map/ppermute | solution.py:288
  86.3 1.4 %shard_map.117.a = f32[4,256,256]{2,1,0:T(8,128)S(1)} custom-call(f32[192,256]{1,0:T(8,128)S(1)} %collective-permute-done.20.fa, f32[192,256]{1,0:T(8,128)S(1)} %collective-permute-done.21.fb, f32[192,256]{1,0:T(8,128)S(1)} %collective-permute-done.22.fc, f32[192,256]{1,0:T(8,128)S(1)} %shard_map.116.fd, bf16[4,384,256]{2,1,0:T(8,128)(2,1)S(1)} %get-tuple-element.59.mha, ...), custom_call_target="tpu_custom_call" | custom-call | tf_op jit(solution)/shard_map/pallas_call | solution.py:289
  87.7 0.8 collective-permute-done.23.b
  88.8 4.6 %collective-permute-start.25 = (f32[256,256]{1,0:T(8,128)S(1)}, f32[256,256]{1,0:T(8,128)S(1)}, u32[]{:S(2)}, u32[]{:S(2)}) collective-permute-start(f32[256,256]{1,0:T(8,128)S(1)} %get-tuple-element.69), channel_id=1, source_target_pairs={{0,2},{1,3},{2,0},{3,1},{4,6},{5,7},{6,4},{7,5},{8,10},{9,11},{10,... | collective-permute-start | bytes 786440 | tf_op jit(solution)/shard_map/ppermute | solution.py:291
  93.5 0.6 copy-done.5
  94.1 1.8 %shard_map.114 = (f32[256,256]{1,0:T(8,128)S(1)}, f32[256,128]{1,0:T(8,128)S(1)}) custom-call(s32[3]{0:T(128)S(1)} %pad_add_fusion.2.place, s32[2,5]{1,0:T(2,128)S(1)} %copy-done.5, s32[2]{0:T(128)S(1)} %copy-done.6, s32[2]{0:T(128)S(1)} %copy-done.7, f32[256,256]{1,0:T(8,128)S(1)} %copy-done, f32[264,256]{1,0:T(8,128)S(1)} %pad_add_fusion.refs_0_.own, ...), custom_call_target="tpu_custom_call" | custom-call | tf_op jit(solution)/shard_map/pallas_call | solution.py:296
  95.8 2.7 %collective-permute-done.24.a = f32[256,256]{1,0:T(8,128)S(1)} collective-permute-done((f32[256,256]{1,0:T(8,128)S(1)}, f32[256,256]{1,0:T(8,128)S(1)}, u32[]{:S(2)}, u32[]{:S(2)}) %collective-permute-start.24) | collective-permute-done | bytes 262176 | tf_op jit(solution)/shard_map/ppermute | solution.py:292
  98.6 6.5 %collective-permute-done.25.b = f32[256,256]{1,0:T(8,128)S(1)} collective-permute-done((f32[256,256]{1,0:T(8,128)S(1)}, f32[256,256]{1,0:T(8,128)S(1)}, u32[]{:S(2)}, u32[]{:S(2)}) %collective-permute-start.25) | collective-permute-done | bytes 262176 | tf_op jit(solution)/shard_map/ppermute | solution.py:291
  105.0 1.5 %shard_map.120 = f32[256,256]{1,0:T(8,128)} custom-call(f32[256,256]{1,0:T(8,128)S(1)} %get-tuple-element.53.base, f32[256,128]{1,0:T(8,128)S(1)} %get-tuple-element.54.mask, f32[256,256]{1,0:T(8,128)S(1)} %get-tuple-element.67.own, f32[256,256]{1,0:T(8,128)S(1)} %collective-permute-done.24.a, f32[256,256]{1,0:T(8,128)S(1)} %collective-permute-done.25.b, ...), custom_call_target="tpu_custom_call" | custom-call | tf_op jit(solution)/shard_map/pallas_call | solution.py:302
  (48 shorter events, 1.2 us)
Async XLA Ops:
  0.7 1.1 %copy-start.9 = (f32[3,256]{1,0:T(4,128)S(1)}, f32[3,256]{1,0:T(4,128)}, u32[]{:S(2)}) copy-start(f32[3,256]{1,0:T(4,128)} %param.12) | copy-start | bytes 9220
  1.8 5.2 %copy-start.10 = (f32[3,48]{1,0:T(4,128)S(1)}, f32[3,48]{1,0:T(4,128)}, u32[]{:S(2)}) copy-start(f32[3,48]{1,0:T(4,128)} %param.16) | copy-start | bytes 1732
  1.8 5.2 %copy-start.8 = (f32[48,256]{1,0:T(8,128)S(1)}, f32[48,256]{1,0:T(8,128)}, u32[]{:S(2)}) copy-start(f32[48,256]{1,0:T(8,128)} %param.17) | copy-start | bytes 147460
  1.9 29.7 %copy-start.1 = (f32[256,256]{1,0:T(8,128)S(1)}, f32[256,256]{1,0:T(8,128)}, u32[]{:S(2)}) copy-start(f32[256,256]{1,0:T(8,128)} %w_val.3) | copy-start | bytes 786436
  1.9 24.2 %collective-permute-start = (f32[264,256]{1,0:T(8,128)S(1)}, f32[264,256]{1,0:T(8,128)S(1)}, u32[]{:S(2)}, u32[]{:S(2)}) collective-permute-start(f32[264,256]{1,0:T(8,128)S(1)} %pad_add_fusion.refs_0_.own), channel_id=1, source_target_pairs={{0,1},{1,2},{2,3},{3,0},{4,5},{5,6},{6,7},{7,4},{8,9},{9,10},{10,1... | collective-permute-start | bytes 811016 | tf_op jit(solution)/shard_map/ppermute | solution.py:221
  4.0 22.1 %collective-permute-start.1 = (f32[264,256]{1,0:T(8,128)S(1)}, f32[264,256]{1,0:T(8,128)S(1)}, u32[]{:S(2)}, u32[]{:S(2)}) collective-permute-start(f32[264,256]{1,0:T(8,128)S(1)} %pad_add_fusion.refs_0_.own), channel_id=1, source_target_pairs={{0,3},{1,0},{2,1},{3,2},{4,7},{5,4},{6,5},{7,6},{8,11},{9,8},{10,9... | collective-permute-start | bytes 811016 | tf_op jit(solution)/shard_map/ppermute | solution.py:221
  5.3 20.7 %collective-permute-start.6 = (f32[264,256]{1,0:T(8,128)S(1)}, f32[264,256]{1,0:T(8,128)S(1)}, u32[]{:S(2)}, u32[]{:S(2)}) collective-permute-start(f32[264,256]{1,0:T(8,128)S(1)} %pad_add_fusion.refs_0_.own), channel_id=1, source_target_pairs={{0,2},{1,3},{2,0},{3,1},{4,6},{5,7},{6,4},{7,5},{8,10},{9,11},{10,... | collective-permute-start | bytes 811016 | tf_op jit(solution)/shard_map/ppermute | solution.py:221
  7.1 4.9 %collective-permute-start.2 = (f32[32,256]{1,0:T(8,128)S(1)}, f32[32,256]{1,0:T(8,128)S(1)}, u32[]{:S(2)}, u32[]{:S(2)}) collective-permute-start(f32[32,256]{1,0:T(8,128)S(1)} %pad_add_fusion.1.a), channel_id=1, source_target_pairs={{0,48},{16,0},{32,16},{48,32},{1,49},{17,1},{33,17},{49,33},{2,50}... | collective-permute-start | bytes 98312 | tf_op jit(solution)/shard_map/ppermute | solution.py:221
  10.9 4.6 %collective-permute-start.3 = (f32[32,256]{1,0:T(8,128)S(1)}, f32[32,256]{1,0:T(8,128)S(1)}, u32[]{:S(2)}, u32[]{:S(2)}) collective-permute-start(f32[32,256]{1,0:T(8,128)S(1)} %pad_add_fusion.1.a), channel_id=1, source_target_pairs={{0,32},{16,48},{32,0},{48,16},{1,33},{17,49},{33,1},{49,17},{2,34}... | collective-permute-start | bytes 98312 | tf_op jit(solution)/shard_map/ppermute | solution.py:221
  11.9 4.8 %collective-permute-start.4 = (f32[32,256]{1,0:T(8,128)S(1)}, f32[32,256]{1,0:T(8,128)S(1)}, u32[]{:S(2)}, u32[]{:S(2)}) collective-permute-start(f32[32,256]{1,0:T(8,128)S(1)} %pad_add_fusion.1.a), channel_id=1, source_target_pairs={{0,16},{16,32},{32,48},{48,0},{1,17},{17,33},{33,49},{49,1},{2,18}... | collective-permute-start | bytes 98312 | tf_op jit(solution)/shard_map/ppermute | solution.py:221
  16.9 4.3 %collective-permute-start.5 = (f32[96,128]{1,0:T(8,128)S(1)}, f32[96,128]{1,0:T(8,128)S(1)}, u32[]{:S(2)}, u32[]{:S(2)}) collective-permute-start(f32[96,128]{1,0:T(8,128)S(1)} %get-tuple-element.38.kb), channel_id=1, source_target_pairs={{0,4},{4,8},{8,12},{12,0},{1,5},{5,9},{9,13},{13,1},{2,6},{6,10},{... | collective-permute-start | bytes 147464 | tf_op jit(solution)/shard_map/ppermute | solution.py:221
  18.3 4.6 %collective-permute-start.7 = (f32[96,128]{1,0:T(8,128)S(1)}, f32[96,128]{1,0:T(8,128)S(1)}, u32[]{:S(2)}, u32[]{:S(2)}) collective-permute-start(f32[96,128]{1,0:T(8,128)S(1)} %get-tuple-element.38.kb), channel_id=1, source_target_pairs={{0,12},{4,0},{8,4},{12,8},{1,13},{5,1},{9,5},{13,9},{2,14},{6,2},{... | collective-permute-start | bytes 147464 | tf_op jit(solution)/shard_map/ppermute | solution.py:221
  21.2 4.8 %collective-permute-start.8 = (f32[96,128]{1,0:T(8,128)S(1)}, f32[96,128]{1,0:T(8,128)S(1)}, u32[]{:S(2)}, u32[]{:S(2)}) collective-permute-start(f32[96,128]{1,0:T(8,128)S(1)} %get-tuple-element.38.kb), channel_id=1, source_target_pairs={{0,8},{4,12},{8,0},{12,4},{1,9},{5,13},{9,1},{13,5},{2,10},{6,14},... | collective-permute-start | bytes 147464 | tf_op jit(solution)/shard_map/ppermute | solution.py:221
  26.1 6.1 %collective-permute-start.9 = (f32[264,256]{1,0:T(8,128)S(1)}, f32[264,256]{1,0:T(8,128)S(1)}, u32[]{:S(2)}, u32[]{:S(2)}) collective-permute-start(f32[264,256]{1,0:T(8,128)S(1)} %pad_add_fusion.refs_0_.own), channel_id=1, source_target_pairs={{0,64},{64,0},{1,65},{65,1},{2,66},{66,2},{3,67},{67,3},{4,68},{68... | collective-permute-start | bytes 811016 | tf_op jit(solution)/shard_map/ppermute | solution.py:268
  30.9 1.6 %collective-permute-start.10 = (f32[264,256]{1,0:T(8,128)S(1)}, f32[264,256]{1,0:T(8,128)S(1)}, u32[]{:S(2)}, u32[]{:S(2)}) collective-permute-start(f32[264,256]{1,0:T(8,128)S(1)} %collective-permute-done.1.refs_1_.high), channel_id=1, source_target_pairs={{0,64},{64,0},{1,65},{65,1},{2,66},{66,2},{3,67},{67,3},{4,68},{68... | collective-permute-start | bytes 811016 | tf_op jit(solution)/shard_map/ppermute | solution.py:268
  31.0 1.9 %collective-permute-start.11 = (f32[264,256]{1,0:T(8,128)S(1)}, f32[264,256]{1,0:T(8,128)S(1)}, u32[]{:S(2)}, u32[]{:S(2)}) collective-permute-start(f32[264,256]{1,0:T(8,128)S(1)} %collective-permute-done.6.refs_2_), channel_id=1, source_target_pairs={{0,64},{64,0},{1,65},{65,1},{2,66},{66,2},{3,67},{67,3},{4,68},{68... | collective-permute-start | bytes 811016 | tf_op jit(solution)/shard_map/ppermute | solution.py:268
  31.5 1.8 %collective-permute-start.12 = (f32[264,256]{1,0:T(8,128)S(1)}, f32[264,256]{1,0:T(8,128)S(1)}, u32[]{:S(2)}, u32[]{:S(2)}) collective-permute-start(f32[264,256]{1,0:T(8,128)S(1)} %collective-permute-done.refs_3_.low), channel_id=1, source_target_pairs={{0,64},{64,0},{1,65},{65,1},{2,66},{66,2},{3,67},{67,3},{4,68},{68... | collective-permute-start | bytes 811016 | tf_op jit(solution)/shard_map/ppermute | solution.py:268
  38.1 15.9 %collective-permute-start.13 = (f32[264,256]{1,0:T(8,128)S(1)}, f32[264,256]{1,0:T(8,128)S(1)}, u32[]{:S(2)}, u32[]{:S(2)}) collective-permute-start(f32[264,256]{1,0:T(8,128)S(1)} %pad_add_fusion.refs_0_.own), channel_id=1, source_target_pairs={{3,4},{7,8},{11,12},{15,16},{19,20},{23,24},{27,28},{31,32},{35,36... | collective-permute-start | bytes 811016 | tf_op jit(solution)/shard_map/ppermute | solution.py:279
  44.3 10.1 %collective-permute-start.14 = (f32[192,256]{1,0:T(8,128)S(1)}, f32[192,256]{1,0:T(8,128)S(1)}, u32[]{:S(2)}, u32[]{:S(2)}) collective-permute-start(f32[192,256]{1,0:T(8,128)S(1)} %get-tuple-element.50), channel_id=1, source_target_pairs={{0,4},{4,8},{8,12},{12,0},{1,5},{5,9},{9,13},{13,1},{2,6},{6,10},{... | collective-permute-start | bytes 589832 | tf_op jit(solution)/shard_map/ppermute | solution.py:278
  44.4 13.7 %collective-permute-start.15 = (f32[192,256]{1,0:T(8,128)S(1)}, f32[192,256]{1,0:T(8,128)S(1)}, u32[]{:S(2)}, u32[]{:S(2)}) collective-permute-start(f32[192,256]{1,0:T(8,128)S(1)} %get-tuple-element.56), channel_id=1, source_target_pairs={{0,8},{4,12},{8,0},{12,4},{1,9},{5,13},{9,1},{13,5},{2,10},{6,14},... | collective-permute-start | bytes 589832 | tf_op jit(solution)/shard_map/ppermute | solution.py:277
  48.7 9.5 %collective-permute-start.16 = (f32[192,256]{1,0:T(8,128)S(1)}, f32[192,256]{1,0:T(8,128)S(1)}, u32[]{:S(2)}, u32[]{:S(2)}) collective-permute-start(f32[192,256]{1,0:T(8,128)S(1)} %get-tuple-element.57), channel_id=1, source_target_pairs={{0,12},{4,0},{8,4},{12,8},{1,13},{5,1},{9,5},{13,9},{2,14},{6,2},{... | collective-permute-start | bytes 589832 | tf_op jit(solution)/shard_map/ppermute | solution.py:281
  58.2 6.6 %collective-permute-start.17 = (f32[192,256]{1,0:T(8,128)S(1)}, f32[192,256]{1,0:T(8,128)S(1)}, u32[]{:S(2)}, u32[]{:S(2)}) collective-permute-start(f32[192,256]{1,0:T(8,128)S(1)} %shard_map.115.a), channel_id=1, source_target_pairs={{0,48},{16,0},{32,16},{48,32},{1,49},{17,1},{33,17},{49,33},{2,50}... | collective-permute-start | bytes 589832 | tf_op jit(solution)/shard_map/ppermute | solution.py:221
  60.0 6.0 %collective-permute-start.18 = (f32[192,256]{1,0:T(8,128)S(1)}, f32[192,256]{1,0:T(8,128)S(1)}, u32[]{:S(2)}, u32[]{:S(2)}) collective-permute-start(f32[192,256]{1,0:T(8,128)S(1)} %shard_map.115.a), channel_id=1, source_target_pairs={{0,32},{16,48},{32,0},{48,16},{1,33},{17,49},{33,1},{49,17},{2,34}... | collective-permute-start | bytes 589832 | tf_op jit(solution)/shard_map/ppermute | solution.py:221
  62.3 9.2 %collective-permute-start.19 = (f32[192,256]{1,0:T(8,128)S(1)}, f32[192,256]{1,0:T(8,128)S(1)}, u32[]{:S(2)}, u32[]{:S(2)}) collective-permute-start(f32[192,256]{1,0:T(8,128)S(1)} %shard_map.115.a), channel_id=1, source_target_pairs={{0,16},{16,32},{32,48},{48,0},{1,17},{17,33},{33,49},{49,1},{2,18}... | collective-permute-start | bytes 589832 | tf_op jit(solution)/shard_map/ppermute | solution.py:221
  71.6 6.4 %collective-permute-start.20 = (f32[192,256]{1,0:T(8,128)S(1)}, f32[192,256]{1,0:T(8,128)S(1)}, u32[]{:S(2)}, u32[]{:S(2)}) collective-permute-start(f32[192,256]{1,0:T(8,128)S(1)} %shard_map.116.fd), channel_id=1, source_target_pairs={{0,8},{4,12},{8,0},{12,4},{1,9},{5,13},{9,1},{13,5},{2,10},{6,14},... | collective-permute-start | bytes 589832 | tf_op jit(solution)/shard_map/ppermute | solution.py:221
  74.3 5.3 %collective-permute-start.21 = (f32[192,256]{1,0:T(8,128)S(1)}, f32[192,256]{1,0:T(8,128)S(1)}, u32[]{:S(2)}, u32[]{:S(2)}) collective-permute-start(f32[192,256]{1,0:T(8,128)S(1)} %shard_map.116.fd), channel_id=1, source_target_pairs={{0,12},{4,0},{8,4},{12,8},{1,13},{5,1},{9,5},{13,9},{2,14},{6,2},{... | collective-permute-start | bytes 589832 | tf_op jit(solution)/shard_map/ppermute | solution.py:221
  74.3 9.3 %collective-permute-start.22 = (f32[192,256]{1,0:T(8,128)S(1)}, f32[192,256]{1,0:T(8,128)S(1)}, u32[]{:S(2)}, u32[]{:S(2)}) collective-permute-start(f32[192,256]{1,0:T(8,128)S(1)} %shard_map.116.fd), channel_id=1, source_target_pairs={{0,4},{4,8},{8,12},{12,0},{1,5},{5,9},{9,13},{13,1},{2,6},{6,10},{... | collective-permute-start | bytes 589832 | tf_op jit(solution)/shard_map/ppermute | solution.py:221
  85.0 3.6 %collective-permute-start.23 = (f32[4,256,256]{2,1,0:T(8,128)S(1)}, f32[4,256,256]{2,1,0:T(8,128)S(1)}, u32[]{:S(2)}, u32[]{:S(2)}) collective-permute-start(f32[4,256,256]{2,1,0:T(8,128)S(1)} %shard_map.118), channel_id=1, source_target_pairs={{0,64},{64,0},{1,65},{65,1},{2,66},{66,2},{3,67},{67,3},{4,68},{68... | collective-permute-start | bytes 3145736 | tf_op jit(solution)/shard_map/ppermute | solution.py:288
  87.7 5.7 %copy-start = (f32[256,256]{1,0:T(8,128)S(1)}, f32[256,256]{1,0:T(8,128)}, u32[]{:S(2)}) copy-start(f32[256,256]{1,0:T(8,128)} %feats.1) | copy-start | bytes 786436
  87.7 5.7 %copy-start.4 = (f32[256,256]{1,0:T(8,128)S(1)}, f32[256,256]{1,0:T(8,128)}, u32[]{:S(2)}) copy-start(f32[256,256]{1,0:T(8,128)} %w_msg.1) | copy-start | bytes 786436
  88.7 9.9 %collective-permute-start.24 = (f32[256,256]{1,0:T(8,128)S(1)}, f32[256,256]{1,0:T(8,128)S(1)}, u32[]{:S(2)}, u32[]{:S(2)}) collective-permute-start(f32[256,256]{1,0:T(8,128)S(1)} %get-tuple-element.68), channel_id=1, source_target_pairs={{0,1},{1,2},{2,3},{3,0},{4,5},{5,6},{6,7},{7,4},{8,9},{9,10},{10,1... | collective-permute-start | bytes 786440 | tf_op jit(solution)/shard_map/ppermute | solution.py:292
  88.8 16.3 %collective-permute-start.25 = (f32[256,256]{1,0:T(8,128)S(1)}, f32[256,256]{1,0:T(8,128)S(1)}, u32[]{:S(2)}, u32[]{:S(2)}) collective-permute-start(f32[256,256]{1,0:T(8,128)S(1)} %get-tuple-element.69), channel_id=1, source_target_pairs={{0,2},{1,3},{2,0},{3,1},{4,6},{5,7},{6,4},{7,5},{8,10},{9,11},{10,... | collective-permute-start | bytes 786440 | tf_op jit(solution)/shard_map/ppermute | solution.py:291
  93.4 11.7 %collective-permute-start.26 = (f32[256,256]{1,0:T(8,128)S(1)}, f32[256,256]{1,0:T(8,128)S(1)}, u32[]{:S(2)}, u32[]{:S(2)}) collective-permute-start(f32[256,256]{1,0:T(8,128)S(1)} %get-tuple-element.70), channel_id=1, source_target_pairs={{0,3},{1,0},{2,1},{3,2},{4,7},{5,4},{6,5},{7,6},{8,11},{9,8},{10,9... | collective-permute-start | bytes 786440 | tf_op jit(solution)/shard_map/ppermute | solution.py:293
  93.4 0.7 copy-start.5
  93.4 0.7 copy-start.6
  93.4 0.7 copy-start.7
  94.1 11.0 %copy-start.2 = (f32[256,256]{1,0:T(8,128)S(1)}, f32[256,256]{1,0:T(8,128)}, u32[]{:S(2)}) copy-start(f32[256,256]{1,0:T(8,128)} %w_one.1) | copy-start | bytes 786436
  94.1 11.0 %copy-start.3 = (f32[256,256]{1,0:T(8,128)S(1)}, f32[256,256]{1,0:T(8,128)}, u32[]{:S(2)}) copy-start(f32[256,256]{1,0:T(8,128)} %w_two.1) | copy-start | bytes 786436

commit v4 on v2

v4 whole, which is shorter than its diff:
```python
import math

import jax
import jax.numpy as jnp
from jax import lax
from jax.experimental import pallas as pl
from jax.experimental.pallas import tpu as pltpu
from jax.sharding import Mesh
from jax.sharding import PartitionSpec as P

Z, Y, X = "waves_0", "waves_1", "waves_2"
WAVES = (Z, Y, X)
ROWS_WAVES = ("rows", Z, Y, X)
F32 = jnp.float32
BF16 = jnp.bfloat16

SIN_POLY = (6.283185280154403, -10.33542015333633, 5.100154773052372, -1.1965808225334407, 0.15531182448662934)
COS_POLY = (0.9999999997791529, -4.934802136928833, 4.058709154760502, -1.335211949366169, 0.23493706849740192, -0.0243959319559508)
ROUNDER = 12582912.0


def horner(coeffs, u):
    out = coeffs[-1]
    for c in coeffs[-2::-1]:
        out = out * u + c
    return out


def split(a):
    high = a.astype(BF16)
    return high, (a - high.astype(F32)).astype(BF16)


def thirds(a):
    high = a.astype(BF16).astype(F32)
    rest = a - high
    middle = rest.astype(BF16).astype(F32)
    return high, middle, rest - middle


def dot(a, b):
    return jnp.dot(a, b, preferred_element_type=F32)


def dot3(a, b):
    return dot(a[0], b[0]) + (dot(a[1], b[0]) + dot(a[0], b[1]))


def call(kernel, outs, n_in, scratch=(), smem=(), flops=0, limit=16 << 20):
    def space(i):
        return pltpu.SMEM if i in smem else pltpu.VMEM

    return pl.pallas_call(
        kernel,
        out_shape=outs,
        in_specs=[pl.BlockSpec(memory_space=space(i)) for i in range(n_in)],
        out_specs=jax.tree.map(lambda _: pl.BlockSpec(memory_space=pltpu.VMEM), outs),
        scratch_shapes=scratch,
        cost_estimate=pl.CostEstimate(flops=flops, bytes_accessed=1 << 16, transcendentals=0),
        compiler_params=pltpu.CompilerParams(vmem_limit_bytes=limit),
    )


def live_rows(block, cells, cell):
    slots = cells * cell
    row = lax.broadcasted_iota(jnp.int32, (slots, 1), 0).astype(F32)
    limit = block[slots + 3 : slots + 4, 0:1]
    for c in range(1, cells):
        limit = jnp.where(row < c * cell, limit, c * cell + block[slots + 3 : slots + 4, c : c + 1])
    return row < limit


def lattice(own, groups):
    def kernel(kv, out, flat):
        flat[...] = jnp.zeros(flat.shape, F32)
        pad = jnp.zeros((8, flat.shape[1] - 128), F32)
        for g in range(groups):
            flat[...] += pltpu.roll(jnp.concatenate([kv[g], pad], axis=1), g * own, 1)
        kh, km, kl = thirds(flat[...])
        out[...] = jnp.concatenate([kh, kh, km, kh, km, kl], axis=0).T.astype(BF16)

    return kernel


def forward(cells, cell, count, own, groups, first):
    slots = cells * cell

    def kernel(lhs, w_val, *refs):
        chunks, refs = refs[:count], refs[count:]
        if not first:
            before, refs = refs[0], refs[1:]
        out, mh, ml = refs
        w = split(w_val[...])
        for j, chunk in enumerate(chunks):
            live = live_rows(chunk, cells, cell)
            v = split(jnp.where(live, dot3(split(chunk[:slots]), w), 0.0))
            ph, pm, pl_ = thirds(chunk[slots : slots + 8])
            turns = dot(lhs[...], jnp.concatenate([ph, pm, ph, pl_, pm, ph], axis=0).astype(BF16))
            for g in range(groups):
                t = turns[g * own : (g + 1) * own]
                f = t - ((t + ROUNDER) - ROUNDER)
                u = f * f
                s = f * horner(SIN_POLY, u)
                c = horner(COS_POLY, u)
                both = jnp.concatenate([1.0 - 0.5 * (s * s), s * c], axis=0)
                rows = slice(2 * own * g, 2 * own * (g + 1))
                mh[j, rows], ml[j, rows] = split(both)
            part = dot3((mh[j], ml[j]), v)
            if j:
                out[...] += part
            elif first:
                out[...] = part
            else:
                out[...] = before[...] + part

    return kernel


def filtered(scale):
    def kernel(half, parts, filters, out):
        groups, double, _ = parts.shape
        own = double // 2
        f = filters[pl.ds(pl.multiple_of(half[0] * own, 8), own), :] * scale
        total = parts[0]
        for g in range(1, groups):
            total = total + parts[g]
        total = total * jnp.concatenate([f, f], axis=0)
        for g in range(groups):
            out[g] = total

    return kernel


def turned(f, high, low):
    high[...], low[...] = split(f[...].T)


def backward(chunks):
    def kernel(fh, fl, mh, ml, *outs):
        for j, out in zip(chunks, outs):
            out[...] = dot3((fh[...], fl[...]), (mh[j], ml[j]))

    return kernel


def pairs(*refs):
    count = len(refs) // 3
    for a, b, out in zip(refs[:count], refs[count : 2 * count], refs[2 * count :]):
        out[...] = a[...] + b[...]


def messages(cells, cell, cells_all, nb, last):
    slots = cells * cell

    def kernel(at_x, at_cell, neighbours, nbr_count, own, low, high, edge, w_msg, out, mask):
        x, first = at_x[0], at_cell[0]
        lo = jnp.where(x == 0, edge[...], low[...])
        hi = jnp.where(x == last, edge[...], high[...])
        blocks = (lo, own[...], hi)
        masks = [live_rows(b, cells, cell) for b in blocks]
        parts = [split(jnp.where(m, b[:slots], 0.0)) for m, b in zip(masks, blocks)]
        wide = [tuple(p[k][c * cell : (c + 1) * cell] for k in range(2)) for p in parts for c in range(cells)]
        pos = [
            b[slots : slots + 3, c * cell : (c + 1) * cell] for b in blocks for c in range(cells)
        ]
        cols = own[slots : slots + 8].T
        eye = lax.broadcasted_iota(jnp.int32, (cell, cell), 0) == lax.broadcasted_iota(jnp.int32, (cell, cell), 1)
        gathered = []
        for c in range(cells):
            mine = cols[c * cell : (c + 1) * cell]
            acc = None
            for step in range(2 * cells + 1):
                other = c + step
                local = other - cells
                target = lax.rem(first + local + cells_all, cells_all)
                listed = jnp.float32(0.0)
                for b in range(nb):
                    hit = (neighbours[c, b] == target) & (b < nbr_count[c])
                    listed = listed + jnp.where(hit, jnp.float32(1.0), jnp.float32(0.0))
                near = pos[other]
                d0 = mine[:, 0:1] - near[0:1]
                d1 = mine[:, 1:2] - near[1:2]
                d2 = mine[:, 2:3] - near[2:3]
                weight = jnp.exp(-0.125 * (d0 * d0 + d1 * d1 + d2 * d2)) * listed
                if step == cells:
                    weight = jnp.where(eye, 0.0, weight)
                part = dot3(split(weight), wide[other])
                acc = part if acc is None else acc + part
            gathered.append(acc)
        total = jnp.concatenate(gathered, axis=0)
        live = masks[1]
        msg = 0.125 * dot3(split(total), split(w_msg[...]))
        out[...] = own[:slots] + jnp.where(live, msg, 0.0)
        mask[...] = jnp.broadcast_to(jnp.where(live, 1.0, 0.0), mask.shape)

    return kernel


def finish():
    def kernel(base, mask, a, b, c, w_one, w_two, out):
        spectral = a[...] + (b[...] + c[...])
        u = base[...] + spectral.T
        normed = u / jnp.sqrt(jnp.mean(u * u, axis=1, keepdims=True) + 1e-06)
        v = dot3(split(normed), split(w_one[...]))
        hidden = v / (1.0 + jnp.exp(-v))
        out[...] = (u + dot3(split(hidden), split(w_two[...]))) * mask[:, 0:1]

    return kernel


def shift(axis, by):
    size = lax.axis_size(axis)
    return [(i, (i + by) % size) for i in range(size)]


def shards(
    feats, positions, cell_counts, neighbours, nbr_count, kvec, filters, w_msg, w_val, w_one, w_two
):
    cells = cell_counts.shape[0]
    slots, width = feats.shape
    cell = slots // cells
    devices = lax.axis_size(ROWS_WAVES)
    nx = lax.axis_size(X)
    rows = lax.axis_size("rows")
    group = lax.axis_size((Z, Y))
    own_waves = kvec.shape[1] // rows
    waves = own_waves * group
    half = lax.axis_index("rows").astype(jnp.int32)
    x = lax.axis_index(X).astype(jnp.int32)
    first = lax.axis_index(ROWS_WAVES).astype(jnp.int32) * cells

    def floats(*dims):
        return jax.ShapeDtypeStruct(dims, F32)

    def halves(*dims):
        return jax.ShapeDtypeStruct(dims, BF16)

    counts = cell_counts.astype(F32)[None]
    payload = jnp.pad(feats, ((0, 8), (0, 0))) + jnp.pad(positions, ((slots, 5), (0, 0)))
    payload = payload + jnp.pad(counts, ((slots + 3, 4), (0, width - cells)))
    near2 = lax.ppermute(payload, X, shift(X, 2))
    above = lax.ppermute(payload, X, shift(X, -1))
    below = lax.ppermute(payload, X, shift(X, 1))
    other = [lax.ppermute(payload, "rows", shift("rows", 1))]

    kv = lax.dynamic_slice_in_dim(kvec * (0.5 / math.pi), half * own_waves, own_waves, 1)
    kv = jnp.pad(kv, ((0, 8 - kv.shape[0]), (0, 128 - own_waves)))
    kv = lax.all_to_all(jnp.broadcast_to(kv[None], (group, *kv.shape)), (Z, Y), 0, 0, tiled=True)
    kv, near2, above, below, again = lax.optimization_barrier((kv, near2, above, below, payload))
    ends = [(d, (d + 1) % devices) for d in range(devices) if d % nx == nx - 1]
    ends = ends + [(b, a) for a, b in ends]
    edge = lax.ppermute(again, ROWS_WAVES, ends)

    lhs = call(lattice(own_waves, group), halves(waves, 48), 1, [pltpu.VMEM((8, waves), F32)])(kv)
    line = (payload, above, below, near2)
    other += [lax.ppermute(c, "rows", shift("rows", 1)) for c in line[1:]]
    count = len(line)
    wide = halves(count, 2 * waves, slots)
    sums = floats(2 * waves, width)
    work = 12 * count * waves * slots * width
    part, *mine = call(forward(cells, cell, count, own_waves, group, True), (sums, wide, wide), 2 + count, flops=work)(
        lhs, w_val, *line
    )
    part, *theirs = call(forward(cells, cell, count, own_waves, group, False), (sums, wide, wide), 3 + count, flops=work)(
        lhs, w_val, *other, part
    )
    part, edge = lax.optimization_barrier((part, edge))
    parts = lax.all_to_all(part.reshape(group, 2 * own_waves, width), (Z, Y), 0, 0, tiled=True)
    scale = 1.0 / math.sqrt(float(slots * devices) * float(waves * rows * nx))
    spread = call(filtered(scale), floats(*parts.shape), 3, smem=(0,))(half.reshape(1), parts, filters)
    f = lax.all_to_all(spread, (Z, Y), 0, 0, tiled=True).reshape(2 * waves, width)

    ft = call(turned, (halves(width, 2 * waves),) * 2, 1)(f)
    one = floats(width, slots)
    swap = shift("rows", 1)

    def back(chunks, ft, waves_of):
        flops = len(chunks) * work // count
        return call(backward(chunks), (one,) * len(chunks), 4, flops=flops)(*ft, *waves_of)

    (far,) = back((3,), ft, theirs)
    there = lax.ppermute(far, "rows", swap)
    ft = lax.optimization_barrier((*ft, far))[:2]
    rest = [lax.ppermute(r, "rows", swap) for r in back((0, 1, 2), ft, theirs)]
    (e3,) = call(pairs, (one,), 2)(*back((3,), ft, mine), there)
    e3, *ft = lax.optimization_barrier((e3, *ft))
    e3 = lax.ppermute(e3, X, shift(X, 2))
    near = back((0, 1, 2), ft, mine)
    e0, e1, e2 = call(pairs, (one,) * 3, 6)(*near, *rest)
    e1 = lax.ppermute(e1, X, shift(X, 1))
    e2 = lax.ppermute(e2, X, shift(X, -1))

    base, mask = call(
        messages(cells, cell, cells * devices, neighbours.shape[1], nx - 1),
        (floats(slots, width), floats(slots, 128)),
        9,
        smem=(0, 1, 2, 3),
        flops=work // 4,
    )(x.reshape(1), first.reshape(1), neighbours, nbr_count, payload, below, above, edge, w_msg)
    (e0,) = call(pairs, (one,), 2)(e0, e3)
    return call(finish(), floats(slots, width), 7)(base, mask, e0, e1, e2, w_one, w_two)


def solution(mesh):
    torus = Mesh(mesh.devices.reshape(mesh.shape["rows"], 4, 4, 4), ROWS_WAVES)
    return jax.shard_map(
        shards,
        mesh=torus,
        in_specs=(
            P(ROWS_WAVES, None),
            P(None, ROWS_WAVES),
            P(ROWS_WAVES),
            P(ROWS_WAVES, None),
            P(ROWS_WAVES),
            P(None, WAVES),
            P(WAVES, None),
            P(),
            P(),
            P(),
            P(),
        ),
        out_specs=P(ROWS_WAVES, None),
        check_vma=False,
    )
```

time: 100 us -> 97.2 us (0.972)
  waiting for transfers between devices: 19.5 us -> 14.3 us
  starting transfers between devices: 25.6 us -> 29.3 us
  local copies, waits for them, and re-layouts: 5.01 us -> 1.71 us
  Pallas kernels: 14.9 us -> 16.2 us
    ppermute x5 -> x8, starting transfers between devices: 17.9 us -> 11 us  [the longest x1 5.15 us: shards(): edge = lax.ppermute(again, ROWS_WAVES, ends)]
    all_to_all x1, starting transfers between devices: 3.52 us -> 7.77 us  [shards(): lax.all_to_all(jnp.broadcast_to(kv[None], (group, *kv.shape)), (Z, Y), 0,...]
    ppermute x1, starting transfers between devices: 0.01 us -> 3.65 us  [shards(): near2 = lax.ppermute(payload, X, shift(X, 2))]
    unnamed x25 -> x16, local copies, waits for them, and re-layouts: 4.31 us -> 0.99 us
    all_to_all x1, waiting for transfers between devices: 7.27 us -> 4.64 us  [shards(): lax.all_to_all(jnp.broadcast_to(kv[None], (group, *kv.shape)), (Z, Y), 0,...]
    ppermute x3, starting transfers between devices: 0.93 us -> 3.53 us  [shards(): other += [lax.ppermute(c, 'rows', shift('rows', 1)) for c in line[1:]]]
    ppermute x1, waiting for transfers between devices: 2.28 us -> 0.01 us  [shards(): above = lax.ppermute(payload, X, shift(X, -1))]
    ppermute x1, starting transfers between devices: 2.7 us -> 0.86 us  [shards(): above = lax.ppermute(payload, X, shift(X, -1))]
  transfers between devices with their start and end apart: 13 -> 16, of which waited for: 5 -> 4; matrix products, arithmetic and copies ran while one was open for 2% -> 1% of each run, Pallas kernels for 7% -> 14%
where the time goes in v4:
time: 97.2 us; the launch traced here: 96.8 us
  blocking collectives  32.8 us (34%)
  starting transfers between devices  29.3 us (30%)
  Pallas kernels  16.2 us (17%)
  waiting for transfers between devices  14.3 us (15%)
  other arithmetic  2.33 us (2%)
  local copies, waits for them, and re-layouts  1.71 us (2%)
    all_to_all x1, blocking collectives, shards(): lax.all_to_all(part.reshape(group, 2 * own_waves, width), (Z, Y), 0, 0, t...  16.7 us
    all_to_all x1, blocking collectives, shards(): lax.all_to_all(spread, (Z, Y), 0, 0, tiled=True).reshape(2 * waves, width)  16.1 us
    all_to_all x1, starting transfers between devices, shards(): lax.all_to_all(jnp.broadcast_to(kv[None], (group, *kv.shape)), (Z, Y), 0,...  7.77 us
    ppermute x1, waiting for transfers between devices, shards(): e1 = lax.ppermute(e1, X, shift(X, 1))  6.13 us
    ppermute x1, starting transfers between devices, shards(): edge = lax.ppermute(again, ROWS_WAVES, ends)  5.15 us
    all_to_all x1, waiting for transfers between devices, shards(): lax.all_to_all(jnp.broadcast_to(kv[None], (group, *kv.shape)), (Z, Y), 0,...  4.64 us
    pallas_call x1, Pallas kernels, shards(): call(forward(cells, cell, count, own_waves, group, False), (sums, wide, w...  4.15 us
    pallas_call x1, Pallas kernels, shards(): call(forward(cells, cell, count, own_waves, group, True), (sums, wide, wi...  4.13 us
  transfers between devices with their start and end apart: 16, of which 4 were waited for; matrix products, arithmetic and copies ran while one was open for 1% of the time, Pallas kernels for 14%

profile of v4, /device:TPU:1, one launch (start us, length us, event | category | flops | bytes accessed | tf_op | source)
XLA Modules:
  0.0 96.8 jit_solution(15147614657598031699)
XLA Ops:
  0.0 0.7 convert_bitcast_fusion
  0.7 1.0 %pad_add_fusion.refs_0_.own = f32[264,256]{1,0:T(8,128)S(1)} fusion(f32[1,2]{1,0:T(1,128)S(1)} %convert_bitcast_fusion, f32[3,256]{1,0:T(4,128)} %param.12, f32[256,256]{1,0:T(8,128)} %param.11), kind=kLoop, calls=%fused_computation | loop fusion | flops 135168 | bytes 535560 | tf_op jit(solution)/shard_map/add | solution.py:240
  1.6 3.7 %collective-permute-start = (f32[264,256]{1,0:T(8,128)S(1)}, f32[264,256]{1,0:T(8,128)S(1)}, u32[]{:S(2)}, u32[]{:S(2)}) collective-permute-start(f32[264,256]{1,0:T(8,128)S(1)} %pad_add_fusion.refs_0_.own), channel_id=1, source_target_pairs={{0,2},{1,3},{2,0},{3,1},{4,6},{5,7},{6,4},{7,5},{8,10},{9,11},{10,... | collective-permute-start | bytes 811016 | tf_op jit(solution)/shard_map/ppermute | solution.py:241
  5.3 0.9 collective-permute-start.1
  6.2 0.6 collective-permute-start.2
  6.8 0.7 broadcast_multiply_fusion
  7.5 0.1 constant_dynamic-slice_fusion
  7.5 0.6 broadcast_in_dim.10
  8.2 7.8 %all-to-all-start = ((f32[16,8,128]{2,1,0:T(8,128)}), f32[16,8,128]{2,1,0:T(8,128)S(1)}, u32[]{:S(2)}, u32[]{:S(2)}) async-start(f32[16,8,128]{2,1,0:T(8,128)} %broadcast_in_dim.10), calls=%async_computation | async-start | bytes 131072 | tf_op jit(solution)/shard_map/all_to_all | solution.py:248
  15.9 1.9 %collective-permute-start.3 = (f32[264,256]{1,0:T(8,128)S(1)}, f32[264,256]{1,0:T(8,128)S(1)}, u32[]{:S(2)}, u32[]{:S(2)}) collective-permute-start(f32[264,256]{1,0:T(8,128)S(1)} %pad_add_fusion.refs_0_.own), channel_id=1, source_target_pairs={{0,64},{64,0},{1,65},{65,1},{2,66},{66,2},{3,67},{67,3},{4,68},{68... | collective-permute-start | bytes 811016 | tf_op jit(solution)/shard_map/ppermute | solution.py:244
  17.8 4.6 %all-to-all-done.kv = f32[16,8,128]{2,1,0:T(8,128)S(1)} async-done(((f32[16,8,128]{2,1,0:T(8,128)}), f32[16,8,128]{2,1,0:T(8,128)S(1)}, u32[]{:S(2)}, u32[]{:S(2)}) %all-to-all-start) | async-done | bytes 65568 | tf_op jit(solution)/shard_map/all_to_all | solution.py:248
  22.5 0.0 collective-permute-done.refs_3_
  22.5 0.0 collective-permute-done.1.refs_1_.high
  22.5 3.0 %collective-permute-start.4 = (f32[264,256]{1,0:T(8,128)S(1)}, f32[264,256]{1,0:T(8,128)S(1)}, u32[]{:S(2)}, u32[]{:S(2)}) collective-permute-start(f32[264,256]{1,0:T(8,128)S(1)} %collective-permute-done.1.refs_1_.high), channel_id=1, source_target_pairs={{0,64},{64,0},{1,65},{65,1},{2,66},{66,2},{3,67},{67,3},{4,68},{68... | collective-permute-start | bytes 811016 | tf_op jit(solution)/shard_map/ppermute | solution.py:256
  25.5 0.1 collective-permute-start.5
  25.6 0.4 collective-permute-start.6
  26.0 5.2 %collective-permute-start.7 = (f32[264,256]{1,0:T(8,128)S(1)}, f32[264,256]{1,0:T(8,128)S(1)}, u32[]{:S(2)}, u32[]{:S(2)}) collective-permute-start(f32[264,256]{1,0:T(8,128)S(1)} %pad_add_fusion.refs_0_.own), channel_id=1, source_target_pairs={{3,4},{7,8},{11,12},{15,16},{19,20},{23,24},{27,28},{31,32},{35,36... | collective-permute-start | bytes 811016 | tf_op jit(solution)/shard_map/ppermute | solution.py:252
  31.2 0.2 shard_map.109.lhs
  31.4 0.0 copy-start.6
  31.4 0.9 copy-done.6
  32.3 4.1 %shard_map.110 = (f32[768,256]{1,0:T(8,128)S(1)}, bf16[4,768,256]{2,1,0:T(8,128)(2,1)S(1)}, bf16[4,768,256]{2,1,0:T(8,128)(2,1)S(1)}) custom-call(bf16[384,48]{1,0:T(8,128)(2,1)S(1)} %shard_map.109.lhs, f32[256,256]{1,0:T(8,128)S(1)} %copy-done.6, f32[264,256]{1,0:T(8,128)S(1)} %pad_add_fusion.refs_0_.own, ...), custom_call_target="tpu_custom_call" | custom-call | flops 1207959552 | bytes 65536 | tf_op jit(solution)/shard_map/pallas_call | solution.py:261
  36.5 4.1 %shard_map.111 = (f32[768,256]{1,0:T(8,128)S(1)}, bf16[4,768,256]{2,1,0:T(8,128)(2,1)S(1)}, bf16[4,768,256]{2,1,0:T(8,128)(2,1)S(1)}) custom-call(bf16[384,48]{1,0:T(8,128)(2,1)S(1)} %shard_map.109.lhs, f32[256,256]{1,0:T(8,128)S(1)} %copy-done.7, f32[264,256]{1,0:T(8,128)S(1)} %collective-permute-done.3.refs_0_, ...), custom_call_target="tpu_custom_call" | custom-call | flops 1207959552 | bytes 65536 | tf_op jit(solution)/shard_map/pallas_call | solution.py:264
  40.7 0.0 copy-start.3
  40.7 0.8 collective-permute-done.7.edge
  41.5 16.7 %all_to_all.15.parts = f32[16,48,256]{2,1,0:T(8,128)S(1)} all-to-all(f32[16,48,256]{2,1,0:T(8,128)S(1)} %bitcast.8), channel_id=1, replica_groups=mesh['rows'=2,'waves_0'=4,'waves_1'=4,'waves_2'=4] {'waves_0','waves_1'}, dimensions={0} | all-to-all | bytes 1572864 | tf_op jit(solution)/shard_map/all_to_all | solution.py:268
  58.2 0.1 shard_map.113
  58.3 16.1 %all_to_all.16 = f32[16,48,256]{2,1,0:T(8,128)S(1)} all-to-all(f32[16,48,256]{2,1,0:T(8,128)S(1)} %shard_map.113), channel_id=1, replica_groups=mesh['rows'=2,'waves_0'=4,'waves_1'=4,'waves_2'=4] {'waves_0','waves_1'}, dimensions={0} | all-to-all | bytes 1572864 | tf_op jit(solution)/shard_map/all_to_all | solution.py:271
  74.4 0.3 shard_map.114
  74.6 0.5 shard_map.115
  75.1 2.2 %collective-permute-start.8 = (f32[256,256]{1,0:T(8,128)S(1)}, f32[256,256]{1,0:T(8,128)S(1)}, u32[]{:S(2)}, u32[]{:S(2)}) collective-permute-start(f32[256,256]{1,0:T(8,128)S(1)} %shard_map.115), channel_id=1, source_target_pairs={{0,64},{64,0},{1,65},{65,1},{2,66},{66,2},{3,67},{67,3},{4,68},{68... | collective-permute-start | bytes 786440 | tf_op jit(solution)/shard_map/ppermute | solution.py:282
  77.3 1.1 %shard_map.119 = (f32[256,256]{1,0:T(8,128)S(1)}, f32[256,256]{1,0:T(8,128)S(1)}, f32[256,256]{1,0:T(8,128)S(1)}) custom-call(bf16[256,768]{1,0:T(8,128)(2,1)S(1)} %get-tuple-element.55.fh, bf16[256,768]{1,0:T(8,128)(2,1)S(1)} %get-tuple-element.56.fl, bf16[4,768,256]{2,1,0:T(8,128)(2,1)S(1)} %get-tuple-element.49.mh, ...), custom_call_target="tpu_custom_call" | custom-call | flops 905969664 | bytes 65536 | tf_op jit(solution)/shard_map/pallas_call | solution.py:279
  78.4 0.1 collective-permute-start.10
  78.5 0.5 collective-permute-start.11
  79.0 0.3 collective-permute-start.9
  79.3 0.5 shard_map.116.refs_0_
  79.8 0.1 collective-permute-start.12
  79.9 1.1 %shard_map.118 = (f32[256,256]{1,0:T(8,128)S(1)}, f32[256,256]{1,0:T(8,128)S(1)}, f32[256,256]{1,0:T(8,128)S(1)}) custom-call(bf16[256,768]{1,0:T(8,128)(2,1)S(1)} %get-tuple-element.55.fh, bf16[256,768]{1,0:T(8,128)(2,1)S(1)} %get-tuple-element.56.fl, bf16[4,768,256]{2,1,0:T(8,128)(2,1)S(1)} %get-tuple-element.53.mh, ...), custom_call_target="tpu_custom_call" | custom-call | flops 905969664 | bytes 65536 | tf_op jit(solution)/shard_map/pallas_call | solution.py:279
  81.0 0.0 copy-start
  81.0 0.0 copy-start.4
  81.0 0.0 copy-start.5
  81.0 0.0 copy-start.1
  81.0 0.0 copy-start.2
  81.1 0.8 shard_map.120
  81.8 2.7 %collective-permute-start.13 = (f32[256,256]{1,0:T(8,128)}, f32[256,256]{1,0:T(8,128)S(1)}, u32[]{:S(2)}, u32[]{:S(2)}) collective-permute-start(f32[256,256]{1,0:T(8,128)} %get-tuple-element.65), channel_id=1, source_target_pairs={{0,1},{1,2},{2,3},{3,0},{4,5},{5,6},{6,7},{7,4},{8,9},{9,10},{10,1... | collective-permute-start | bytes 786440 | tf_op jit(solution)/shard_map/ppermute | solution.py:290
  84.6 1.9 %shard_map.112 = (f32[256,256]{1,0:T(8,128)S(1)}, f32[256,128]{1,0:T(8,128)S(1)}) custom-call(s32[1]{0:T(128)} %bitcast.at_x, s32[1]{0:T(128)} %bitcast.1.at_cell, s32[2,5]{1,0:T(2,128)S(1)} %copy-done.4, s32[2]{0:T(128)S(1)} %copy-done.5, f32[264,256]{1,0:T(8,128)S(1)} %pad_add_fusion.refs_0_.own, f32[264,256]{1,0:T(8,128)S(1)} %collective-permute-done.2.refs_2_.low, ...), custom_call_target="tpu_custom_call" | custom-call | flops 301989888 | bytes 65536 | tf_op jit(solution)/shard_map/pallas_call | solution.py:293
  86.4 2.6 %collective-permute-done.12.refs_1_ = f32[256,256]{1,0:T(8,128)S(1)} collective-permute-done((f32[256,256]{1,0:T(8,128)S(1)}, f32[256,256]{1,0:T(8,128)S(1)}, u32[]{:S(2)}, u32[]{:S(2)}) %collective-permute-start.12) | collective-permute-done | bytes 262176 | tf_op jit(solution)/shard_map/ppermute | solution.py:287
  89.1 6.1 %collective-permute-done.13.b = f32[256,256]{1,0:T(8,128)S(1)} collective-permute-done((f32[256,256]{1,0:T(8,128)}, f32[256,256]{1,0:T(8,128)S(1)}, u32[]{:S(2)}, u32[]{:S(2)}) %collective-permute-start.13) | collective-permute-done | bytes 262176 | tf_op jit(solution)/shard_map/ppermute | solution.py:290
  95.3 1.5 %shard_map.122 = f32[256,256]{1,0:T(8,128)} custom-call(f32[256,256]{1,0:T(8,128)S(1)} %get-tuple-element.44.base, f32[256,128]{1,0:T(8,128)S(1)} %get-tuple-element.45.mask, f32[256,256]{1,0:T(8,128)S(1)} %shard_map.121.a, f32[256,256]{1,0:T(8,128)S(1)} %collective-permute-done.13.b, f32[256,256]{1,0:T(8,128)S(1)} %collective-permute-done.14.c, ...), custom_call_target="tpu_custom_call" | custom-call | bytes 65536 | tf_op jit(solution)/shard_map/pallas_call | solution.py:301
  (22 shorter events, 0.1 us)
Async XLA Ops:
  1.6 20.8 %collective-permute-start = (f32[264,256]{1,0:T(8,128)S(1)}, f32[264,256]{1,0:T(8,128)S(1)}, u32[]{:S(2)}, u32[]{:S(2)}) collective-permute-start(f32[264,256]{1,0:T(8,128)S(1)} %pad_add_fusion.refs_0_.own), channel_id=1, source_target_pairs={{0,2},{1,3},{2,0},{3,1},{4,6},{5,7},{6,4},{7,5},{8,10},{9,11},{10,... | collective-permute-start | bytes 811016 | tf_op jit(solution)/shard_map/ppermute | solution.py:241
  5.3 17.2 %collective-permute-start.1 = (f32[264,256]{1,0:T(8,128)S(1)}, f32[264,256]{1,0:T(8,128)S(1)}, u32[]{:S(2)}, u32[]{:S(2)}) collective-permute-start(f32[264,256]{1,0:T(8,128)S(1)} %pad_add_fusion.refs_0_.own), channel_id=1, source_target_pairs={{0,3},{1,0},{2,1},{3,2},{4,7},{5,4},{6,5},{7,6},{8,11},{9,8},{10,9... | collective-permute-start | bytes 811016 | tf_op jit(solution)/shard_map/ppermute | solution.py:242
  6.2 16.3 %collective-permute-start.2 = (f32[264,256]{1,0:T(8,128)S(1)}, f32[264,256]{1,0:T(8,128)S(1)}, u32[]{:S(2)}, u32[]{:S(2)}) collective-permute-start(f32[264,256]{1,0:T(8,128)S(1)} %pad_add_fusion.refs_0_.own), channel_id=1, source_target_pairs={{0,1},{1,2},{2,3},{3,0},{4,5},{5,6},{6,7},{7,4},{8,9},{9,10},{10,1... | collective-permute-start | bytes 811016 | tf_op jit(solution)/shard_map/ppermute | solution.py:243
  8.2 14.3 %all-to-all-start = ((f32[16,8,128]{2,1,0:T(8,128)}), f32[16,8,128]{2,1,0:T(8,128)S(1)}, u32[]{:S(2)}, u32[]{:S(2)}) async-start(f32[16,8,128]{2,1,0:T(8,128)} %broadcast_in_dim.10), calls=%async_computation | async-start | bytes 131072 | tf_op jit(solution)/shard_map/all_to_all | solution.py:248
  15.9 20.5 %collective-permute-start.3 = (f32[264,256]{1,0:T(8,128)S(1)}, f32[264,256]{1,0:T(8,128)S(1)}, u32[]{:S(2)}, u32[]{:S(2)}) collective-permute-start(f32[264,256]{1,0:T(8,128)S(1)} %pad_add_fusion.refs_0_.own), channel_id=1, source_target_pairs={{0,64},{64,0},{1,65},{65,1},{2,66},{66,2},{3,67},{67,3},{4,68},{68... | collective-permute-start | bytes 811016 | tf_op jit(solution)/shard_map/ppermute | solution.py:244
  22.5 14.0 %collective-permute-start.4 = (f32[264,256]{1,0:T(8,128)S(1)}, f32[264,256]{1,0:T(8,128)S(1)}, u32[]{:S(2)}, u32[]{:S(2)}) collective-permute-start(f32[264,256]{1,0:T(8,128)S(1)} %collective-permute-done.1.refs_1_.high), channel_id=1, source_target_pairs={{0,64},{64,0},{1,65},{65,1},{2,66},{66,2},{3,67},{67,3},{4,68},{68... | collective-permute-start | bytes 811016 | tf_op jit(solution)/shard_map/ppermute | solution.py:256
  25.5 11.0 %collective-permute-start.5 = (f32[264,256]{1,0:T(8,128)S(1)}, f32[264,256]{1,0:T(8,128)S(1)}, u32[]{:S(2)}, u32[]{:S(2)}) collective-permute-start(f32[264,256]{1,0:T(8,128)S(1)} %collective-permute-done.2.refs_2_.low), channel_id=1, source_target_pairs={{0,64},{64,0},{1,65},{65,1},{2,66},{66,2},{3,67},{67,3},{4,68},{68... | collective-permute-start | bytes 811016 | tf_op jit(solution)/shard_map/ppermute | solution.py:256
  25.6 10.9 %collective-permute-start.6 = (f32[264,256]{1,0:T(8,128)S(1)}, f32[264,256]{1,0:T(8,128)S(1)}, u32[]{:S(2)}, u32[]{:S(2)}) collective-permute-start(f32[264,256]{1,0:T(8,128)S(1)} %collective-permute-done.refs_3_), channel_id=1, source_target_pairs={{0,64},{64,0},{1,65},{65,1},{2,66},{66,2},{3,67},{67,3},{4,68},{68... | collective-permute-start | bytes 811016 | tf_op jit(solution)/shard_map/ppermute | solution.py:256
  26.0 15.5 %collective-permute-start.7 = (f32[264,256]{1,0:T(8,128)S(1)}, f32[264,256]{1,0:T(8,128)S(1)}, u32[]{:S(2)}, u32[]{:S(2)}) collective-permute-start(f32[264,256]{1,0:T(8,128)S(1)} %pad_add_fusion.refs_0_.own), channel_id=1, source_target_pairs={{3,4},{7,8},{11,12},{15,16},{19,20},{23,24},{27,28},{31,32},{35,36... | collective-permute-start | bytes 811016 | tf_op jit(solution)/shard_map/ppermute | solution.py:252
  31.4 1.0 copy-start.6
  32.3 4.2 %copy-start.7 = (f32[256,256]{1,0:T(8,128)S(1)}, f32[256,256]{1,0:T(8,128)}, u32[]{:S(2)}) copy-start(f32[256,256]{1,0:T(8,128)} %w_val.3) | copy-start | bytes 786436
  40.7 17.5 %copy-start.3 = (f32[48,256]{1,0:T(8,128)S(1)}, f32[48,256]{1,0:T(8,128)}, u32[]{:S(2)}) copy-start(f32[48,256]{1,0:T(8,128)} %filters.1) | copy-start | bytes 147460
  75.1 4.6 %collective-permute-start.8 = (f32[256,256]{1,0:T(8,128)S(1)}, f32[256,256]{1,0:T(8,128)S(1)}, u32[]{:S(2)}, u32[]{:S(2)}) collective-permute-start(f32[256,256]{1,0:T(8,128)S(1)} %shard_map.115), channel_id=1, source_target_pairs={{0,64},{64,0},{1,65},{65,1},{2,66},{66,2},{3,67},{67,3},{4,68},{68... | collective-permute-start | bytes 786440 | tf_op jit(solution)/shard_map/ppermute | solution.py:282
  78.4 2.6 %collective-permute-start.10 = (f32[256,256]{1,0:T(8,128)S(1)}, f32[256,256]{1,0:T(8,128)S(1)}, u32[]{:S(2)}, u32[]{:S(2)}) collective-permute-start(f32[256,256]{1,0:T(8,128)S(1)} %get-tuple-element.61), channel_id=1, source_target_pairs={{0,64},{64,0},{1,65},{65,1},{2,66},{66,2},{3,67},{67,3},{4,68},{68... | collective-permute-start | bytes 786440 | tf_op jit(solution)/shard_map/ppermute | solution.py:284
  78.5 2.5 %collective-permute-start.11 = (f32[256,256]{1,0:T(8,128)S(1)}, f32[256,256]{1,0:T(8,128)S(1)}, u32[]{:S(2)}, u32[]{:S(2)}) collective-permute-start(f32[256,256]{1,0:T(8,128)S(1)} %get-tuple-element.62), channel_id=1, source_target_pairs={{0,64},{64,0},{1,65},{65,1},{2,66},{66,2},{3,67},{67,3},{4,68},{68... | collective-permute-start | bytes 786440 | tf_op jit(solution)/shard_map/ppermute | solution.py:284
  79.0 2.0 %collective-permute-start.9 = (f32[256,256]{1,0:T(8,128)S(1)}, f32[256,256]{1,0:T(8,128)S(1)}, u32[]{:S(2)}, u32[]{:S(2)}) collective-permute-start(f32[256,256]{1,0:T(8,128)S(1)} %get-tuple-element.60), channel_id=1, source_target_pairs={{0,64},{64,0},{1,65},{65,1},{2,66},{66,2},{3,67},{67,3},{4,68},{68... | collective-permute-start | bytes 786440 | tf_op jit(solution)/shard_map/ppermute | solution.py:284
  79.8 9.3 %collective-permute-start.12 = (f32[256,256]{1,0:T(8,128)S(1)}, f32[256,256]{1,0:T(8,128)S(1)}, u32[]{:S(2)}, u32[]{:S(2)}) collective-permute-start(f32[256,256]{1,0:T(8,128)S(1)} %shard_map.117), channel_id=1, source_target_pairs={{0,2},{1,3},{2,0},{3,1},{4,6},{5,7},{6,4},{7,5},{8,10},{9,11},{10,... | collective-permute-start | bytes 786440 | tf_op jit(solution)/shard_map/ppermute | solution.py:287
  81.0 3.6 %copy-start = (f32[256,256]{1,0:T(8,128)S(1)}, f32[256,256]{1,0:T(8,128)}, u32[]{:S(2)}) copy-start(f32[256,256]{1,0:T(8,128)} %w_msg.1) | copy-start | bytes 786436
  81.0 3.6 %copy-start.4 = (s32[2,5]{1,0:T(2,128)S(1)}, s32[2,5]{1,0:T(2,128)}, u32[]{:S(2)}) copy-start(s32[2,5]{1,0:T(2,128)} %neighbours.1) | copy-start | bytes 124
  81.0 3.6 %copy-start.5 = (s32[2]{0:T(128)S(1)}, s32[2]{0:T(128)}, u32[]{:S(2)}) copy-start(s32[2]{0:T(128)} %nbr_count.1) | copy-start | bytes 28
  81.0 14.2 %copy-start.1 = (f32[256,256]{1,0:T(8,128)S(1)}, f32[256,256]{1,0:T(8,128)}, u32[]{:S(2)}) copy-start(f32[256,256]{1,0:T(8,128)} %w_one.1) | copy-start | bytes 786436
  81.0 14.2 %copy-start.2 = (f32[256,256]{1,0:T(8,128)S(1)}, f32[256,256]{1,0:T(8,128)}, u32[]{:S(2)}) copy-start(f32[256,256]{1,0:T(8,128)} %w_two.1) | copy-start | bytes 786436
  81.8 13.4 %collective-permute-start.13 = (f32[256,256]{1,0:T(8,128)}, f32[256,256]{1,0:T(8,128)S(1)}, u32[]{:S(2)}, u32[]{:S(2)}) collective-permute-start(f32[256,256]{1,0:T(8,128)} %get-tuple-element.65), channel_id=1, source_target_pairs={{0,1},{1,2},{2,3},{3,0},{4,5},{5,6},{6,7},{7,4},{8,9},{9,10},{10,1... | collective-permute-start | bytes 786440 | tf_op jit(solution)/shard_map/ppermute | solution.py:290
  84.5 10.7 %collective-permute-start.14 = (f32[256,256]{1,0:T(8,128)S(1)}, f32[256,256]{1,0:T(8,128)S(1)}, u32[]{:S(2)}, u32[]{:S(2)}) collective-permute-start(f32[256,256]{1,0:T(8,128)S(1)} %get-tuple-element.66), channel_id=1, source_target_pairs={{0,3},{1,0},{2,1},{3,2},{4,7},{5,4},{6,5},{7,6},{8,11},{9,8},{10,9... | collective-permute-start | bytes 786440 | tf_op jit(solution)/shard_map/ppermute | solution.py:291

commit v5 on v4

--- a/solution.py
+++ b/solution.py
@@ -71,7 +71,8 @@
 
 
 def lattice(own, groups):
-    def kernel(kv, out, flat):
+    def kernel(kv, w_val, out, wh, wl, flat):
+        wh[...], wl[...] = split(w_val[...])
         flat[...] = jnp.zeros(flat.shape, F32)
         pad = jnp.zeros((8, flat.shape[1] - 128), F32)
         for g in range(groups):
@@ -85,12 +86,12 @@
 def forward(cells, cell, count, own, groups, first):
     slots = cells * cell
 
-    def kernel(lhs, w_val, *refs):
+    def kernel(lhs, wh, wl, *refs):
         chunks, refs = refs[:count], refs[count:]
         if not first:
             before, refs = refs[0], refs[1:]
         out, mh, ml = refs
-        w = split(w_val[...])
+        w = wh[...], wl[...]
         for j, chunk in enumerate(chunks):
             live = live_rows(chunk, cells, cell)
             v = split(jnp.where(live, dot3(split(chunk[:slots]), w), 0.0))
@@ -136,9 +137,12 @@
 
 
 def backward(chunks):
-    def kernel(fh, fl, mh, ml, *outs):
-        for j, out in zip(chunks, outs):
-            out[...] = dot3((fh[...], fl[...]), (mh[j], ml[j]))
+    def kernel(fh, fl, mh, ml, *refs):
+        count = len(chunks)
+        outs, added = refs[-count:], refs[:-count]
+        for j, out in enumerate(outs):
+            part = dot3((fh[...], fl[...]), (mh[chunks[j]], ml[chunks[j]]))
+            out[...] = part + added[j][...] if added else part
 
     return kernel
 
@@ -242,29 +246,34 @@
     above = lax.ppermute(payload, X, shift(X, -1))
     below = lax.ppermute(payload, X, shift(X, 1))
     other = [lax.ppermute(payload, "rows", shift("rows", 1))]
-
     kv = lax.dynamic_slice_in_dim(kvec * (0.5 / math.pi), half * own_waves, own_waves, 1)
     kv = jnp.pad(kv, ((0, 8 - kv.shape[0]), (0, 128 - own_waves)))
-    kv = lax.all_to_all(jnp.broadcast_to(kv[None], (group, *kv.shape)), (Z, Y), 0, 0, tiled=True)
-    kv, near2, above, below, again = lax.optimization_barrier((kv, near2, above, below, payload))
+    kv = jnp.broadcast_to(kv[None], (group, *kv.shape))
+    kv, again = lax.optimization_barrier((kv, payload))
+    kv = lax.all_to_all(kv, (Z, Y), 0, 0, tiled=True)
     ends = [(d, (d + 1) % devices) for d in range(devices) if d % nx == nx - 1]
     ends = ends + [(b, a) for a, b in ends]
     edge = lax.ppermute(again, ROWS_WAVES, ends)
-
-    lhs = call(lattice(own_waves, group), halves(waves, 48), 1, [pltpu.VMEM((8, waves), F32)])(kv)
+    lhs, *w = call(
+        lattice(own_waves, group),
+        (halves(waves, 48), halves(width, width), halves(width, width)),
+        2,
+        [pltpu.VMEM((8, waves), F32)],
+    )(kv, w_val)
+    lhs, near2, above, below = lax.optimization_barrier((lhs, near2, above, below))
     line = (payload, above, below, near2)
     other += [lax.ppermute(c, "rows", shift("rows", 1)) for c in line[1:]]
+    lhs, edge = lax.optimization_barrier((lhs, edge))
     count = len(line)
     wide = halves(count, 2 * waves, slots)
     sums = floats(2 * waves, width)
     work = 12 * count * waves * slots * width
-    part, *mine = call(forward(cells, cell, count, own_waves, group, True), (sums, wide, wide), 2 + count, flops=work)(
-        lhs, w_val, *line
+    part, *mine = call(forward(cells, cell, count, own_waves, group, True), (sums, wide, wide), 3 + count, flops=work)(
+        lhs, *w, *line
     )
-    part, *theirs = call(forward(cells, cell, count, own_waves, group, False), (sums, wide, wide), 3 + count, flops=work)(
-        lhs, w_val, *other, part
+    part, *theirs = call(forward(cells, cell, count, own_waves, group, False), (sums, wide, wide), 4 + count, flops=work)(
+        lhs, *w, *other, part
     )
-    part, edge = lax.optimization_barrier((part, edge))
     parts = lax.all_to_all(part.reshape(group, 2 * own_waves, width), (Z, Y), 0, 0, tiled=True)
     scale = 1.0 / math.sqrt(float(slots * devices) * float(waves * rows * nx))
     spread = call(filtered(scale), floats(*parts.shape), 3, smem=(0,))(half.reshape(1), parts, filters)
@@ -274,19 +283,19 @@
     one = floats(width, slots)
     swap = shift("rows", 1)
 
-    def back(chunks, ft, waves_of):
+    def back(chunks, ft, waves_of, *added):
         flops = len(chunks) * work // count
-        return call(backward(chunks), (one,) * len(chunks), 4, flops=flops)(*ft, *waves_of)
+        outs = (one,) * len(chunks)
+        return call(backward(chunks), outs, 4 + len(added), flops=flops)(*ft, *waves_of, *added)
 
     (far,) = back((3,), ft, theirs)
     there = lax.ppermute(far, "rows", swap)
     ft = lax.optimization_barrier((*ft, far))[:2]
     rest = [lax.ppermute(r, "rows", swap) for r in back((0, 1, 2), ft, theirs)]
-    (e3,) = call(pairs, (one,), 2)(*back((3,), ft, mine), there)
+    (e3,) = back((3,), ft, mine, there)
     e3, *ft = lax.optimization_barrier((e3, *ft))
     e3 = lax.ppermute(e3, X, shift(X, 2))
-    near = back((0, 1, 2), ft, mine)
-    e0, e1, e2 = call(pairs, (one,) * 3, 6)(*near, *rest)
+    e0, e1, e2 = back((0, 1, 2), ft, mine, *rest)
     e1 = lax.ppermute(e1, X, shift(X, 1))
     e2 = lax.ppermute(e2, X, shift(X, -1))
 

time: 97.2 us -> 98 us (level)
  waiting for transfers between devices: 14.3 us -> 18.7 us
  starting transfers between devices: 29.3 us -> 25.6 us
    all_to_all x1, waiting for transfers between devices: 4.64 us -> 9.73 us  [shards(): kv = lax.all_to_all(kv, (Z, Y), 0, 0, tiled=True)]
    ppermute x1, starting transfers between devices: 5.15 us -> 10.1 us  [shards(): edge = lax.ppermute(again, ROWS_WAVES, ends)]
    all_to_all x1, starting transfers between devices: 7.77 us -> 3.51 us  [shards(): kv = lax.all_to_all(kv, (Z, Y), 0, 0, tiled=True)]
    ppermute x3, starting transfers between devices: 3.53 us -> 0.98 us  [shards(): other += [lax.ppermute(c, 'rows', shift('rows', 1)) for c in line[1:]]]
    ppermute x1, starting transfers between devices: 3.65 us -> 1.65 us  [shards(): near2 = lax.ppermute(payload, X, shift(X, 2))]
    ppermute x1, starting transfers between devices: 1.87 us -> 0.09 us  [shards(): other = [lax.ppermute(payload, 'rows', shift('rows', 1))]]
    ppermute x1, starting transfers between devices: 0.61 us -> 2.11 us  [shards(): below = lax.ppermute(payload, X, shift(X, 1))]
    pallas_call x7 -> x5, Pallas kernels: 4.12 us -> 4.02 us  [the longest x4 3.82 us: back(): call(backward(chunks), outs, 4 + len(added), flops=flops)]
  transfers between devices with their start and end apart: 16 -> 16, of which waited for: 4 -> 6; matrix products, arithmetic and copies ran while one was open for 1% -> 1% of each run, Pallas kernels for 14% -> 10%
where the time goes in v5:
time: 98 us; the launch traced here: 97.7 us
  blocking collectives  33 us (34%)
  starting transfers between devices  25.6 us (26%)
  waiting for transfers between devices  18.7 us (19%)
  Pallas kernels  16.2 us (17%)
  other arithmetic  2.33 us (2%)
  local copies, waits for them, and re-layouts  1.7 us (2%)
    all_to_all x1, blocking collectives, shards(): lax.all_to_all(part.reshape(group, 2 * own_waves, width), (Z, Y), 0, 0, t...  16.9 us
    all_to_all x1, blocking collectives, shards(): lax.all_to_all(spread, (Z, Y), 0, 0, tiled=True).reshape(2 * waves, width)  16.1 us
    ppermute x1, starting transfers between devices, shards(): edge = lax.ppermute(again, ROWS_WAVES, ends)  10.1 us
    all_to_all x1, waiting for transfers between devices, shards(): kv = lax.all_to_all(kv, (Z, Y), 0, 0, tiled=True)  9.73 us
    ppermute x1, waiting for transfers between devices, shards(): e1 = lax.ppermute(e1, X, shift(X, 1))  6.13 us
    pallas_call x1, Pallas kernels, shards(): call(forward(cells, cell, count, own_waves, group, False), (sums, wide, w...  4.17 us
    pallas_call x1, Pallas kernels, shards(): call(forward(cells, cell, count, own_waves, group, True), (sums, wide, wi...  4.15 us
    pallas_call x4, Pallas kernels, back(): call(backward(chunks), outs, 4 + len(added), flops=flops)  3.82 us
  transfers between devices with their start and end apart: 16, of which 6 were waited for; matrix products, arithmetic and copies ran while one was open for 1% of the time, Pallas kernels for 10%

profile of v5, /device:TPU:1, one launch (start us, length us, event | category | flops | bytes accessed | tf_op | source)
XLA Modules:
  0.0 97.7 jit_solution(9706902726989262199)
XLA Ops:
  0.0 0.7 convert_bitcast_fusion
  0.7 1.0 %pad_add_fusion.own.refs_0_ = f32[264,256]{1,0:T(8,128)S(1)} fusion(f32[1,2]{1,0:T(1,128)S(1)} %convert_bitcast_fusion, f32[3,256]{1,0:T(4,128)} %param.12, f32[256,256]{1,0:T(8,128)} %param.11), kind=kLoop, calls=%fused_computation | loop fusion | flops 135168 | bytes 535560 | tf_op jit(solution)/shard_map/add | solution.py:244
  1.6 2.1 %collective-permute-start.2 = (f32[264,256]{1,0:T(8,128)S(1)}, f32[264,256]{1,0:T(8,128)S(1)}, u32[]{:S(2)}, u32[]{:S(2)}) collective-permute-start(f32[264,256]{1,0:T(8,128)S(1)} %pad_add_fusion.own.refs_0_), channel_id=1, source_target_pairs={{0,1},{1,2},{2,3},{3,0},{4,5},{5,6},{6,7},{7,4},{8,9},{9,10},{10,1... | collective-permute-start | bytes 811016 | tf_op jit(solution)/shard_map/ppermute | solution.py:247
  3.8 1.3 %collective-permute-start.1 = (f32[264,256]{1,0:T(8,128)S(1)}, f32[264,256]{1,0:T(8,128)S(1)}, u32[]{:S(2)}, u32[]{:S(2)}) collective-permute-start(f32[264,256]{1,0:T(8,128)S(1)} %pad_add_fusion.own.refs_0_), channel_id=1, source_target_pairs={{0,3},{1,0},{2,1},{3,2},{4,7},{5,4},{6,5},{7,6},{8,11},{9,8},{10,9... | collective-permute-start | bytes 811016 | tf_op jit(solution)/shard_map/ppermute | solution.py:246
  5.1 1.6 %collective-permute-start = (f32[264,256]{1,0:T(8,128)S(1)}, f32[264,256]{1,0:T(8,128)S(1)}, u32[]{:S(2)}, u32[]{:S(2)}) collective-permute-start(f32[264,256]{1,0:T(8,128)S(1)} %pad_add_fusion.own.refs_0_), channel_id=1, source_target_pairs={{0,2},{1,3},{2,0},{3,1},{4,6},{5,7},{6,4},{7,5},{8,10},{9,11},{10,... | collective-permute-start | bytes 811016 | tf_op jit(solution)/shard_map/ppermute | solution.py:245
  6.8 0.7 broadcast_multiply_fusion
  7.4 0.1 constant_dynamic-slice_fusion
  7.5 0.6 broadcast_in_dim.10
  8.2 10.1 %collective-permute-start.3 = (f32[264,256]{1,0:T(8,128)S(1)}, f32[264,256]{1,0:T(8,128)S(1)}, u32[]{:S(2)}, u32[]{:S(2)}) collective-permute-start(f32[264,256]{1,0:T(8,128)S(1)} %pad_add_fusion.own.refs_0_), channel_id=1, source_target_pairs={{3,4},{7,8},{11,12},{15,16},{19,20},{23,24},{27,28},{31,32},{35,36... | collective-permute-start | bytes 811016 | tf_op jit(solution)/shard_map/ppermute | solution.py:256
  18.2 3.5 %all-to-all-start = ((f32[16,8,128]{2,1,0:T(8,128)}), f32[16,8,128]{2,1,0:T(8,128)S(1)}, u32[]{:S(2)}, u32[]{:S(2)}) async-start(f32[16,8,128]{2,1,0:T(8,128)} %broadcast_in_dim.10), calls=%async_computation | async-start | bytes 131072 | tf_op jit(solution)/shard_map/all_to_all | solution.py:253
  21.8 0.1 collective-permute-start.4
  21.9 9.7 %all-to-all-done.kv = f32[16,8,128]{2,1,0:T(8,128)S(1)} async-done(((f32[16,8,128]{2,1,0:T(8,128)}), f32[16,8,128]{2,1,0:T(8,128)S(1)}, u32[]{:S(2)}, u32[]{:S(2)}) %all-to-all-start) | async-done | bytes 65568 | tf_op jit(solution)/shard_map/all_to_all | solution.py:253
  31.6 0.9 copy-done.3
  32.5 0.2 shard_map.109
  32.8 0.0 collective-permute-done.1.high.refs_1_
  32.8 0.0 collective-permute-done.refs_3_
  32.8 0.5 collective-permute-start.7
  33.3 0.1 collective-permute-start.6
  33.4 0.4 collective-permute-start.5
  33.8 0.0 collective-permute-done.3.edge
  33.8 4.2 %shard_map.111 = (f32[768,256]{1,0:T(8,128)S(1)}, bf16[4,768,256]{2,1,0:T(8,128)(2,1)S(1)}, bf16[4,768,256]{2,1,0:T(8,128)(2,1)S(1)}) custom-call(bf16[384,48]{1,0:T(8,128)(2,1)S(1)} %get-tuple-element.46.lhs, bf16[256,256]{1,0:T(8,128)(2,1)S(1)} %get-tuple-element.47.wh, bf16[256,256]{1,0:T(8,128)(2,1)S(1)} %get-tuple-element.48.wl, ...), custom_call_target="tpu_custom_call" | custom-call | flops 1207959552 | bytes 65536 | tf_op jit(solution)/shard_map/pallas_call | solution.py:271
  38.0 4.2 %shard_map.112 = (f32[768,256]{1,0:T(8,128)S(1)}, bf16[4,768,256]{2,1,0:T(8,128)(2,1)S(1)}, bf16[4,768,256]{2,1,0:T(8,128)(2,1)S(1)}) custom-call(bf16[384,48]{1,0:T(8,128)(2,1)S(1)} %get-tuple-element.46.lhs, bf16[256,256]{1,0:T(8,128)(2,1)S(1)} %get-tuple-element.47.wh, bf16[256,256]{1,0:T(8,128)(2,1)S(1)} %get-tuple-element.48.wl, ...), custom_call_target="tpu_custom_call" | custom-call | flops 1207959552 | bytes 65536 | tf_op jit(solution)/shard_map/pallas_call | solution.py:274
  42.1 0.0 copy-start.4
  42.2 16.9 %all_to_all.15.parts = f32[16,48,256]{2,1,0:T(8,128)S(1)} all-to-all(f32[16,48,256]{2,1,0:T(8,128)S(1)} %bitcast.8), channel_id=1, replica_groups=mesh['rows'=2,'waves_0'=4,'waves_1'=4,'waves_2'=4] {'waves_0','waves_1'}, dimensions={0} | all-to-all | bytes 1572864 | tf_op jit(solution)/shard_map/all_to_all | solution.py:277
  59.1 0.1 shard_map.113
  59.2 16.1 %all_to_all.16 = f32[16,48,256]{2,1,0:T(8,128)S(1)} all-to-all(f32[16,48,256]{2,1,0:T(8,128)S(1)} %shard_map.113), channel_id=1, replica_groups=mesh['rows'=2,'waves_0'=4,'waves_1'=4,'waves_2'=4] {'waves_0','waves_1'}, dimensions={0} | all-to-all | bytes 1572864 | tf_op jit(solution)/shard_map/all_to_all | solution.py:280
  75.2 0.3 shard_map.114
  75.5 0.5 shard_map.115
  76.0 2.2 %collective-permute-start.8 = (f32[256,256]{1,0:T(8,128)S(1)}, f32[256,256]{1,0:T(8,128)S(1)}, u32[]{:S(2)}, u32[]{:S(2)}) collective-permute-start(f32[256,256]{1,0:T(8,128)S(1)} %shard_map.115), channel_id=1, source_target_pairs={{0,64},{64,0},{1,65},{65,1},{2,66},{66,2},{3,67},{67,3},{4,68},{68... | collective-permute-start | bytes 786440 | tf_op jit(solution)/shard_map/ppermute | solution.py:292
  78.2 1.1 %shard_map.117 = (f32[256,256]{1,0:T(8,128)S(1)}, f32[256,256]{1,0:T(8,128)S(1)}, f32[256,256]{1,0:T(8,128)S(1)}) custom-call(bf16[256,768]{1,0:T(8,128)(2,1)S(1)} %get-tuple-element.60.fh, bf16[256,768]{1,0:T(8,128)(2,1)S(1)} %get-tuple-element.61.fl, bf16[4,768,256]{2,1,0:T(8,128)(2,1)S(1)} %get-tuple-element.54.mh, ...), custom_call_target="tpu_custom_call" | custom-call | flops 905969664 | bytes 65536 | tf_op jit(solution)/shard_map/pallas_call | solution.py:289
  79.2 0.1 collective-permute-start.9
  79.3 0.5 collective-permute-start.10
  79.8 0.3 collective-permute-start.11
  80.1 0.5 shard_map.116
  80.6 0.0 copy-start
  80.6 0.0 copy-start.5
  80.6 0.0 copy-start.6
  80.6 0.1 collective-permute-start.12
  80.7 0.1 collective-permute-done.9.refs_0_
  80.8 0.4 collective-permute-done.10.refs_1_
  81.2 0.4 collective-permute-done.11.refs_2_
  81.6 1.8 %shard_map.118 = (f32[256,256]{1,0:T(8,128)S(1)}, f32[256,256]{1,0:T(8,128)}, f32[256,256]{1,0:T(8,128)S(1)}) custom-call(bf16[256,768]{1,0:T(8,128)(2,1)S(1)} %get-tuple-element.60.fh, bf16[256,768]{1,0:T(8,128)(2,1)S(1)} %get-tuple-element.61.fl, bf16[4,768,256]{2,1,0:T(8,128)(2,1)S(1)} %get-tuple-element.58.mh, ...), custom_call_target="tpu_custom_call" | custom-call | flops 905969664 | bytes 65536 | tf_op jit(solution)/shard_map/pallas_call | solution.py:289
  83.4 1.8 %collective-permute-start.13 = (f32[256,256]{1,0:T(8,128)}, f32[256,256]{1,0:T(8,128)S(1)}, u32[]{:S(2)}, u32[]{:S(2)}) collective-permute-start(f32[256,256]{1,0:T(8,128)} %get-tuple-element.67), channel_id=1, source_target_pairs={{0,1},{1,2},{2,3},{3,0},{4,5},{5,6},{6,7},{7,4},{8,9},{9,10},{10,1... | collective-permute-start | bytes 786440 | tf_op jit(solution)/shard_map/ppermute | solution.py:299
  85.2 0.9 collective-permute-start.14
  86.1 1.9 %shard_map.110 = (f32[256,256]{1,0:T(8,128)S(1)}, f32[256,128]{1,0:T(8,128)S(1)}) custom-call(s32[1]{0:T(128)} %bitcast.at_x, s32[1]{0:T(128)} %bitcast.1.at_cell, s32[2,5]{1,0:T(2,128)S(1)} %copy-done.5, s32[2]{0:T(128)S(1)} %copy-done.6, f32[264,256]{1,0:T(8,128)S(1)} %pad_add_fusion.own.refs_0_, f32[264,256]{1,0:T(8,128)S(1)} %collective-permute-done.2.low.refs_2_, ...), custom_call_target="tpu_custom_call" | custom-call | flops 301989888 | bytes 65536 | tf_op jit(solution)/shard_map/pallas_call | solution.py:302
  88.0 2.0 %collective-permute-done.12.refs_1_ = f32[256,256]{1,0:T(8,128)S(1)} collective-permute-done((f32[256,256]{1,0:T(8,128)S(1)}, f32[256,256]{1,0:T(8,128)S(1)}, u32[]{:S(2)}, u32[]{:S(2)}) %collective-permute-start.12) | collective-permute-done | bytes 262176 | tf_op jit(solution)/shard_map/ppermute | solution.py:297
  90.0 6.1 %collective-permute-done.13.b = f32[256,256]{1,0:T(8,128)S(1)} collective-permute-done((f32[256,256]{1,0:T(8,128)}, f32[256,256]{1,0:T(8,128)S(1)}, u32[]{:S(2)}, u32[]{:S(2)}) %collective-permute-start.13) | collective-permute-done | bytes 262176 | tf_op jit(solution)/shard_map/ppermute | solution.py:299
  96.1 1.5 %shard_map.120 = f32[256,256]{1,0:T(8,128)} custom-call(f32[256,256]{1,0:T(8,128)S(1)} %get-tuple-element.44.base, f32[256,128]{1,0:T(8,128)S(1)} %get-tuple-element.45.mask, f32[256,256]{1,0:T(8,128)S(1)} %shard_map.119.a, f32[256,256]{1,0:T(8,128)S(1)} %collective-permute-done.13.b, f32[256,256]{1,0:T(8,128)S(1)} %collective-permute-done.14.c, ...), custom_call_target="tpu_custom_call" | custom-call | bytes 65536 | tf_op jit(solution)/shard_map/pallas_call | solution.py:310
  (18 shorter events, 0.1 us)
Async XLA Ops:
  1.6 31.1 %collective-permute-start.2 = (f32[264,256]{1,0:T(8,128)S(1)}, f32[264,256]{1,0:T(8,128)S(1)}, u32[]{:S(2)}, u32[]{:S(2)}) collective-permute-start(f32[264,256]{1,0:T(8,128)S(1)} %pad_add_fusion.own.refs_0_), channel_id=1, source_target_pairs={{0,1},{1,2},{2,3},{3,0},{4,5},{5,6},{6,7},{7,4},{8,9},{9,10},{10,1... | collective-permute-start | bytes 811016 | tf_op jit(solution)/shard_map/ppermute | solution.py:247
  3.8 29.0 %collective-permute-start.1 = (f32[264,256]{1,0:T(8,128)S(1)}, f32[264,256]{1,0:T(8,128)S(1)}, u32[]{:S(2)}, u32[]{:S(2)}) collective-permute-start(f32[264,256]{1,0:T(8,128)S(1)} %pad_add_fusion.own.refs_0_), channel_id=1, source_target_pairs={{0,3},{1,0},{2,1},{3,2},{4,7},{5,4},{6,5},{7,6},{8,11},{9,8},{10,9... | collective-permute-start | bytes 811016 | tf_op jit(solution)/shard_map/ppermute | solution.py:246
  5.1 27.7 %collective-permute-start = (f32[264,256]{1,0:T(8,128)S(1)}, f32[264,256]{1,0:T(8,128)S(1)}, u32[]{:S(2)}, u32[]{:S(2)}) collective-permute-start(f32[264,256]{1,0:T(8,128)S(1)} %pad_add_fusion.own.refs_0_), channel_id=1, source_target_pairs={{0,2},{1,3},{2,0},{3,1},{4,6},{5,7},{6,4},{7,5},{8,10},{9,11},{10,... | collective-permute-start | bytes 811016 | tf_op jit(solution)/shard_map/ppermute | solution.py:245
  8.2 25.6 %collective-permute-start.3 = (f32[264,256]{1,0:T(8,128)S(1)}, f32[264,256]{1,0:T(8,128)S(1)}, u32[]{:S(2)}, u32[]{:S(2)}) collective-permute-start(f32[264,256]{1,0:T(8,128)S(1)} %pad_add_fusion.own.refs_0_), channel_id=1, source_target_pairs={{3,4},{7,8},{11,12},{15,16},{19,20},{23,24},{27,28},{31,32},{35,36... | collective-permute-start | bytes 811016 | tf_op jit(solution)/shard_map/ppermute | solution.py:256
  18.2 13.3 %all-to-all-start = ((f32[16,8,128]{2,1,0:T(8,128)}), f32[16,8,128]{2,1,0:T(8,128)S(1)}, u32[]{:S(2)}, u32[]{:S(2)}) async-start(f32[16,8,128]{2,1,0:T(8,128)} %broadcast_in_dim.10), calls=%async_computation | async-start | bytes 131072 | tf_op jit(solution)/shard_map/all_to_all | solution.py:253
  21.8 16.2 %collective-permute-start.4 = (f32[264,256]{1,0:T(8,128)S(1)}, f32[264,256]{1,0:T(8,128)S(1)}, u32[]{:S(2)}, u32[]{:S(2)}) collective-permute-start(f32[264,256]{1,0:T(8,128)S(1)} %pad_add_fusion.own.refs_0_), channel_id=1, source_target_pairs={{0,64},{64,0},{1,65},{65,1},{2,66},{66,2},{3,67},{67,3},{4,68},{68... | collective-permute-start | bytes 811016 | tf_op jit(solution)/shard_map/ppermute | solution.py:248
  31.6 1.0 copy-start.3
  32.8 5.2 %collective-permute-start.7 = (f32[264,256]{1,0:T(8,128)S(1)}, f32[264,256]{1,0:T(8,128)S(1)}, u32[]{:S(2)}, u32[]{:S(2)}) collective-permute-start(f32[264,256]{1,0:T(8,128)S(1)} %collective-permute-done.refs_3_), channel_id=1, source_target_pairs={{0,64},{64,0},{1,65},{65,1},{2,66},{66,2},{3,67},{67,3},{4,68},{68... | collective-permute-start | bytes 811016 | tf_op jit(solution)/shard_map/ppermute | solution.py:265
  33.3 4.7 %collective-permute-start.6 = (f32[264,256]{1,0:T(8,128)S(1)}, f32[264,256]{1,0:T(8,128)S(1)}, u32[]{:S(2)}, u32[]{:S(2)}) collective-permute-start(f32[264,256]{1,0:T(8,128)S(1)} %collective-permute-done.2.low.refs_2_), channel_id=1, source_target_pairs={{0,64},{64,0},{1,65},{65,1},{2,66},{66,2},{3,67},{67,3},{4,68},{68... | collective-permute-start | bytes 811016 | tf_op jit(solution)/shard_map/ppermute | solution.py:265
  33.4 4.6 %collective-permute-start.5 = (f32[264,256]{1,0:T(8,128)S(1)}, f32[264,256]{1,0:T(8,128)S(1)}, u32[]{:S(2)}, u32[]{:S(2)}) collective-permute-start(f32[264,256]{1,0:T(8,128)S(1)} %collective-permute-done.1.high.refs_1_), channel_id=1, source_target_pairs={{0,64},{64,0},{1,65},{65,1},{2,66},{66,2},{3,67},{67,3},{4,68},{68... | collective-permute-start | bytes 811016 | tf_op jit(solution)/shard_map/ppermute | solution.py:265
  42.1 16.9 %copy-start.4 = (f32[48,256]{1,0:T(8,128)S(1)}, f32[48,256]{1,0:T(8,128)}, u32[]{:S(2)}) copy-start(f32[48,256]{1,0:T(8,128)} %filters.1) | copy-start | bytes 147460
  76.0 4.1 %collective-permute-start.8 = (f32[256,256]{1,0:T(8,128)S(1)}, f32[256,256]{1,0:T(8,128)S(1)}, u32[]{:S(2)}, u32[]{:S(2)}) collective-permute-start(f32[256,256]{1,0:T(8,128)S(1)} %shard_map.115), channel_id=1, source_target_pairs={{0,64},{64,0},{1,65},{65,1},{2,66},{66,2},{3,67},{67,3},{4,68},{68... | collective-permute-start | bytes 786440 | tf_op jit(solution)/shard_map/ppermute | solution.py:292
  79.2 1.6 %collective-permute-start.9 = (f32[256,256]{1,0:T(8,128)S(1)}, f32[256,256]{1,0:T(8,128)S(1)}, u32[]{:S(2)}, u32[]{:S(2)}) collective-permute-start(f32[256,256]{1,0:T(8,128)S(1)} %get-tuple-element.62), channel_id=1, source_target_pairs={{0,64},{64,0},{1,65},{65,1},{2,66},{66,2},{3,67},{67,3},{4,68},{68... | collective-permute-start | bytes 786440 | tf_op jit(solution)/shard_map/ppermute | solution.py:294
  79.3 1.9 %collective-permute-start.10 = (f32[256,256]{1,0:T(8,128)S(1)}, f32[256,256]{1,0:T(8,128)S(1)}, u32[]{:S(2)}, u32[]{:S(2)}) collective-permute-start(f32[256,256]{1,0:T(8,128)S(1)} %get-tuple-element.63), channel_id=1, source_target_pairs={{0,64},{64,0},{1,65},{65,1},{2,66},{66,2},{3,67},{67,3},{4,68},{68... | collective-permute-start | bytes 786440 | tf_op jit(solution)/shard_map/ppermute | solution.py:294
  79.8 1.8 %collective-permute-start.11 = (f32[256,256]{1,0:T(8,128)S(1)}, f32[256,256]{1,0:T(8,128)S(1)}, u32[]{:S(2)}, u32[]{:S(2)}) collective-permute-start(f32[256,256]{1,0:T(8,128)S(1)} %get-tuple-element.64), channel_id=1, source_target_pairs={{0,64},{64,0},{1,65},{65,1},{2,66},{66,2},{3,67},{67,3},{4,68},{68... | collective-permute-start | bytes 786440 | tf_op jit(solution)/shard_map/ppermute | solution.py:294
  80.6 5.5 %copy-start = (f32[256,256]{1,0:T(8,128)S(1)}, f32[256,256]{1,0:T(8,128)}, u32[]{:S(2)}) copy-start(f32[256,256]{1,0:T(8,128)} %w_msg.1) | copy-start | bytes 786436
  80.6 5.5 %copy-start.5 = (s32[2,5]{1,0:T(2,128)S(1)}, s32[2,5]{1,0:T(2,128)}, u32[]{:S(2)}) copy-start(s32[2,5]{1,0:T(2,128)} %neighbours.1) | copy-start | bytes 124
  80.6 5.5 %copy-start.6 = (s32[2]{0:T(128)S(1)}, s32[2]{0:T(128)}, u32[]{:S(2)}) copy-start(s32[2]{0:T(128)} %nbr_count.1) | copy-start | bytes 28
  80.6 9.3 %collective-permute-start.12 = (f32[256,256]{1,0:T(8,128)S(1)}, f32[256,256]{1,0:T(8,128)S(1)}, u32[]{:S(2)}, u32[]{:S(2)}) collective-permute-start(f32[256,256]{1,0:T(8,128)S(1)} %shard_map.116), channel_id=1, source_target_pairs={{0,2},{1,3},{2,0},{3,1},{4,6},{5,7},{6,4},{7,5},{8,10},{9,11},{10,... | collective-permute-start | bytes 786440 | tf_op jit(solution)/shard_map/ppermute | solution.py:297
  83.4 12.7 %copy-start.1 = (f32[256,256]{1,0:T(8,128)S(1)}, f32[256,256]{1,0:T(8,128)}, u32[]{:S(2)}) copy-start(f32[256,256]{1,0:T(8,128)} %w_one.1) | copy-start | bytes 786436
  83.4 12.7 %copy-start.2 = (f32[256,256]{1,0:T(8,128)S(1)}, f32[256,256]{1,0:T(8,128)}, u32[]{:S(2)}) copy-start(f32[256,256]{1,0:T(8,128)} %w_two.1) | copy-start | bytes 786436
  83.4 12.7 %collective-permute-start.13 = (f32[256,256]{1,0:T(8,128)}, f32[256,256]{1,0:T(8,128)S(1)}, u32[]{:S(2)}, u32[]{:S(2)}) collective-permute-start(f32[256,256]{1,0:T(8,128)} %get-tuple-element.67), channel_id=1, source_target_pairs={{0,1},{1,2},{2,3},{3,0},{4,5},{5,6},{6,7},{7,4},{8,9},{9,10},{10,1... | collective-permute-start | bytes 786440 | tf_op jit(solution)/shard_map/ppermute | solution.py:299
  85.2 10.9 %collective-permute-start.14 = (f32[256,256]{1,0:T(8,128)S(1)}, f32[256,256]{1,0:T(8,128)S(1)}, u32[]{:S(2)}, u32[]{:S(2)}) collective-permute-start(f32[256,256]{1,0:T(8,128)S(1)} %get-tuple-element.68), channel_id=1, source_target_pairs={{0,3},{1,0},{2,1},{3,2},{4,7},{5,4},{6,5},{7,6},{8,11},{9,8},{10,9... | collective-permute-start | bytes 786440 | tf_op jit(solution)/shard_map/ppermute | solution.py:300

commit v6 on v5

--- a/solution.py
+++ b/solution.py
@@ -15,7 +15,7 @@
 BF16 = jnp.bfloat16
 
 SIN_POLY = (6.283185280154403, -10.33542015333633, 5.100154773052372, -1.1965808225334407, 0.15531182448662934)
-COS_POLY = (0.9999999997791529, -4.934802136928833, 4.058709154760502, -1.335211949366169, 0.23493706849740192, -0.0243959319559508)
+COS_POLY = (0.999999953027512, -4.934792802489427, 4.058410790762133, -1.3318729727851486, 0.21968242357146)
 ROUNDER = 12582912.0
 
 
@@ -83,6 +83,18 @@
     return kernel
 
 
+def pack(own, groups):
+    def kernel(half, kvec, out, wide):
+        wide[...] = jnp.zeros(wide.shape, F32)
+        wide[0:3, 0 : 2 * own] = kvec[...] * (0.5 / math.pi)
+        k = jnp.where(half[0] == 0, wide[...], pltpu.roll(wide[...], 128 - own, 1))
+        k = jnp.where(lax.broadcasted_iota(jnp.int32, k.shape, 1) < own, k, 0.0)
+        for g in range(groups):
+            out[g] = k
+
+    return kernel
+
+
 def forward(cells, cell, count, own, groups, first):
     slots = cells * cell
 
@@ -92,27 +104,29 @@
             before, refs = refs[0], refs[1:]
         out, mh, ml = refs
         w = wh[...], wl[...]
-        for j, chunk in enumerate(chunks):
+        turns, right = [], []
+        for chunk in chunks:
             live = live_rows(chunk, cells, cell)
-            v = split(jnp.where(live, dot3(split(chunk[:slots]), w), 0.0))
+            vh, vl = split(jnp.where(live, dot3(split(chunk[:slots]), w), 0.0))
+            right += [vh, vh, vl]
             ph, pm, pl_ = thirds(chunk[slots : slots + 8])
-            turns = dot(lhs[...], jnp.concatenate([ph, pm, ph, pl_, pm, ph], axis=0).astype(BF16))
-            for g in range(groups):
-                t = turns[g * own : (g + 1) * own]
-                f = t - ((t + ROUNDER) - ROUNDER)
-                u = f * f
-                s = f * horner(SIN_POLY, u)
-                c = horner(COS_POLY, u)
-                both = jnp.concatenate([1.0 - 0.5 * (s * s), s * c], axis=0)
-                rows = slice(2 * own * g, 2 * own * (g + 1))
-                mh[j, rows], ml[j, rows] = split(both)
-            part = dot3((mh[j], ml[j]), v)
-            if j:
-                out[...] += part
-            elif first:
-                out[...] = part
-            else:
-                out[...] = before[...] + part
+            turns.append(dot(lhs[...], jnp.concatenate([ph, pm, ph, pl_, pm, ph], axis=0).astype(BF16)))
+        right = jnp.concatenate(right, axis=0)
+        for part in range(2):
+            for j in range(count):
+                for g in range(part * groups // 2, (part + 1) * groups // 2):
+                    t = turns[j][g * own : (g + 1) * own]
+                    f = t - ((t + ROUNDER) - ROUNDER)
+                    u = f * f
+                    s = f * horner(SIN_POLY, u)
+                    c = horner(COS_POLY, u)
+                    both = jnp.concatenate([1.0 - 0.5 * (s * s), s * c], axis=0)
+                    rows = slice(2 * own * g, 2 * own * (g + 1))
+                    mh[j, rows], ml[j, rows] = split(both)
+            rows = slice(part * own * groups, (part + 1) * own * groups)
+            left = [m[j, rows] for j in range(count) for m in (mh, ml, mh)]
+            total = dot(jnp.concatenate(left, axis=1), right)
+            out[rows] = total if first else before[rows] + total
 
     return kernel
 
@@ -137,12 +151,12 @@
 
 
 def backward(chunks):
-    def kernel(fh, fl, mh, ml, *refs):
+    def kernel(fh, fl, mh0, ml0, mh1, ml1, *refs):
         count = len(chunks)
         outs, added = refs[-count:], refs[:-count]
-        for j, out in enumerate(outs):
-            part = dot3((fh[...], fl[...]), (mh[chunks[j]], ml[chunks[j]]))
-            out[...] = part + added[j][...] if added else part
+        for j, (rest, at) in enumerate(chunks):
+            part = dot3((fh[...], fl[...]), (mh1[at], ml1[at]) if rest else (mh0[at], ml0[at]))
+            outs[j][...] = part + added[j][...] if added else part
 
     return kernel
 
@@ -245,35 +259,40 @@
     near2 = lax.ppermute(payload, X, shift(X, 2))
     above = lax.ppermute(payload, X, shift(X, -1))
     below = lax.ppermute(payload, X, shift(X, 1))
-    other = [lax.ppermute(payload, "rows", shift("rows", 1))]
-    kv = lax.dynamic_slice_in_dim(kvec * (0.5 / math.pi), half * own_waves, own_waves, 1)
-    kv = jnp.pad(kv, ((0, 8 - kv.shape[0]), (0, 128 - own_waves)))
-    kv = jnp.broadcast_to(kv[None], (group, *kv.shape))
+    kv = call(pack(own_waves, group), floats(group, 8, 128), 2, [pltpu.VMEM((8, 128), F32)], smem=(0,))(
+        half.reshape(1), kvec
+    )
     kv, again = lax.optimization_barrier((kv, payload))
-    kv = lax.all_to_all(kv, (Z, Y), 0, 0, tiled=True)
     ends = [(d, (d + 1) % devices) for d in range(devices) if d % nx == nx - 1]
     ends = ends + [(b, a) for a, b in ends]
     edge = lax.ppermute(again, ROWS_WAVES, ends)
+    kv = lax.all_to_all(kv, (Z, Y), 0, 0, tiled=True)
     lhs, *w = call(
         lattice(own_waves, group),
         (halves(waves, 48), halves(width, width), halves(width, width)),
         2,
         [pltpu.VMEM((8, waves), F32)],
     )(kv, w_val)
-    lhs, near2, above, below = lax.optimization_barrier((lhs, near2, above, below))
-    line = (payload, above, below, near2)
-    other += [lax.ppermute(c, "rows", shift("rows", 1)) for c in line[1:]]
-    lhs, edge = lax.optimization_barrier((lhs, edge))
-    count = len(line)
-    wide = halves(count, 2 * waves, slots)
-    sums = floats(2 * waves, width)
-    work = 12 * count * waves * slots * width
-    part, *mine = call(forward(cells, cell, count, own_waves, group, True), (sums, wide, wide), 3 + count, flops=work)(
-        lhs, *w, *line
-    )
-    part, *theirs = call(forward(cells, cell, count, own_waves, group, False), (sums, wide, wide), 4 + count, flops=work)(
-        lhs, *w, *other, part
-    )
+
+    unit = 12 * waves * slots * width
+
+    def sums(chunks, *before):
+        count = len(chunks)
+        m = halves(count, 2 * waves, slots)
+        return call(
+            forward(cells, cell, count, own_waves, group, not before),
+            (floats(2 * waves, width), m, m),
+            3 + count + len(before),
+            flops=count * unit,
+        )(lhs, *w, *chunks, *before)
+
+    part, *m_own = sums((payload,))
+    part, near2, above, below = lax.optimization_barrier((part, near2, above, below))
+    swap = shift("rows", 1)
+    other = [lax.ppermute(c, "rows", swap) for c in (again, above, below, near2)]
+    part, edge = lax.optimization_barrier((part, edge))
+    part, *m_line = sums((above, below, near2), part)
+    part, *m_other = sums(other, part)
     parts = lax.all_to_all(part.reshape(group, 2 * own_waves, width), (Z, Y), 0, 0, tiled=True)
     scale = 1.0 / math.sqrt(float(slots * devices) * float(waves * rows * nx))
     spread = call(filtered(scale), floats(*parts.shape), 3, smem=(0,))(half.reshape(1), parts, filters)
@@ -281,21 +300,21 @@
 
     ft = call(turned, (halves(width, 2 * waves),) * 2, 1)(f)
     one = floats(width, slots)
-    swap = shift("rows", 1)
-
-    def back(chunks, ft, waves_of, *added):
-        flops = len(chunks) * work // count
+
+    def back(chunks, ft, m, *added):
         outs = (one,) * len(chunks)
-        return call(backward(chunks), outs, 4 + len(added), flops=flops)(*ft, *waves_of, *added)
-
-    (far,) = back((3,), ft, theirs)
+        return call(backward(chunks), outs, 6 + len(added), flops=len(chunks) * unit)(*ft, *m, *added)
+
+    theirs = *m_other, *m_other
+    mine = *m_own, *m_line
+    (far,) = back(((0, 3),), ft, theirs)
     there = lax.ppermute(far, "rows", swap)
     ft = lax.optimization_barrier((*ft, far))[:2]
-    rest = [lax.ppermute(r, "rows", swap) for r in back((0, 1, 2), ft, theirs)]
-    (e3,) = back((3,), ft, mine, there)
+    rest = [lax.ppermute(r, "rows", swap) for r in back(((0, 0), (0, 1), (0, 2)), ft, theirs)]
+    (e3,) = back(((1, 2),), ft, mine, there)
     e3, *ft = lax.optimization_barrier((e3, *ft))
     e3 = lax.ppermute(e3, X, shift(X, 2))
-    e0, e1, e2 = back((0, 1, 2), ft, mine, *rest)
+    e0, e1, e2 = back(((0, 0), (1, 0), (1, 1)), ft, mine, *rest)
     e1 = lax.ppermute(e1, X, shift(X, 1))
     e2 = lax.ppermute(e2, X, shift(X, -1))
 
@@ -304,7 +323,7 @@
         (floats(slots, width), floats(slots, 128)),
         9,
         smem=(0, 1, 2, 3),
-        flops=work // 4,
+        flops=unit,
     )(x.reshape(1), first.reshape(1), neighbours, nbr_count, payload, below, above, edge, w_msg)
     (e0,) = call(pairs, (one,), 2)(e0, e3)
     return call(finish(), floats(slots, width), 7)(base, mask, e0, e1, e2, w_one, w_two)

time: 98 us -> 91.4 us (0.933)
  waiting for transfers between devices: 18.7 us -> 11.2 us
  starting transfers between devices: 25.6 us -> 31.4 us
  blocking collectives: 33 us -> 29.6 us
    all_to_all x1, waiting for transfers between devices: 9.73 us -> 0.01 us  [shards(): kv = lax.all_to_all(kv, (Z, Y), 0, 0, tiled=True)]
    all_to_all x1, starting transfers between devices: 3.51 us -> 7.77 us  [shards(): kv = lax.all_to_all(kv, (Z, Y), 0, 0, tiled=True)]
    ppermute x1, waiting for transfers between devices: 0.01 us -> 2.84 us  [shards(): edge = lax.ppermute(again, ROWS_WAVES, ends)]
    all_to_all x1, blocking collectives: 16.1 us -> 14.4 us  [shards(): lax.all_to_all(spread, (Z, Y), 0, 0, tiled=True).reshape(2 * waves, width)]
    ppermute x1, starting transfers between devices: 2.17 us -> 3.81 us  [shards(): there = lax.ppermute(far, 'rows', swap)]
    all_to_all x1, blocking collectives: 16.9 us -> 15.3 us  [shards(): lax.all_to_all(part.reshape(group, 2 * own_waves, width), (Z, Y), 0, 0, t...]
    ppermute x1, waiting for transfers between devices: 1.95 us -> 0.75 us  [shards(): e3 = lax.ppermute(e3, X, shift(X, 2))]
    ppermute x1, starting transfers between devices: 1.76 us -> 2.96 us  [shards(): e1 = lax.ppermute(e1, X, shift(X, 1))]
  transfers between devices with their start and end apart: 16 -> 16, of which waited for: 6 -> 7; matrix products, arithmetic and copies ran while one was open for 1% -> 0% of each run, Pallas kernels for 10% -> 11%
where the time goes in v6:
time: 91.4 us; the launch traced here: 91.1 us
  starting transfers between devices  31.4 us (34%)
  blocking collectives  29.6 us (32%)
  Pallas kernels  15.3 us (17%)
  waiting for transfers between devices  11.2 us (12%)
  local copies, waits for them, and re-layouts  1.66 us (2%)
  other arithmetic  1.64 us (2%)
    all_to_all x1, blocking collectives, shards(): lax.all_to_all(part.reshape(group, 2 * own_waves, width), (Z, Y), 0, 0, t...  15.3 us
    all_to_all x1, blocking collectives, shards(): lax.all_to_all(spread, (Z, Y), 0, 0, tiled=True).reshape(2 * waves, width)  14.4 us
    ppermute x1, starting transfers between devices, shards(): edge = lax.ppermute(again, ROWS_WAVES, ends)  9.13 us
    all_to_all x1, starting transfers between devices, shards(): kv = lax.all_to_all(kv, (Z, Y), 0, 0, tiled=True)  7.77 us
    pallas_call x3, Pallas kernels, sums(): call(forward(cells, cell, count, own_waves, group, not before), (floats(2...  6.77 us
    ppermute x1, waiting for transfers between devices, shards(): e1 = lax.ppermute(e1, X, shift(X, 1))  6.42 us
    pallas_call x4, Pallas kernels, back(): call(backward(chunks), outs, 6 + len(added), flops=len(chunks) * unit)  3.82 us
    ppermute x1, starting transfers between devices, shards(): there = lax.ppermute(far, 'rows', swap)  3.81 us
  transfers between devices with their start and end apart: 16, of which 7 were waited for; matrix products, arithmetic and copies ran while one was open for 0% of the time, Pallas kernels for 11%

profile of v6, /device:TPU:1, one launch (start us, length us, event | category | flops | bytes accessed | tf_op | source)
XLA Modules:
  0.0 91.1 jit_solution(13596256506716185882)
XLA Ops:
  0.0 0.7 convert_bitcast_fusion
  0.7 1.0 %pad_add_fusion.refs_0_.own = f32[264,256]{1,0:T(8,128)S(1)} fusion(f32[1,2]{1,0:T(1,128)S(1)} %convert_bitcast_fusion, f32[3,256]{1,0:T(4,128)} %param.12, f32[256,256]{1,0:T(8,128)} %param.11), kind=kLoop, calls=%fused_computation | loop fusion | flops 135168 | bytes 535560 | tf_op jit(solution)/shard_map/add | solution.py:258
  1.6 2.1 %collective-permute-start.2 = (f32[264,256]{1,0:T(8,128)S(1)}, f32[264,256]{1,0:T(8,128)S(1)}, u32[]{:S(2)}, u32[]{:S(2)}) collective-permute-start(f32[264,256]{1,0:T(8,128)S(1)} %pad_add_fusion.refs_0_.own), channel_id=1, source_target_pairs={{0,1},{1,2},{2,3},{3,0},{4,5},{5,6},{6,7},{7,4},{8,9},{9,10},{10,1... | collective-permute-start | bytes 811016 | tf_op jit(solution)/shard_map/ppermute | solution.py:261
  3.8 1.3 %collective-permute-start.1 = (f32[264,256]{1,0:T(8,128)S(1)}, f32[264,256]{1,0:T(8,128)S(1)}, u32[]{:S(2)}, u32[]{:S(2)}) collective-permute-start(f32[264,256]{1,0:T(8,128)S(1)} %pad_add_fusion.refs_0_.own), channel_id=1, source_target_pairs={{0,3},{1,0},{2,1},{3,2},{4,7},{5,4},{6,5},{7,6},{8,11},{9,8},{10,9... | collective-permute-start | bytes 811016 | tf_op jit(solution)/shard_map/ppermute | solution.py:260
  5.1 1.6 %collective-permute-start = (f32[264,256]{1,0:T(8,128)S(1)}, f32[264,256]{1,0:T(8,128)S(1)}, u32[]{:S(2)}, u32[]{:S(2)}) collective-permute-start(f32[264,256]{1,0:T(8,128)S(1)} %pad_add_fusion.refs_0_.own), channel_id=1, source_target_pairs={{0,2},{1,3},{2,0},{3,1},{4,6},{5,7},{6,4},{7,5},{8,10},{9,11},{10,... | collective-permute-start | bytes 811016 | tf_op jit(solution)/shard_map/ppermute | solution.py:259
  6.8 0.7 copy-done.5
  7.4 0.7 shard_map.109
  8.1 7.8 %all-to-all-start = ((f32[16,8,128]{2,1,0:T(8,128)}), f32[16,8,128]{2,1,0:T(8,128)S(1)}, u32[]{:S(2)}, u32[]{:S(2)}) async-start(f32[16,8,128]{2,1,0:T(8,128)} %shard_map.109), calls=%async_computation | async-start | bytes 131072 | tf_op jit(solution)/shard_map/all_to_all | solution.py:269
  15.9 9.1 %collective-permute-start.3 = (f32[264,256]{1,0:T(8,128)S(1)}, f32[264,256]{1,0:T(8,128)S(1)}, u32[]{:S(2)}, u32[]{:S(2)}) collective-permute-start(f32[264,256]{1,0:T(8,128)S(1)} %pad_add_fusion.refs_0_.own), channel_id=1, source_target_pairs={{3,4},{7,8},{11,12},{15,16},{19,20},{23,24},{27,28},{31,32},{35,36... | collective-permute-start | bytes 811016 | tf_op jit(solution)/shard_map/ppermute | solution.py:268
  25.1 0.1 collective-permute-start.4
  25.2 0.0 all-to-all-done.kv
  25.2 0.0 copy-start.3
  25.2 0.9 %copy-done.3 = f32[256,256]{1,0:T(8,128)S(1)} copy-done((f32[256,256]{1,0:T(8,128)S(1)}, f32[256,256]{1,0:T(8,128)}, u32[]{:S(2)}) %copy-start.3) | copy-done | bytes 262168
  26.1 0.2 shard_map.110
  26.3 1.0 %shard_map.111 = (f32[768,256]{1,0:T(8,128)S(1)}, bf16[1,768,256]{2,1,0:T(8,128)(2,1)S(1)}, bf16[1,768,256]{2,1,0:T(8,128)(2,1)S(1)}) custom-call(bf16[384,48]{1,0:T(8,128)(2,1)S(1)} %get-tuple-element.41.lhs, bf16[256,256]{1,0:T(8,128)(2,1)S(1)} %get-tuple-element.42.wh, bf16[256,256]{1,0:T(8,128)(2,1)S(1)} %get-tuple-element.43.wl, ...), custom_call_target="tpu_custom_call" | custom-call | flops 301989888 | bytes 65536 | tf_op jit(solution)/shard_map/pallas_call | solution.py:282
  27.4 0.6 collective-permute-start.7
  28.0 0.1 collective-permute-start.6
  28.1 0.4 collective-permute-start.5
  28.5 2.8 %collective-permute-done.3.edge = f32[264,256]{1,0:T(8,128)S(1)} collective-permute-done((f32[264,256]{1,0:T(8,128)S(1)}, f32[264,256]{1,0:T(8,128)S(1)}, u32[]{:S(2)}, u32[]{:S(2)}) %collective-permute-start.3) | collective-permute-done | bytes 270368 | tf_op jit(solution)/shard_map/ppermute | solution.py:268
  31.3 2.5 %shard_map.113 = (f32[768,256]{1,0:T(8,128)S(1)}, bf16[3,768,256]{2,1,0:T(8,128)(2,1)S(1)}, bf16[3,768,256]{2,1,0:T(8,128)(2,1)S(1)}) custom-call(bf16[384,48]{1,0:T(8,128)(2,1)S(1)} %get-tuple-element.41.lhs, bf16[256,256]{1,0:T(8,128)(2,1)S(1)} %get-tuple-element.42.wh, bf16[256,256]{1,0:T(8,128)(2,1)S(1)} %get-tuple-element.43.wl, ...), custom_call_target="tpu_custom_call" | custom-call | flops 905969664 | bytes 65536 | tf_op jit(solution)/shard_map/pallas_call | solution.py:282
  33.9 3.2 %shard_map.114 = (f32[768,256]{1,0:T(8,128)S(1)}, bf16[4,768,256]{2,1,0:T(8,128)(2,1)S(1)}, bf16[4,768,256]{2,1,0:T(8,128)(2,1)S(1)}) custom-call(bf16[384,48]{1,0:T(8,128)(2,1)S(1)} %get-tuple-element.41.lhs, bf16[256,256]{1,0:T(8,128)(2,1)S(1)} %get-tuple-element.42.wh, bf16[256,256]{1,0:T(8,128)(2,1)S(1)} %get-tuple-element.43.wl, ...), custom_call_target="tpu_custom_call" | custom-call | flops 1207959552 | bytes 65536 | tf_op jit(solution)/shard_map/pallas_call | solution.py:282
  37.1 0.0 copy-start.4
  37.1 15.3 %all_to_all.15.parts = f32[16,48,256]{2,1,0:T(8,128)S(1)} all-to-all(f32[16,48,256]{2,1,0:T(8,128)S(1)} %bitcast.8), channel_id=1, replica_groups=mesh['rows'=2,'waves_0'=4,'waves_1'=4,'waves_2'=4] {'waves_0','waves_1'}, dimensions={0} | all-to-all | bytes 1572864 | tf_op jit(solution)/shard_map/all_to_all | solution.py:296
  52.4 0.1 shard_map.115
  52.5 14.4 %all_to_all.16 = f32[16,48,256]{2,1,0:T(8,128)S(1)} all-to-all(f32[16,48,256]{2,1,0:T(8,128)S(1)} %shard_map.115), channel_id=1, replica_groups=mesh['rows'=2,'waves_0'=4,'waves_1'=4,'waves_2'=4] {'waves_0','waves_1'}, dimensions={0} | all-to-all | bytes 1572864 | tf_op jit(solution)/shard_map/all_to_all | solution.py:299
  66.9 0.3 shard_map.116
  67.1 0.5 shard_map.117
  67.6 3.8 %collective-permute-start.8 = (f32[256,256]{1,0:T(8,128)S(1)}, f32[256,256]{1,0:T(8,128)S(1)}, u32[]{:S(2)}, u32[]{:S(2)}) collective-permute-start(f32[256,256]{1,0:T(8,128)S(1)} %shard_map.117), channel_id=1, source_target_pairs={{0,64},{64,0},{1,65},{65,1},{2,66},{66,2},{3,67},{67,3},{4,68},{68... | collective-permute-start | bytes 786440 | tf_op jit(solution)/shard_map/ppermute | solution.py:311
  71.4 1.1 %shard_map.119 = (f32[256,256]{1,0:T(8,128)S(1)}, f32[256,256]{1,0:T(8,128)S(1)}, f32[256,256]{1,0:T(8,128)S(1)}) custom-call(bf16[256,768]{1,0:T(8,128)(2,1)S(1)} %get-tuple-element.66.fh, bf16[256,768]{1,0:T(8,128)(2,1)S(1)} %get-tuple-element.67.fl, bf16[4,768,256]{2,1,0:T(8,128)(2,1)S(1)} %get-tuple-element.58.mh0.mh1, ...), custom_call_target="tpu_custom_call" | custom-call | flops 905969664 | bytes 65536 | tf_op jit(solution)/shard_map/pallas_call | solution.py:306
  72.5 0.1 collective-permute-start.9
  72.6 0.5 collective-permute-start.10
  73.1 0.1 collective-permute-start.11
  73.2 0.5 shard_map.118
  73.7 0.0 copy-start
  73.7 0.0 copy-start.6
  73.7 0.0 copy-start.7
  73.7 0.3 collective-permute-start.12
  74.0 0.1 collective-permute-done.9.refs_0_
  74.1 0.4 collective-permute-done.10.refs_1_
  74.5 0.4 collective-permute-done.11.refs_2_
  74.9 1.8 %shard_map.120 = (f32[256,256]{1,0:T(8,128)S(1)}, f32[256,256]{1,0:T(8,128)}, f32[256,256]{1,0:T(8,128)S(1)}) custom-call(bf16[256,768]{1,0:T(8,128)(2,1)S(1)} %get-tuple-element.66.fh, bf16[256,768]{1,0:T(8,128)(2,1)S(1)} %get-tuple-element.67.fl, bf16[1,768,256]{2,1,0:T(8,128)(2,1)S(1)} %get-tuple-element.62.mh0, ...), custom_call_target="tpu_custom_call" | custom-call | flops 905969664 | bytes 65536 | tf_op jit(solution)/shard_map/pallas_call | solution.py:306
  76.7 3.0 %collective-permute-start.13 = (f32[256,256]{1,0:T(8,128)}, f32[256,256]{1,0:T(8,128)S(1)}, u32[]{:S(2)}, u32[]{:S(2)}) collective-permute-start(f32[256,256]{1,0:T(8,128)} %get-tuple-element.73), channel_id=1, source_target_pairs={{0,1},{1,2},{2,3},{3,0},{4,5},{5,6},{6,7},{7,4},{8,9},{9,10},{10,1... | collective-permute-start | bytes 786440 | tf_op jit(solution)/shard_map/ppermute | solution.py:318
  79.6 0.5 collective-permute-start.14
  80.1 1.9 %shard_map.112 = (f32[256,256]{1,0:T(8,128)S(1)}, f32[256,128]{1,0:T(8,128)S(1)}) custom-call(s32[1]{0:T(128)} %bitcast.at_x, s32[1]{0:T(128)} %bitcast.1.at_cell, s32[2,5]{1,0:T(2,128)S(1)} %copy-done.6, s32[2]{0:T(128)S(1)} %copy-done.7, f32[264,256]{1,0:T(8,128)S(1)} %pad_add_fusion.refs_0_.own, f32[264,256]{1,0:T(8,128)S(1)} %collective-permute-done.2.low.refs_1_, ...), custom_call_target="tpu_custom_call" | custom-call | flops 301989888 | bytes 65536 | tf_op jit(solution)/shard_map/pallas_call | solution.py:321
  82.0 0.8 collective-permute-done.12.refs_1_
  82.8 6.4 %collective-permute-done.13.b = f32[256,256]{1,0:T(8,128)S(1)} collective-permute-done((f32[256,256]{1,0:T(8,128)}, f32[256,256]{1,0:T(8,128)S(1)}, u32[]{:S(2)}, u32[]{:S(2)}) %collective-permute-start.13) | collective-permute-done | bytes 262176 | tf_op jit(solution)/shard_map/ppermute | solution.py:318
  89.2 0.3 collective-permute-done.14.c
  89.5 1.5 %shard_map.122 = f32[256,256]{1,0:T(8,128)} custom-call(f32[256,256]{1,0:T(8,128)S(1)} %get-tuple-element.50.base, f32[256,128]{1,0:T(8,128)S(1)} %get-tuple-element.51.mask, f32[256,256]{1,0:T(8,128)S(1)} %shard_map.121.a, f32[256,256]{1,0:T(8,128)S(1)} %collective-permute-done.13.b, f32[256,256]{1,0:T(8,128)S(1)} %collective-permute-done.14.c, ...), custom_call_target="tpu_custom_call" | custom-call | bytes 65536 | tf_op jit(solution)/shard_map/pallas_call | solution.py:329
  (18 shorter events, 0.1 us)
Async XLA Ops:
  1.6 25.7 %collective-permute-start.2 = (f32[264,256]{1,0:T(8,128)S(1)}, f32[264,256]{1,0:T(8,128)S(1)}, u32[]{:S(2)}, u32[]{:S(2)}) collective-permute-start(f32[264,256]{1,0:T(8,128)S(1)} %pad_add_fusion.refs_0_.own), channel_id=1, source_target_pairs={{0,1},{1,2},{2,3},{3,0},{4,5},{5,6},{6,7},{7,4},{8,9},{9,10},{10,1... | collective-permute-start | bytes 811016 | tf_op jit(solution)/shard_map/ppermute | solution.py:261
  3.8 23.6 %collective-permute-start.1 = (f32[264,256]{1,0:T(8,128)S(1)}, f32[264,256]{1,0:T(8,128)S(1)}, u32[]{:S(2)}, u32[]{:S(2)}) collective-permute-start(f32[264,256]{1,0:T(8,128)S(1)} %pad_add_fusion.refs_0_.own), channel_id=1, source_target_pairs={{0,3},{1,0},{2,1},{3,2},{4,7},{5,4},{6,5},{7,6},{8,11},{9,8},{10,9... | collective-permute-start | bytes 811016 | tf_op jit(solution)/shard_map/ppermute | solution.py:260
  5.1 22.3 %collective-permute-start = (f32[264,256]{1,0:T(8,128)S(1)}, f32[264,256]{1,0:T(8,128)S(1)}, u32[]{:S(2)}, u32[]{:S(2)}) collective-permute-start(f32[264,256]{1,0:T(8,128)S(1)} %pad_add_fusion.refs_0_.own), channel_id=1, source_target_pairs={{0,2},{1,3},{2,0},{3,1},{4,6},{5,7},{6,4},{7,5},{8,10},{9,11},{10,... | collective-permute-start | bytes 811016 | tf_op jit(solution)/shard_map/ppermute | solution.py:259
  6.8 0.7 copy-start.5
  8.1 17.0 %all-to-all-start = ((f32[16,8,128]{2,1,0:T(8,128)}), f32[16,8,128]{2,1,0:T(8,128)S(1)}, u32[]{:S(2)}, u32[]{:S(2)}) async-start(f32[16,8,128]{2,1,0:T(8,128)} %shard_map.109), calls=%async_computation | async-start | bytes 131072 | tf_op jit(solution)/shard_map/all_to_all | solution.py:269
  15.9 15.4 %collective-permute-start.3 = (f32[264,256]{1,0:T(8,128)S(1)}, f32[264,256]{1,0:T(8,128)S(1)}, u32[]{:S(2)}, u32[]{:S(2)}) collective-permute-start(f32[264,256]{1,0:T(8,128)S(1)} %pad_add_fusion.refs_0_.own), channel_id=1, source_target_pairs={{3,4},{7,8},{11,12},{15,16},{19,20},{23,24},{27,28},{31,32},{35,36... | collective-permute-start | bytes 811016 | tf_op jit(solution)/shard_map/ppermute | solution.py:268
  25.1 8.8 %collective-permute-start.4 = (f32[264,256]{1,0:T(8,128)S(1)}, f32[264,256]{1,0:T(8,128)S(1)}, u32[]{:S(2)}, u32[]{:S(2)}) collective-permute-start(f32[264,256]{1,0:T(8,128)S(1)} %pad_add_fusion.refs_0_.own), channel_id=1, source_target_pairs={{0,64},{64,0},{1,65},{65,1},{2,66},{66,2},{3,67},{67,3},{4,68},{68... | collective-permute-start | bytes 811016 | tf_op jit(solution)/shard_map/ppermute | solution.py:292
  25.2 1.0 %copy-start.3 = (f32[256,256]{1,0:T(8,128)S(1)}, f32[256,256]{1,0:T(8,128)}, u32[]{:S(2)}) copy-start(f32[256,256]{1,0:T(8,128)} %w_val.1) | copy-start | bytes 786436
  27.4 6.5 %collective-permute-start.7 = (f32[264,256]{1,0:T(8,128)S(1)}, f32[264,256]{1,0:T(8,128)S(1)}, u32[]{:S(2)}, u32[]{:S(2)}) collective-permute-start(f32[264,256]{1,0:T(8,128)S(1)} %collective-permute-done.refs_2_), channel_id=1, source_target_pairs={{0,64},{64,0},{1,65},{65,1},{2,66},{66,2},{3,67},{67,3},{4,68},{68... | collective-permute-start | bytes 811016 | tf_op jit(solution)/shard_map/ppermute | solution.py:292
  28.0 5.9 %collective-permute-start.6 = (f32[264,256]{1,0:T(8,128)S(1)}, f32[264,256]{1,0:T(8,128)S(1)}, u32[]{:S(2)}, u32[]{:S(2)}) collective-permute-start(f32[264,256]{1,0:T(8,128)S(1)} %collective-permute-done.2.low.refs_1_), channel_id=1, source_target_pairs={{0,64},{64,0},{1,65},{65,1},{2,66},{66,2},{3,67},{67,3},{4,68},{68... | collective-permute-start | bytes 811016 | tf_op jit(solution)/shard_map/ppermute | solution.py:292
  28.1 5.8 %collective-permute-start.5 = (f32[264,256]{1,0:T(8,128)S(1)}, f32[264,256]{1,0:T(8,128)S(1)}, u32[]{:S(2)}, u32[]{:S(2)}) collective-permute-start(f32[264,256]{1,0:T(8,128)S(1)} %collective-permute-done.1.high.refs_0_), channel_id=1, source_target_pairs={{0,64},{64,0},{1,65},{65,1},{2,66},{66,2},{3,67},{67,3},{4,68},{68... | collective-permute-start | bytes 811016 | tf_op jit(solution)/shard_map/ppermute | solution.py:292
  37.1 15.3 %copy-start.4 = (f32[48,256]{1,0:T(8,128)S(1)}, f32[48,256]{1,0:T(8,128)}, u32[]{:S(2)}) copy-start(f32[48,256]{1,0:T(8,128)} %filters.1) | copy-start | bytes 147460
  67.6 5.6 %collective-permute-start.8 = (f32[256,256]{1,0:T(8,128)S(1)}, f32[256,256]{1,0:T(8,128)S(1)}, u32[]{:S(2)}, u32[]{:S(2)}) collective-permute-start(f32[256,256]{1,0:T(8,128)S(1)} %shard_map.117), channel_id=1, source_target_pairs={{0,64},{64,0},{1,65},{65,1},{2,66},{66,2},{3,67},{67,3},{4,68},{68... | collective-permute-start | bytes 786440 | tf_op jit(solution)/shard_map/ppermute | solution.py:311
  72.5 1.6 %collective-permute-start.9 = (f32[256,256]{1,0:T(8,128)S(1)}, f32[256,256]{1,0:T(8,128)S(1)}, u32[]{:S(2)}, u32[]{:S(2)}) collective-permute-start(f32[256,256]{1,0:T(8,128)S(1)} %get-tuple-element.68), channel_id=1, source_target_pairs={{0,64},{64,0},{1,65},{65,1},{2,66},{66,2},{3,67},{67,3},{4,68},{68... | collective-permute-start | bytes 786440 | tf_op jit(solution)/shard_map/ppermute | solution.py:313
  72.6 1.9 %collective-permute-start.10 = (f32[256,256]{1,0:T(8,128)S(1)}, f32[256,256]{1,0:T(8,128)S(1)}, u32[]{:S(2)}, u32[]{:S(2)}) collective-permute-start(f32[256,256]{1,0:T(8,128)S(1)} %get-tuple-element.69), channel_id=1, source_target_pairs={{0,64},{64,0},{1,65},{65,1},{2,66},{66,2},{3,67},{67,3},{4,68},{68... | collective-permute-start | bytes 786440 | tf_op jit(solution)/shard_map/ppermute | solution.py:313
  73.1 1.8 %collective-permute-start.11 = (f32[256,256]{1,0:T(8,128)S(1)}, f32[256,256]{1,0:T(8,128)S(1)}, u32[]{:S(2)}, u32[]{:S(2)}) collective-permute-start(f32[256,256]{1,0:T(8,128)S(1)} %get-tuple-element.70), channel_id=1, source_target_pairs={{0,64},{64,0},{1,65},{65,1},{2,66},{66,2},{3,67},{67,3},{4,68},{68... | collective-permute-start | bytes 786440 | tf_op jit(solution)/shard_map/ppermute | solution.py:313
  73.7 6.4 %copy-start = (f32[256,256]{1,0:T(8,128)S(1)}, f32[256,256]{1,0:T(8,128)}, u32[]{:S(2)}) copy-start(f32[256,256]{1,0:T(8,128)} %w_msg.1) | copy-start | bytes 786436
  73.7 6.4 %copy-start.6 = (s32[2,5]{1,0:T(2,128)S(1)}, s32[2,5]{1,0:T(2,128)}, u32[]{:S(2)}) copy-start(s32[2,5]{1,0:T(2,128)} %neighbours.1) | copy-start | bytes 124
  73.7 6.4 %copy-start.7 = (s32[2]{0:T(128)S(1)}, s32[2]{0:T(128)}, u32[]{:S(2)}) copy-start(s32[2]{0:T(128)} %nbr_count.1) | copy-start | bytes 28
  73.7 9.0 %collective-permute-start.12 = (f32[256,256]{1,0:T(8,128)S(1)}, f32[256,256]{1,0:T(8,128)S(1)}, u32[]{:S(2)}, u32[]{:S(2)}) collective-permute-start(f32[256,256]{1,0:T(8,128)S(1)} %shard_map.118), channel_id=1, source_target_pairs={{0,2},{1,3},{2,0},{3,1},{4,6},{5,7},{6,4},{7,5},{8,10},{9,11},{10,... | collective-permute-start | bytes 786440 | tf_op jit(solution)/shard_map/ppermute | solution.py:316
  76.7 12.8 %copy-start.1 = (f32[256,256]{1,0:T(8,128)S(1)}, f32[256,256]{1,0:T(8,128)}, u32[]{:S(2)}) copy-start(f32[256,256]{1,0:T(8,128)} %w_one.1) | copy-start | bytes 786436
  76.7 12.8 %copy-start.2 = (f32[256,256]{1,0:T(8,128)S(1)}, f32[256,256]{1,0:T(8,128)}, u32[]{:S(2)}) copy-start(f32[256,256]{1,0:T(8,128)} %w_two.1) | copy-start | bytes 786436
  76.7 12.5 %collective-permute-start.13 = (f32[256,256]{1,0:T(8,128)}, f32[256,256]{1,0:T(8,128)S(1)}, u32[]{:S(2)}, u32[]{:S(2)}) collective-permute-start(f32[256,256]{1,0:T(8,128)} %get-tuple-element.73), channel_id=1, source_target_pairs={{0,1},{1,2},{2,3},{3,0},{4,5},{5,6},{6,7},{7,4},{8,9},{9,10},{10,1... | collective-permute-start | bytes 786440 | tf_op jit(solution)/shard_map/ppermute | solution.py:318
  79.6 9.9 %collective-permute-start.14 = (f32[256,256]{1,0:T(8,128)S(1)}, f32[256,256]{1,0:T(8,128)S(1)}, u32[]{:S(2)}, u32[]{:S(2)}) collective-permute-start(f32[256,256]{1,0:T(8,128)S(1)} %get-tuple-element.74), channel_id=1, source_target_pairs={{0,3},{1,0},{2,1},{3,2},{4,7},{5,4},{6,5},{7,6},{8,11},{9,8},{10,9... | collective-permute-start | bytes 786440 | tf_op jit(solution)/shard_map/ppermute | solution.py:319

commit v7 on v6

--- a/solution.py
+++ b/solution.py
@@ -46,7 +46,7 @@
     return dot(a[0], b[0]) + (dot(a[1], b[0]) + dot(a[0], b[1]))
 
 
-def call(kernel, outs, n_in, scratch=(), smem=(), flops=0, limit=16 << 20):
+def call(kernel, outs, n_in, scratch=(), smem=(), flops=0, limit=8 << 20):
     def space(i):
         return pltpu.SMEM if i in smem else pltpu.VMEM
 
@@ -71,8 +71,7 @@
 
 
 def lattice(own, groups):
-    def kernel(kv, w_val, out, wh, wl, flat):
-        wh[...], wl[...] = split(w_val[...])
+    def kernel(kv, out, flat):
         flat[...] = jnp.zeros(flat.shape, F32)
         pad = jnp.zeros((8, flat.shape[1] - 128), F32)
         for g in range(groups):
@@ -83,48 +82,72 @@
     return kernel
 
 
-def pack(own, groups):
-    def kernel(half, kvec, out, wide):
-        wide[...] = jnp.zeros(wide.shape, F32)
-        wide[0:3, 0 : 2 * own] = kvec[...] * (0.5 / math.pi)
-        k = jnp.where(half[0] == 0, wide[...], pltpu.roll(wide[...], 128 - own, 1))
-        k = jnp.where(lax.broadcasted_iota(jnp.int32, k.shape, 1) < own, k, 0.0)
+def pack(slots, own, groups):
+    def kernel(own_block, out):
+        rows = own_block[slots : slots + 8, :128] * (0.5 / math.pi)
+        rows = pltpu.roll(rows, 4, 0)
+        k = jnp.where(lax.axis_index("rows") == 0, rows, pltpu.roll(rows, 128 - own, 1))
+        lane = lax.broadcasted_iota(jnp.int32, k.shape, 1)
+        line = lax.broadcasted_iota(jnp.int32, k.shape, 0)
+        k = jnp.where((lane < own) & (line < 3), k, 0.0)
         for g in range(groups):
             out[g] = k
 
     return kernel
 
 
+def own_trig(slots, own, groups):
+    def kernel(lhs, chunk, mh, ml):
+        turns = dot(lhs[...], spots(chunk, slots))
+        for g in range(groups):
+            rows = slice(2 * own * g, 2 * own * (g + 1))
+            mh[0, rows], ml[0, rows] = split(cos_and_sin(turns[g * own : (g + 1) * own]))
+
+    return kernel
+
+
+def spots(chunk, slots):
+    x, y, z = thirds(jnp.where(lax.broadcasted_iota(jnp.int32, (8, slots), 0) < 3, chunk[slots : slots + 8], 0.0))
+    return jnp.concatenate([x, y, x, z, y, x], axis=0).astype(BF16)
+
+
+def cos_and_sin(t):
+    f = t - ((t + ROUNDER) - ROUNDER)
+    u = f * f
+    s = f * horner(SIN_POLY, u)
+    c = horner(COS_POLY, u)
+    return jnp.concatenate([1.0 - 0.5 * (s * s), s * c], axis=0)
+
+
 def forward(cells, cell, count, own, groups, first):
     slots = cells * cell
 
-    def kernel(lhs, wh, wl, *refs):
+    def kernel(lhs, w_val, *refs):
         chunks, refs = refs[:count], refs[count:]
-        if not first:
+        if first:
+            ready, refs = refs[:2], refs[2:]
+        else:
             before, refs = refs[0], refs[1:]
         out, mh, ml = refs
-        w = wh[...], wl[...]
+        skip = 1 if first else 0
+        w = split(w_val[...])
         turns, right = [], []
-        for chunk in chunks:
+        for j, chunk in enumerate(chunks):
             live = live_rows(chunk, cells, cell)
             vh, vl = split(jnp.where(live, dot3(split(chunk[:slots]), w), 0.0))
             right += [vh, vh, vl]
-            ph, pm, pl_ = thirds(chunk[slots : slots + 8])
-            turns.append(dot(lhs[...], jnp.concatenate([ph, pm, ph, pl_, pm, ph], axis=0).astype(BF16)))
+            turns.append(dot(lhs[...], spots(chunk, slots)) if j >= skip else None)
         right = jnp.concatenate(right, axis=0)
         for part in range(2):
-            for j in range(count):
+            for j in range(skip, count):
                 for g in range(part * groups // 2, (part + 1) * groups // 2):
-                    t = turns[j][g * own : (g + 1) * own]
-                    f = t - ((t + ROUNDER) - ROUNDER)
-                    u = f * f
-                    s = f * horner(SIN_POLY, u)
-                    c = horner(COS_POLY, u)
-                    both = jnp.concatenate([1.0 - 0.5 * (s * s), s * c], axis=0)
                     rows = slice(2 * own * g, 2 * own * (g + 1))
-                    mh[j, rows], ml[j, rows] = split(both)
+                    pieces = split(cos_and_sin(turns[j][g * own : (g + 1) * own]))
+                    mh[j - skip, rows], ml[j - skip, rows] = pieces
             rows = slice(part * own * groups, (part + 1) * own * groups)
-            left = [m[j, rows] for j in range(count) for m in (mh, ml, mh)]
+            pairs_of = [(ready[0][0, rows], ready[1][0, rows])] if first else []
+            pairs_of += [(mh[j, rows], ml[j, rows]) for j in range(count - skip)]
+            left = [m for high, low in pairs_of for m in (high, low, high)]
             total = dot(jnp.concatenate(left, axis=1), right)
             out[rows] = total if first else before[rows] + total
 
@@ -132,10 +155,10 @@
 
 
 def filtered(scale):
-    def kernel(half, parts, filters, out):
+    def kernel(parts, filters, out):
         groups, double, _ = parts.shape
         own = double // 2
-        f = filters[pl.ds(pl.multiple_of(half[0] * own, 8), own), :] * scale
+        f = jnp.where(lax.axis_index("rows") == 0, filters[:own], filters[own:]) * scale
         total = parts[0]
         for g in range(1, groups):
             total = total + parts[g]
@@ -144,6 +167,10 @@
             out[g] = total
 
     return kernel
+
+
+def line_end(below, above, out):
+    out[...] = jnp.where(lax.axis_index(X) == 0, below[...], above[...])
 
 
 def turned(f, high, low):
@@ -170,8 +197,8 @@
 def messages(cells, cell, cells_all, nb, last):
     slots = cells * cell
 
-    def kernel(at_x, at_cell, neighbours, nbr_count, own, low, high, edge, w_msg, out, mask):
-        x, first = at_x[0], at_cell[0]
+    def kernel(neighbours, nbr_count, own, low, high, edge, w_msg, out, mask):
+        x, first = lax.axis_index(X), lax.axis_index(ROWS_WAVES) * cells
         lo = jnp.where(x == 0, edge[...], low[...])
         hi = jnp.where(x == last, edge[...], high[...])
         blocks = (lo, own[...], hi)
@@ -243,9 +270,6 @@
     group = lax.axis_size((Z, Y))
     own_waves = kvec.shape[1] // rows
     waves = own_waves * group
-    half = lax.axis_index("rows").astype(jnp.int32)
-    x = lax.axis_index(X).astype(jnp.int32)
-    first = lax.axis_index(ROWS_WAVES).astype(jnp.int32) * cells
 
     def floats(*dims):
         return jax.ShapeDtypeStruct(dims, F32)
@@ -256,48 +280,43 @@
     counts = cell_counts.astype(F32)[None]
     payload = jnp.pad(feats, ((0, 8), (0, 0))) + jnp.pad(positions, ((slots, 5), (0, 0)))
     payload = payload + jnp.pad(counts, ((slots + 3, 4), (0, width - cells)))
+    payload = payload + jnp.pad(kvec, ((slots + 4, 1), (0, width - kvec.shape[1])))
     near2 = lax.ppermute(payload, X, shift(X, 2))
     above = lax.ppermute(payload, X, shift(X, -1))
     below = lax.ppermute(payload, X, shift(X, 1))
-    kv = call(pack(own_waves, group), floats(group, 8, 128), 2, [pltpu.VMEM((8, 128), F32)], smem=(0,))(
-        half.reshape(1), kvec
-    )
-    kv, again = lax.optimization_barrier((kv, payload))
-    ends = [(d, (d + 1) % devices) for d in range(devices) if d % nx == nx - 1]
-    ends = ends + [(b, a) for a, b in ends]
-    edge = lax.ppermute(again, ROWS_WAVES, ends)
+    kv = call(pack(slots, own_waves, group), floats(group, 8, 128), 1)(payload)
     kv = lax.all_to_all(kv, (Z, Y), 0, 0, tiled=True)
-    lhs, *w = call(
-        lattice(own_waves, group),
-        (halves(waves, 48), halves(width, width), halves(width, width)),
-        2,
-        [pltpu.VMEM((8, waves), F32)],
-    )(kv, w_val)
+    lhs = call(lattice(own_waves, group), halves(waves, 48), 1, [pltpu.VMEM((8, waves), F32)])(kv)
 
     unit = 12 * waves * slots * width
 
-    def sums(chunks, *before):
+    def sums(chunks, first, *more):
         count = len(chunks)
-        m = halves(count, 2 * waves, slots)
+        m = halves(count - 1 if first else count, 2 * waves, slots)
         return call(
-            forward(cells, cell, count, own_waves, group, not before),
+            forward(cells, cell, count, own_waves, group, first),
             (floats(2 * waves, width), m, m),
-            3 + count + len(before),
+            2 + count + len(more),
             flops=count * unit,
-        )(lhs, *w, *chunks, *before)
-
-    part, *m_own = sums((payload,))
-    part, near2, above, below = lax.optimization_barrier((part, near2, above, below))
+        )(lhs, w_val, *chunks, *more)
+
+    m_own = call(own_trig(slots, own_waves, group), (halves(1, 2 * waves, slots),) * 2, 2, flops=unit)(lhs, payload)
+    *m_own, near2, above, below = lax.optimization_barrier((*m_own, near2, above, below))
     swap = shift("rows", 1)
-    other = [lax.ppermute(c, "rows", swap) for c in (again, above, below, near2)]
-    part, edge = lax.optimization_barrier((part, edge))
-    part, *m_line = sums((above, below, near2), part)
-    part, *m_other = sums(other, part)
+    other = [lax.ppermute(c, "rows", swap) for c in (payload, above, below, near2)]
+    part, *m_line = sums((payload, above, below, near2), True, *m_own)
+    part, *m_other = sums(other, False, part)
+    passed = call(line_end, floats(*payload.shape), 2)(below, above)
+    part, passed = lax.optimization_barrier((part, passed))
     parts = lax.all_to_all(part.reshape(group, 2 * own_waves, width), (Z, Y), 0, 0, tiled=True)
     scale = 1.0 / math.sqrt(float(slots * devices) * float(waves * rows * nx))
-    spread = call(filtered(scale), floats(*parts.shape), 3, smem=(0,))(half.reshape(1), parts, filters)
+    spread = call(filtered(scale), floats(*parts.shape), 2)(parts, filters)
     f = lax.all_to_all(spread, (Z, Y), 0, 0, tiled=True).reshape(2 * waves, width)
 
+    ends = [(d, (d + nx) % devices) for d in range(devices) if d % nx == 0]
+    ends += [(d, (d - nx) % devices) for d in range(devices) if d % nx == nx - 1]
+    f, passed = lax.optimization_barrier((f, passed))
+    edge = lax.ppermute(passed, ROWS_WAVES, ends)
     ft = call(turned, (halves(width, 2 * waves),) * 2, 1)(f)
     one = floats(width, slots)
 
@@ -321,10 +340,10 @@
     base, mask = call(
         messages(cells, cell, cells * devices, neighbours.shape[1], nx - 1),
         (floats(slots, width), floats(slots, 128)),
-        9,
-        smem=(0, 1, 2, 3),
+        7,
+        smem=(0, 1),
         flops=unit,
-    )(x.reshape(1), first.reshape(1), neighbours, nbr_count, payload, below, above, edge, w_msg)
+    )(neighbours, nbr_count, payload, below, above, edge, w_msg)
     (e0,) = call(pairs, (one,), 2)(e0, e3)
     return call(finish(), floats(slots, width), 7)(base, mask, e0, e1, e2, w_one, w_two)
 

time: 91.4 us -> 90.9 us (level)
  starting transfers between devices: 31.4 us -> 27.3 us
  blocking collectives: 29.6 us -> 33.1 us
  waiting for transfers between devices: 11.2 us -> 13.6 us
  local copies, waits for them, and re-layouts: 1.66 us -> 0.04 us
    ppermute x1, starting transfers between devices: 9.13 us -> 2.36 us  [shards(): edge = lax.ppermute(passed, ROWS_WAVES, ends)]
    all_to_all x1, waiting for transfers between devices: 0.01 us -> 4.64 us  [shards(): kv = lax.all_to_all(kv, (Z, Y), 0, 0, tiled=True)]
    ppermute x4, starting transfers between devices: 1.16 us -> 5.41 us  [shards(): lax.ppermute(c, 'rows', swap)]
    ppermute x1, waiting for transfers between devices: 6.42 us -> 2.66 us  [shards(): e1 = lax.ppermute(e1, X, shift(X, 1))]
    ppermute x1, waiting for transfers between devices: 2.84 us -> 5.86 us  [shards(): edge = lax.ppermute(passed, ROWS_WAVES, ends)]
    ppermute x1, starting transfers between devices: 1.65 us -> 3.65 us  [shards(): near2 = lax.ppermute(payload, X, shift(X, 2))]
    all_to_all x1, blocking collectives: 15.3 us -> 17.1 us  [shards(): lax.all_to_all(part.reshape(group, 2 * own_waves, width), (Z, Y), 0, 0, t...]
    all_to_all x1, blocking collectives: 14.4 us -> 16.1 us  [shards(): lax.all_to_all(spread, (Z, Y), 0, 0, tiled=True).reshape(2 * waves, width)]
  transfers between devices with their start and end apart: 16 -> 16, of which waited for: 7 -> 4; matrix products, arithmetic and copies ran while one was open for 0% -> 0% of each run, Pallas kernels for 11% -> 10%
where the time goes in v7:
time: 90.9 us; the launch traced here: 90.5 us
  blocking collectives  33.1 us (36%)
  starting transfers between devices  27.3 us (30%)
  Pallas kernels  14.5 us (16%)
  waiting for transfers between devices  13.6 us (15%)
  other arithmetic  1.7 us (2%)
    all_to_all x1, blocking collectives, shards(): lax.all_to_all(part.reshape(group, 2 * own_waves, width), (Z, Y), 0, 0, t...  17.1 us
    all_to_all x1, blocking collectives, shards(): lax.all_to_all(spread, (Z, Y), 0, 0, tiled=True).reshape(2 * waves, width)  16.1 us
    all_to_all x1, starting transfers between devices, shards(): kv = lax.all_to_all(kv, (Z, Y), 0, 0, tiled=True)  7.77 us
    pallas_call x2, Pallas kernels, sums(): call(forward(cells, cell, count, own_waves, group, first), (floats(2 * wa...  6.04 us
    ppermute x1, waiting for transfers between devices, shards(): edge = lax.ppermute(passed, ROWS_WAVES, ends)  5.86 us
    ppermute x4, starting transfers between devices, shards(): lax.ppermute(c, 'rows', swap)  5.41 us
    all_to_all x1, waiting for transfers between devices, shards(): kv = lax.all_to_all(kv, (Z, Y), 0, 0, tiled=True)  4.64 us
    ppermute x1, starting transfers between devices, shards(): e1 = lax.ppermute(e1, X, shift(X, 1))  3.72 us
  transfers between devices with their start and end apart: 16, of which 4 were waited for; matrix products, arithmetic and copies ran while one was open for 0% of the time, Pallas kernels for 10%

profile of v7, /device:TPU:1, one launch (start us, length us, event | category | flops | bytes accessed | tf_op | source)
XLA Modules:
  0.0 90.5 jit_solution(9737719174369043390)
XLA Ops:
  0.0 0.7 convert_bitcast_fusion
  0.7 1.0 %pad_add_fusion.own_block.chunk.refs_0_.own = f32[264,256]{1,0:T(8,128)S(1)} fusion(f32[3,48]{1,0:T(4,128)} %param.16, f32[1,2]{1,0:T(1,128)S(1)} %convert_bitcast_fusion, f32[3,256]{1,0:T(4,128)} %param.12, f32[256,256]{1,0:T(8,128)} %param.11), kind=kLoop, calls=%fused_computation | loop fusion | flops 202752 | bytes 536136 | tf_op jit(solution)/shard_map/add | solution.py:283
  1.7 3.7 %collective-permute-start = (f32[264,256]{1,0:T(8,128)S(1)}, f32[264,256]{1,0:T(8,128)S(1)}, u32[]{:S(2)}, u32[]{:S(2)}) collective-permute-start(f32[264,256]{1,0:T(8,128)S(1)} %pad_add_fusion.own_block.chunk.refs_0_.own), channel_id=1, source_target_pairs={{0,2},{1,3},{2,0},{3,1},{4,6},{5,7},{6,4},{7,5},{8,10},{9,11},{10,... | collective-permute-start | bytes 811016 | tf_op jit(solution)/shard_map/ppermute | solution.py:284
  5.4 0.9 collective-permute-start.1
  6.2 0.6 collective-permute-start.2
  6.8 0.7 shard_map.109
  7.5 7.8 %all-to-all-start = ((f32[16,8,128]{2,1,0:T(8,128)}), f32[16,8,128]{2,1,0:T(8,128)S(1)}, u32[]{:S(2)}, u32[]{:S(2)}) async-start(f32[16,8,128]{2,1,0:T(8,128)} %shard_map.109), calls=%async_computation | async-start | bytes 131072 | tf_op jit(solution)/shard_map/all_to_all | solution.py:288
  15.3 1.9 %collective-permute-start.3 = (f32[264,256]{1,0:T(8,128)S(1)}, f32[264,256]{1,0:T(8,128)S(1)}, u32[]{:S(2)}, u32[]{:S(2)}) collective-permute-start(f32[264,256]{1,0:T(8,128)S(1)} %pad_add_fusion.own_block.chunk.refs_0_.own), channel_id=1, source_target_pairs={{0,64},{64,0},{1,65},{65,1},{2,66},{66,2},{3,67},{67,3},{4,68},{68... | collective-permute-start | bytes 811016 | tf_op jit(solution)/shard_map/ppermute | solution.py:306
  17.2 4.6 %all-to-all-done.kv = f32[16,8,128]{2,1,0:T(8,128)S(1)} async-done(((f32[16,8,128]{2,1,0:T(8,128)}), f32[16,8,128]{2,1,0:T(8,128)S(1)}, u32[]{:S(2)}, u32[]{:S(2)}) %all-to-all-start) | async-done | bytes 65568 | tf_op jit(solution)/shard_map/all_to_all | solution.py:288
  21.8 0.2 shard_map.110.lhs
  22.0 0.5 shard_map.111
  22.6 0.0 collective-permute-done.1.refs_1_.above.high
  22.6 0.0 collective-permute-done.2.refs_2_.below.low
  22.6 3.0 %collective-permute-start.4 = (f32[264,256]{1,0:T(8,128)S(1)}, f32[264,256]{1,0:T(8,128)S(1)}, u32[]{:S(2)}, u32[]{:S(2)}) collective-permute-start(f32[264,256]{1,0:T(8,128)S(1)} %collective-permute-done.1.refs_1_.above.high), channel_id=1, source_target_pairs={{0,64},{64,0},{1,65},{65,1},{2,66},{66,2},{3,67},{67,3},{4,68},{68... | collective-permute-start | bytes 811016 | tf_op jit(solution)/shard_map/ppermute | solution.py:306
  25.6 0.1 collective-permute-start.5
  25.7 0.4 collective-permute-start.6
  26.2 2.8 %shard_map.112 = (f32[768,256]{1,0:T(8,128)S(1)}, bf16[3,768,256]{2,1,0:T(8,128)(2,1)S(1)}, bf16[3,768,256]{2,1,0:T(8,128)(2,1)S(1)}) custom-call(bf16[384,48]{1,0:T(8,128)(2,1)S(1)} %shard_map.110.lhs, f32[256,256]{1,0:T(8,128)S(1)} %copy-done.6, f32[264,256]{1,0:T(8,128)S(1)} %pad_add_fusion.own_block.chunk.refs_0_.own, ...), custom_call_target="tpu_custom_call" | custom-call | flops 1207959552 | bytes 65536 | tf_op jit(solution)/shard_map/pallas_call | solution.py:296
  29.0 0.0 collective-permute-done.3.refs_0_
  29.0 0.0 collective-permute-done.4.refs_1_
  29.0 3.3 %shard_map.113 = (f32[768,256]{1,0:T(8,128)S(1)}, bf16[4,768,256]{2,1,0:T(8,128)(2,1)S(1)}, bf16[4,768,256]{2,1,0:T(8,128)(2,1)S(1)}) custom-call(bf16[384,48]{1,0:T(8,128)(2,1)S(1)} %shard_map.110.lhs, f32[256,256]{1,0:T(8,128)S(1)} %copy-done.6, f32[264,256]{1,0:T(8,128)S(1)} %collective-permute-done.3.refs_0_, ...), custom_call_target="tpu_custom_call" | custom-call | flops 1207959552 | bytes 65536 | tf_op jit(solution)/shard_map/pallas_call | solution.py:296
  32.3 0.0 copy-start.3
  32.3 17.1 %all_to_all.15.parts = f32[16,48,256]{2,1,0:T(8,128)S(1)} all-to-all(f32[16,48,256]{2,1,0:T(8,128)S(1)} %bitcast.5), channel_id=1, replica_groups=mesh['rows'=2,'waves_0'=4,'waves_1'=4,'waves_2'=4] {'waves_0','waves_1'}, dimensions={0} | all-to-all | bytes 1572864 | tf_op jit(solution)/shard_map/all_to_all | solution.py:311
  49.4 0.1 shard_map.115
  49.5 16.1 %all_to_all.16 = f32[16,48,256]{2,1,0:T(8,128)S(1)} all-to-all(f32[16,48,256]{2,1,0:T(8,128)S(1)} %shard_map.115), channel_id=1, replica_groups=mesh['rows'=2,'waves_0'=4,'waves_1'=4,'waves_2'=4] {'waves_0','waves_1'}, dimensions={0} | all-to-all | bytes 1572864 | tf_op jit(solution)/shard_map/all_to_all | solution.py:314
  65.6 0.3 shard_map.117
  65.8 0.5 shard_map.118
  66.3 2.2 %collective-permute-start.8 = (f32[256,256]{1,0:T(8,128)S(1)}, f32[256,256]{1,0:T(8,128)S(1)}, u32[]{:S(2)}, u32[]{:S(2)}) collective-permute-start(f32[256,256]{1,0:T(8,128)S(1)} %shard_map.118), channel_id=1, source_target_pairs={{0,64},{64,0},{1,65},{65,1},{2,66},{66,2},{3,67},{67,3},{4,68},{68... | collective-permute-start | bytes 786440 | tf_op jit(solution)/shard_map/ppermute | solution.py:330
  68.5 1.1 %shard_map.120 = (f32[256,256]{1,0:T(8,128)S(1)}, f32[256,256]{1,0:T(8,128)S(1)}, f32[256,256]{1,0:T(8,128)S(1)}) custom-call(bf16[256,768]{1,0:T(8,128)(2,1)S(1)} %get-tuple-element.60.fh, bf16[256,768]{1,0:T(8,128)(2,1)S(1)} %get-tuple-element.61.fl, bf16[4,768,256]{2,1,0:T(8,128)(2,1)S(1)} %get-tuple-element.54.mh0.mh1, ...), custom_call_target="tpu_custom_call" | custom-call | flops 905969664 | bytes 65536 | tf_op jit(solution)/shard_map/pallas_call | solution.py:325
  69.6 0.1 collective-permute-start.10
  69.7 0.5 collective-permute-start.11
  70.2 0.1 collective-permute-start.9
  70.3 2.4 %collective-permute-start.7 = (f32[264,256]{1,0:T(8,128)S(1)}, f32[264,256]{1,0:T(8,128)S(1)}, u32[]{:S(2)}, u32[]{:S(2)}) collective-permute-start(f32[264,256]{1,0:T(8,128)S(1)} %shard_map.114), channel_id=1, source_target_pairs={{0,4},{4,8},{8,12},{12,16},{16,20},{20,24},{24,28},{28,32},{32,36}... | collective-permute-start | bytes 811016 | tf_op jit(solution)/shard_map/ppermute | solution.py:319
  72.6 0.0 collective-permute-done.8.refs_0_
  72.7 0.5 shard_map.119
  73.1 0.0 copy-start.2
  73.2 0.0 copy-start.4
  73.2 0.0 copy-start.5
  73.2 0.1 collective-permute-start.12
  73.3 0.0 collective-permute-done.11.refs_2_
  73.3 1.1 %shard_map.121 = (f32[256,256]{1,0:T(8,128)S(1)}, f32[256,256]{1,0:T(8,128)S(1)}, f32[256,256]{1,0:T(8,128)S(1)}) custom-call(bf16[256,768]{1,0:T(8,128)(2,1)S(1)} %get-tuple-element.60.fh, bf16[256,768]{1,0:T(8,128)(2,1)S(1)} %get-tuple-element.61.fl, bf16[1,768,256]{2,1,0:T(8,128)(2,1)S(1)} %get-tuple-element.42.refs_4_.mh0, ...), custom_call_target="tpu_custom_call" | custom-call | flops 905969664 | bytes 65536 | tf_op jit(solution)/shard_map/pallas_call | solution.py:325
  74.4 0.0 copy-start
  74.4 0.0 copy-start.1
  74.4 3.7 %collective-permute-start.13 = (f32[256,256]{1,0:T(8,128)S(1)}, f32[256,256]{1,0:T(8,128)S(1)}, u32[]{:S(2)}, u32[]{:S(2)}) collective-permute-start(f32[256,256]{1,0:T(8,128)S(1)} %get-tuple-element.67), channel_id=1, source_target_pairs={{0,1},{1,2},{2,3},{3,0},{4,5},{5,6},{6,7},{7,4},{8,9},{9,10},{10,1... | collective-permute-start | bytes 786440 | tf_op jit(solution)/shard_map/ppermute | solution.py:337
  78.1 5.9 %collective-permute-done.7.edge = f32[264,256]{1,0:T(8,128)S(1)} collective-permute-done((f32[264,256]{1,0:T(8,128)S(1)}, f32[264,256]{1,0:T(8,128)S(1)}, u32[]{:S(2)}, u32[]{:S(2)}) %collective-permute-start.7) | collective-permute-done | bytes 270368 | tf_op jit(solution)/shard_map/ppermute | solution.py:319
  84.0 1.9 %shard_map.116 = (f32[256,256]{1,0:T(8,128)S(1)}, f32[256,128]{1,0:T(8,128)S(1)}) custom-call(s32[2,5]{1,0:T(2,128)S(1)} %copy-done.4, s32[2]{0:T(128)S(1)} %copy-done.5, f32[264,256]{1,0:T(8,128)S(1)} %pad_add_fusion.own_block.chunk.refs_0_.own, f32[264,256]{1,0:T(8,128)S(1)} %collective-permute-done.2.refs_2_.below.low, ...), custom_call_target="tpu_custom_call" | custom-call | flops 301989888 | bytes 65536 | tf_op jit(solution)/shard_map/pallas_call | solution.py:340
  86.0 2.7 %collective-permute-done.13.b = f32[256,256]{1,0:T(8,128)S(1)} collective-permute-done((f32[256,256]{1,0:T(8,128)S(1)}, f32[256,256]{1,0:T(8,128)S(1)}, u32[]{:S(2)}, u32[]{:S(2)}) %collective-permute-start.13) | collective-permute-done | bytes 262176 | tf_op jit(solution)/shard_map/ppermute | solution.py:337
  88.6 0.4 collective-permute-done.14.c
  89.0 1.5 %shard_map.123 = f32[256,256]{1,0:T(8,128)} custom-call(f32[256,256]{1,0:T(8,128)S(1)} %get-tuple-element.49.base, f32[256,128]{1,0:T(8,128)S(1)} %get-tuple-element.50.mask, f32[256,256]{1,0:T(8,128)S(1)} %shard_map.122.a, f32[256,256]{1,0:T(8,128)S(1)} %collective-permute-done.13.b, f32[256,256]{1,0:T(8,128)S(1)} %collective-permute-done.14.c, ...), custom_call_target="tpu_custom_call" | custom-call | bytes 65536 | tf_op jit(solution)/shard_map/pallas_call | solution.py:348
  (17 shorter events, 0.1 us)
Async XLA Ops:
  0.0 26.2 %copy-start.6 = (f32[256,256]{1,0:T(8,128)S(1)}, f32[256,256]{1,0:T(8,128)}, u32[]{:S(2)}) copy-start(f32[256,256]{1,0:T(8,128)} %w_val.3) | copy-start | bytes 786436
  1.7 20.9 %collective-permute-start = (f32[264,256]{1,0:T(8,128)S(1)}, f32[264,256]{1,0:T(8,128)S(1)}, u32[]{:S(2)}, u32[]{:S(2)}) collective-permute-start(f32[264,256]{1,0:T(8,128)S(1)} %pad_add_fusion.own_block.chunk.refs_0_.own), channel_id=1, source_target_pairs={{0,2},{1,3},{2,0},{3,1},{4,6},{5,7},{6,4},{7,5},{8,10},{9,11},{10,... | collective-permute-start | bytes 811016 | tf_op jit(solution)/shard_map/ppermute | solution.py:284
  5.4 17.2 %collective-permute-start.1 = (f32[264,256]{1,0:T(8,128)S(1)}, f32[264,256]{1,0:T(8,128)S(1)}, u32[]{:S(2)}, u32[]{:S(2)}) collective-permute-start(f32[264,256]{1,0:T(8,128)S(1)} %pad_add_fusion.own_block.chunk.refs_0_.own), channel_id=1, source_target_pairs={{0,3},{1,0},{2,1},{3,2},{4,7},{5,4},{6,5},{7,6},{8,11},{9,8},{10,9... | collective-permute-start | bytes 811016 | tf_op jit(solution)/shard_map/ppermute | solution.py:285
  6.2 16.4 %collective-permute-start.2 = (f32[264,256]{1,0:T(8,128)S(1)}, f32[264,256]{1,0:T(8,128)S(1)}, u32[]{:S(2)}, u32[]{:S(2)}) collective-permute-start(f32[264,256]{1,0:T(8,128)S(1)} %pad_add_fusion.own_block.chunk.refs_0_.own), channel_id=1, source_target_pairs={{0,1},{1,2},{2,3},{3,0},{4,5},{5,6},{6,7},{7,4},{8,9},{9,10},{10,1... | collective-permute-start | bytes 811016 | tf_op jit(solution)/shard_map/ppermute | solution.py:286
  7.5 14.3 %all-to-all-start = ((f32[16,8,128]{2,1,0:T(8,128)}), f32[16,8,128]{2,1,0:T(8,128)S(1)}, u32[]{:S(2)}, u32[]{:S(2)}) async-start(f32[16,8,128]{2,1,0:T(8,128)} %shard_map.109), calls=%async_computation | async-start | bytes 131072 | tf_op jit(solution)/shard_map/all_to_all | solution.py:288
  15.3 13.7 %collective-permute-start.3 = (f32[264,256]{1,0:T(8,128)S(1)}, f32[264,256]{1,0:T(8,128)S(1)}, u32[]{:S(2)}, u32[]{:S(2)}) collective-permute-start(f32[264,256]{1,0:T(8,128)S(1)} %pad_add_fusion.own_block.chunk.refs_0_.own), channel_id=1, source_target_pairs={{0,64},{64,0},{1,65},{65,1},{2,66},{66,2},{3,67},{67,3},{4,68},{68... | collective-permute-start | bytes 811016 | tf_op jit(solution)/shard_map/ppermute | solution.py:306
  22.6 6.4 %collective-permute-start.4 = (f32[264,256]{1,0:T(8,128)S(1)}, f32[264,256]{1,0:T(8,128)S(1)}, u32[]{:S(2)}, u32[]{:S(2)}) collective-permute-start(f32[264,256]{1,0:T(8,128)S(1)} %collective-permute-done.1.refs_1_.above.high), channel_id=1, source_target_pairs={{0,64},{64,0},{1,65},{65,1},{2,66},{66,2},{3,67},{67,3},{4,68},{68... | collective-permute-start | bytes 811016 | tf_op jit(solution)/shard_map/ppermute | solution.py:306
  25.6 3.4 %collective-permute-start.5 = (f32[264,256]{1,0:T(8,128)S(1)}, f32[264,256]{1,0:T(8,128)S(1)}, u32[]{:S(2)}, u32[]{:S(2)}) collective-permute-start(f32[264,256]{1,0:T(8,128)S(1)} %collective-permute-done.2.refs_2_.below.low), channel_id=1, source_target_pairs={{0,64},{64,0},{1,65},{65,1},{2,66},{66,2},{3,67},{67,3},{4,68},{68... | collective-permute-start | bytes 811016 | tf_op jit(solution)/shard_map/ppermute | solution.py:306
  25.7 3.3 %collective-permute-start.6 = (f32[264,256]{1,0:T(8,128)S(1)}, f32[264,256]{1,0:T(8,128)S(1)}, u32[]{:S(2)}, u32[]{:S(2)}) collective-permute-start(f32[264,256]{1,0:T(8,128)S(1)} %collective-permute-done.refs_3_), channel_id=1, source_target_pairs={{0,64},{64,0},{1,65},{65,1},{2,66},{66,2},{3,67},{67,3},{4,68},{68... | collective-permute-start | bytes 811016 | tf_op jit(solution)/shard_map/ppermute | solution.py:306
  32.3 17.1 %copy-start.3 = (f32[48,256]{1,0:T(8,128)S(1)}, f32[48,256]{1,0:T(8,128)}, u32[]{:S(2)}) copy-start(f32[48,256]{1,0:T(8,128)} %filters.1) | copy-start | bytes 147460
  66.3 6.3 %collective-permute-start.8 = (f32[256,256]{1,0:T(8,128)S(1)}, f32[256,256]{1,0:T(8,128)S(1)}, u32[]{:S(2)}, u32[]{:S(2)}) collective-permute-start(f32[256,256]{1,0:T(8,128)S(1)} %shard_map.118), channel_id=1, source_target_pairs={{0,64},{64,0},{1,65},{65,1},{2,66},{66,2},{3,67},{67,3},{4,68},{68... | collective-permute-start | bytes 786440 | tf_op jit(solution)/shard_map/ppermute | solution.py:330
  69.6 3.7 %collective-permute-start.10 = (f32[256,256]{1,0:T(8,128)S(1)}, f32[256,256]{1,0:T(8,128)S(1)}, u32[]{:S(2)}, u32[]{:S(2)}) collective-permute-start(f32[256,256]{1,0:T(8,128)S(1)} %get-tuple-element.63), channel_id=1, source_target_pairs={{0,64},{64,0},{1,65},{65,1},{2,66},{66,2},{3,67},{67,3},{4,68},{68... | collective-permute-start | bytes 786440 | tf_op jit(solution)/shard_map/ppermute | solution.py:332
  69.7 3.6 %collective-permute-start.11 = (f32[256,256]{1,0:T(8,128)S(1)}, f32[256,256]{1,0:T(8,128)S(1)}, u32[]{:S(2)}, u32[]{:S(2)}) collective-permute-start(f32[256,256]{1,0:T(8,128)S(1)} %get-tuple-element.64), channel_id=1, source_target_pairs={{0,64},{64,0},{1,65},{65,1},{2,66},{66,2},{3,67},{67,3},{4,68},{68... | collective-permute-start | bytes 786440 | tf_op jit(solution)/shard_map/ppermute | solution.py:332
  70.2 3.1 %collective-permute-start.9 = (f32[256,256]{1,0:T(8,128)S(1)}, f32[256,256]{1,0:T(8,128)S(1)}, u32[]{:S(2)}, u32[]{:S(2)}) collective-permute-start(f32[256,256]{1,0:T(8,128)S(1)} %get-tuple-element.62), channel_id=1, source_target_pairs={{0,64},{64,0},{1,65},{65,1},{2,66},{66,2},{3,67},{67,3},{4,68},{68... | collective-permute-start | bytes 786440 | tf_op jit(solution)/shard_map/ppermute | solution.py:332
  70.3 13.7 %collective-permute-start.7 = (f32[264,256]{1,0:T(8,128)S(1)}, f32[264,256]{1,0:T(8,128)S(1)}, u32[]{:S(2)}, u32[]{:S(2)}) collective-permute-start(f32[264,256]{1,0:T(8,128)S(1)} %shard_map.114), channel_id=1, source_target_pairs={{0,4},{4,8},{8,12},{12,16},{16,20},{20,24},{24,28},{28,32},{32,36}... | collective-permute-start | bytes 811016 | tf_op jit(solution)/shard_map/ppermute | solution.py:319
  73.1 10.9 %copy-start.2 = (f32[256,256]{1,0:T(8,128)S(1)}, f32[256,256]{1,0:T(8,128)}, u32[]{:S(2)}) copy-start(f32[256,256]{1,0:T(8,128)} %w_msg.1) | copy-start | bytes 786436
  73.2 10.9 %copy-start.4 = (s32[2,5]{1,0:T(2,128)S(1)}, s32[2,5]{1,0:T(2,128)}, u32[]{:S(2)}) copy-start(s32[2,5]{1,0:T(2,128)} %neighbours.1) | copy-start | bytes 124
  73.2 10.9 %copy-start.5 = (s32[2]{0:T(128)S(1)}, s32[2]{0:T(128)}, u32[]{:S(2)}) copy-start(s32[2]{0:T(128)} %nbr_count.1) | copy-start | bytes 28
  73.2 12.7 %collective-permute-start.12 = (f32[256,256]{1,0:T(8,128)S(1)}, f32[256,256]{1,0:T(8,128)S(1)}, u32[]{:S(2)}, u32[]{:S(2)}) collective-permute-start(f32[256,256]{1,0:T(8,128)S(1)} %shard_map.119), channel_id=1, source_target_pairs={{0,2},{1,3},{2,0},{3,1},{4,6},{5,7},{6,4},{7,5},{8,10},{9,11},{10,... | collective-permute-start | bytes 786440 | tf_op jit(solution)/shard_map/ppermute | solution.py:335
  74.4 14.6 %copy-start = (f32[256,256]{1,0:T(8,128)S(1)}, f32[256,256]{1,0:T(8,128)}, u32[]{:S(2)}) copy-start(f32[256,256]{1,0:T(8,128)} %w_one.1) | copy-start | bytes 786436
  74.4 14.6 %copy-start.1 = (f32[256,256]{1,0:T(8,128)S(1)}, f32[256,256]{1,0:T(8,128)}, u32[]{:S(2)}) copy-start(f32[256,256]{1,0:T(8,128)} %w_two.1) | copy-start | bytes 786436
  74.4 14.2 %collective-permute-start.13 = (f32[256,256]{1,0:T(8,128)S(1)}, f32[256,256]{1,0:T(8,128)S(1)}, u32[]{:S(2)}, u32[]{:S(2)}) collective-permute-start(f32[256,256]{1,0:T(8,128)S(1)} %get-tuple-element.67), channel_id=1, source_target_pairs={{0,1},{1,2},{2,3},{3,0},{4,5},{5,6},{6,7},{7,4},{8,9},{9,10},{10,1... | collective-permute-start | bytes 786440 | tf_op jit(solution)/shard_map/ppermute | solution.py:337
  78.1 10.8 %collective-permute-start.14 = (f32[256,256]{1,0:T(8,128)S(1)}, f32[256,256]{1,0:T(8,128)S(1)}, u32[]{:S(2)}, u32[]{:S(2)}) collective-permute-start(f32[256,256]{1,0:T(8,128)S(1)} %get-tuple-element.68), channel_id=1, source_target_pairs={{0,3},{1,0},{2,1},{3,2},{4,7},{5,4},{6,5},{7,6},{8,11},{9,8},{10,9... | collective-permute-start | bytes 786440 | tf_op jit(solution)/shard_map/ppermute | solution.py:338

commit v8 on v7

--- a/solution.py
+++ b/solution.py
@@ -46,7 +46,7 @@
     return dot(a[0], b[0]) + (dot(a[1], b[0]) + dot(a[0], b[1]))
 
 
-def call(kernel, outs, n_in, scratch=(), smem=(), flops=0, limit=8 << 20):
+def call(kernel, outs, n_in, scratch=(), smem=(), flops=0, alias={}, limit=8 << 20):
     def space(i):
         return pltpu.SMEM if i in smem else pltpu.VMEM
 
@@ -56,6 +56,7 @@
         in_specs=[pl.BlockSpec(memory_space=space(i)) for i in range(n_in)],
         out_specs=jax.tree.map(lambda _: pl.BlockSpec(memory_space=pltpu.VMEM), outs),
         scratch_shapes=scratch,
+        input_output_aliases=alias,
         cost_estimate=pl.CostEstimate(flops=flops, bytes_accessed=1 << 16, transcendentals=0),
         compiler_params=pltpu.CompilerParams(vmem_limit_bytes=limit),
     )
@@ -68,6 +69,13 @@
     for c in range(1, cells):
         limit = jnp.where(row < c * cell, limit, c * cell + block[slots + 3 : slots + 4, c : c + 1])
     return row < limit
+
+
+def stamp(slots, cells):
+    def kernel(counts, _, out):
+        out[slots + 3 : slots + 4, 0:cells] = counts[...].astype(F32).reshape(1, cells)
+
+    return kernel
 
 
 def lattice(own, groups):
@@ -173,8 +181,13 @@
     out[...] = jnp.where(lax.axis_index(X) == 0, below[...], above[...])
 
 
-def turned(f, high, low):
-    high[...], low[...] = split(f[...].T)
+def backward_first(at):
+    def kernel(f, mh, ml, out, high, low):
+        ft = split(f[...].T)
+        high[...], low[...] = ft
+        out[...] = dot3(ft, (mh[at], ml[at]))
+
+    return kernel
 
 
 def backward(chunks):
@@ -277,14 +290,16 @@
     def halves(*dims):
         return jax.ShapeDtypeStruct(dims, BF16)
 
-    counts = cell_counts.astype(F32)[None]
     payload = jnp.pad(feats, ((0, 8), (0, 0))) + jnp.pad(positions, ((slots, 5), (0, 0)))
-    payload = payload + jnp.pad(counts, ((slots + 3, 4), (0, width - cells)))
     payload = payload + jnp.pad(kvec, ((slots + 4, 1), (0, width - kvec.shape[1])))
+    payload = call(stamp(slots, cells), floats(*payload.shape), 2, alias={1: 0})(cell_counts, payload)
     near2 = lax.ppermute(payload, X, shift(X, 2))
     above = lax.ppermute(payload, X, shift(X, -1))
     below = lax.ppermute(payload, X, shift(X, 1))
     kv = call(pack(slots, own_waves, group), floats(group, 8, 128), 1)(payload)
+    kv, again = lax.optimization_barrier((kv, payload))
+    swap = shift("rows", 1)
+    beside = lax.ppermute(again, "rows", swap)
     kv = lax.all_to_all(kv, (Z, Y), 0, 0, tiled=True)
     lhs = call(lattice(own_waves, group), halves(waves, 48), 1, [pltpu.VMEM((8, waves), F32)])(kv)
 
@@ -301,10 +316,11 @@
         )(lhs, w_val, *chunks, *more)
 
     m_own = call(own_trig(slots, own_waves, group), (halves(1, 2 * waves, slots),) * 2, 2, flops=unit)(lhs, payload)
-    *m_own, near2, above, below = lax.optimization_barrier((*m_own, near2, above, below))
-    swap = shift("rows", 1)
-    other = [lax.ppermute(c, "rows", swap) for c in (payload, above, below, near2)]
-    part, *m_line = sums((payload, above, below, near2), True, *m_own)
+    part, *m_beside = sums((payload, beside), True, *m_own)
+    part, near2, above, below = lax.optimization_barrier((part, near2, above, below))
+    line = (above, below, near2)
+    other = [lax.ppermute(c, "rows", swap) for c in line]
+    part, *m_line = sums(line, False, part)
     part, *m_other = sums(other, False, part)
     passed = call(line_end, floats(*payload.shape), 2)(below, above)
     part, passed = lax.optimization_barrier((part, passed))
@@ -313,26 +329,24 @@
     spread = call(filtered(scale), floats(*parts.shape), 2)(parts, filters)
     f = lax.all_to_all(spread, (Z, Y), 0, 0, tiled=True).reshape(2 * waves, width)
 
-    ends = [(d, (d + nx) % devices) for d in range(devices) if d % nx == 0]
-    ends += [(d, (d - nx) % devices) for d in range(devices) if d % nx == nx - 1]
-    f, passed = lax.optimization_barrier((f, passed))
-    edge = lax.ppermute(passed, ROWS_WAVES, ends)
-    ft = call(turned, (halves(width, 2 * waves),) * 2, 1)(f)
     one = floats(width, slots)
 
     def back(chunks, ft, m, *added):
         outs = (one,) * len(chunks)
         return call(backward(chunks), outs, 6 + len(added), flops=len(chunks) * unit)(*ft, *m, *added)
 
-    theirs = *m_other, *m_other
+    theirs = *m_beside, *m_other
     mine = *m_own, *m_line
-    (far,) = back(((0, 3),), ft, theirs)
+    far, *ft = call(backward_first(2), (one, *(halves(width, 2 * waves),) * 2), 3, flops=unit)(f, *m_other)
     there = lax.ppermute(far, "rows", swap)
     ft = lax.optimization_barrier((*ft, far))[:2]
-    rest = [lax.ppermute(r, "rows", swap) for r in back(((0, 0), (0, 1), (0, 2)), ft, theirs)]
+    rest = [lax.ppermute(r, "rows", swap) for r in back(((0, 0), (1, 0), (1, 1)), ft, theirs)]
     (e3,) = back(((1, 2),), ft, mine, there)
-    e3, *ft = lax.optimization_barrier((e3, *ft))
+    e3, passed, *ft = lax.optimization_barrier((e3, passed, *ft))
     e3 = lax.ppermute(e3, X, shift(X, 2))
+    ends = [(d, (d + nx) % devices) for d in range(devices) if d % nx == 0]
+    ends += [(d, (d - nx) % devices) for d in range(devices) if d % nx == nx - 1]
+    edge = lax.ppermute(passed, ROWS_WAVES, ends)
     e0, e1, e2 = back(((0, 0), (1, 0), (1, 1)), ft, mine, *rest)
     e1 = lax.ppermute(e1, X, shift(X, 1))
     e2 = lax.ppermute(e2, X, shift(X, -1))

time: 90.9 us -> 89 us (0.979)
  blocking collectives: 33.1 us -> 47.3 us
  starting transfers between devices: 27.3 us -> 17.9 us
  waiting for transfers between devices: 13.6 us -> 7.48 us
    all_to_all x0 -> x1, blocking collectives: none -> 14.1 us  [shards(): kv = lax.all_to_all(kv, (Z, Y), 0, 0, tiled=True)]
    all_to_all x1 -> x0, starting transfers between devices: 7.77 us -> none  [shards(): kv = lax.all_to_all(kv, (Z, Y), 0, 0, tiled=True)]
    all_to_all x1 -> x0, waiting for transfers between devices: 4.64 us -> none  [shards(): kv = lax.all_to_all(kv, (Z, Y), 0, 0, tiled=True)]
    ppermute x1, starting transfers between devices: 3.72 us -> 0.46 us  [shards(): e1 = lax.ppermute(e1, X, shift(X, 1))]
    ppermute x1, starting transfers between devices: 0.01 us -> 2.95 us  [shards(): e2 = lax.ppermute(e2, X, shift(X, -1))]
    ppermute x1, waiting for transfers between devices: 2.66 us -> 0.01 us  [shards(): e1 = lax.ppermute(e1, X, shift(X, 1))]
    ppermute x1, waiting for transfers between devices: 0.01 us -> 1.47 us  [shards(): e3 = lax.ppermute(e3, X, shift(X, 2))]
    ppermute x4, starting transfers between devices: 5.41 us -> 4.34 us  [the longest x3 2.9 us: shards(): other = [lax.ppermute(c, 'rows', swap) for c in line]]
  transfers between devices with their start and end apart: 16 -> 15, of which waited for: 4 -> 2; matrix products, arithmetic and copies ran while one was open for 0% -> 0% of each run, Pallas kernels for 10% -> 10%
where the time goes in v8:
time: 89 us; the launch traced here: 88.7 us
  blocking collectives  47.3 us (53%)
  starting transfers between devices  17.9 us (20%)
  Pallas kernels  14.1 us (16%)
  waiting for transfers between devices  7.48 us (8%)
  other arithmetic  1 us (1%)
    all_to_all x1, blocking collectives, shards(): lax.all_to_all(part.reshape(group, 2 * own_waves, width), (Z, Y), 0, 0, t...  17.1 us
    all_to_all x1, blocking collectives, shards(): lax.all_to_all(spread, (Z, Y), 0, 0, tiled=True).reshape(2 * waves, width)  16.1 us
    all_to_all x1, blocking collectives, shards(): kv = lax.all_to_all(kv, (Z, Y), 0, 0, tiled=True)  14.1 us
    pallas_call x3, Pallas kernels, sums(): call(forward(cells, cell, count, own_waves, group, first), (floats(2 * wa...  6.36 us
    ppermute x1, waiting for transfers between devices, shards(): edge = lax.ppermute(passed, ROWS_WAVES, ends)  5.98 us
    ppermute x1, starting transfers between devices, shards(): e2 = lax.ppermute(e2, X, shift(X, -1))  2.95 us
    ppermute x3, starting transfers between devices, shards(): other = [lax.ppermute(c, 'rows', swap) for c in line]  2.9 us
    ppermute x1, starting transfers between devices, shards(): near2 = lax.ppermute(payload, X, shift(X, 2))  2.84 us
  transfers between devices with their start and end apart: 15, of which 2 were waited for; matrix products, arithmetic and copies ran while one was open for 0% of the time, Pallas kernels for 10%

profile of v8, /device:TPU:1, one launch (start us, length us, event | category | flops | bytes accessed | tf_op | source)
XLA Modules:
  0.0 88.7 jit_solution(7371900640237853264)
XLA Ops:
  0.0 1.0 %pad_add_fusion._ = f32[264,256]{1,0:T(8,128)S(1)} fusion(f32[3,48]{1,0:T(4,128)} %param.16, f32[3,256]{1,0:T(4,128)} %param.12, f32[256,256]{1,0:T(8,128)} %param.11), kind=kLoop, calls=%fused_computation | loop fusion | flops 135168 | bytes 536128 | tf_op jit(solution)/shard_map/add | solution.py:294
  1.0 0.0 copy-start.5
  1.0 0.6 copy-done.5
  1.7 0.1 shard_map.110
  1.7 1.4 %collective-permute-start = (f32[264,256]{1,0:T(8,128)S(1)}, f32[264,256]{1,0:T(8,128)S(1)}, u32[]{:S(2)}, u32[]{:S(2)}) collective-permute-start(f32[264,256]{1,0:T(8,128)S(1)} %shard_map.109.own_block.chunk.refs_0_.own), channel_id=1, source_target_pairs={{0,64},{64,0},{1,65},{65,1},{2,66},{66,2},{3,67},{67,3},{4,68},{68... | collective-permute-start | bytes 811016 | tf_op jit(solution)/shard_map/ppermute | solution.py:302
  3.2 2.8 %collective-permute-start.1 = (f32[264,256]{1,0:T(8,128)S(1)}, f32[264,256]{1,0:T(8,128)S(1)}, u32[]{:S(2)}, u32[]{:S(2)}) collective-permute-start(f32[264,256]{1,0:T(8,128)S(1)} %shard_map.109.own_block.chunk.refs_0_.own), channel_id=1, source_target_pairs={{0,2},{1,3},{2,0},{3,1},{4,6},{5,7},{6,4},{7,5},{8,10},{9,11},{10,... | collective-permute-start | bytes 811016 | tf_op jit(solution)/shard_map/ppermute | solution.py:296
  6.0 0.9 collective-permute-start.2
  6.9 0.6 collective-permute-start.3
  7.5 14.1 %all_to_all.15.kv = f32[16,8,128]{2,1,0:T(8,128)S(1)} all-to-all(f32[16,8,128]{2,1,0:T(8,128)S(1)} %shard_map.110), channel_id=1, replica_groups=mesh['rows'=2,'waves_0'=4,'waves_1'=4,'waves_2'=4] {'waves_0','waves_1'}, dimensions={0} | all-to-all | bytes 131072 | tf_op jit(solution)/shard_map/all_to_all | solution.py:303
  21.6 0.2 shard_map.111.lhs
  21.8 0.5 shard_map.112
  22.4 0.0 collective-permute-done.refs_1_
  22.4 1.4 %shard_map.113 = (f32[768,256]{1,0:T(8,128)S(1)}, bf16[1,768,256]{2,1,0:T(8,128)(2,1)S(1)}, bf16[1,768,256]{2,1,0:T(8,128)(2,1)S(1)}) custom-call(bf16[384,48]{1,0:T(8,128)(2,1)S(1)} %shard_map.111.lhs, f32[256,256]{1,0:T(8,128)S(1)} %copy-done.7, f32[264,256]{1,0:T(8,128)S(1)} %shard_map.109.own_block.chunk.refs_0_.own, ...), custom_call_target="tpu_custom_call" | custom-call | flops 603979776 | bytes 65536 | tf_op jit(solution)/shard_map/pallas_call | solution.py:311
  23.8 0.0 collective-permute-done.1.refs_2_
  23.8 0.0 collective-permute-done.3.refs_1_.below.low
  23.8 2.4 %collective-permute-start.4 = (f32[264,256]{1,0:T(8,128)S(1)}, f32[264,256]{1,0:T(8,128)S(1)}, u32[]{:S(2)}, u32[]{:S(2)}) collective-permute-start(f32[264,256]{1,0:T(8,128)S(1)} %collective-permute-done.2.refs_0_.above.high), channel_id=1, source_target_pairs={{0,64},{64,0},{1,65},{65,1},{2,66},{66,2},{3,67},{67,3},{4,68},{68... | collective-permute-start | bytes 811016 | tf_op jit(solution)/shard_map/ppermute | solution.py:322
  26.2 0.1 collective-permute-start.5
  26.3 0.4 collective-permute-start.6
  26.7 2.5 %shard_map.114 = (f32[768,256]{1,0:T(8,128)S(1)}, bf16[3,768,256]{2,1,0:T(8,128)(2,1)S(1)}, bf16[3,768,256]{2,1,0:T(8,128)(2,1)S(1)}) custom-call(bf16[384,48]{1,0:T(8,128)(2,1)S(1)} %shard_map.111.lhs, f32[256,256]{1,0:T(8,128)S(1)} %copy-done.7, f32[264,256]{1,0:T(8,128)S(1)} %collective-permute-done.2.refs_0_.above.high, ...), custom_call_target="tpu_custom_call" | custom-call | flops 905969664 | bytes 65536 | tf_op jit(solution)/shard_map/pallas_call | solution.py:311
  29.3 0.0 collective-permute-done.5.refs_1_
  29.3 0.0 collective-permute-done.6.refs_2_
  29.3 2.5 %shard_map.115 = (f32[768,256]{1,0:T(8,128)S(1)}, bf16[3,768,256]{2,1,0:T(8,128)(2,1)S(1)}, bf16[3,768,256]{2,1,0:T(8,128)(2,1)S(1)}) custom-call(bf16[384,48]{1,0:T(8,128)(2,1)S(1)} %shard_map.111.lhs, f32[256,256]{1,0:T(8,128)S(1)} %copy-done.7, f32[264,256]{1,0:T(8,128)S(1)} %collective-permute-done.4.refs_0_, ...), custom_call_target="tpu_custom_call" | custom-call | flops 905969664 | bytes 65536 | tf_op jit(solution)/shard_map/pallas_call | solution.py:311
  31.8 0.0 copy-start.3
  31.8 17.1 %all_to_all.16.parts = f32[16,48,256]{2,1,0:T(8,128)S(1)} all-to-all(f32[16,48,256]{2,1,0:T(8,128)S(1)} %bitcast.3), channel_id=1, replica_groups=mesh['rows'=2,'waves_0'=4,'waves_1'=4,'waves_2'=4] {'waves_0','waves_1'}, dimensions={0} | all-to-all | bytes 1572864 | tf_op jit(solution)/shard_map/all_to_all | solution.py:327
  48.9 0.1 shard_map.117
  49.0 16.1 %all_to_all.17 = f32[16,48,256]{2,1,0:T(8,128)S(1)} all-to-all(f32[16,48,256]{2,1,0:T(8,128)S(1)} %shard_map.117), channel_id=1, replica_groups=mesh['rows'=2,'waves_0'=4,'waves_1'=4,'waves_2'=4] {'waves_0','waves_1'}, dimensions={0} | all-to-all | bytes 1572864 | tf_op jit(solution)/shard_map/all_to_all | solution.py:330
  65.0 0.6 shard_map.118
  65.6 2.2 %collective-permute-start.7 = (f32[256,256]{1,0:T(8,128)S(1)}, f32[256,256]{1,0:T(8,128)S(1)}, u32[]{:S(2)}, u32[]{:S(2)}) collective-permute-start(f32[256,256]{1,0:T(8,128)S(1)} %get-tuple-element.57), channel_id=1, source_target_pairs={{0,64},{64,0},{1,65},{65,1},{2,66},{66,2},{3,67},{67,3},{4,68},{68... | collective-permute-start | bytes 786440 | tf_op jit(solution)/shard_map/ppermute | solution.py:341
  67.8 1.1 %shard_map.121 = (f32[256,256]{1,0:T(8,128)S(1)}, f32[256,256]{1,0:T(8,128)S(1)}, f32[256,256]{1,0:T(8,128)S(1)}) custom-call(bf16[256,768]{1,0:T(8,128)(2,1)S(1)} %get-tuple-element.66.fh, bf16[256,768]{1,0:T(8,128)(2,1)S(1)} %get-tuple-element.67.fl, bf16[1,768,256]{2,1,0:T(8,128)(2,1)S(1)} %get-tuple-element.68.mh0, ...), custom_call_target="tpu_custom_call" | custom-call | flops 905969664 | bytes 65536 | tf_op jit(solution)/shard_map/pallas_call | solution.py:336
  68.9 0.1 collective-permute-start.10
  69.0 0.5 collective-permute-start.11
  69.5 0.1 collective-permute-start.9
  69.6 0.0 collective-permute-done.7.refs_0_
  69.6 0.5 shard_map.119
  70.1 0.0 copy-start.2
  70.1 0.0 copy-start.4
  70.1 0.0 copy-start.6
  70.1 0.8 collective-permute-start.12
  70.9 2.2 %collective-permute-start.8 = (f32[264,256]{1,0:T(8,128)S(1)}, f32[264,256]{1,0:T(8,128)S(1)}, u32[]{:S(2)}, u32[]{:S(2)}) collective-permute-start(f32[264,256]{1,0:T(8,128)S(1)} %shard_map.116), channel_id=1, source_target_pairs={{0,4},{4,8},{8,12},{12,16},{16,20},{20,24},{24,28},{28,32},{32,36}... | collective-permute-start | bytes 811016 | tf_op jit(solution)/shard_map/ppermute | solution.py:349
  73.2 1.1 %shard_map.122 = (f32[256,256]{1,0:T(8,128)S(1)}, f32[256,256]{1,0:T(8,128)S(1)}, f32[256,256]{1,0:T(8,128)S(1)}) custom-call(bf16[256,768]{1,0:T(8,128)(2,1)S(1)} %get-tuple-element.66.fh, bf16[256,768]{1,0:T(8,128)(2,1)S(1)} %get-tuple-element.67.fl, bf16[1,768,256]{2,1,0:T(8,128)(2,1)S(1)} %get-tuple-element.43.refs_2_.mh0, ...), custom_call_target="tpu_custom_call" | custom-call | flops 905969664 | bytes 65536 | tf_op jit(solution)/shard_map/pallas_call | solution.py:336
  74.3 0.0 copy-start
  74.3 0.0 copy-start.1
  74.3 0.5 collective-permute-start.13
  74.8 3.0 %collective-permute-start.14 = (f32[256,256]{1,0:T(8,128)S(1)}, f32[256,256]{1,0:T(8,128)S(1)}, u32[]{:S(2)}, u32[]{:S(2)}) collective-permute-start(f32[256,256]{1,0:T(8,128)S(1)} %get-tuple-element.76), channel_id=1, source_target_pairs={{0,3},{1,0},{2,1},{3,2},{4,7},{5,4},{6,5},{7,6},{8,11},{9,8},{10,9... | collective-permute-start | bytes 786440 | tf_op jit(solution)/shard_map/ppermute | solution.py:352
  77.7 1.5 %collective-permute-done.12.refs_1_ = f32[256,256]{1,0:T(8,128)S(1)} collective-permute-done((f32[256,256]{1,0:T(8,128)S(1)}, f32[256,256]{1,0:T(8,128)S(1)}, u32[]{:S(2)}, u32[]{:S(2)}) %collective-permute-start.12) | collective-permute-done | bytes 262176 | tf_op jit(solution)/shard_map/ppermute | solution.py:346
  79.2 6.0 %collective-permute-done.8.edge = f32[264,256]{1,0:T(8,128)S(1)} collective-permute-done((f32[264,256]{1,0:T(8,128)S(1)}, f32[264,256]{1,0:T(8,128)S(1)}, u32[]{:S(2)}, u32[]{:S(2)}) %collective-permute-start.8) | collective-permute-done | bytes 270368 | tf_op jit(solution)/shard_map/ppermute | solution.py:349
  85.2 1.9 %shard_map.120 = (f32[256,256]{1,0:T(8,128)S(1)}, f32[256,128]{1,0:T(8,128)S(1)}) custom-call(s32[2,5]{1,0:T(2,128)S(1)} %copy-done.4, s32[2]{0:T(128)S(1)} %copy-done.6, f32[264,256]{1,0:T(8,128)S(1)} %shard_map.109.own_block.chunk.refs_0_.own, f32[264,256]{1,0:T(8,128)S(1)} %collective-permute-done.3.refs_1_.below.low, ...), custom_call_target="tpu_custom_call" | custom-call | flops 301989888 | bytes 65536 | tf_op jit(solution)/shard_map/pallas_call | solution.py:354
  87.2 1.6 %shard_map.124 = f32[256,256]{1,0:T(8,128)} custom-call(f32[256,256]{1,0:T(8,128)S(1)} %get-tuple-element.64.base, f32[256,128]{1,0:T(8,128)S(1)} %get-tuple-element.65.mask, f32[256,256]{1,0:T(8,128)S(1)} %shard_map.123.a, f32[256,256]{1,0:T(8,128)S(1)} %collective-permute-done.13.b, f32[256,256]{1,0:T(8,128)S(1)} %collective-permute-done.14.c, ...), custom_call_target="tpu_custom_call" | custom-call | bytes 65536 | tf_op jit(solution)/shard_map/pallas_call | solution.py:362
  (18 shorter events, 0.1 us)
Async XLA Ops:
  1.0 0.7 copy-start.5
  1.7 20.7 %copy-start.7 = (f32[256,256]{1,0:T(8,128)S(1)}, f32[256,256]{1,0:T(8,128)}, u32[]{:S(2)}) copy-start(f32[256,256]{1,0:T(8,128)} %w_val.5) | copy-start | bytes 786436
  1.7 20.6 %collective-permute-start = (f32[264,256]{1,0:T(8,128)S(1)}, f32[264,256]{1,0:T(8,128)S(1)}, u32[]{:S(2)}, u32[]{:S(2)}) collective-permute-start(f32[264,256]{1,0:T(8,128)S(1)} %shard_map.109.own_block.chunk.refs_0_.own), channel_id=1, source_target_pairs={{0,64},{64,0},{1,65},{65,1},{2,66},{66,2},{3,67},{67,3},{4,68},{68... | collective-permute-start | bytes 811016 | tf_op jit(solution)/shard_map/ppermute | solution.py:302
  3.2 20.6 %collective-permute-start.1 = (f32[264,256]{1,0:T(8,128)S(1)}, f32[264,256]{1,0:T(8,128)S(1)}, u32[]{:S(2)}, u32[]{:S(2)}) collective-permute-start(f32[264,256]{1,0:T(8,128)S(1)} %shard_map.109.own_block.chunk.refs_0_.own), channel_id=1, source_target_pairs={{0,2},{1,3},{2,0},{3,1},{4,6},{5,7},{6,4},{7,5},{8,10},{9,11},{10,... | collective-permute-start | bytes 811016 | tf_op jit(solution)/shard_map/ppermute | solution.py:296
  6.0 17.8 %collective-permute-start.2 = (f32[264,256]{1,0:T(8,128)S(1)}, f32[264,256]{1,0:T(8,128)S(1)}, u32[]{:S(2)}, u32[]{:S(2)}) collective-permute-start(f32[264,256]{1,0:T(8,128)S(1)} %shard_map.109.own_block.chunk.refs_0_.own), channel_id=1, source_target_pairs={{0,3},{1,0},{2,1},{3,2},{4,7},{5,4},{6,5},{7,6},{8,11},{9,8},{10,9... | collective-permute-start | bytes 811016 | tf_op jit(solution)/shard_map/ppermute | solution.py:297
  6.9 16.9 %collective-permute-start.3 = (f32[264,256]{1,0:T(8,128)S(1)}, f32[264,256]{1,0:T(8,128)S(1)}, u32[]{:S(2)}, u32[]{:S(2)}) collective-permute-start(f32[264,256]{1,0:T(8,128)S(1)} %shard_map.109.own_block.chunk.refs_0_.own), channel_id=1, source_target_pairs={{0,1},{1,2},{2,3},{3,0},{4,5},{5,6},{6,7},{7,4},{8,9},{9,10},{10,1... | collective-permute-start | bytes 811016 | tf_op jit(solution)/shard_map/ppermute | solution.py:298
  23.8 5.4 %collective-permute-start.4 = (f32[264,256]{1,0:T(8,128)S(1)}, f32[264,256]{1,0:T(8,128)S(1)}, u32[]{:S(2)}, u32[]{:S(2)}) collective-permute-start(f32[264,256]{1,0:T(8,128)S(1)} %collective-permute-done.2.refs_0_.above.high), channel_id=1, source_target_pairs={{0,64},{64,0},{1,65},{65,1},{2,66},{66,2},{3,67},{67,3},{4,68},{68... | collective-permute-start | bytes 811016 | tf_op jit(solution)/shard_map/ppermute | solution.py:322
  26.2 3.1 %collective-permute-start.5 = (f32[264,256]{1,0:T(8,128)S(1)}, f32[264,256]{1,0:T(8,128)S(1)}, u32[]{:S(2)}, u32[]{:S(2)}) collective-permute-start(f32[264,256]{1,0:T(8,128)S(1)} %collective-permute-done.3.refs_1_.below.low), channel_id=1, source_target_pairs={{0,64},{64,0},{1,65},{65,1},{2,66},{66,2},{3,67},{67,3},{4,68},{68... | collective-permute-start | bytes 811016 | tf_op jit(solution)/shard_map/ppermute | solution.py:322
  26.3 3.0 %collective-permute-start.6 = (f32[264,256]{1,0:T(8,128)S(1)}, f32[264,256]{1,0:T(8,128)S(1)}, u32[]{:S(2)}, u32[]{:S(2)}) collective-permute-start(f32[264,256]{1,0:T(8,128)S(1)} %collective-permute-done.1.refs_2_), channel_id=1, source_target_pairs={{0,64},{64,0},{1,65},{65,1},{2,66},{66,2},{3,67},{67,3},{4,68},{68... | collective-permute-start | bytes 811016 | tf_op jit(solution)/shard_map/ppermute | solution.py:322
  31.8 17.1 %copy-start.3 = (f32[48,256]{1,0:T(8,128)S(1)}, f32[48,256]{1,0:T(8,128)}, u32[]{:S(2)}) copy-start(f32[48,256]{1,0:T(8,128)} %filters.1) | copy-start | bytes 147460
  65.6 4.0 %collective-permute-start.7 = (f32[256,256]{1,0:T(8,128)S(1)}, f32[256,256]{1,0:T(8,128)S(1)}, u32[]{:S(2)}, u32[]{:S(2)}) collective-permute-start(f32[256,256]{1,0:T(8,128)S(1)} %get-tuple-element.57), channel_id=1, source_target_pairs={{0,64},{64,0},{1,65},{65,1},{2,66},{66,2},{3,67},{67,3},{4,68},{68... | collective-permute-start | bytes 786440 | tf_op jit(solution)/shard_map/ppermute | solution.py:341
  68.9 4.2 %collective-permute-start.10 = (f32[256,256]{1,0:T(8,128)S(1)}, f32[256,256]{1,0:T(8,128)S(1)}, u32[]{:S(2)}, u32[]{:S(2)}) collective-permute-start(f32[256,256]{1,0:T(8,128)S(1)} %get-tuple-element.71), channel_id=1, source_target_pairs={{0,64},{64,0},{1,65},{65,1},{2,66},{66,2},{3,67},{67,3},{4,68},{68... | collective-permute-start | bytes 786440 | tf_op jit(solution)/shard_map/ppermute | solution.py:343
  69.0 4.1 %collective-permute-start.11 = (f32[256,256]{1,0:T(8,128)S(1)}, f32[256,256]{1,0:T(8,128)S(1)}, u32[]{:S(2)}, u32[]{:S(2)}) collective-permute-start(f32[256,256]{1,0:T(8,128)S(1)} %get-tuple-element.72), channel_id=1, source_target_pairs={{0,64},{64,0},{1,65},{65,1},{2,66},{66,2},{3,67},{67,3},{4,68},{68... | collective-permute-start | bytes 786440 | tf_op jit(solution)/shard_map/ppermute | solution.py:343
  69.5 3.6 %collective-permute-start.9 = (f32[256,256]{1,0:T(8,128)S(1)}, f32[256,256]{1,0:T(8,128)S(1)}, u32[]{:S(2)}, u32[]{:S(2)}) collective-permute-start(f32[256,256]{1,0:T(8,128)S(1)} %get-tuple-element.70), channel_id=1, source_target_pairs={{0,64},{64,0},{1,65},{65,1},{2,66},{66,2},{3,67},{67,3},{4,68},{68... | collective-permute-start | bytes 786440 | tf_op jit(solution)/shard_map/ppermute | solution.py:343
  70.1 15.1 %copy-start.2 = (f32[256,256]{1,0:T(8,128)S(1)}, f32[256,256]{1,0:T(8,128)}, u32[]{:S(2)}) copy-start(f32[256,256]{1,0:T(8,128)} %w_msg.1) | copy-start | bytes 786436
  70.1 15.1 %copy-start.4 = (s32[2,5]{1,0:T(2,128)S(1)}, s32[2,5]{1,0:T(2,128)}, u32[]{:S(2)}) copy-start(s32[2,5]{1,0:T(2,128)} %neighbours.1) | copy-start | bytes 124
  70.1 15.1 %copy-start.6 = (s32[2]{0:T(128)S(1)}, s32[2]{0:T(128)}, u32[]{:S(2)}) copy-start(s32[2]{0:T(128)} %nbr_count.1) | copy-start | bytes 28
  70.1 9.1 %collective-permute-start.12 = (f32[256,256]{1,0:T(8,128)S(1)}, f32[256,256]{1,0:T(8,128)S(1)}, u32[]{:S(2)}, u32[]{:S(2)}) collective-permute-start(f32[256,256]{1,0:T(8,128)S(1)} %shard_map.119), channel_id=1, source_target_pairs={{0,2},{1,3},{2,0},{3,1},{4,6},{5,7},{6,4},{7,5},{8,10},{9,11},{10,... | collective-permute-start | bytes 786440 | tf_op jit(solution)/shard_map/ppermute | solution.py:346
  70.9 14.3 %collective-permute-start.8 = (f32[264,256]{1,0:T(8,128)S(1)}, f32[264,256]{1,0:T(8,128)S(1)}, u32[]{:S(2)}, u32[]{:S(2)}) collective-permute-start(f32[264,256]{1,0:T(8,128)S(1)} %shard_map.116), channel_id=1, source_target_pairs={{0,4},{4,8},{8,12},{12,16},{16,20},{20,24},{24,28},{28,32},{32,36}... | collective-permute-start | bytes 811016 | tf_op jit(solution)/shard_map/ppermute | solution.py:349
  74.3 12.9 %copy-start = (f32[256,256]{1,0:T(8,128)S(1)}, f32[256,256]{1,0:T(8,128)}, u32[]{:S(2)}) copy-start(f32[256,256]{1,0:T(8,128)} %w_one.1) | copy-start | bytes 786436
  74.3 12.9 %copy-start.1 = (f32[256,256]{1,0:T(8,128)S(1)}, f32[256,256]{1,0:T(8,128)}, u32[]{:S(2)}) copy-start(f32[256,256]{1,0:T(8,128)} %w_two.1) | copy-start | bytes 786436
  74.3 12.8 %collective-permute-start.13 = (f32[256,256]{1,0:T(8,128)S(1)}, f32[256,256]{1,0:T(8,128)S(1)}, u32[]{:S(2)}, u32[]{:S(2)}) collective-permute-start(f32[256,256]{1,0:T(8,128)S(1)} %get-tuple-element.75), channel_id=1, source_target_pairs={{0,1},{1,2},{2,3},{3,0},{4,5},{5,6},{6,7},{7,4},{8,9},{9,10},{10,1... | collective-permute-start | bytes 786440 | tf_op jit(solution)/shard_map/ppermute | solution.py:351
  74.8 12.4 %collective-permute-start.14 = (f32[256,256]{1,0:T(8,128)S(1)}, f32[256,256]{1,0:T(8,128)S(1)}, u32[]{:S(2)}, u32[]{:S(2)}) collective-permute-start(f32[256,256]{1,0:T(8,128)S(1)} %get-tuple-element.76), channel_id=1, source_target_pairs={{0,3},{1,0},{2,1},{3,2},{4,7},{5,4},{6,5},{7,6},{8,11},{9,8},{10,9... | collective-permute-start | bytes 786440 | tf_op jit(solution)/shard_map/ppermute | solution.py:352

commit v9 on v8

--- a/solution.py
+++ b/solution.py
@@ -185,18 +185,21 @@
     def kernel(f, mh, ml, out, high, low):
         ft = split(f[...].T)
         high[...], low[...] = ft
-        out[...] = dot3(ft, (mh[at], ml[at]))
-
-    return kernel
-
-
-def backward(chunks):
+        out[0] = dot3(ft, (mh[at], ml[at]))
+
+    return kernel
+
+
+def backward(chunks, stacked, adds):
     def kernel(fh, fl, mh0, ml0, mh1, ml1, *refs):
-        count = len(chunks)
-        outs, added = refs[-count:], refs[:-count]
+        added, outs = refs[0] if adds else None, refs[1:] if adds else refs
         for j, (rest, at) in enumerate(chunks):
             part = dot3((fh[...], fl[...]), (mh1[at], ml1[at]) if rest else (mh0[at], ml0[at]))
-            outs[j][...] = part + added[j][...] if added else part
+            part = part + added[j] if adds else part
+            if stacked:
+                outs[0][j] = part
+            else:
+                outs[j][...] = part
 
     return kernel
 
@@ -331,23 +334,27 @@
 
     one = floats(width, slots)
 
-    def back(chunks, ft, m, *added):
-        outs = (one,) * len(chunks)
-        return call(backward(chunks), outs, 6 + len(added), flops=len(chunks) * unit)(*ft, *m, *added)
+    def back(chunks, ft, m, *added, stacked=False):
+        count = len(chunks)
+        outs = floats(count, width, slots) if stacked else (one,) * count
+        kernel = backward(chunks, stacked, bool(added))
+        return call(kernel, outs, 6 + len(added), flops=count * unit)(*ft, *m, *added)
 
     theirs = *m_beside, *m_other
     mine = *m_own, *m_line
-    far, *ft = call(backward_first(2), (one, *(halves(width, 2 * waves),) * 2), 3, flops=unit)(f, *m_other)
+    outs = floats(1, width, slots), *(halves(width, 2 * waves),) * 2
+    far, *ft = call(backward_first(2), outs, 3, flops=unit)(f, *m_other)
     there = lax.ppermute(far, "rows", swap)
     ft = lax.optimization_barrier((*ft, far))[:2]
-    rest = [lax.ppermute(r, "rows", swap) for r in back(((0, 0), (1, 0), (1, 1)), ft, theirs)]
+    rest = back(((0, 0), (1, 0), (1, 1)), ft, theirs, stacked=True)
     (e3,) = back(((1, 2),), ft, mine, there)
-    e3, passed, *ft = lax.optimization_barrier((e3, passed, *ft))
+    e3, passed, rest, *ft = lax.optimization_barrier((e3, passed, rest, *ft))
+    rest = lax.ppermute(rest, "rows", swap)
     e3 = lax.ppermute(e3, X, shift(X, 2))
     ends = [(d, (d + nx) % devices) for d in range(devices) if d % nx == 0]
     ends += [(d, (d - nx) % devices) for d in range(devices) if d % nx == nx - 1]
     edge = lax.ppermute(passed, ROWS_WAVES, ends)
-    e0, e1, e2 = back(((0, 0), (1, 0), (1, 1)), ft, mine, *rest)
+    e0, e1, e2 = back(((0, 0), (1, 0), (1, 1)), ft, mine, rest)
     e1 = lax.ppermute(e1, X, shift(X, 1))
     e2 = lax.ppermute(e2, X, shift(X, -1))
 

time: 89 us -> 88.6 us (level)
    ppermute x1, waiting for transfers between devices: 1.47 us -> 0.01 us  [shards(): e3 = lax.ppermute(e3, X, shift(X, 2))]
    ppermute x1, waiting for transfers between devices: 5.98 us -> 7.4 us  [shards(): edge = lax.ppermute(passed, ROWS_WAVES, ends)]
  transfers between devices with their start and end apart: 15 -> 13, of which waited for: 2 -> 2; matrix products, arithmetic and copies ran while one was open for 0% -> 0% of each run, Pallas kernels for 10% -> 10%
where the time goes in v9:
time: 88.6 us; the launch traced here: 88.3 us
  blocking collectives  47.3 us (53%)
  starting transfers between devices  17.5 us (20%)
  Pallas kernels  14.1 us (16%)
  waiting for transfers between devices  7.5 us (8%)
  other arithmetic  1 us (1%)
    all_to_all x1, blocking collectives, shards(): lax.all_to_all(part.reshape(group, 2 * own_waves, width), (Z, Y), 0, 0, t...  17.1 us
    all_to_all x1, blocking collectives, shards(): lax.all_to_all(spread, (Z, Y), 0, 0, tiled=True).reshape(2 * waves, width)  16.1 us
    all_to_all x1, blocking collectives, shards(): kv = lax.all_to_all(kv, (Z, Y), 0, 0, tiled=True)  14.1 us
    ppermute x1, waiting for transfers between devices, shards(): edge = lax.ppermute(passed, ROWS_WAVES, ends)  7.4 us
    pallas_call x3, Pallas kernels, sums(): call(forward(cells, cell, count, own_waves, group, first), (floats(2 * wa...  6.37 us
    ppermute x3, starting transfers between devices, shards(): other = [lax.ppermute(c, 'rows', swap) for c in line]  2.9 us
    ppermute x1, starting transfers between devices, shards(): near2 = lax.ppermute(payload, X, shift(X, 2))  2.84 us
    ppermute x1, starting transfers between devices, shards(): e2 = lax.ppermute(e2, X, shift(X, -1))  2.81 us
  transfers between devices with their start and end apart: 13, of which 2 were waited for; matrix products, arithmetic and copies ran while one was open for 0% of the time, Pallas kernels for 10%

profile of v9, /device:TPU:1, one launch (start us, length us, event | category | flops | bytes accessed | tf_op | source)
XLA Modules:
  0.0 88.3 jit_solution(13914434299154175814)
XLA Ops:
  0.0 1.0 %pad_add_fusion._ = f32[264,256]{1,0:T(8,128)S(1)} fusion(f32[3,48]{1,0:T(4,128)} %param.16, f32[3,256]{1,0:T(4,128)} %param.12, f32[256,256]{1,0:T(8,128)} %param.11), kind=kLoop, calls=%fused_computation | loop fusion | flops 135168 | bytes 536128 | tf_op jit(solution)/shard_map/add | solution.py:297
  1.0 0.0 copy-start.5
  1.0 0.6 copy-done.5
  1.7 0.1 shard_map.110
  1.7 1.4 %collective-permute-start = (f32[264,256]{1,0:T(8,128)S(1)}, f32[264,256]{1,0:T(8,128)S(1)}, u32[]{:S(2)}, u32[]{:S(2)}) collective-permute-start(f32[264,256]{1,0:T(8,128)S(1)} %shard_map.109.own_block.chunk.refs_0_.own), channel_id=1, source_target_pairs={{0,64},{64,0},{1,65},{65,1},{2,66},{66,2},{3,67},{67,3},{4,68},{68... | collective-permute-start | bytes 811016 | tf_op jit(solution)/shard_map/ppermute | solution.py:305
  3.2 2.8 %collective-permute-start.1 = (f32[264,256]{1,0:T(8,128)S(1)}, f32[264,256]{1,0:T(8,128)S(1)}, u32[]{:S(2)}, u32[]{:S(2)}) collective-permute-start(f32[264,256]{1,0:T(8,128)S(1)} %shard_map.109.own_block.chunk.refs_0_.own), channel_id=1, source_target_pairs={{0,2},{1,3},{2,0},{3,1},{4,6},{5,7},{6,4},{7,5},{8,10},{9,11},{10,... | collective-permute-start | bytes 811016 | tf_op jit(solution)/shard_map/ppermute | solution.py:299
  6.0 0.9 collective-permute-start.2
  6.9 0.6 collective-permute-start.3
  7.5 14.1 %all_to_all.15.kv = f32[16,8,128]{2,1,0:T(8,128)S(1)} all-to-all(f32[16,8,128]{2,1,0:T(8,128)S(1)} %shard_map.110), channel_id=1, replica_groups=mesh['rows'=2,'waves_0'=4,'waves_1'=4,'waves_2'=4] {'waves_0','waves_1'}, dimensions={0} | all-to-all | bytes 131072 | tf_op jit(solution)/shard_map/all_to_all | solution.py:306
  21.6 0.2 shard_map.111.lhs
  21.8 0.5 shard_map.112
  22.4 0.0 collective-permute-done.refs_1_
  22.4 1.4 %shard_map.113 = (f32[768,256]{1,0:T(8,128)S(1)}, bf16[1,768,256]{2,1,0:T(8,128)(2,1)S(1)}, bf16[1,768,256]{2,1,0:T(8,128)(2,1)S(1)}) custom-call(bf16[384,48]{1,0:T(8,128)(2,1)S(1)} %shard_map.111.lhs, f32[256,256]{1,0:T(8,128)S(1)} %copy-done.7, f32[264,256]{1,0:T(8,128)S(1)} %shard_map.109.own_block.chunk.refs_0_.own, ...), custom_call_target="tpu_custom_call" | custom-call | flops 603979776 | bytes 65536 | tf_op jit(solution)/shard_map/pallas_call | solution.py:314
  23.8 0.0 collective-permute-done.1.refs_2_
  23.8 0.0 collective-permute-done.2.refs_0_.above.high
  23.8 0.0 collective-permute-done.3.refs_1_.below.low
  23.8 2.4 %collective-permute-start.4 = (f32[264,256]{1,0:T(8,128)S(1)}, f32[264,256]{1,0:T(8,128)S(1)}, u32[]{:S(2)}, u32[]{:S(2)}) collective-permute-start(f32[264,256]{1,0:T(8,128)S(1)} %collective-permute-done.2.refs_0_.above.high), channel_id=1, source_target_pairs={{0,64},{64,0},{1,65},{65,1},{2,66},{66,2},{3,67},{67,3},{4,68},{68... | collective-permute-start | bytes 811016 | tf_op jit(solution)/shard_map/ppermute | solution.py:325
  26.2 0.1 collective-permute-start.5
  26.3 0.4 collective-permute-start.6
  26.7 2.5 %shard_map.114 = (f32[768,256]{1,0:T(8,128)S(1)}, bf16[3,768,256]{2,1,0:T(8,128)(2,1)S(1)}, bf16[3,768,256]{2,1,0:T(8,128)(2,1)S(1)}) custom-call(bf16[384,48]{1,0:T(8,128)(2,1)S(1)} %shard_map.111.lhs, f32[256,256]{1,0:T(8,128)S(1)} %copy-done.7, f32[264,256]{1,0:T(8,128)S(1)} %collective-permute-done.2.refs_0_.above.high, ...), custom_call_target="tpu_custom_call" | custom-call | flops 905969664 | bytes 65536 | tf_op jit(solution)/shard_map/pallas_call | solution.py:314
  29.3 0.0 collective-permute-done.5.refs_1_
  29.3 0.0 collective-permute-done.6.refs_2_
  29.3 2.5 %shard_map.115 = (f32[768,256]{1,0:T(8,128)S(1)}, bf16[3,768,256]{2,1,0:T(8,128)(2,1)S(1)}, bf16[3,768,256]{2,1,0:T(8,128)(2,1)S(1)}) custom-call(bf16[384,48]{1,0:T(8,128)(2,1)S(1)} %shard_map.111.lhs, f32[256,256]{1,0:T(8,128)S(1)} %copy-done.7, f32[264,256]{1,0:T(8,128)S(1)} %collective-permute-done.4.refs_0_, ...), custom_call_target="tpu_custom_call" | custom-call | flops 905969664 | bytes 65536 | tf_op jit(solution)/shard_map/pallas_call | solution.py:314
  31.8 0.0 copy-start.3
  31.8 17.1 %all_to_all.16.parts = f32[16,48,256]{2,1,0:T(8,128)S(1)} all-to-all(f32[16,48,256]{2,1,0:T(8,128)S(1)} %bitcast.3), channel_id=1, replica_groups=mesh['rows'=2,'waves_0'=4,'waves_1'=4,'waves_2'=4] {'waves_0','waves_1'}, dimensions={0} | all-to-all | bytes 1572864 | tf_op jit(solution)/shard_map/all_to_all | solution.py:330
  48.9 0.1 shard_map.117
  49.0 16.1 %all_to_all.17 = f32[16,48,256]{2,1,0:T(8,128)S(1)} all-to-all(f32[16,48,256]{2,1,0:T(8,128)S(1)} %shard_map.117), channel_id=1, replica_groups=mesh['rows'=2,'waves_0'=4,'waves_1'=4,'waves_2'=4] {'waves_0','waves_1'}, dimensions={0} | all-to-all | bytes 1572864 | tf_op jit(solution)/shard_map/all_to_all | solution.py:333
  65.1 0.6 shard_map.118
  65.6 2.2 %collective-permute-start.7 = (f32[1,256,256]{2,1,0:T(8,128)S(1)}, f32[1,256,256]{2,1,0:T(8,128)S(1)}, u32[]{:S(2)}, u32[]{:S(2)}) collective-permute-start(f32[1,256,256]{2,1,0:T(8,128)S(1)} %get-tuple-element.55), channel_id=1, source_target_pairs={{0,64},{64,0},{1,65},{65,1},{2,66},{66,2},{3,67},{67,3},{4,68},{68... | collective-permute-start | bytes 786440 | tf_op jit(solution)/shard_map/ppermute | solution.py:347
  67.8 1.1 %shard_map.120 = f32[3,256,256]{2,1,0:T(8,128)S(1)} custom-call(bf16[256,768]{1,0:T(8,128)(2,1)S(1)} %get-tuple-element.66.fh, bf16[256,768]{1,0:T(8,128)(2,1)S(1)} %get-tuple-element.67.fl, bf16[1,768,256]{2,1,0:T(8,128)(2,1)S(1)} %get-tuple-element.61.mh0, bf16[1,768,256]{2,1,0:T(8,128)(2,1)S(1)} %get-tuple-element.62.ml0, ...), custom_call_target="tpu_custom_call" | custom-call | flops 905969664 | bytes 65536 | tf_op jit(solution)/shard_map/pallas_call | solution.py:341
  68.9 0.1 collective-permute-done.7.refs_0_
  69.0 0.5 shard_map.119
  69.5 0.0 copy-start.2
  69.5 0.0 copy-start.4
  69.5 0.0 copy-start.6
  69.5 0.5 collective-permute-start.9
  70.0 0.7 collective-permute-start.10
  70.7 2.2 %collective-permute-start.8 = (f32[264,256]{1,0:T(8,128)S(1)}, f32[264,256]{1,0:T(8,128)S(1)}, u32[]{:S(2)}, u32[]{:S(2)}) collective-permute-start(f32[264,256]{1,0:T(8,128)S(1)} %shard_map.116), channel_id=1, source_target_pairs={{0,4},{4,8},{8,12},{12,16},{16,20},{20,24},{24,28},{28,32},{32,36}... | collective-permute-start | bytes 811016 | tf_op jit(solution)/shard_map/ppermute | solution.py:356
  72.9 0.0 collective-permute-done.9.refs_0_
  72.9 1.1 %shard_map.122 = (f32[256,256]{1,0:T(8,128)S(1)}, f32[256,256]{1,0:T(8,128)S(1)}, f32[256,256]{1,0:T(8,128)S(1)}) custom-call(bf16[256,768]{1,0:T(8,128)(2,1)S(1)} %get-tuple-element.66.fh, bf16[256,768]{1,0:T(8,128)(2,1)S(1)} %get-tuple-element.67.fl, bf16[1,768,256]{2,1,0:T(8,128)(2,1)S(1)} %get-tuple-element.41.refs_2_.mh0, ...), custom_call_target="tpu_custom_call" | custom-call | flops 905969664 | bytes 65536 | tf_op jit(solution)/shard_map/pallas_call | solution.py:341
  74.0 0.0 copy-start
  74.0 0.0 copy-start.1
  74.0 0.5 collective-permute-start.11
  74.5 2.8 %collective-permute-start.12 = (f32[256,256]{1,0:T(8,128)S(1)}, f32[256,256]{1,0:T(8,128)S(1)}, u32[]{:S(2)}, u32[]{:S(2)}) collective-permute-start(f32[256,256]{1,0:T(8,128)S(1)} %get-tuple-element.72), channel_id=1, source_target_pairs={{0,3},{1,0},{2,1},{3,2},{4,7},{5,4},{6,5},{7,6},{8,11},{9,8},{10,9... | collective-permute-start | bytes 786440 | tf_op jit(solution)/shard_map/ppermute | solution.py:359
  77.3 7.4 %collective-permute-done.8.edge = f32[264,256]{1,0:T(8,128)S(1)} collective-permute-done((f32[264,256]{1,0:T(8,128)S(1)}, f32[264,256]{1,0:T(8,128)S(1)}, u32[]{:S(2)}, u32[]{:S(2)}) %collective-permute-start.8) | collective-permute-done | bytes 270368 | tf_op jit(solution)/shard_map/ppermute | solution.py:356
  84.7 1.9 %shard_map.121 = (f32[256,256]{1,0:T(8,128)S(1)}, f32[256,128]{1,0:T(8,128)S(1)}) custom-call(s32[2,5]{1,0:T(2,128)S(1)} %copy-done.4, s32[2]{0:T(128)S(1)} %copy-done.6, f32[264,256]{1,0:T(8,128)S(1)} %shard_map.109.own_block.chunk.refs_0_.own, f32[264,256]{1,0:T(8,128)S(1)} %collective-permute-done.3.refs_1_.below.low, ...), custom_call_target="tpu_custom_call" | custom-call | flops 301989888 | bytes 65536 | tf_op jit(solution)/shard_map/pallas_call | solution.py:361
  86.7 0.0 collective-permute-done.12.c
  86.7 1.5 %shard_map.124 = f32[256,256]{1,0:T(8,128)} custom-call(f32[256,256]{1,0:T(8,128)S(1)} %get-tuple-element.64.base, f32[256,128]{1,0:T(8,128)S(1)} %get-tuple-element.65.mask, f32[256,256]{1,0:T(8,128)S(1)} %shard_map.123.a, f32[256,256]{1,0:T(8,128)S(1)} %collective-permute-done.11.b, f32[256,256]{1,0:T(8,128)S(1)} %collective-permute-done.12.c, ...), custom_call_target="tpu_custom_call" | custom-call | bytes 65536 | tf_op jit(solution)/shard_map/pallas_call | solution.py:369
  (14 shorter events, 0.1 us)
Async XLA Ops:
  1.0 0.7 copy-start.5
  1.7 20.7 %copy-start.7 = (f32[256,256]{1,0:T(8,128)S(1)}, f32[256,256]{1,0:T(8,128)}, u32[]{:S(2)}) copy-start(f32[256,256]{1,0:T(8,128)} %w_val.5) | copy-start | bytes 786436
  1.7 20.6 %collective-permute-start = (f32[264,256]{1,0:T(8,128)S(1)}, f32[264,256]{1,0:T(8,128)S(1)}, u32[]{:S(2)}, u32[]{:S(2)}) collective-permute-start(f32[264,256]{1,0:T(8,128)S(1)} %shard_map.109.own_block.chunk.refs_0_.own), channel_id=1, source_target_pairs={{0,64},{64,0},{1,65},{65,1},{2,66},{66,2},{3,67},{67,3},{4,68},{68... | collective-permute-start | bytes 811016 | tf_op jit(solution)/shard_map/ppermute | solution.py:305
  3.2 20.6 %collective-permute-start.1 = (f32[264,256]{1,0:T(8,128)S(1)}, f32[264,256]{1,0:T(8,128)S(1)}, u32[]{:S(2)}, u32[]{:S(2)}) collective-permute-start(f32[264,256]{1,0:T(8,128)S(1)} %shard_map.109.own_block.chunk.refs_0_.own), channel_id=1, source_target_pairs={{0,2},{1,3},{2,0},{3,1},{4,6},{5,7},{6,4},{7,5},{8,10},{9,11},{10,... | collective-permute-start | bytes 811016 | tf_op jit(solution)/shard_map/ppermute | solution.py:299
  6.0 17.8 %collective-permute-start.2 = (f32[264,256]{1,0:T(8,128)S(1)}, f32[264,256]{1,0:T(8,128)S(1)}, u32[]{:S(2)}, u32[]{:S(2)}) collective-permute-start(f32[264,256]{1,0:T(8,128)S(1)} %shard_map.109.own_block.chunk.refs_0_.own), channel_id=1, source_target_pairs={{0,3},{1,0},{2,1},{3,2},{4,7},{5,4},{6,5},{7,6},{8,11},{9,8},{10,9... | collective-permute-start | bytes 811016 | tf_op jit(solution)/shard_map/ppermute | solution.py:300
  6.9 16.9 %collective-permute-start.3 = (f32[264,256]{1,0:T(8,128)S(1)}, f32[264,256]{1,0:T(8,128)S(1)}, u32[]{:S(2)}, u32[]{:S(2)}) collective-permute-start(f32[264,256]{1,0:T(8,128)S(1)} %shard_map.109.own_block.chunk.refs_0_.own), channel_id=1, source_target_pairs={{0,1},{1,2},{2,3},{3,0},{4,5},{5,6},{6,7},{7,4},{8,9},{9,10},{10,1... | collective-permute-start | bytes 811016 | tf_op jit(solution)/shard_map/ppermute | solution.py:301
  23.8 5.4 %collective-permute-start.4 = (f32[264,256]{1,0:T(8,128)S(1)}, f32[264,256]{1,0:T(8,128)S(1)}, u32[]{:S(2)}, u32[]{:S(2)}) collective-permute-start(f32[264,256]{1,0:T(8,128)S(1)} %collective-permute-done.2.refs_0_.above.high), channel_id=1, source_target_pairs={{0,64},{64,0},{1,65},{65,1},{2,66},{66,2},{3,67},{67,3},{4,68},{68... | collective-permute-start | bytes 811016 | tf_op jit(solution)/shard_map/ppermute | solution.py:325
  26.2 3.1 %collective-permute-start.5 = (f32[264,256]{1,0:T(8,128)S(1)}, f32[264,256]{1,0:T(8,128)S(1)}, u32[]{:S(2)}, u32[]{:S(2)}) collective-permute-start(f32[264,256]{1,0:T(8,128)S(1)} %collective-permute-done.3.refs_1_.below.low), channel_id=1, source_target_pairs={{0,64},{64,0},{1,65},{65,1},{2,66},{66,2},{3,67},{67,3},{4,68},{68... | collective-permute-start | bytes 811016 | tf_op jit(solution)/shard_map/ppermute | solution.py:325
  26.3 3.0 %collective-permute-start.6 = (f32[264,256]{1,0:T(8,128)S(1)}, f32[264,256]{1,0:T(8,128)S(1)}, u32[]{:S(2)}, u32[]{:S(2)}) collective-permute-start(f32[264,256]{1,0:T(8,128)S(1)} %collective-permute-done.1.refs_2_), channel_id=1, source_target_pairs={{0,64},{64,0},{1,65},{65,1},{2,66},{66,2},{3,67},{67,3},{4,68},{68... | collective-permute-start | bytes 811016 | tf_op jit(solution)/shard_map/ppermute | solution.py:325
  31.8 17.1 %copy-start.3 = (f32[48,256]{1,0:T(8,128)S(1)}, f32[48,256]{1,0:T(8,128)}, u32[]{:S(2)}) copy-start(f32[48,256]{1,0:T(8,128)} %filters.1) | copy-start | bytes 147460
  65.6 3.3 %collective-permute-start.7 = (f32[1,256,256]{2,1,0:T(8,128)S(1)}, f32[1,256,256]{2,1,0:T(8,128)S(1)}, u32[]{:S(2)}, u32[]{:S(2)}) collective-permute-start(f32[1,256,256]{2,1,0:T(8,128)S(1)} %get-tuple-element.55), channel_id=1, source_target_pairs={{0,64},{64,0},{1,65},{65,1},{2,66},{66,2},{3,67},{67,3},{4,68},{68... | collective-permute-start | bytes 786440 | tf_op jit(solution)/shard_map/ppermute | solution.py:347
  69.5 15.2 %copy-start.2 = (f32[256,256]{1,0:T(8,128)S(1)}, f32[256,256]{1,0:T(8,128)}, u32[]{:S(2)}) copy-start(f32[256,256]{1,0:T(8,128)} %w_msg.1) | copy-start | bytes 786436
  69.5 15.2 %copy-start.4 = (s32[2,5]{1,0:T(2,128)S(1)}, s32[2,5]{1,0:T(2,128)}, u32[]{:S(2)}) copy-start(s32[2,5]{1,0:T(2,128)} %neighbours.1) | copy-start | bytes 124
  69.5 15.2 %copy-start.6 = (s32[2]{0:T(128)S(1)}, s32[2]{0:T(128)}, u32[]{:S(2)}) copy-start(s32[2]{0:T(128)} %nbr_count.1) | copy-start | bytes 28
  69.5 3.4 %collective-permute-start.9 = (f32[3,256,256]{2,1,0:T(8,128)S(1)}, f32[3,256,256]{2,1,0:T(8,128)S(1)}, u32[]{:S(2)}, u32[]{:S(2)}) collective-permute-start(f32[3,256,256]{2,1,0:T(8,128)S(1)} %shard_map.120), channel_id=1, source_target_pairs={{0,64},{64,0},{1,65},{65,1},{2,66},{66,2},{3,67},{67,3},{4,68},{68... | collective-permute-start | bytes 2359304 | tf_op jit(solution)/shard_map/ppermute | solution.py:352
  70.0 16.7 %collective-permute-start.10 = (f32[256,256]{1,0:T(8,128)S(1)}, f32[256,256]{1,0:T(8,128)S(1)}, u32[]{:S(2)}, u32[]{:S(2)}) collective-permute-start(f32[256,256]{1,0:T(8,128)S(1)} %shard_map.119), channel_id=1, source_target_pairs={{0,2},{1,3},{2,0},{3,1},{4,6},{5,7},{6,4},{7,5},{8,10},{9,11},{10,... | collective-permute-start | bytes 786440 | tf_op jit(solution)/shard_map/ppermute | solution.py:353
  70.7 14.0 %collective-permute-start.8 = (f32[264,256]{1,0:T(8,128)S(1)}, f32[264,256]{1,0:T(8,128)S(1)}, u32[]{:S(2)}, u32[]{:S(2)}) collective-permute-start(f32[264,256]{1,0:T(8,128)S(1)} %shard_map.116), channel_id=1, source_target_pairs={{0,4},{4,8},{8,12},{12,16},{16,20},{20,24},{24,28},{28,32},{32,36}... | collective-permute-start | bytes 811016 | tf_op jit(solution)/shard_map/ppermute | solution.py:356
  74.0 12.7 %copy-start = (f32[256,256]{1,0:T(8,128)S(1)}, f32[256,256]{1,0:T(8,128)}, u32[]{:S(2)}) copy-start(f32[256,256]{1,0:T(8,128)} %w_one.1) | copy-start | bytes 786436
  74.0 12.7 %copy-start.1 = (f32[256,256]{1,0:T(8,128)S(1)}, f32[256,256]{1,0:T(8,128)}, u32[]{:S(2)}) copy-start(f32[256,256]{1,0:T(8,128)} %w_two.1) | copy-start | bytes 786436
  74.0 12.6 %collective-permute-start.11 = (f32[256,256]{1,0:T(8,128)S(1)}, f32[256,256]{1,0:T(8,128)S(1)}, u32[]{:S(2)}, u32[]{:S(2)}) collective-permute-start(f32[256,256]{1,0:T(8,128)S(1)} %get-tuple-element.71), channel_id=1, source_target_pairs={{0,1},{1,2},{2,3},{3,0},{4,5},{5,6},{6,7},{7,4},{8,9},{9,10},{10,1... | collective-permute-start | bytes 786440 | tf_op jit(solution)/shard_map/ppermute | solution.py:358
  74.5 12.2 %collective-permute-start.12 = (f32[256,256]{1,0:T(8,128)S(1)}, f32[256,256]{1,0:T(8,128)S(1)}, u32[]{:S(2)}, u32[]{:S(2)}) collective-permute-start(f32[256,256]{1,0:T(8,128)S(1)} %get-tuple-element.72), channel_id=1, source_target_pairs={{0,3},{1,0},{2,1},{3,2},{4,7},{5,4},{6,5},{7,6},{8,11},{9,8},{10,9... | collective-permute-start | bytes 786440 | tf_op jit(solution)/shard_map/ppermute | solution.py:359

commit v10 on v9

--- a/solution.py
+++ b/solution.py
@@ -332,6 +332,10 @@
     spread = call(filtered(scale), floats(*parts.shape), 2)(parts, filters)
     f = lax.all_to_all(spread, (Z, Y), 0, 0, tiled=True).reshape(2 * waves, width)
 
+    f, passed = lax.optimization_barrier((f, passed))
+    ends = [(d, (d + nx) % devices) for d in range(devices) if d % nx == 0]
+    ends += [(d, (d - nx) % devices) for d in range(devices) if d % nx == nx - 1]
+    edge = lax.ppermute(passed, ROWS_WAVES, ends)
     one = floats(width, slots)
 
     def back(chunks, ft, m, *added, stacked=False):
@@ -348,12 +352,9 @@
     ft = lax.optimization_barrier((*ft, far))[:2]
     rest = back(((0, 0), (1, 0), (1, 1)), ft, theirs, stacked=True)
     (e3,) = back(((1, 2),), ft, mine, there)
-    e3, passed, rest, *ft = lax.optimization_barrier((e3, passed, rest, *ft))
+    e3, rest, *ft = lax.optimization_barrier((e3, rest, *ft))
     rest = lax.ppermute(rest, "rows", swap)
     e3 = lax.ppermute(e3, X, shift(X, 2))
-    ends = [(d, (d + nx) % devices) for d in range(devices) if d % nx == 0]
-    ends += [(d, (d - nx) % devices) for d in range(devices) if d % nx == nx - 1]
-    edge = lax.ppermute(passed, ROWS_WAVES, ends)
     e0, e1, e2 = back(((0, 0), (1, 0), (1, 1)), ft, mine, rest)
     e1 = lax.ppermute(e1, X, shift(X, 1))
     e2 = lax.ppermute(e2, X, shift(X, -1))

time: 88.6 us -> 89.7 us (1.012)
  waiting for transfers between devices: 7.5 us -> 8.89 us
    ppermute x1, starting transfers between devices: 0.46 us -> 3.45 us  [shards(): e1 = lax.ppermute(e1, X, shift(X, 1))]
    ppermute x1, starting transfers between devices: 2.81 us -> 0.01 us  [shards(): e2 = lax.ppermute(e2, X, shift(X, -1))]
    ppermute x1, waiting for transfers between devices: 0.01 us -> 2.4 us  [shards(): e1 = lax.ppermute(e1, X, shift(X, 1))]
    ppermute x1, waiting for transfers between devices: 7.4 us -> 6.39 us  [shards(): edge = lax.ppermute(passed, ROWS_WAVES, ends)]
  transfers between devices with their start and end apart: 13 -> 13, of which waited for: 2 -> 3; matrix products, arithmetic and copies ran while one was open for 0% -> 0% of each run, Pallas kernels for 10% -> 10%
where the time goes in v10:
time: 89.7 us; the launch traced here: 89.4 us
  blocking collectives  47.3 us (53%)
  starting transfers between devices  17.2 us (19%)
  Pallas kernels  14.1 us (16%)
  waiting for transfers between devices  8.89 us (10%)
  other arithmetic  1 us (1%)
    all_to_all x1, blocking collectives, shards(): lax.all_to_all(part.reshape(group, 2 * own_waves, width), (Z, Y), 0, 0, t...  17.1 us
    all_to_all x1, blocking collectives, shards(): lax.all_to_all(spread, (Z, Y), 0, 0, tiled=True).reshape(2 * waves, width)  16.1 us
    all_to_all x1, blocking collectives, shards(): kv = lax.all_to_all(kv, (Z, Y), 0, 0, tiled=True)  14.1 us
    ppermute x1, waiting for transfers between devices, shards(): edge = lax.ppermute(passed, ROWS_WAVES, ends)  6.39 us
    pallas_call x3, Pallas kernels, sums(): call(forward(cells, cell, count, own_waves, group, first), (floats(2 * wa...  6.37 us
    ppermute x1, starting transfers between devices, shards(): e1 = lax.ppermute(e1, X, shift(X, 1))  3.45 us
    ppermute x3, starting transfers between devices, shards(): other = [lax.ppermute(c, 'rows', swap) for c in line]  2.9 us
    ppermute x1, starting transfers between devices, shards(): near2 = lax.ppermute(payload, X, shift(X, 2))  2.84 us
  transfers between devices with their start and end apart: 13, of which 3 were waited for; matrix products, arithmetic and copies ran while one was open for 0% of the time, Pallas kernels for 10%

profile of v10, /device:TPU:1, one launch (start us, length us, event | category | flops | bytes accessed | tf_op | source)
XLA Modules:
  0.0 89.4 jit_solution(12603116577944322906)
XLA Ops:
  0.0 1.0 %pad_add_fusion._ = f32[264,256]{1,0:T(8,128)S(1)} fusion(f32[3,48]{1,0:T(4,128)} %param.16, f32[3,256]{1,0:T(4,128)} %param.12, f32[256,256]{1,0:T(8,128)} %param.11), kind=kLoop, calls=%fused_computation | loop fusion | flops 135168 | bytes 536128 | tf_op jit(solution)/shard_map/add | solution.py:297
  1.0 0.0 copy-start.5
  1.0 0.6 copy-done.5
  1.7 0.1 shard_map.110
  1.7 1.4 %collective-permute-start = (f32[264,256]{1,0:T(8,128)S(1)}, f32[264,256]{1,0:T(8,128)S(1)}, u32[]{:S(2)}, u32[]{:S(2)}) collective-permute-start(f32[264,256]{1,0:T(8,128)S(1)} %shard_map.109.own_block.chunk.refs_0_.own), channel_id=1, source_target_pairs={{0,64},{64,0},{1,65},{65,1},{2,66},{66,2},{3,67},{67,3},{4,68},{68... | collective-permute-start | bytes 811016 | tf_op jit(solution)/shard_map/ppermute | solution.py:305
  3.2 2.8 %collective-permute-start.1 = (f32[264,256]{1,0:T(8,128)S(1)}, f32[264,256]{1,0:T(8,128)S(1)}, u32[]{:S(2)}, u32[]{:S(2)}) collective-permute-start(f32[264,256]{1,0:T(8,128)S(1)} %shard_map.109.own_block.chunk.refs_0_.own), channel_id=1, source_target_pairs={{0,2},{1,3},{2,0},{3,1},{4,6},{5,7},{6,4},{7,5},{8,10},{9,11},{10,... | collective-permute-start | bytes 811016 | tf_op jit(solution)/shard_map/ppermute | solution.py:299
  6.0 0.9 collective-permute-start.2
  6.9 0.6 collective-permute-start.3
  7.5 14.1 %all_to_all.15.kv = f32[16,8,128]{2,1,0:T(8,128)S(1)} all-to-all(f32[16,8,128]{2,1,0:T(8,128)S(1)} %shard_map.110), channel_id=1, replica_groups=mesh['rows'=2,'waves_0'=4,'waves_1'=4,'waves_2'=4] {'waves_0','waves_1'}, dimensions={0} | all-to-all | bytes 131072 | tf_op jit(solution)/shard_map/all_to_all | solution.py:306
  21.6 0.2 shard_map.111.lhs
  21.8 0.5 shard_map.112
  22.4 0.0 collective-permute-done.refs_1_
  22.4 1.4 %shard_map.113 = (f32[768,256]{1,0:T(8,128)S(1)}, bf16[1,768,256]{2,1,0:T(8,128)(2,1)S(1)}, bf16[1,768,256]{2,1,0:T(8,128)(2,1)S(1)}) custom-call(bf16[384,48]{1,0:T(8,128)(2,1)S(1)} %shard_map.111.lhs, f32[256,256]{1,0:T(8,128)S(1)} %copy-done.7, f32[264,256]{1,0:T(8,128)S(1)} %shard_map.109.own_block.chunk.refs_0_.own, ...), custom_call_target="tpu_custom_call" | custom-call | flops 603979776 | bytes 65536 | tf_op jit(solution)/shard_map/pallas_call | solution.py:314
  23.8 0.0 collective-permute-done.1.refs_2_
  23.8 0.0 collective-permute-done.2.refs_0_.above.high
  23.8 0.0 collective-permute-done.3.refs_1_.below.low
  23.8 2.4 %collective-permute-start.4 = (f32[264,256]{1,0:T(8,128)S(1)}, f32[264,256]{1,0:T(8,128)S(1)}, u32[]{:S(2)}, u32[]{:S(2)}) collective-permute-start(f32[264,256]{1,0:T(8,128)S(1)} %collective-permute-done.2.refs_0_.above.high), channel_id=1, source_target_pairs={{0,64},{64,0},{1,65},{65,1},{2,66},{66,2},{3,67},{67,3},{4,68},{68... | collective-permute-start | bytes 811016 | tf_op jit(solution)/shard_map/ppermute | solution.py:325
  26.2 0.1 collective-permute-start.5
  26.3 0.4 collective-permute-start.6
  26.7 2.5 %shard_map.114 = (f32[768,256]{1,0:T(8,128)S(1)}, bf16[3,768,256]{2,1,0:T(8,128)(2,1)S(1)}, bf16[3,768,256]{2,1,0:T(8,128)(2,1)S(1)}) custom-call(bf16[384,48]{1,0:T(8,128)(2,1)S(1)} %shard_map.111.lhs, f32[256,256]{1,0:T(8,128)S(1)} %copy-done.7, f32[264,256]{1,0:T(8,128)S(1)} %collective-permute-done.2.refs_0_.above.high, ...), custom_call_target="tpu_custom_call" | custom-call | flops 905969664 | bytes 65536 | tf_op jit(solution)/shard_map/pallas_call | solution.py:314
  29.2 0.0 collective-permute-done.4.refs_0_
  29.3 0.0 collective-permute-done.6.refs_2_
  29.3 2.5 %shard_map.115 = (f32[768,256]{1,0:T(8,128)S(1)}, bf16[3,768,256]{2,1,0:T(8,128)(2,1)S(1)}, bf16[3,768,256]{2,1,0:T(8,128)(2,1)S(1)}) custom-call(bf16[384,48]{1,0:T(8,128)(2,1)S(1)} %shard_map.111.lhs, f32[256,256]{1,0:T(8,128)S(1)} %copy-done.7, f32[264,256]{1,0:T(8,128)S(1)} %collective-permute-done.4.refs_0_, ...), custom_call_target="tpu_custom_call" | custom-call | flops 905969664 | bytes 65536 | tf_op jit(solution)/shard_map/pallas_call | solution.py:314
  31.8 0.0 copy-start.3
  31.8 17.1 %all_to_all.16.parts = f32[16,48,256]{2,1,0:T(8,128)S(1)} all-to-all(f32[16,48,256]{2,1,0:T(8,128)S(1)} %bitcast.3), channel_id=1, replica_groups=mesh['rows'=2,'waves_0'=4,'waves_1'=4,'waves_2'=4] {'waves_0','waves_1'}, dimensions={0} | all-to-all | bytes 1572864 | tf_op jit(solution)/shard_map/all_to_all | solution.py:330
  48.9 0.1 shard_map.117
  49.0 16.1 %all_to_all.17 = f32[16,48,256]{2,1,0:T(8,128)S(1)} all-to-all(f32[16,48,256]{2,1,0:T(8,128)S(1)} %shard_map.117), channel_id=1, replica_groups=mesh['rows'=2,'waves_0'=4,'waves_1'=4,'waves_2'=4] {'waves_0','waves_1'}, dimensions={0} | all-to-all | bytes 1572864 | tf_op jit(solution)/shard_map/all_to_all | solution.py:333
  65.1 0.6 shard_map.119
  65.6 2.2 %collective-permute-start.8 = (f32[1,256,256]{2,1,0:T(8,128)S(1)}, f32[1,256,256]{2,1,0:T(8,128)S(1)}, u32[]{:S(2)}, u32[]{:S(2)}) collective-permute-start(f32[1,256,256]{2,1,0:T(8,128)S(1)} %get-tuple-element.61), channel_id=1, source_target_pairs={{0,64},{64,0},{1,65},{65,1},{2,66},{66,2},{3,67},{67,3},{4,68},{68... | collective-permute-start | bytes 786440 | tf_op jit(solution)/shard_map/ppermute | solution.py:351
  67.8 1.1 %shard_map.121 = f32[3,256,256]{2,1,0:T(8,128)S(1)} custom-call(bf16[256,768]{1,0:T(8,128)(2,1)S(1)} %get-tuple-element.68.fh, bf16[256,768]{1,0:T(8,128)(2,1)S(1)} %get-tuple-element.69.fl, bf16[1,768,256]{2,1,0:T(8,128)(2,1)S(1)} %get-tuple-element.66.mh0, bf16[1,768,256]{2,1,0:T(8,128)(2,1)S(1)} %get-tuple-element.67.ml0, ...), custom_call_target="tpu_custom_call" | custom-call | flops 905969664 | bytes 65536 | tf_op jit(solution)/shard_map/pallas_call | solution.py:345
  68.9 0.1 collective-permute-done.8.refs_0_
  69.0 0.5 shard_map.120
  69.5 0.0 copy-start.2
  69.5 0.0 copy-start.4
  69.5 0.0 copy-start.6
  69.5 0.5 collective-permute-start.9
  70.0 2.2 %collective-permute-start.7 = (f32[264,256]{1,0:T(8,128)S(1)}, f32[264,256]{1,0:T(8,128)S(1)}, u32[]{:S(2)}, u32[]{:S(2)}) collective-permute-start(f32[264,256]{1,0:T(8,128)S(1)} %shard_map.116), channel_id=1, source_target_pairs={{0,4},{4,8},{8,12},{12,16},{16,20},{20,24},{24,28},{28,32},{32,36}... | collective-permute-start | bytes 811016 | tf_op jit(solution)/shard_map/ppermute | solution.py:338
  72.2 0.3 collective-permute-start.10
  72.4 0.0 collective-permute-done.9.refs_0_
  72.4 1.1 %shard_map.122 = (f32[256,256]{1,0:T(8,128)S(1)}, f32[256,256]{1,0:T(8,128)S(1)}, f32[256,256]{1,0:T(8,128)S(1)}) custom-call(bf16[256,768]{1,0:T(8,128)(2,1)S(1)} %get-tuple-element.68.fh, bf16[256,768]{1,0:T(8,128)(2,1)S(1)} %get-tuple-element.69.fl, bf16[1,768,256]{2,1,0:T(8,128)(2,1)S(1)} %get-tuple-element.42.refs_2_.mh0, ...), custom_call_target="tpu_custom_call" | custom-call | flops 905969664 | bytes 65536 | tf_op jit(solution)/shard_map/pallas_call | solution.py:345
  73.5 0.0 copy-start
  73.6 0.0 copy-start.1
  73.6 3.4 %collective-permute-start.11 = (f32[256,256]{1,0:T(8,128)S(1)}, f32[256,256]{1,0:T(8,128)S(1)}, u32[]{:S(2)}, u32[]{:S(2)}) collective-permute-start(f32[256,256]{1,0:T(8,128)S(1)} %get-tuple-element.73), channel_id=1, source_target_pairs={{0,1},{1,2},{2,3},{3,0},{4,5},{5,6},{6,7},{7,4},{8,9},{9,10},{10,1... | collective-permute-start | bytes 786440 | tf_op jit(solution)/shard_map/ppermute | solution.py:359
  77.0 6.4 %collective-permute-done.7.edge = f32[264,256]{1,0:T(8,128)S(1)} collective-permute-done((f32[264,256]{1,0:T(8,128)S(1)}, f32[264,256]{1,0:T(8,128)S(1)}, u32[]{:S(2)}, u32[]{:S(2)}) %collective-permute-start.7) | collective-permute-done | bytes 270368 | tf_op jit(solution)/shard_map/ppermute | solution.py:338
  83.4 1.9 %shard_map.118 = (f32[256,256]{1,0:T(8,128)S(1)}, f32[256,128]{1,0:T(8,128)S(1)}) custom-call(s32[2,5]{1,0:T(2,128)S(1)} %copy-done.4, s32[2]{0:T(128)S(1)} %copy-done.6, f32[264,256]{1,0:T(8,128)S(1)} %shard_map.109.own_block.chunk.refs_0_.own, f32[264,256]{1,0:T(8,128)S(1)} %collective-permute-done.3.refs_1_.below.low, ...), custom_call_target="tpu_custom_call" | custom-call | flops 301989888 | bytes 65536 | tf_op jit(solution)/shard_map/pallas_call | solution.py:362
  85.3 0.0 collective-permute-done.10.refs_1_
  85.4 2.4 %collective-permute-done.11.b = f32[256,256]{1,0:T(8,128)S(1)} collective-permute-done((f32[256,256]{1,0:T(8,128)S(1)}, f32[256,256]{1,0:T(8,128)S(1)}, u32[]{:S(2)}, u32[]{:S(2)}) %collective-permute-start.11) | collective-permute-done | bytes 262176 | tf_op jit(solution)/shard_map/ppermute | solution.py:359
  87.8 1.5 %shard_map.124 = f32[256,256]{1,0:T(8,128)} custom-call(f32[256,256]{1,0:T(8,128)S(1)} %get-tuple-element.54.base, f32[256,128]{1,0:T(8,128)S(1)} %get-tuple-element.55.mask, f32[256,256]{1,0:T(8,128)S(1)} %shard_map.123.a, f32[256,256]{1,0:T(8,128)S(1)} %collective-permute-done.11.b, f32[256,256]{1,0:T(8,128)S(1)} %collective-permute-done.12.c, ...), custom_call_target="tpu_custom_call" | custom-call | bytes 65536 | tf_op jit(solution)/shard_map/pallas_call | solution.py:370
  (14 shorter events, 0.1 us)
Async XLA Ops:
  1.0 0.7 copy-start.5
  1.7 20.7 %copy-start.7 = (f32[256,256]{1,0:T(8,128)S(1)}, f32[256,256]{1,0:T(8,128)}, u32[]{:S(2)}) copy-start(f32[256,256]{1,0:T(8,128)} %w_val.5) | copy-start | bytes 786436
  1.7 20.6 %collective-permute-start = (f32[264,256]{1,0:T(8,128)S(1)}, f32[264,256]{1,0:T(8,128)S(1)}, u32[]{:S(2)}, u32[]{:S(2)}) collective-permute-start(f32[264,256]{1,0:T(8,128)S(1)} %shard_map.109.own_block.chunk.refs_0_.own), channel_id=1, source_target_pairs={{0,64},{64,0},{1,65},{65,1},{2,66},{66,2},{3,67},{67,3},{4,68},{68... | collective-permute-start | bytes 811016 | tf_op jit(solution)/shard_map/ppermute | solution.py:305
  3.2 20.6 %collective-permute-start.1 = (f32[264,256]{1,0:T(8,128)S(1)}, f32[264,256]{1,0:T(8,128)S(1)}, u32[]{:S(2)}, u32[]{:S(2)}) collective-permute-start(f32[264,256]{1,0:T(8,128)S(1)} %shard_map.109.own_block.chunk.refs_0_.own), channel_id=1, source_target_pairs={{0,2},{1,3},{2,0},{3,1},{4,6},{5,7},{6,4},{7,5},{8,10},{9,11},{10,... | collective-permute-start | bytes 811016 | tf_op jit(solution)/shard_map/ppermute | solution.py:299
  6.0 17.8 %collective-permute-start.2 = (f32[264,256]{1,0:T(8,128)S(1)}, f32[264,256]{1,0:T(8,128)S(1)}, u32[]{:S(2)}, u32[]{:S(2)}) collective-permute-start(f32[264,256]{1,0:T(8,128)S(1)} %shard_map.109.own_block.chunk.refs_0_.own), channel_id=1, source_target_pairs={{0,3},{1,0},{2,1},{3,2},{4,7},{5,4},{6,5},{7,6},{8,11},{9,8},{10,9... | collective-permute-start | bytes 811016 | tf_op jit(solution)/shard_map/ppermute | solution.py:300
  6.9 16.9 %collective-permute-start.3 = (f32[264,256]{1,0:T(8,128)S(1)}, f32[264,256]{1,0:T(8,128)S(1)}, u32[]{:S(2)}, u32[]{:S(2)}) collective-permute-start(f32[264,256]{1,0:T(8,128)S(1)} %shard_map.109.own_block.chunk.refs_0_.own), channel_id=1, source_target_pairs={{0,1},{1,2},{2,3},{3,0},{4,5},{5,6},{6,7},{7,4},{8,9},{9,10},{10,1... | collective-permute-start | bytes 811016 | tf_op jit(solution)/shard_map/ppermute | solution.py:301
  23.8 5.4 %collective-permute-start.4 = (f32[264,256]{1,0:T(8,128)S(1)}, f32[264,256]{1,0:T(8,128)S(1)}, u32[]{:S(2)}, u32[]{:S(2)}) collective-permute-start(f32[264,256]{1,0:T(8,128)S(1)} %collective-permute-done.2.refs_0_.above.high), channel_id=1, source_target_pairs={{0,64},{64,0},{1,65},{65,1},{2,66},{66,2},{3,67},{67,3},{4,68},{68... | collective-permute-start | bytes 811016 | tf_op jit(solution)/shard_map/ppermute | solution.py:325
  26.2 3.1 %collective-permute-start.5 = (f32[264,256]{1,0:T(8,128)S(1)}, f32[264,256]{1,0:T(8,128)S(1)}, u32[]{:S(2)}, u32[]{:S(2)}) collective-permute-start(f32[264,256]{1,0:T(8,128)S(1)} %collective-permute-done.3.refs_1_.below.low), channel_id=1, source_target_pairs={{0,64},{64,0},{1,65},{65,1},{2,66},{66,2},{3,67},{67,3},{4,68},{68... | collective-permute-start | bytes 811016 | tf_op jit(solution)/shard_map/ppermute | solution.py:325
  26.3 3.0 %collective-permute-start.6 = (f32[264,256]{1,0:T(8,128)S(1)}, f32[264,256]{1,0:T(8,128)S(1)}, u32[]{:S(2)}, u32[]{:S(2)}) collective-permute-start(f32[264,256]{1,0:T(8,128)S(1)} %collective-permute-done.1.refs_2_), channel_id=1, source_target_pairs={{0,64},{64,0},{1,65},{65,1},{2,66},{66,2},{3,67},{67,3},{4,68},{68... | collective-permute-start | bytes 811016 | tf_op jit(solution)/shard_map/ppermute | solution.py:325
  31.8 17.1 %copy-start.3 = (f32[48,256]{1,0:T(8,128)S(1)}, f32[48,256]{1,0:T(8,128)}, u32[]{:S(2)}) copy-start(f32[48,256]{1,0:T(8,128)} %filters.1) | copy-start | bytes 147460
  65.6 3.3 %collective-permute-start.8 = (f32[1,256,256]{2,1,0:T(8,128)S(1)}, f32[1,256,256]{2,1,0:T(8,128)S(1)}, u32[]{:S(2)}, u32[]{:S(2)}) collective-permute-start(f32[1,256,256]{2,1,0:T(8,128)S(1)} %get-tuple-element.61), channel_id=1, source_target_pairs={{0,64},{64,0},{1,65},{65,1},{2,66},{66,2},{3,67},{67,3},{4,68},{68... | collective-permute-start | bytes 786440 | tf_op jit(solution)/shard_map/ppermute | solution.py:351
  69.5 13.9 %copy-start.2 = (f32[256,256]{1,0:T(8,128)S(1)}, f32[256,256]{1,0:T(8,128)}, u32[]{:S(2)}) copy-start(f32[256,256]{1,0:T(8,128)} %w_msg.1) | copy-start | bytes 786436
  69.5 13.9 %copy-start.4 = (s32[2,5]{1,0:T(2,128)S(1)}, s32[2,5]{1,0:T(2,128)}, u32[]{:S(2)}) copy-start(s32[2,5]{1,0:T(2,128)} %neighbours.1) | copy-start | bytes 124
  69.5 13.9 %copy-start.6 = (s32[2]{0:T(128)S(1)}, s32[2]{0:T(128)}, u32[]{:S(2)}) copy-start(s32[2]{0:T(128)} %nbr_count.1) | copy-start | bytes 28
  69.5 2.9 %collective-permute-start.9 = (f32[3,256,256]{2,1,0:T(8,128)S(1)}, f32[3,256,256]{2,1,0:T(8,128)S(1)}, u32[]{:S(2)}, u32[]{:S(2)}) collective-permute-start(f32[3,256,256]{2,1,0:T(8,128)S(1)} %shard_map.121), channel_id=1, source_target_pairs={{0,64},{64,0},{1,65},{65,1},{2,66},{66,2},{3,67},{67,3},{4,68},{68... | collective-permute-start | bytes 2359304 | tf_op jit(solution)/shard_map/ppermute | solution.py:356
  70.0 13.4 %collective-permute-start.7 = (f32[264,256]{1,0:T(8,128)S(1)}, f32[264,256]{1,0:T(8,128)S(1)}, u32[]{:S(2)}, u32[]{:S(2)}) collective-permute-start(f32[264,256]{1,0:T(8,128)S(1)} %shard_map.116), channel_id=1, source_target_pairs={{0,4},{4,8},{8,12},{12,16},{16,20},{20,24},{24,28},{28,32},{32,36}... | collective-permute-start | bytes 811016 | tf_op jit(solution)/shard_map/ppermute | solution.py:338
  72.2 13.2 %collective-permute-start.10 = (f32[256,256]{1,0:T(8,128)S(1)}, f32[256,256]{1,0:T(8,128)S(1)}, u32[]{:S(2)}, u32[]{:S(2)}) collective-permute-start(f32[256,256]{1,0:T(8,128)S(1)} %shard_map.120), channel_id=1, source_target_pairs={{0,2},{1,3},{2,0},{3,1},{4,6},{5,7},{6,4},{7,5},{8,10},{9,11},{10,... | collective-permute-start | bytes 786440 | tf_op jit(solution)/shard_map/ppermute | solution.py:357
  73.5 14.2 %copy-start = (f32[256,256]{1,0:T(8,128)S(1)}, f32[256,256]{1,0:T(8,128)}, u32[]{:S(2)}) copy-start(f32[256,256]{1,0:T(8,128)} %w_one.1) | copy-start | bytes 786436
  73.6 14.2 %copy-start.1 = (f32[256,256]{1,0:T(8,128)S(1)}, f32[256,256]{1,0:T(8,128)}, u32[]{:S(2)}) copy-start(f32[256,256]{1,0:T(8,128)} %w_two.1) | copy-start | bytes 786436
  73.6 14.2 %collective-permute-start.11 = (f32[256,256]{1,0:T(8,128)S(1)}, f32[256,256]{1,0:T(8,128)S(1)}, u32[]{:S(2)}, u32[]{:S(2)}) collective-permute-start(f32[256,256]{1,0:T(8,128)S(1)} %get-tuple-element.73), channel_id=1, source_target_pairs={{0,1},{1,2},{2,3},{3,0},{4,5},{5,6},{6,7},{7,4},{8,9},{9,10},{10,1... | collective-permute-start | bytes 786440 | tf_op jit(solution)/shard_map/ppermute | solution.py:359
  77.0 10.8 %collective-permute-start.12 = (f32[256,256]{1,0:T(8,128)S(1)}, f32[256,256]{1,0:T(8,128)S(1)}, u32[]{:S(2)}, u32[]{:S(2)}) collective-permute-start(f32[256,256]{1,0:T(8,128)S(1)} %get-tuple-element.74), channel_id=1, source_target_pairs={{0,3},{1,0},{2,1},{3,2},{4,7},{5,4},{6,5},{7,6},{8,11},{9,8},{10,9... | collective-permute-start | bytes 786440 | tf_op jit(solution)/shard_map/ppermute | solution.py:360

commit v11 on v9

--- a/solution.py
+++ b/solution.py
@@ -210,49 +210,80 @@
         out[...] = a[...] + b[...]
 
 
+def listed_factor(neighbours, nbr_count, c, target, nb):
+    listed = jnp.float32(0.0)
+    for b in range(nb):
+        hit = (neighbours[c, b] == target) & (b < nbr_count[c])
+        listed = listed + jnp.where(hit, jnp.float32(1.0), jnp.float32(0.0))
+    return listed
+
+
+def gather(neighbours, nbr_count, mine, blocks, use, cells, cell, cells_all, nb):
+    slots = cells * cell
+    first = lax.axis_index(ROWS_WAVES) * cells
+    wide, pos = {}, {}
+    for k in use:
+        live = live_rows(blocks[k], cells, cell)
+        halves = split(jnp.where(live, blocks[k][:slots], 0.0))
+        for c in range(cells):
+            wide[k * cells + c] = tuple(p[c * cell : (c + 1) * cell] for p in halves)
+            pos[k * cells + c] = blocks[k][slots : slots + 3, c * cell : (c + 1) * cell]
+    eye = lax.broadcasted_iota(jnp.int32, (cell, cell), 0) == lax.broadcasted_iota(jnp.int32, (cell, cell), 1)
+    gathered = []
+    for c in range(cells):
+        here = mine[c * cell : (c + 1) * cell]
+        acc = jnp.zeros((cell, blocks[use[0]].shape[1]), F32)
+        for step in range(2 * cells + 1):
+            other = c + step
+            if other not in wide:
+                continue
+            target = lax.rem(first + other - cells + cells_all, cells_all)
+            near = pos[other]
+            d0 = here[:, 0:1] - near[0:1]
+            d1 = here[:, 1:2] - near[1:2]
+            d2 = here[:, 2:3] - near[2:3]
+            weight = jnp.exp(-0.125 * (d0 * d0 + d1 * d1 + d2 * d2))
+            weight = weight * listed_factor(neighbours, nbr_count, c, target, nb)
+            if step == cells:
+                weight = jnp.where(eye, 0.0, weight)
+            acc = acc + dot3(split(weight), wide[other])
+        gathered.append(acc)
+    return jnp.concatenate(gathered, axis=0)
+
+
 def messages(cells, cell, cells_all, nb, last):
     slots = cells * cell
 
-    def kernel(neighbours, nbr_count, own, low, high, edge, w_msg, out, mask):
-        x, first = lax.axis_index(X), lax.axis_index(ROWS_WAVES) * cells
-        lo = jnp.where(x == 0, edge[...], low[...])
-        hi = jnp.where(x == last, edge[...], high[...])
-        blocks = (lo, own[...], hi)
-        masks = [live_rows(b, cells, cell) for b in blocks]
-        parts = [split(jnp.where(m, b[:slots], 0.0)) for m, b in zip(masks, blocks)]
-        wide = [tuple(p[k][c * cell : (c + 1) * cell] for k in range(2)) for p in parts for c in range(cells)]
-        pos = [
-            b[slots : slots + 3, c * cell : (c + 1) * cell] for b in blocks for c in range(cells)
-        ]
-        cols = own[slots : slots + 8].T
-        eye = lax.broadcasted_iota(jnp.int32, (cell, cell), 0) == lax.broadcasted_iota(jnp.int32, (cell, cell), 1)
-        gathered = []
-        for c in range(cells):
-            mine = cols[c * cell : (c + 1) * cell]
-            acc = None
-            for step in range(2 * cells + 1):
-                other = c + step
-                local = other - cells
-                target = lax.rem(first + local + cells_all, cells_all)
-                listed = jnp.float32(0.0)
-                for b in range(nb):
-                    hit = (neighbours[c, b] == target) & (b < nbr_count[c])
-                    listed = listed + jnp.where(hit, jnp.float32(1.0), jnp.float32(0.0))
-                near = pos[other]
-                d0 = mine[:, 0:1] - near[0:1]
-                d1 = mine[:, 1:2] - near[1:2]
-                d2 = mine[:, 2:3] - near[2:3]
-                weight = jnp.exp(-0.125 * (d0 * d0 + d1 * d1 + d2 * d2)) * listed
-                if step == cells:
-                    weight = jnp.where(eye, 0.0, weight)
-                part = dot3(split(weight), wide[other])
-                acc = part if acc is None else acc + part
-            gathered.append(acc)
-        total = jnp.concatenate(gathered, axis=0)
-        live = masks[1]
+    def kernel(neighbours, nbr_count, own, low, high, w_msg, out, mask):
+        x = lax.axis_index(X)
+        lo = jnp.where(x == 0, 0.0, low[...])
+        hi = jnp.where(x == last, 0.0, high[...])
+        blocks = lo, own[...], hi
+        mine = own[slots : slots + 8].T
+        total = gather(neighbours, nbr_count, mine, blocks, (0, 1, 2), cells, cell, cells_all, nb)
+        live = live_rows(own, cells, cell)
         msg = 0.125 * dot3(split(total), split(w_msg[...]))
         out[...] = own[:slots] + jnp.where(live, msg, 0.0)
         mask[...] = jnp.broadcast_to(jnp.where(live, 1.0, 0.0), mask.shape)
+
+    return kernel
+
+
+def end_messages(cells, cell, cells_all, nb, last):
+    slots = cells * cell
+
+    def kernel(neighbours, nbr_count, base, own, edge, w_msg, out):
+        x = lax.axis_index(X)
+        out[...] = base[...]
+        for at, side in ((0, 0), (last, 2)):
+
+            @pl.when(x == at)
+            def _(side=side):
+                mine = own[slots : slots + 8].T
+                blocks = {side: edge[...]}
+                total = gather(neighbours, nbr_count, mine, blocks, (side,), cells, cell, cells_all, nb)
+                msg = 0.125 * dot3(split(total), split(w_msg[...]))
+                out[...] = base[...] + jnp.where(live_rows(own, cells, cell), msg, 0.0)
 
     return kernel
 
@@ -358,13 +389,13 @@
     e1 = lax.ppermute(e1, X, shift(X, 1))
     e2 = lax.ppermute(e2, X, shift(X, -1))
 
-    base, mask = call(
-        messages(cells, cell, cells * devices, neighbours.shape[1], nx - 1),
-        (floats(slots, width), floats(slots, 128)),
-        7,
-        smem=(0, 1),
-        flops=unit,
-    )(neighbours, nbr_count, payload, below, above, edge, w_msg)
+    sizes = cells, cell, cells * devices, neighbours.shape[1], nx - 1
+    base, mask = call(messages(*sizes), (floats(slots, width), floats(slots, 128)), 6, smem=(0, 1))(
+        neighbours, nbr_count, payload, below, above, w_msg
+    )
+    base = call(end_messages(*sizes), floats(slots, width), 6, smem=(0, 1))(
+        neighbours, nbr_count, base, payload, edge, w_msg
+    )
     (e0,) = call(pairs, (one,), 2)(e0, e3)
     return call(finish(), floats(slots, width), 7)(base, mask, e0, e1, e2, w_one, w_two)
 

time: 88.6 us -> 88.1 us (level)
  waiting for transfers between devices: 7.5 us -> 5.59 us
  Pallas kernels: 14.1 us -> 15.5 us
    ppermute x1, waiting for transfers between devices: 7.4 us -> 5.5 us  [shards(): edge = lax.ppermute(passed, ROWS_WAVES, ends)]
    pallas_call x1 -> x2, Pallas kernels: 1.91 us -> 3.35 us  [the longest x1 1.9 us: shards(): call(messages(*sizes), (floats(slots, width), floats(slots, 128)), 6, sme...]
  transfers between devices with their start and end apart: 13 -> 13, of which waited for: 2 -> 2; matrix products, arithmetic and copies ran while one was open for 0% -> 0% of each run, Pallas kernels for 10% -> 12%
where the time goes in v11:
time: 88.1 us; the launch traced here: 87.8 us
  blocking collectives  47.3 us (54%)
  starting transfers between devices  17.5 us (20%)
  Pallas kernels  15.5 us (18%)
  waiting for transfers between devices  5.59 us (6%)
  other arithmetic  1 us (1%)
    all_to_all x1, blocking collectives, shards(): lax.all_to_all(part.reshape(group, 2 * own_waves, width), (Z, Y), 0, 0, t...  17.1 us
    all_to_all x1, blocking collectives, shards(): lax.all_to_all(spread, (Z, Y), 0, 0, tiled=True).reshape(2 * waves, width)  16.1 us
    all_to_all x1, blocking collectives, shards(): kv = lax.all_to_all(kv, (Z, Y), 0, 0, tiled=True)  14.1 us
    pallas_call x3, Pallas kernels, sums(): call(forward(cells, cell, count, own_waves, group, first), (floats(2 * wa...  6.34 us
    ppermute x1, waiting for transfers between devices, shards(): edge = lax.ppermute(passed, ROWS_WAVES, ends)  5.5 us
    ppermute x3, starting transfers between devices, shards(): other = [lax.ppermute(c, 'rows', swap) for c in line]  2.9 us
    ppermute x1, starting transfers between devices, shards(): near2 = lax.ppermute(payload, X, shift(X, 2))  2.84 us
    ppermute x1, starting transfers between devices, shards(): e2 = lax.ppermute(e2, X, shift(X, -1))  2.79 us
  transfers between devices with their start and end apart: 13, of which 2 were waited for; matrix products, arithmetic and copies ran while one was open for 0% of the time, Pallas kernels for 12%

profile of v11, /device:TPU:1, one launch (start us, length us, event | category | flops | bytes accessed | tf_op | source)
XLA Modules:
  0.0 87.8 jit_solution(5868352146417819757)
XLA Ops:
  0.0 1.0 %pad_add_fusion._ = f32[264,256]{1,0:T(8,128)S(1)} fusion(f32[3,48]{1,0:T(4,128)} %param.16, f32[3,256]{1,0:T(4,128)} %param.12, f32[256,256]{1,0:T(8,128)} %param.11), kind=kLoop, calls=%fused_computation | loop fusion | flops 135168 | bytes 536128 | tf_op jit(solution)/shard_map/add | solution.py:328
  1.0 0.0 copy-start.6
  1.0 0.6 copy-done.6
  1.7 0.1 shard_map.110
  1.7 1.4 %collective-permute-start = (f32[264,256]{1,0:T(8,128)S(1)}, f32[264,256]{1,0:T(8,128)S(1)}, u32[]{:S(2)}, u32[]{:S(2)}) collective-permute-start(f32[264,256]{1,0:T(8,128)S(1)} %shard_map.109.own_block.chunk.refs_0_.own), channel_id=1, source_target_pairs={{0,64},{64,0},{1,65},{65,1},{2,66},{66,2},{3,67},{67,3},{4,68},{68... | collective-permute-start | bytes 811016 | tf_op jit(solution)/shard_map/ppermute | solution.py:336
  3.2 2.8 %collective-permute-start.1 = (f32[264,256]{1,0:T(8,128)S(1)}, f32[264,256]{1,0:T(8,128)S(1)}, u32[]{:S(2)}, u32[]{:S(2)}) collective-permute-start(f32[264,256]{1,0:T(8,128)S(1)} %shard_map.109.own_block.chunk.refs_0_.own), channel_id=1, source_target_pairs={{0,2},{1,3},{2,0},{3,1},{4,6},{5,7},{6,4},{7,5},{8,10},{9,11},{10,... | collective-permute-start | bytes 811016 | tf_op jit(solution)/shard_map/ppermute | solution.py:330
  6.0 0.9 collective-permute-start.2
  6.9 0.6 collective-permute-start.3
  7.5 14.1 %all_to_all.15.kv = f32[16,8,128]{2,1,0:T(8,128)S(1)} all-to-all(f32[16,8,128]{2,1,0:T(8,128)S(1)} %shard_map.110), channel_id=1, replica_groups=mesh['rows'=2,'waves_0'=4,'waves_1'=4,'waves_2'=4] {'waves_0','waves_1'}, dimensions={0} | all-to-all | bytes 131072 | tf_op jit(solution)/shard_map/all_to_all | solution.py:337
  21.6 0.2 shard_map.111.lhs
  21.8 0.5 shard_map.112
  22.4 0.0 collective-permute-done.refs_1_
  22.4 1.4 %shard_map.113 = (f32[768,256]{1,0:T(8,128)S(1)}, bf16[1,768,256]{2,1,0:T(8,128)(2,1)S(1)}, bf16[1,768,256]{2,1,0:T(8,128)(2,1)S(1)}) custom-call(bf16[384,48]{1,0:T(8,128)(2,1)S(1)} %shard_map.111.lhs, f32[256,256]{1,0:T(8,128)S(1)} %copy-done.7, f32[264,256]{1,0:T(8,128)S(1)} %shard_map.109.own_block.chunk.refs_0_.own, ...), custom_call_target="tpu_custom_call" | custom-call | flops 603979776 | bytes 65536 | tf_op jit(solution)/shard_map/pallas_call | solution.py:345
  23.8 0.0 collective-permute-done.1.refs_2_
  23.8 0.0 collective-permute-done.2.high.refs_0_.above
  23.8 0.0 collective-permute-done.3.low.refs_1_.below
  23.8 2.4 %collective-permute-start.4 = (f32[264,256]{1,0:T(8,128)S(1)}, f32[264,256]{1,0:T(8,128)S(1)}, u32[]{:S(2)}, u32[]{:S(2)}) collective-permute-start(f32[264,256]{1,0:T(8,128)S(1)} %collective-permute-done.2.high.refs_0_.above), channel_id=1, source_target_pairs={{0,64},{64,0},{1,65},{65,1},{2,66},{66,2},{3,67},{67,3},{4,68},{68... | collective-permute-start | bytes 811016 | tf_op jit(solution)/shard_map/ppermute | solution.py:356
  26.2 0.1 collective-permute-start.5
  26.3 0.4 collective-permute-start.6
  26.7 2.5 %shard_map.115 = (f32[768,256]{1,0:T(8,128)S(1)}, bf16[3,768,256]{2,1,0:T(8,128)(2,1)S(1)}, bf16[3,768,256]{2,1,0:T(8,128)(2,1)S(1)}) custom-call(bf16[384,48]{1,0:T(8,128)(2,1)S(1)} %shard_map.111.lhs, f32[256,256]{1,0:T(8,128)S(1)} %copy-done.7, f32[264,256]{1,0:T(8,128)S(1)} %collective-permute-done.2.high.refs_0_.above, ...), custom_call_target="tpu_custom_call" | custom-call | flops 905969664 | bytes 65536 | tf_op jit(solution)/shard_map/pallas_call | solution.py:345
  29.2 0.0 collective-permute-done.6.refs_2_
  29.3 2.5 %shard_map.116 = (f32[768,256]{1,0:T(8,128)S(1)}, bf16[3,768,256]{2,1,0:T(8,128)(2,1)S(1)}, bf16[3,768,256]{2,1,0:T(8,128)(2,1)S(1)}) custom-call(bf16[384,48]{1,0:T(8,128)(2,1)S(1)} %shard_map.111.lhs, f32[256,256]{1,0:T(8,128)S(1)} %copy-done.7, f32[264,256]{1,0:T(8,128)S(1)} %collective-permute-done.4.refs_0_, ...), custom_call_target="tpu_custom_call" | custom-call | flops 905969664 | bytes 65536 | tf_op jit(solution)/shard_map/pallas_call | solution.py:345
  31.7 0.0 copy-start.3
  31.8 17.1 %all_to_all.16.parts = f32[16,48,256]{2,1,0:T(8,128)S(1)} all-to-all(f32[16,48,256]{2,1,0:T(8,128)S(1)} %bitcast.3), channel_id=1, replica_groups=mesh['rows'=2,'waves_0'=4,'waves_1'=4,'waves_2'=4] {'waves_0','waves_1'}, dimensions={0} | all-to-all | bytes 1572864 | tf_op jit(solution)/shard_map/all_to_all | solution.py:361
  48.9 0.1 shard_map.118
  49.0 16.1 %all_to_all.17 = f32[16,48,256]{2,1,0:T(8,128)S(1)} all-to-all(f32[16,48,256]{2,1,0:T(8,128)S(1)} %shard_map.118), channel_id=1, replica_groups=mesh['rows'=2,'waves_0'=4,'waves_1'=4,'waves_2'=4] {'waves_0','waves_1'}, dimensions={0} | all-to-all | bytes 1572864 | tf_op jit(solution)/shard_map/all_to_all | solution.py:364
  65.0 0.6 shard_map.119
  65.6 2.2 %collective-permute-start.7 = (f32[1,256,256]{2,1,0:T(8,128)S(1)}, f32[1,256,256]{2,1,0:T(8,128)S(1)}, u32[]{:S(2)}, u32[]{:S(2)}) collective-permute-start(f32[1,256,256]{2,1,0:T(8,128)S(1)} %get-tuple-element.56), channel_id=1, source_target_pairs={{0,64},{64,0},{1,65},{65,1},{2,66},{66,2},{3,67},{67,3},{4,68},{68... | collective-permute-start | bytes 786440 | tf_op jit(solution)/shard_map/ppermute | solution.py:378
  67.8 1.1 %shard_map.121 = f32[3,256,256]{2,1,0:T(8,128)S(1)} custom-call(bf16[256,768]{1,0:T(8,128)(2,1)S(1)} %get-tuple-element.66.fh, bf16[256,768]{1,0:T(8,128)(2,1)S(1)} %get-tuple-element.67.fl, bf16[1,768,256]{2,1,0:T(8,128)(2,1)S(1)} %get-tuple-element.62.mh0, bf16[1,768,256]{2,1,0:T(8,128)(2,1)S(1)} %get-tuple-element.63.ml0, ...), custom_call_target="tpu_custom_call" | custom-call | flops 905969664 | bytes 65536 | tf_op jit(solution)/shard_map/pallas_call | solution.py:372
  68.9 0.1 collective-permute-done.7.refs_0_
  69.0 0.5 shard_map.120
  69.4 0.0 copy-start
  69.5 0.0 copy-start.4
  69.5 0.0 copy-start.5
  69.5 0.5 collective-permute-start.9
  69.9 0.8 collective-permute-start.10
  70.7 2.2 %collective-permute-start.8 = (f32[264,256]{1,0:T(8,128)S(1)}, f32[264,256]{1,0:T(8,128)S(1)}, u32[]{:S(2)}, u32[]{:S(2)}) collective-permute-start(f32[264,256]{1,0:T(8,128)S(1)} %shard_map.117), channel_id=1, source_target_pairs={{0,4},{4,8},{8,12},{12,16},{16,20},{20,24},{24,28},{28,32},{32,36}... | collective-permute-start | bytes 811016 | tf_op jit(solution)/shard_map/ppermute | solution.py:387
  72.9 0.0 collective-permute-done.9.refs_0_
  72.9 1.1 %shard_map.123 = (f32[256,256]{1,0:T(8,128)S(1)}, f32[256,256]{1,0:T(8,128)S(1)}, f32[256,256]{1,0:T(8,128)S(1)}) custom-call(bf16[256,768]{1,0:T(8,128)(2,1)S(1)} %get-tuple-element.66.fh, bf16[256,768]{1,0:T(8,128)(2,1)S(1)} %get-tuple-element.67.fl, bf16[1,768,256]{2,1,0:T(8,128)(2,1)S(1)} %get-tuple-element.41.refs_2_.mh0, ...), custom_call_target="tpu_custom_call" | custom-call | flops 905969664 | bytes 65536 | tf_op jit(solution)/shard_map/pallas_call | solution.py:372
  74.0 0.5 collective-permute-start.11
  74.5 2.8 %collective-permute-start.12 = (f32[256,256]{1,0:T(8,128)S(1)}, f32[256,256]{1,0:T(8,128)S(1)}, u32[]{:S(2)}, u32[]{:S(2)}) collective-permute-start(f32[256,256]{1,0:T(8,128)S(1)} %get-tuple-element.72), channel_id=1, source_target_pairs={{0,3},{1,0},{2,1},{3,2},{4,7},{5,4},{6,5},{7,6},{8,11},{9,8},{10,9... | collective-permute-start | bytes 786440 | tf_op jit(solution)/shard_map/ppermute | solution.py:390
  77.3 1.9 %shard_map.114 = (f32[256,256]{1,0:T(8,128)S(1)}, f32[256,128]{1,0:T(8,128)S(1)}) custom-call(s32[2,5]{1,0:T(2,128)S(1)} %copy-done.4, s32[2]{0:T(128)S(1)} %copy-done.5, f32[264,256]{1,0:T(8,128)S(1)} %shard_map.109.own_block.chunk.refs_0_.own, f32[264,256]{1,0:T(8,128)S(1)} %collective-permute-done.3.low.refs_1_.below, ...), custom_call_target="tpu_custom_call" | custom-call | bytes 65536 | tf_op jit(solution)/shard_map/pallas_call | solution.py:393
  79.2 0.0 copy-start.1
  79.2 0.0 copy-start.2
  79.2 5.5 %collective-permute-done.8.edge = f32[264,256]{1,0:T(8,128)S(1)} collective-permute-done((f32[264,256]{1,0:T(8,128)S(1)}, f32[264,256]{1,0:T(8,128)S(1)}, u32[]{:S(2)}, u32[]{:S(2)}) %collective-permute-start.8) | collective-permute-done | bytes 270368 | tf_op jit(solution)/shard_map/ppermute | solution.py:387
  84.7 1.4 %shard_map.122.base = f32[256,256]{1,0:T(8,128)S(1)} custom-call(s32[2,5]{1,0:T(2,128)S(1)} %copy-done.4, s32[2]{0:T(128)S(1)} %copy-done.5, f32[256,256]{1,0:T(8,128)S(1)} %get-tuple-element.46.base, f32[264,256]{1,0:T(8,128)S(1)} %shard_map.109.own_block.chunk.refs_0_.own, f32[264,256]{1,0:T(8,128)S(1)} %collective-permute-done.8.edge, f32[256,256]{1,0:T(8,128)S(1)} %copy-done), custom_call_target="tpu_custom_call" | custom-call | bytes 65536 | tf_op jit(solution)/shard_map/pallas_call | solution.py:396
  86.2 0.0 collective-permute-done.12.c
  86.2 1.6 %shard_map.125 = f32[256,256]{1,0:T(8,128)} custom-call(f32[256,256]{1,0:T(8,128)S(1)} %shard_map.122.base, f32[256,128]{1,0:T(8,128)S(1)} %get-tuple-element.65.mask, f32[256,256]{1,0:T(8,128)S(1)} %shard_map.124.a, f32[256,256]{1,0:T(8,128)S(1)} %collective-permute-done.11.b, f32[256,256]{1,0:T(8,128)S(1)} %collective-permute-done.12.c, ...), custom_call_target="tpu_custom_call" | custom-call | bytes 65536 | tf_op jit(solution)/shard_map/pallas_call | solution.py:400
  (15 shorter events, 0.1 us)
Async XLA Ops:
  1.0 0.7 copy-start.6
  1.7 20.7 %copy-start.7 = (f32[256,256]{1,0:T(8,128)S(1)}, f32[256,256]{1,0:T(8,128)}, u32[]{:S(2)}) copy-start(f32[256,256]{1,0:T(8,128)} %w_val.5) | copy-start | bytes 786436
  1.7 20.6 %collective-permute-start = (f32[264,256]{1,0:T(8,128)S(1)}, f32[264,256]{1,0:T(8,128)S(1)}, u32[]{:S(2)}, u32[]{:S(2)}) collective-permute-start(f32[264,256]{1,0:T(8,128)S(1)} %shard_map.109.own_block.chunk.refs_0_.own), channel_id=1, source_target_pairs={{0,64},{64,0},{1,65},{65,1},{2,66},{66,2},{3,67},{67,3},{4,68},{68... | collective-permute-start | bytes 811016 | tf_op jit(solution)/shard_map/ppermute | solution.py:336
  3.2 20.6 %collective-permute-start.1 = (f32[264,256]{1,0:T(8,128)S(1)}, f32[264,256]{1,0:T(8,128)S(1)}, u32[]{:S(2)}, u32[]{:S(2)}) collective-permute-start(f32[264,256]{1,0:T(8,128)S(1)} %shard_map.109.own_block.chunk.refs_0_.own), channel_id=1, source_target_pairs={{0,2},{1,3},{2,0},{3,1},{4,6},{5,7},{6,4},{7,5},{8,10},{9,11},{10,... | collective-permute-start | bytes 811016 | tf_op jit(solution)/shard_map/ppermute | solution.py:330
  6.0 17.7 %collective-permute-start.2 = (f32[264,256]{1,0:T(8,128)S(1)}, f32[264,256]{1,0:T(8,128)S(1)}, u32[]{:S(2)}, u32[]{:S(2)}) collective-permute-start(f32[264,256]{1,0:T(8,128)S(1)} %shard_map.109.own_block.chunk.refs_0_.own), channel_id=1, source_target_pairs={{0,3},{1,0},{2,1},{3,2},{4,7},{5,4},{6,5},{7,6},{8,11},{9,8},{10,9... | collective-permute-start | bytes 811016 | tf_op jit(solution)/shard_map/ppermute | solution.py:331
  6.9 16.9 %collective-permute-start.3 = (f32[264,256]{1,0:T(8,128)S(1)}, f32[264,256]{1,0:T(8,128)S(1)}, u32[]{:S(2)}, u32[]{:S(2)}) collective-permute-start(f32[264,256]{1,0:T(8,128)S(1)} %shard_map.109.own_block.chunk.refs_0_.own), channel_id=1, source_target_pairs={{0,1},{1,2},{2,3},{3,0},{4,5},{5,6},{6,7},{7,4},{8,9},{9,10},{10,1... | collective-permute-start | bytes 811016 | tf_op jit(solution)/shard_map/ppermute | solution.py:332
  23.8 5.4 %collective-permute-start.4 = (f32[264,256]{1,0:T(8,128)S(1)}, f32[264,256]{1,0:T(8,128)S(1)}, u32[]{:S(2)}, u32[]{:S(2)}) collective-permute-start(f32[264,256]{1,0:T(8,128)S(1)} %collective-permute-done.2.high.refs_0_.above), channel_id=1, source_target_pairs={{0,64},{64,0},{1,65},{65,1},{2,66},{66,2},{3,67},{67,3},{4,68},{68... | collective-permute-start | bytes 811016 | tf_op jit(solution)/shard_map/ppermute | solution.py:356
  26.2 3.0 %collective-permute-start.5 = (f32[264,256]{1,0:T(8,128)S(1)}, f32[264,256]{1,0:T(8,128)S(1)}, u32[]{:S(2)}, u32[]{:S(2)}) collective-permute-start(f32[264,256]{1,0:T(8,128)S(1)} %collective-permute-done.3.low.refs_1_.below), channel_id=1, source_target_pairs={{0,64},{64,0},{1,65},{65,1},{2,66},{66,2},{3,67},{67,3},{4,68},{68... | collective-permute-start | bytes 811016 | tf_op jit(solution)/shard_map/ppermute | solution.py:356
  26.3 3.0 %collective-permute-start.6 = (f32[264,256]{1,0:T(8,128)S(1)}, f32[264,256]{1,0:T(8,128)S(1)}, u32[]{:S(2)}, u32[]{:S(2)}) collective-permute-start(f32[264,256]{1,0:T(8,128)S(1)} %collective-permute-done.1.refs_2_), channel_id=1, source_target_pairs={{0,64},{64,0},{1,65},{65,1},{2,66},{66,2},{3,67},{67,3},{4,68},{68... | collective-permute-start | bytes 811016 | tf_op jit(solution)/shard_map/ppermute | solution.py:356
  31.7 17.1 %copy-start.3 = (f32[48,256]{1,0:T(8,128)S(1)}, f32[48,256]{1,0:T(8,128)}, u32[]{:S(2)}) copy-start(f32[48,256]{1,0:T(8,128)} %filters.1) | copy-start | bytes 147460
  65.6 3.3 %collective-permute-start.7 = (f32[1,256,256]{2,1,0:T(8,128)S(1)}, f32[1,256,256]{2,1,0:T(8,128)S(1)}, u32[]{:S(2)}, u32[]{:S(2)}) collective-permute-start(f32[1,256,256]{2,1,0:T(8,128)S(1)} %get-tuple-element.56), channel_id=1, source_target_pairs={{0,64},{64,0},{1,65},{65,1},{2,66},{66,2},{3,67},{67,3},{4,68},{68... | collective-permute-start | bytes 786440 | tf_op jit(solution)/shard_map/ppermute | solution.py:378
  69.4 7.8 %copy-start = (f32[256,256]{1,0:T(8,128)S(1)}, f32[256,256]{1,0:T(8,128)}, u32[]{:S(2)}) copy-start(f32[256,256]{1,0:T(8,128)} %w_msg.3) | copy-start | bytes 786436
  69.5 7.8 %copy-start.4 = (s32[2,5]{1,0:T(2,128)S(1)}, s32[2,5]{1,0:T(2,128)}, u32[]{:S(2)}) copy-start(s32[2,5]{1,0:T(2,128)} %neighbours.3) | copy-start | bytes 124
  69.5 7.8 %copy-start.5 = (s32[2]{0:T(128)S(1)}, s32[2]{0:T(128)}, u32[]{:S(2)}) copy-start(s32[2]{0:T(128)} %nbr_count.3) | copy-start | bytes 28
  69.5 3.4 %collective-permute-start.9 = (f32[3,256,256]{2,1,0:T(8,128)S(1)}, f32[3,256,256]{2,1,0:T(8,128)S(1)}, u32[]{:S(2)}, u32[]{:S(2)}) collective-permute-start(f32[3,256,256]{2,1,0:T(8,128)S(1)} %shard_map.121), channel_id=1, source_target_pairs={{0,64},{64,0},{1,65},{65,1},{2,66},{66,2},{3,67},{67,3},{4,68},{68... | collective-permute-start | bytes 2359304 | tf_op jit(solution)/shard_map/ppermute | solution.py:383
  69.9 16.2 %collective-permute-start.10 = (f32[256,256]{1,0:T(8,128)S(1)}, f32[256,256]{1,0:T(8,128)S(1)}, u32[]{:S(2)}, u32[]{:S(2)}) collective-permute-start(f32[256,256]{1,0:T(8,128)S(1)} %shard_map.120), channel_id=1, source_target_pairs={{0,2},{1,3},{2,0},{3,1},{4,6},{5,7},{6,4},{7,5},{8,10},{9,11},{10,... | collective-permute-start | bytes 786440 | tf_op jit(solution)/shard_map/ppermute | solution.py:384
  70.7 14.0 %collective-permute-start.8 = (f32[264,256]{1,0:T(8,128)S(1)}, f32[264,256]{1,0:T(8,128)S(1)}, u32[]{:S(2)}, u32[]{:S(2)}) collective-permute-start(f32[264,256]{1,0:T(8,128)S(1)} %shard_map.117), channel_id=1, source_target_pairs={{0,4},{4,8},{8,12},{12,16},{16,20},{20,24},{24,28},{28,32},{32,36}... | collective-permute-start | bytes 811016 | tf_op jit(solution)/shard_map/ppermute | solution.py:387
  74.0 12.2 %collective-permute-start.11 = (f32[256,256]{1,0:T(8,128)S(1)}, f32[256,256]{1,0:T(8,128)S(1)}, u32[]{:S(2)}, u32[]{:S(2)}) collective-permute-start(f32[256,256]{1,0:T(8,128)S(1)} %get-tuple-element.71), channel_id=1, source_target_pairs={{0,1},{1,2},{2,3},{3,0},{4,5},{5,6},{6,7},{7,4},{8,9},{9,10},{10,1... | collective-permute-start | bytes 786440 | tf_op jit(solution)/shard_map/ppermute | solution.py:389
  74.5 11.7 %collective-permute-start.12 = (f32[256,256]{1,0:T(8,128)S(1)}, f32[256,256]{1,0:T(8,128)S(1)}, u32[]{:S(2)}, u32[]{:S(2)}) collective-permute-start(f32[256,256]{1,0:T(8,128)S(1)} %get-tuple-element.72), channel_id=1, source_target_pairs={{0,3},{1,0},{2,1},{3,2},{4,7},{5,4},{6,5},{7,6},{8,11},{9,8},{10,9... | collective-permute-start | bytes 786440 | tf_op jit(solution)/shard_map/ppermute | solution.py:390
  79.2 7.0 %copy-start.1 = (f32[256,256]{1,0:T(8,128)S(1)}, f32[256,256]{1,0:T(8,128)}, u32[]{:S(2)}) copy-start(f32[256,256]{1,0:T(8,128)} %w_one.1) | copy-start | bytes 786436
  79.2 7.0 %copy-start.2 = (f32[256,256]{1,0:T(8,128)S(1)}, f32[256,256]{1,0:T(8,128)}, u32[]{:S(2)}) copy-start(f32[256,256]{1,0:T(8,128)} %w_two.1) | copy-start | bytes 786436

commit v12 on v11

--- a/solution.py
+++ b/solution.py
@@ -254,15 +254,18 @@
 def messages(cells, cell, cells_all, nb, last):
     slots = cells * cell
 
-    def kernel(neighbours, nbr_count, own, low, high, w_msg, out, mask):
+    def kernel(neighbours, nbr_count, own, low, high, w_msg, w_one, w_two, out, mask, cols, *parts):
         x = lax.axis_index(X)
         lo = jnp.where(x == 0, 0.0, low[...])
         hi = jnp.where(x == last, 0.0, high[...])
         blocks = lo, own[...], hi
         mine = own[slots : slots + 8].T
+        cols[...] = mine
+        for k, w in enumerate((w_msg, w_one, w_two)):
+            parts[2 * k][...], parts[2 * k + 1][...] = split(w[...])
         total = gather(neighbours, nbr_count, mine, blocks, (0, 1, 2), cells, cell, cells_all, nb)
         live = live_rows(own, cells, cell)
-        msg = 0.125 * dot3(split(total), split(w_msg[...]))
+        msg = 0.125 * dot3(split(total), (parts[0][...], parts[1][...]))
         out[...] = own[:slots] + jnp.where(live, msg, 0.0)
         mask[...] = jnp.broadcast_to(jnp.where(live, 1.0, 0.0), mask.shape)
 
@@ -270,32 +273,28 @@
 
 
 def end_messages(cells, cell, cells_all, nb, last):
-    slots = cells * cell
-
-    def kernel(neighbours, nbr_count, base, own, edge, w_msg, out):
+    def kernel(neighbours, nbr_count, _, mask, cols, edge, wh, wl, out):
         x = lax.axis_index(X)
-        out[...] = base[...]
         for at, side in ((0, 0), (last, 2)):
 
             @pl.when(x == at)
             def _(side=side):
-                mine = own[slots : slots + 8].T
                 blocks = {side: edge[...]}
-                total = gather(neighbours, nbr_count, mine, blocks, (side,), cells, cell, cells_all, nb)
-                msg = 0.125 * dot3(split(total), split(w_msg[...]))
-                out[...] = base[...] + jnp.where(live_rows(own, cells, cell), msg, 0.0)
+                total = gather(neighbours, nbr_count, cols[...], blocks, (side,), cells, cell, cells_all, nb)
+                msg = 0.125 * dot3(split(total), (wh[...], wl[...]))
+                out[...] = out[...] + msg * mask[:, 0:1]
 
     return kernel
 
 
 def finish():
-    def kernel(base, mask, a, b, c, w_one, w_two, out):
+    def kernel(base, mask, a, b, c, oh, ol, th, tl, out):
         spectral = a[...] + (b[...] + c[...])
         u = base[...] + spectral.T
         normed = u / jnp.sqrt(jnp.mean(u * u, axis=1, keepdims=True) + 1e-06)
-        v = dot3(split(normed), split(w_one[...]))
+        v = dot3(split(normed), (oh[...], ol[...]))
         hidden = v / (1.0 + jnp.exp(-v))
-        out[...] = (u + dot3(split(hidden), split(w_two[...]))) * mask[:, 0:1]
+        out[...] = (u + dot3(split(hidden), (th[...], tl[...]))) * mask[:, 0:1]
 
     return kernel
 
@@ -390,14 +389,16 @@
     e2 = lax.ppermute(e2, X, shift(X, -1))
 
     sizes = cells, cell, cells * devices, neighbours.shape[1], nx - 1
-    base, mask = call(messages(*sizes), (floats(slots, width), floats(slots, 128)), 6, smem=(0, 1))(
-        neighbours, nbr_count, payload, below, above, w_msg
+    sizes = cells, cell, cells * devices, neighbours.shape[1], nx - 1
+    outs = floats(slots, width), floats(slots, 128), floats(slots, 8), *(halves(width, width),) * 6
+    base, mask, cols, *w = call(messages(*sizes), outs, 8, smem=(0, 1))(
+        neighbours, nbr_count, payload, below, above, w_msg, w_one, w_two
     )
-    base = call(end_messages(*sizes), floats(slots, width), 6, smem=(0, 1))(
-        neighbours, nbr_count, base, payload, edge, w_msg
+    base = call(end_messages(*sizes), floats(slots, width), 8, smem=(0, 1), alias={2: 0})(
+        neighbours, nbr_count, base, mask, cols, edge, *w[:2]
     )
     (e0,) = call(pairs, (one,), 2)(e0, e3)
-    return call(finish(), floats(slots, width), 7)(base, mask, e0, e1, e2, w_one, w_two)
+    return call(finish(), floats(slots, width), 9)(base, mask, e0, e1, e2, *w[2:])
 
 
 def solution(mesh):

time: 88.1 us -> 88 us (level)
  no operation moved by 1% of the time
where the time goes in v12:
time: 88 us; the launch traced here: 87.7 us
  blocking collectives  47.3 us (54%)
  starting transfers between devices  17.5 us (20%)
  Pallas kernels  15.5 us (18%)
  waiting for transfers between devices  5.48 us (6%)
  other arithmetic  1 us (1%)
    all_to_all x1, blocking collectives, shards(): lax.all_to_all(part.reshape(group, 2 * own_waves, width), (Z, Y), 0, 0, t...  17.1 us
    all_to_all x1, blocking collectives, shards(): lax.all_to_all(spread, (Z, Y), 0, 0, tiled=True).reshape(2 * waves, width)  16.1 us
    all_to_all x1, blocking collectives, shards(): kv = lax.all_to_all(kv, (Z, Y), 0, 0, tiled=True)  14.1 us
    pallas_call x3, Pallas kernels, sums(): call(forward(cells, cell, count, own_waves, group, first), (floats(2 * wa...  6.37 us
    ppermute x1, waiting for transfers between devices, shards(): edge = lax.ppermute(passed, ROWS_WAVES, ends)  5.38 us
    ppermute x3, starting transfers between devices, shards(): other = [lax.ppermute(c, 'rows', swap) for c in line]  2.9 us
    ppermute x1, starting transfers between devices, shards(): near2 = lax.ppermute(payload, X, shift(X, 2))  2.84 us
    ppermute x1, starting transfers between devices, shards(): e2 = lax.ppermute(e2, X, shift(X, -1))  2.8 us
  transfers between devices with their start and end apart: 13, of which 2 were waited for; matrix products, arithmetic and copies ran while one was open for 0% of the time, Pallas kernels for 12%

profile of v12, /device:TPU:1, one launch (start us, length us, event | category | flops | bytes accessed | tf_op | source)
XLA Modules:
  0.0 87.7 jit_solution(10085500803022087440)
XLA Ops:
  0.0 1.0 %pad_add_fusion._ = f32[264,256]{1,0:T(8,128)S(1)} fusion(f32[3,48]{1,0:T(4,128)} %param.16, f32[3,256]{1,0:T(4,128)} %param.12, f32[256,256]{1,0:T(8,128)} %param.11), kind=kLoop, calls=%fused_computation | loop fusion | flops 135168 | bytes 536128 | tf_op jit(solution)/shard_map/add | solution.py:327
  1.0 0.0 copy-start.6
  1.0 0.6 copy-done.6
  1.7 0.1 shard_map.110
  1.7 1.4 %collective-permute-start = (f32[264,256]{1,0:T(8,128)S(1)}, f32[264,256]{1,0:T(8,128)S(1)}, u32[]{:S(2)}, u32[]{:S(2)}) collective-permute-start(f32[264,256]{1,0:T(8,128)S(1)} %shard_map.109.own_block.chunk.refs_0_.own), channel_id=1, source_target_pairs={{0,64},{64,0},{1,65},{65,1},{2,66},{66,2},{3,67},{67,3},{4,68},{68... | collective-permute-start | bytes 811016 | tf_op jit(solution)/shard_map/ppermute | solution.py:335
  3.2 2.8 %collective-permute-start.1 = (f32[264,256]{1,0:T(8,128)S(1)}, f32[264,256]{1,0:T(8,128)S(1)}, u32[]{:S(2)}, u32[]{:S(2)}) collective-permute-start(f32[264,256]{1,0:T(8,128)S(1)} %shard_map.109.own_block.chunk.refs_0_.own), channel_id=1, source_target_pairs={{0,2},{1,3},{2,0},{3,1},{4,6},{5,7},{6,4},{7,5},{8,10},{9,11},{10,... | collective-permute-start | bytes 811016 | tf_op jit(solution)/shard_map/ppermute | solution.py:329
  6.0 0.9 collective-permute-start.2
  6.9 0.6 collective-permute-start.3
  7.5 14.1 %all_to_all.15.kv = f32[16,8,128]{2,1,0:T(8,128)S(1)} all-to-all(f32[16,8,128]{2,1,0:T(8,128)S(1)} %shard_map.110), channel_id=1, replica_groups=mesh['rows'=2,'waves_0'=4,'waves_1'=4,'waves_2'=4] {'waves_0','waves_1'}, dimensions={0} | all-to-all | bytes 131072 | tf_op jit(solution)/shard_map/all_to_all | solution.py:336
  21.6 0.2 shard_map.111.lhs
  21.8 0.5 shard_map.112
  22.4 1.4 %shard_map.113 = (f32[768,256]{1,0:T(8,128)S(1)}, bf16[1,768,256]{2,1,0:T(8,128)(2,1)S(1)}, bf16[1,768,256]{2,1,0:T(8,128)(2,1)S(1)}) custom-call(bf16[384,48]{1,0:T(8,128)(2,1)S(1)} %shard_map.111.lhs, f32[256,256]{1,0:T(8,128)S(1)} %copy-done.7, f32[264,256]{1,0:T(8,128)S(1)} %shard_map.109.own_block.chunk.refs_0_.own, ...), custom_call_target="tpu_custom_call" | custom-call | flops 603979776 | bytes 65536 | tf_op jit(solution)/shard_map/pallas_call | solution.py:344
  23.8 0.0 collective-permute-done.2.high.refs_0_.above
  23.8 0.0 collective-permute-done.3.low.refs_1_.below
  23.8 2.4 %collective-permute-start.4 = (f32[264,256]{1,0:T(8,128)S(1)}, f32[264,256]{1,0:T(8,128)S(1)}, u32[]{:S(2)}, u32[]{:S(2)}) collective-permute-start(f32[264,256]{1,0:T(8,128)S(1)} %collective-permute-done.2.high.refs_0_.above), channel_id=1, source_target_pairs={{0,64},{64,0},{1,65},{65,1},{2,66},{66,2},{3,67},{67,3},{4,68},{68... | collective-permute-start | bytes 811016 | tf_op jit(solution)/shard_map/ppermute | solution.py:355
  26.2 0.1 collective-permute-start.5
  26.3 0.4 collective-permute-start.6
  26.7 2.5 %shard_map.115 = (f32[768,256]{1,0:T(8,128)S(1)}, bf16[3,768,256]{2,1,0:T(8,128)(2,1)S(1)}, bf16[3,768,256]{2,1,0:T(8,128)(2,1)S(1)}) custom-call(bf16[384,48]{1,0:T(8,128)(2,1)S(1)} %shard_map.111.lhs, f32[256,256]{1,0:T(8,128)S(1)} %copy-done.7, f32[264,256]{1,0:T(8,128)S(1)} %collective-permute-done.2.high.refs_0_.above, ...), custom_call_target="tpu_custom_call" | custom-call | flops 905969664 | bytes 65536 | tf_op jit(solution)/shard_map/pallas_call | solution.py:344
  29.3 0.0 collective-permute-done.5.refs_1_
  29.3 0.0 collective-permute-done.6.refs_2_
  29.3 2.5 %shard_map.116 = (f32[768,256]{1,0:T(8,128)S(1)}, bf16[3,768,256]{2,1,0:T(8,128)(2,1)S(1)}, bf16[3,768,256]{2,1,0:T(8,128)(2,1)S(1)}) custom-call(bf16[384,48]{1,0:T(8,128)(2,1)S(1)} %shard_map.111.lhs, f32[256,256]{1,0:T(8,128)S(1)} %copy-done.7, f32[264,256]{1,0:T(8,128)S(1)} %collective-permute-done.4.refs_0_, ...), custom_call_target="tpu_custom_call" | custom-call | flops 905969664 | bytes 65536 | tf_op jit(solution)/shard_map/pallas_call | solution.py:344
  31.8 0.0 copy-start.3
  31.8 17.1 %all_to_all.16.parts = f32[16,48,256]{2,1,0:T(8,128)S(1)} all-to-all(f32[16,48,256]{2,1,0:T(8,128)S(1)} %bitcast.3), channel_id=1, replica_groups=mesh['rows'=2,'waves_0'=4,'waves_1'=4,'waves_2'=4] {'waves_0','waves_1'}, dimensions={0} | all-to-all | bytes 1572864 | tf_op jit(solution)/shard_map/all_to_all | solution.py:360
  48.9 0.1 shard_map.118
  49.0 16.1 %all_to_all.17 = f32[16,48,256]{2,1,0:T(8,128)S(1)} all-to-all(f32[16,48,256]{2,1,0:T(8,128)S(1)} %shard_map.118), channel_id=1, replica_groups=mesh['rows'=2,'waves_0'=4,'waves_1'=4,'waves_2'=4] {'waves_0','waves_1'}, dimensions={0} | all-to-all | bytes 1572864 | tf_op jit(solution)/shard_map/all_to_all | solution.py:363
  65.1 0.6 shard_map.119
  65.6 2.2 %collective-permute-start.7 = (f32[1,256,256]{2,1,0:T(8,128)S(1)}, f32[1,256,256]{2,1,0:T(8,128)S(1)}, u32[]{:S(2)}, u32[]{:S(2)}) collective-permute-start(f32[1,256,256]{2,1,0:T(8,128)S(1)} %get-tuple-element.65), channel_id=1, source_target_pairs={{0,64},{64,0},{1,65},{65,1},{2,66},{66,2},{3,67},{67,3},{4,68},{68... | collective-permute-start | bytes 786440 | tf_op jit(solution)/shard_map/ppermute | solution.py:377
  67.8 1.1 %shard_map.121 = f32[3,256,256]{2,1,0:T(8,128)S(1)} custom-call(bf16[256,768]{1,0:T(8,128)(2,1)S(1)} %get-tuple-element.76.fh, bf16[256,768]{1,0:T(8,128)(2,1)S(1)} %get-tuple-element.77.fl, bf16[1,768,256]{2,1,0:T(8,128)(2,1)S(1)} %get-tuple-element.71.mh0, bf16[1,768,256]{2,1,0:T(8,128)(2,1)S(1)} %get-tuple-element.72.ml0, ...), custom_call_target="tpu_custom_call" | custom-call | flops 905969664 | bytes 65536 | tf_op jit(solution)/shard_map/pallas_call | solution.py:371
  68.9 0.1 collective-permute-done.7.refs_0_
  69.0 0.5 shard_map.120
  69.5 0.0 copy-start
  69.5 0.0 copy-start.1
  69.5 0.0 copy-start.2
  69.5 0.0 copy-start.4
  69.5 0.0 copy-start.5
  69.5 0.5 collective-permute-start.9
  70.0 0.7 collective-permute-start.10
  70.7 2.2 %collective-permute-start.8 = (f32[264,256]{1,0:T(8,128)S(1)}, f32[264,256]{1,0:T(8,128)S(1)}, u32[]{:S(2)}, u32[]{:S(2)}) collective-permute-start(f32[264,256]{1,0:T(8,128)S(1)} %shard_map.117), channel_id=1, source_target_pairs={{0,4},{4,8},{8,12},{12,16},{16,20},{20,24},{24,28},{28,32},{32,36}... | collective-permute-start | bytes 811016 | tf_op jit(solution)/shard_map/ppermute | solution.py:386
  72.9 0.0 collective-permute-done.9.refs_0_
  72.9 1.1 %shard_map.123 = (f32[256,256]{1,0:T(8,128)S(1)}, f32[256,256]{1,0:T(8,128)S(1)}, f32[256,256]{1,0:T(8,128)S(1)}) custom-call(bf16[256,768]{1,0:T(8,128)(2,1)S(1)} %get-tuple-element.76.fh, bf16[256,768]{1,0:T(8,128)(2,1)S(1)} %get-tuple-element.77.fl, bf16[1,768,256]{2,1,0:T(8,128)(2,1)S(1)} %get-tuple-element.48.refs_2_.mh0, ...), custom_call_target="tpu_custom_call" | custom-call | flops 905969664 | bytes 65536 | tf_op jit(solution)/shard_map/pallas_call | solution.py:371
  74.0 0.5 collective-permute-start.11
  74.5 2.8 %collective-permute-start.12 = (f32[256,256]{1,0:T(8,128)S(1)}, f32[256,256]{1,0:T(8,128)S(1)}, u32[]{:S(2)}, u32[]{:S(2)}) collective-permute-start(f32[256,256]{1,0:T(8,128)S(1)} %get-tuple-element.82), channel_id=1, source_target_pairs={{0,3},{1,0},{2,1},{3,2},{4,7},{5,4},{6,5},{7,6},{8,11},{9,8},{10,9... | collective-permute-start | bytes 786440 | tf_op jit(solution)/shard_map/ppermute | solution.py:389
  77.3 2.0 %shard_map.114 = (f32[256,256]{1,0:T(8,128)S(1)}, f32[256,128]{1,0:T(8,128)S(1)}, f32[256,8]{1,0:T(8,128)S(1)}, bf16[256,256]{1,0:T(8,128)(2,1)S(1)}, bf16[256,2...) custom-call(s32[2,5]{1,0:T(2,128)S(1)} %copy-done.4, ...), custom_call_target="tpu_custom_call" | custom-call | bytes 65536 | tf_op jit(solution)/shard_map/pallas_call | solution.py:394
  79.4 5.4 %collective-permute-done.8.edge = f32[264,256]{1,0:T(8,128)S(1)} collective-permute-done((f32[264,256]{1,0:T(8,128)S(1)}, f32[264,256]{1,0:T(8,128)S(1)}, u32[]{:S(2)}, u32[]{:S(2)}) %collective-permute-start.8) | collective-permute-done | bytes 270368 | tf_op jit(solution)/shard_map/ppermute | solution.py:386
  84.7 1.3 %shard_map.122.base = f32[256,256]{1,0:T(8,128)S(1)} custom-call(s32[2,5]{1,0:T(2,128)S(1)} %copy-done.4, s32[2]{0:T(128)S(1)} %copy-done.5, f32[256,256]{1,0:T(8,128)S(1)} %get-tuple-element.53._, f32[256,128]{1,0:T(8,128)S(1)} %get-tuple-element.54.mask, f32[256,8]{1,0:T(8,128)S(1)} %get-tuple-element.55.cols, ...), custom_call_target="tpu_custom_call", output_to_operand_aliasing={{}: (2, {})} | custom-call | bytes 65536 | tf_op jit(solution)/shard_map/pallas_call | solution.py:397
  86.1 0.0 collective-permute-done.10.refs_1_
  86.1 0.0 collective-permute-done.11.b
  86.1 1.6 %shard_map.125 = f32[256,256]{1,0:T(8,128)} custom-call(f32[256,256]{1,0:T(8,128)S(1)} %shard_map.122.base, f32[256,128]{1,0:T(8,128)S(1)} %get-tuple-element.54.mask, f32[256,256]{1,0:T(8,128)S(1)} %shard_map.124.a, f32[256,256]{1,0:T(8,128)S(1)} %collective-permute-done.11.b, f32[256,256]{1,0:T(8,128)S(1)} %collective-permute-done.12.c, ...), custom_call_target="tpu_custom_call" | custom-call | bytes 65536 | tf_op jit(solution)/shard_map/pallas_call | solution.py:401
  (15 shorter events, 0.1 us)
Async XLA Ops:
  1.0 0.7 copy-start.6
  1.7 20.7 %copy-start.7 = (f32[256,256]{1,0:T(8,128)S(1)}, f32[256,256]{1,0:T(8,128)}, u32[]{:S(2)}) copy-start(f32[256,256]{1,0:T(8,128)} %w_val.5) | copy-start | bytes 786436
  1.7 20.6 %collective-permute-start = (f32[264,256]{1,0:T(8,128)S(1)}, f32[264,256]{1,0:T(8,128)S(1)}, u32[]{:S(2)}, u32[]{:S(2)}) collective-permute-start(f32[264,256]{1,0:T(8,128)S(1)} %shard_map.109.own_block.chunk.refs_0_.own), channel_id=1, source_target_pairs={{0,64},{64,0},{1,65},{65,1},{2,66},{66,2},{3,67},{67,3},{4,68},{68... | collective-permute-start | bytes 811016 | tf_op jit(solution)/shard_map/ppermute | solution.py:335
  3.2 20.6 %collective-permute-start.1 = (f32[264,256]{1,0:T(8,128)S(1)}, f32[264,256]{1,0:T(8,128)S(1)}, u32[]{:S(2)}, u32[]{:S(2)}) collective-permute-start(f32[264,256]{1,0:T(8,128)S(1)} %shard_map.109.own_block.chunk.refs_0_.own), channel_id=1, source_target_pairs={{0,2},{1,3},{2,0},{3,1},{4,6},{5,7},{6,4},{7,5},{8,10},{9,11},{10,... | collective-permute-start | bytes 811016 | tf_op jit(solution)/shard_map/ppermute | solution.py:329
  6.0 17.8 %collective-permute-start.2 = (f32[264,256]{1,0:T(8,128)S(1)}, f32[264,256]{1,0:T(8,128)S(1)}, u32[]{:S(2)}, u32[]{:S(2)}) collective-permute-start(f32[264,256]{1,0:T(8,128)S(1)} %shard_map.109.own_block.chunk.refs_0_.own), channel_id=1, source_target_pairs={{0,3},{1,0},{2,1},{3,2},{4,7},{5,4},{6,5},{7,6},{8,11},{9,8},{10,9... | collective-permute-start | bytes 811016 | tf_op jit(solution)/shard_map/ppermute | solution.py:330
  6.9 16.9 %collective-permute-start.3 = (f32[264,256]{1,0:T(8,128)S(1)}, f32[264,256]{1,0:T(8,128)S(1)}, u32[]{:S(2)}, u32[]{:S(2)}) collective-permute-start(f32[264,256]{1,0:T(8,128)S(1)} %shard_map.109.own_block.chunk.refs_0_.own), channel_id=1, source_target_pairs={{0,1},{1,2},{2,3},{3,0},{4,5},{5,6},{6,7},{7,4},{8,9},{9,10},{10,1... | collective-permute-start | bytes 811016 | tf_op jit(solution)/shard_map/ppermute | solution.py:331
  23.8 5.4 %collective-permute-start.4 = (f32[264,256]{1,0:T(8,128)S(1)}, f32[264,256]{1,0:T(8,128)S(1)}, u32[]{:S(2)}, u32[]{:S(2)}) collective-permute-start(f32[264,256]{1,0:T(8,128)S(1)} %collective-permute-done.2.high.refs_0_.above), channel_id=1, source_target_pairs={{0,64},{64,0},{1,65},{65,1},{2,66},{66,2},{3,67},{67,3},{4,68},{68... | collective-permute-start | bytes 811016 | tf_op jit(solution)/shard_map/ppermute | solution.py:355
  26.2 3.1 %collective-permute-start.5 = (f32[264,256]{1,0:T(8,128)S(1)}, f32[264,256]{1,0:T(8,128)S(1)}, u32[]{:S(2)}, u32[]{:S(2)}) collective-permute-start(f32[264,256]{1,0:T(8,128)S(1)} %collective-permute-done.3.low.refs_1_.below), channel_id=1, source_target_pairs={{0,64},{64,0},{1,65},{65,1},{2,66},{66,2},{3,67},{67,3},{4,68},{68... | collective-permute-start | bytes 811016 | tf_op jit(solution)/shard_map/ppermute | solution.py:355
  26.3 3.0 %collective-permute-start.6 = (f32[264,256]{1,0:T(8,128)S(1)}, f32[264,256]{1,0:T(8,128)S(1)}, u32[]{:S(2)}, u32[]{:S(2)}) collective-permute-start(f32[264,256]{1,0:T(8,128)S(1)} %collective-permute-done.1.refs_2_), channel_id=1, source_target_pairs={{0,64},{64,0},{1,65},{65,1},{2,66},{66,2},{3,67},{67,3},{4,68},{68... | collective-permute-start | bytes 811016 | tf_op jit(solution)/shard_map/ppermute | solution.py:355
  31.8 17.1 %copy-start.3 = (f32[48,256]{1,0:T(8,128)S(1)}, f32[48,256]{1,0:T(8,128)}, u32[]{:S(2)}) copy-start(f32[48,256]{1,0:T(8,128)} %filters.1) | copy-start | bytes 147460
  65.6 3.3 %collective-permute-start.7 = (f32[1,256,256]{2,1,0:T(8,128)S(1)}, f32[1,256,256]{2,1,0:T(8,128)S(1)}, u32[]{:S(2)}, u32[]{:S(2)}) collective-permute-start(f32[1,256,256]{2,1,0:T(8,128)S(1)} %get-tuple-element.65), channel_id=1, source_target_pairs={{0,64},{64,0},{1,65},{65,1},{2,66},{66,2},{3,67},{67,3},{4,68},{68... | collective-permute-start | bytes 786440 | tf_op jit(solution)/shard_map/ppermute | solution.py:377
  69.5 7.8 %copy-start = (f32[256,256]{1,0:T(8,128)S(1)}, f32[256,256]{1,0:T(8,128)}, u32[]{:S(2)}) copy-start(f32[256,256]{1,0:T(8,128)} %w_msg.1) | copy-start | bytes 786436
  69.5 7.8 %copy-start.1 = (f32[256,256]{1,0:T(8,128)S(1)}, f32[256,256]{1,0:T(8,128)}, u32[]{:S(2)}) copy-start(f32[256,256]{1,0:T(8,128)} %w_one.1) | copy-start | bytes 786436
  69.5 7.8 %copy-start.2 = (f32[256,256]{1,0:T(8,128)S(1)}, f32[256,256]{1,0:T(8,128)}, u32[]{:S(2)}) copy-start(f32[256,256]{1,0:T(8,128)} %w_two.1) | copy-start | bytes 786436
  69.5 7.8 %copy-start.4 = (s32[2,5]{1,0:T(2,128)S(1)}, s32[2,5]{1,0:T(2,128)}, u32[]{:S(2)}) copy-start(s32[2,5]{1,0:T(2,128)} %neighbours.3) | copy-start | bytes 124
  69.5 7.8 %copy-start.5 = (s32[2]{0:T(128)S(1)}, s32[2]{0:T(128)}, u32[]{:S(2)}) copy-start(s32[2]{0:T(128)} %nbr_count.3) | copy-start | bytes 28
  69.5 3.4 %collective-permute-start.9 = (f32[3,256,256]{2,1,0:T(8,128)S(1)}, f32[3,256,256]{2,1,0:T(8,128)S(1)}, u32[]{:S(2)}, u32[]{:S(2)}) collective-permute-start(f32[3,256,256]{2,1,0:T(8,128)S(1)} %shard_map.121), channel_id=1, source_target_pairs={{0,64},{64,0},{1,65},{65,1},{2,66},{66,2},{3,67},{67,3},{4,68},{68... | collective-permute-start | bytes 2359304 | tf_op jit(solution)/shard_map/ppermute | solution.py:382
  70.0 16.1 %collective-permute-start.10 = (f32[256,256]{1,0:T(8,128)S(1)}, f32[256,256]{1,0:T(8,128)S(1)}, u32[]{:S(2)}, u32[]{:S(2)}) collective-permute-start(f32[256,256]{1,0:T(8,128)S(1)} %shard_map.120), channel_id=1, source_target_pairs={{0,2},{1,3},{2,0},{3,1},{4,6},{5,7},{6,4},{7,5},{8,10},{9,11},{10,... | collective-permute-start | bytes 786440 | tf_op jit(solution)/shard_map/ppermute | solution.py:383
  70.7 14.0 %collective-permute-start.8 = (f32[264,256]{1,0:T(8,128)S(1)}, f32[264,256]{1,0:T(8,128)S(1)}, u32[]{:S(2)}, u32[]{:S(2)}) collective-permute-start(f32[264,256]{1,0:T(8,128)S(1)} %shard_map.117), channel_id=1, source_target_pairs={{0,4},{4,8},{8,12},{12,16},{16,20},{20,24},{24,28},{28,32},{32,36}... | collective-permute-start | bytes 811016 | tf_op jit(solution)/shard_map/ppermute | solution.py:386
  74.0 12.1 %collective-permute-start.11 = (f32[256,256]{1,0:T(8,128)S(1)}, f32[256,256]{1,0:T(8,128)S(1)}, u32[]{:S(2)}, u32[]{:S(2)}) collective-permute-start(f32[256,256]{1,0:T(8,128)S(1)} %get-tuple-element.81), channel_id=1, source_target_pairs={{0,1},{1,2},{2,3},{3,0},{4,5},{5,6},{6,7},{7,4},{8,9},{9,10},{10,1... | collective-permute-start | bytes 786440 | tf_op jit(solution)/shard_map/ppermute | solution.py:388
  74.5 11.6 %collective-permute-start.12 = (f32[256,256]{1,0:T(8,128)S(1)}, f32[256,256]{1,0:T(8,128)S(1)}, u32[]{:S(2)}, u32[]{:S(2)}) collective-permute-start(f32[256,256]{1,0:T(8,128)S(1)} %get-tuple-element.82), channel_id=1, source_target_pairs={{0,3},{1,0},{2,1},{3,2},{4,7},{5,4},{6,5},{7,6},{8,11},{9,8},{10,9... | collective-permute-start | bytes 786440 | tf_op jit(solution)/shard_map/ppermute | solution.py:389

commit v13 on v12

--- a/solution.py
+++ b/solution.py
@@ -218,9 +218,8 @@
     return listed
 
 
-def gather(neighbours, nbr_count, mine, blocks, use, cells, cell, cells_all, nb):
+def gather(factor, mine, blocks, use, cells, cell):
     slots = cells * cell
-    first = lax.axis_index(ROWS_WAVES) * cells
     wide, pos = {}, {}
     for k in use:
         live = live_rows(blocks[k], cells, cell)
@@ -237,13 +236,12 @@
             other = c + step
             if other not in wide:
                 continue
-            target = lax.rem(first + other - cells + cells_all, cells_all)
             near = pos[other]
             d0 = here[:, 0:1] - near[0:1]
             d1 = here[:, 1:2] - near[1:2]
             d2 = here[:, 2:3] - near[2:3]
             weight = jnp.exp(-0.125 * (d0 * d0 + d1 * d1 + d2 * d2))
-            weight = weight * listed_factor(neighbours, nbr_count, c, target, nb)
+            weight = weight * factor(c, other)
             if step == cells:
                 weight = jnp.where(eye, 0.0, weight)
             acc = acc + dot3(split(weight), wide[other])
@@ -254,7 +252,7 @@
 def messages(cells, cell, cells_all, nb, last):
     slots = cells * cell
 
-    def kernel(neighbours, nbr_count, own, low, high, w_msg, w_one, w_two, out, mask, cols, *parts):
+    def kernel(neighbours, nbr_count, own, low, high, w_msg, w_one, w_two, out, mask, cols, factors, *parts):
         x = lax.axis_index(X)
         lo = jnp.where(x == 0, 0.0, low[...])
         hi = jnp.where(x == last, 0.0, high[...])
@@ -263,7 +261,16 @@
         cols[...] = mine
         for k, w in enumerate((w_msg, w_one, w_two)):
             parts[2 * k][...], parts[2 * k + 1][...] = split(w[...])
-        total = gather(neighbours, nbr_count, mine, blocks, (0, 1, 2), cells, cell, cells_all, nb)
+        first = lax.axis_index(ROWS_WAVES) * cells
+
+        def factor(c, other):
+            target = lax.rem(first + other - cells + cells_all, cells_all)
+            listed = listed_factor(neighbours, nbr_count, c, target, nb)
+            row = 3 * cells * c + other
+            factors[row : row + 1] = jnp.full((1, 128), listed)
+            return listed
+
+        total = gather(factor, mine, blocks, (0, 1, 2), cells, cell)
         live = live_rows(own, cells, cell)
         msg = 0.125 * dot3(split(total), (parts[0][...], parts[1][...]))
         out[...] = own[:slots] + jnp.where(live, msg, 0.0)
@@ -272,15 +279,20 @@
     return kernel
 
 
-def end_messages(cells, cell, cells_all, nb, last):
-    def kernel(neighbours, nbr_count, _, mask, cols, edge, wh, wl, out):
+def end_messages(cells, cell, last):
+    def kernel(_, mask, cols, factors, edge, wh, wl, out):
         x = lax.axis_index(X)
         for at, side in ((0, 0), (last, 2)):
 
             @pl.when(x == at)
             def _(side=side):
                 blocks = {side: edge[...]}
-                total = gather(neighbours, nbr_count, cols[...], blocks, (side,), cells, cell, cells_all, nb)
+
+                def factor(c, other):
+                    row = 3 * cells * c + other
+                    return factors[row : row + 1, 0:1]
+
+                total = gather(factor, cols[...], blocks, (side,), cells, cell)
                 msg = 0.125 * dot3(split(total), (wh[...], wl[...]))
                 out[...] = out[...] + msg * mask[:, 0:1]
 
@@ -390,15 +402,16 @@
 
     sizes = cells, cell, cells * devices, neighbours.shape[1], nx - 1
     sizes = cells, cell, cells * devices, neighbours.shape[1], nx - 1
-    outs = floats(slots, width), floats(slots, 128), floats(slots, 8), *(halves(width, width),) * 6
-    base, mask, cols, *w = call(messages(*sizes), outs, 8, smem=(0, 1))(
+    small = floats(slots, 128), floats(slots, 8), floats(16, 128)
+    outs = floats(slots, width), *small, *(halves(width, width),) * 6
+    base, mask, cols, factors, w0, w1, *w = call(messages(*sizes), outs, 8, smem=(0, 1))(
         neighbours, nbr_count, payload, below, above, w_msg, w_one, w_two
     )
-    base = call(end_messages(*sizes), floats(slots, width), 8, smem=(0, 1), alias={2: 0})(
-        neighbours, nbr_count, base, mask, cols, edge, *w[:2]
+    base = call(end_messages(cells, cell, nx - 1), floats(slots, width), 7, alias={0: 0})(
+        base, mask, cols, factors, edge, w0, w1
     )
     (e0,) = call(pairs, (one,), 2)(e0, e3)
-    return call(finish(), floats(slots, width), 9)(base, mask, e0, e1, e2, *w[2:])
+    return call(finish(), floats(slots, width), 9)(base, mask, e0, e1, e2, *w)
 
 
 def solution(mesh):

time: 88 us -> 87.4 us (level)
  transfers between devices with their start and end apart: 13 -> 13, of which waited for: 2 -> 2; matrix products, arithmetic and copies ran while one was open for 0% -> 0% of each run, Pallas kernels for 12% -> 11%
where the time goes in v13:
time: 87.4 us; the launch traced here: 87.1 us
  blocking collectives  47.3 us (54%)
  starting transfers between devices  17.5 us (20%)
  Pallas kernels  14.9 us (17%)
  waiting for transfers between devices  5.48 us (6%)
  other arithmetic  1 us (1%)
    all_to_all x1, blocking collectives, shards(): lax.all_to_all(part.reshape(group, 2 * own_waves, width), (Z, Y), 0, 0, t...  17.1 us
    all_to_all x1, blocking collectives, shards(): lax.all_to_all(spread, (Z, Y), 0, 0, tiled=True).reshape(2 * waves, width)  16.1 us
    all_to_all x1, blocking collectives, shards(): kv = lax.all_to_all(kv, (Z, Y), 0, 0, tiled=True)  14.1 us
    pallas_call x3, Pallas kernels, sums(): call(forward(cells, cell, count, own_waves, group, first), (floats(2 * wa...  6.37 us
    ppermute x1, waiting for transfers between devices, shards(): edge = lax.ppermute(passed, ROWS_WAVES, ends)  5.38 us
    ppermute x3, starting transfers between devices, shards(): other = [lax.ppermute(c, 'rows', swap) for c in line]  2.9 us
    ppermute x1, starting transfers between devices, shards(): near2 = lax.ppermute(payload, X, shift(X, 2))  2.84 us
    ppermute x1, starting transfers between devices, shards(): e2 = lax.ppermute(e2, X, shift(X, -1))  2.8 us
  transfers between devices with their start and end apart: 13, of which 2 were waited for; matrix products, arithmetic and copies ran while one was open for 0% of the time, Pallas kernels for 11%

profile of v13, /device:TPU:1, one launch (start us, length us, event | category | flops | bytes accessed | tf_op | source)
XLA Modules:
  0.0 87.1 jit_solution(5129779861955804783)
XLA Ops:
  0.0 1.0 %pad_add_fusion._ = f32[264,256]{1,0:T(8,128)S(1)} fusion(f32[3,48]{1,0:T(4,128)} %param.16, f32[3,256]{1,0:T(4,128)} %param.12, f32[256,256]{1,0:T(8,128)} %param.11), kind=kLoop, calls=%fused_computation | loop fusion | flops 135168 | bytes 536128 | tf_op jit(solution)/shard_map/add | solution.py:339
  1.0 0.0 copy-start.6
  1.0 0.6 copy-done.6
  1.7 0.1 shard_map.110
  1.7 1.4 %collective-permute-start = (f32[264,256]{1,0:T(8,128)S(1)}, f32[264,256]{1,0:T(8,128)S(1)}, u32[]{:S(2)}, u32[]{:S(2)}) collective-permute-start(f32[264,256]{1,0:T(8,128)S(1)} %shard_map.109.own_block.chunk.refs_0_.own), channel_id=1, source_target_pairs={{0,64},{64,0},{1,65},{65,1},{2,66},{66,2},{3,67},{67,3},{4,68},{68... | collective-permute-start | bytes 811016 | tf_op jit(solution)/shard_map/ppermute | solution.py:347
  3.2 2.8 %collective-permute-start.1 = (f32[264,256]{1,0:T(8,128)S(1)}, f32[264,256]{1,0:T(8,128)S(1)}, u32[]{:S(2)}, u32[]{:S(2)}) collective-permute-start(f32[264,256]{1,0:T(8,128)S(1)} %shard_map.109.own_block.chunk.refs_0_.own), channel_id=1, source_target_pairs={{0,2},{1,3},{2,0},{3,1},{4,6},{5,7},{6,4},{7,5},{8,10},{9,11},{10,... | collective-permute-start | bytes 811016 | tf_op jit(solution)/shard_map/ppermute | solution.py:341
  6.0 0.9 collective-permute-start.2
  6.9 0.6 collective-permute-start.3
  7.5 14.1 %all_to_all.15.kv = f32[16,8,128]{2,1,0:T(8,128)S(1)} all-to-all(f32[16,8,128]{2,1,0:T(8,128)S(1)} %shard_map.110), channel_id=1, replica_groups=mesh['rows'=2,'waves_0'=4,'waves_1'=4,'waves_2'=4] {'waves_0','waves_1'}, dimensions={0} | all-to-all | bytes 131072 | tf_op jit(solution)/shard_map/all_to_all | solution.py:348
  21.6 0.2 shard_map.111.lhs
  21.8 0.5 shard_map.112
  22.4 1.4 %shard_map.113 = (f32[768,256]{1,0:T(8,128)S(1)}, bf16[1,768,256]{2,1,0:T(8,128)(2,1)S(1)}, bf16[1,768,256]{2,1,0:T(8,128)(2,1)S(1)}) custom-call(bf16[384,48]{1,0:T(8,128)(2,1)S(1)} %shard_map.111.lhs, f32[256,256]{1,0:T(8,128)S(1)} %copy-done.7, f32[264,256]{1,0:T(8,128)S(1)} %shard_map.109.own_block.chunk.refs_0_.own, ...), custom_call_target="tpu_custom_call" | custom-call | flops 603979776 | bytes 65536 | tf_op jit(solution)/shard_map/pallas_call | solution.py:356
  23.8 0.0 collective-permute-done.1.refs_2_
  23.8 0.0 collective-permute-done.2.high.refs_0_.above
  23.8 2.4 %collective-permute-start.4 = (f32[264,256]{1,0:T(8,128)S(1)}, f32[264,256]{1,0:T(8,128)S(1)}, u32[]{:S(2)}, u32[]{:S(2)}) collective-permute-start(f32[264,256]{1,0:T(8,128)S(1)} %collective-permute-done.2.high.refs_0_.above), channel_id=1, source_target_pairs={{0,64},{64,0},{1,65},{65,1},{2,66},{66,2},{3,67},{67,3},{4,68},{68... | collective-permute-start | bytes 811016 | tf_op jit(solution)/shard_map/ppermute | solution.py:367
  26.2 0.1 collective-permute-start.5
  26.3 0.4 collective-permute-start.6
  26.7 2.5 %shard_map.115 = (f32[768,256]{1,0:T(8,128)S(1)}, bf16[3,768,256]{2,1,0:T(8,128)(2,1)S(1)}, bf16[3,768,256]{2,1,0:T(8,128)(2,1)S(1)}) custom-call(bf16[384,48]{1,0:T(8,128)(2,1)S(1)} %shard_map.111.lhs, f32[256,256]{1,0:T(8,128)S(1)} %copy-done.7, f32[264,256]{1,0:T(8,128)S(1)} %collective-permute-done.2.high.refs_0_.above, ...), custom_call_target="tpu_custom_call" | custom-call | flops 905969664 | bytes 65536 | tf_op jit(solution)/shard_map/pallas_call | solution.py:356
  29.2 0.0 collective-permute-done.4.refs_0_
  29.3 0.0 collective-permute-done.5.refs_1_
  29.3 2.5 %shard_map.116 = (f32[768,256]{1,0:T(8,128)S(1)}, bf16[3,768,256]{2,1,0:T(8,128)(2,1)S(1)}, bf16[3,768,256]{2,1,0:T(8,128)(2,1)S(1)}) custom-call(bf16[384,48]{1,0:T(8,128)(2,1)S(1)} %shard_map.111.lhs, f32[256,256]{1,0:T(8,128)S(1)} %copy-done.7, f32[264,256]{1,0:T(8,128)S(1)} %collective-permute-done.4.refs_0_, ...), custom_call_target="tpu_custom_call" | custom-call | flops 905969664 | bytes 65536 | tf_op jit(solution)/shard_map/pallas_call | solution.py:356
  31.8 0.0 copy-start.3
  31.8 17.1 %all_to_all.16.parts = f32[16,48,256]{2,1,0:T(8,128)S(1)} all-to-all(f32[16,48,256]{2,1,0:T(8,128)S(1)} %bitcast.3), channel_id=1, replica_groups=mesh['rows'=2,'waves_0'=4,'waves_1'=4,'waves_2'=4] {'waves_0','waves_1'}, dimensions={0} | all-to-all | bytes 1572864 | tf_op jit(solution)/shard_map/all_to_all | solution.py:372
  48.9 0.1 shard_map.118
  49.0 16.1 %all_to_all.17 = f32[16,48,256]{2,1,0:T(8,128)S(1)} all-to-all(f32[16,48,256]{2,1,0:T(8,128)S(1)} %shard_map.118), channel_id=1, replica_groups=mesh['rows'=2,'waves_0'=4,'waves_1'=4,'waves_2'=4] {'waves_0','waves_1'}, dimensions={0} | all-to-all | bytes 1572864 | tf_op jit(solution)/shard_map/all_to_all | solution.py:375
  65.1 0.6 shard_map.119
  65.6 2.2 %collective-permute-start.7 = (f32[1,256,256]{2,1,0:T(8,128)S(1)}, f32[1,256,256]{2,1,0:T(8,128)S(1)}, u32[]{:S(2)}, u32[]{:S(2)}) collective-permute-start(f32[1,256,256]{2,1,0:T(8,128)S(1)} %get-tuple-element.67), channel_id=1, source_target_pairs={{0,64},{64,0},{1,65},{65,1},{2,66},{66,2},{3,67},{67,3},{4,68},{68... | collective-permute-start | bytes 786440 | tf_op jit(solution)/shard_map/ppermute | solution.py:389
  67.8 1.1 %shard_map.121 = f32[3,256,256]{2,1,0:T(8,128)S(1)} custom-call(bf16[256,768]{1,0:T(8,128)(2,1)S(1)} %get-tuple-element.78.fh, bf16[256,768]{1,0:T(8,128)(2,1)S(1)} %get-tuple-element.79.fl, bf16[1,768,256]{2,1,0:T(8,128)(2,1)S(1)} %get-tuple-element.73.mh0, bf16[1,768,256]{2,1,0:T(8,128)(2,1)S(1)} %get-tuple-element.74.ml0, ...), custom_call_target="tpu_custom_call" | custom-call | flops 905969664 | bytes 65536 | tf_op jit(solution)/shard_map/pallas_call | solution.py:383
  68.9 0.1 collective-permute-done.7.refs_0_
  69.0 0.5 shard_map.120
  69.5 0.0 copy-start
  69.5 0.0 copy-start.1
  69.5 0.0 copy-start.2
  69.5 0.0 copy-start.4
  69.5 0.0 copy-start.5
  69.5 0.5 collective-permute-start.9
  70.0 0.7 collective-permute-start.10
  70.7 2.2 %collective-permute-start.8 = (f32[264,256]{1,0:T(8,128)S(1)}, f32[264,256]{1,0:T(8,128)S(1)}, u32[]{:S(2)}, u32[]{:S(2)}) collective-permute-start(f32[264,256]{1,0:T(8,128)S(1)} %shard_map.117), channel_id=1, source_target_pairs={{0,4},{4,8},{8,12},{12,16},{16,20},{20,24},{24,28},{28,32},{32,36}... | collective-permute-start | bytes 811016 | tf_op jit(solution)/shard_map/ppermute | solution.py:398
  72.9 0.0 collective-permute-done.9.refs_0_
  72.9 1.1 %shard_map.123 = (f32[256,256]{1,0:T(8,128)S(1)}, f32[256,256]{1,0:T(8,128)S(1)}, f32[256,256]{1,0:T(8,128)S(1)}) custom-call(bf16[256,768]{1,0:T(8,128)(2,1)S(1)} %get-tuple-element.78.fh, bf16[256,768]{1,0:T(8,128)(2,1)S(1)} %get-tuple-element.79.fl, bf16[1,768,256]{2,1,0:T(8,128)(2,1)S(1)} %get-tuple-element.49.refs_2_.mh0, ...), custom_call_target="tpu_custom_call" | custom-call | flops 905969664 | bytes 65536 | tf_op jit(solution)/shard_map/pallas_call | solution.py:383
  74.0 0.5 collective-permute-start.11
  74.5 2.8 %collective-permute-start.12 = (f32[256,256]{1,0:T(8,128)S(1)}, f32[256,256]{1,0:T(8,128)S(1)}, u32[]{:S(2)}, u32[]{:S(2)}) collective-permute-start(f32[256,256]{1,0:T(8,128)S(1)} %get-tuple-element.84), channel_id=1, source_target_pairs={{0,3},{1,0},{2,1},{3,2},{4,7},{5,4},{6,5},{7,6},{8,11},{9,8},{10,9... | collective-permute-start | bytes 786440 | tf_op jit(solution)/shard_map/ppermute | solution.py:401
  77.3 2.0 %shard_map.114 = (f32[256,256]{1,0:T(8,128)S(1)}, f32[256,128]{1,0:T(8,128)S(1)}, f32[256,8]{1,0:T(8,128)S(1)}, f32[16,128]{1,0:T(8,128)S(1)}, bf16[256,256]{1,0...) custom-call(s32[2,5]{1,0:T(2,128)S(1)} %copy-done.4, ...), custom_call_target="tpu_custom_call" | custom-call | bytes 65536 | tf_op jit(solution)/shard_map/pallas_call | solution.py:407
  79.3 5.4 %collective-permute-done.8.edge = f32[264,256]{1,0:T(8,128)S(1)} collective-permute-done((f32[264,256]{1,0:T(8,128)S(1)}, f32[264,256]{1,0:T(8,128)S(1)}, u32[]{:S(2)}, u32[]{:S(2)}) %collective-permute-start.8) | collective-permute-done | bytes 270368 | tf_op jit(solution)/shard_map/ppermute | solution.py:398
  84.7 0.8 shard_map.122.base
  85.5 0.0 collective-permute-done.10.refs_1_
  85.6 0.0 collective-permute-done.11.b
  85.6 1.6 %shard_map.125 = f32[256,256]{1,0:T(8,128)} custom-call(f32[256,256]{1,0:T(8,128)S(1)} %shard_map.122.base, f32[256,128]{1,0:T(8,128)S(1)} %get-tuple-element.55.mask, f32[256,256]{1,0:T(8,128)S(1)} %shard_map.124.a, f32[256,256]{1,0:T(8,128)S(1)} %collective-permute-done.11.b, f32[256,256]{1,0:T(8,128)S(1)} %collective-permute-done.12.c, ...), custom_call_target="tpu_custom_call" | custom-call | bytes 65536 | tf_op jit(solution)/shard_map/pallas_call | solution.py:414
  (15 shorter events, 0.1 us)
Async XLA Ops:
  1.0 0.7 copy-start.6
  1.7 20.7 %copy-start.7 = (f32[256,256]{1,0:T(8,128)S(1)}, f32[256,256]{1,0:T(8,128)}, u32[]{:S(2)}) copy-start(f32[256,256]{1,0:T(8,128)} %w_val.5) | copy-start | bytes 786436
  1.7 20.6 %collective-permute-start = (f32[264,256]{1,0:T(8,128)S(1)}, f32[264,256]{1,0:T(8,128)S(1)}, u32[]{:S(2)}, u32[]{:S(2)}) collective-permute-start(f32[264,256]{1,0:T(8,128)S(1)} %shard_map.109.own_block.chunk.refs_0_.own), channel_id=1, source_target_pairs={{0,64},{64,0},{1,65},{65,1},{2,66},{66,2},{3,67},{67,3},{4,68},{68... | collective-permute-start | bytes 811016 | tf_op jit(solution)/shard_map/ppermute | solution.py:347
  3.2 20.6 %collective-permute-start.1 = (f32[264,256]{1,0:T(8,128)S(1)}, f32[264,256]{1,0:T(8,128)S(1)}, u32[]{:S(2)}, u32[]{:S(2)}) collective-permute-start(f32[264,256]{1,0:T(8,128)S(1)} %shard_map.109.own_block.chunk.refs_0_.own), channel_id=1, source_target_pairs={{0,2},{1,3},{2,0},{3,1},{4,6},{5,7},{6,4},{7,5},{8,10},{9,11},{10,... | collective-permute-start | bytes 811016 | tf_op jit(solution)/shard_map/ppermute | solution.py:341
  6.0 17.8 %collective-permute-start.2 = (f32[264,256]{1,0:T(8,128)S(1)}, f32[264,256]{1,0:T(8,128)S(1)}, u32[]{:S(2)}, u32[]{:S(2)}) collective-permute-start(f32[264,256]{1,0:T(8,128)S(1)} %shard_map.109.own_block.chunk.refs_0_.own), channel_id=1, source_target_pairs={{0,3},{1,0},{2,1},{3,2},{4,7},{5,4},{6,5},{7,6},{8,11},{9,8},{10,9... | collective-permute-start | bytes 811016 | tf_op jit(solution)/shard_map/ppermute | solution.py:342
  6.9 16.9 %collective-permute-start.3 = (f32[264,256]{1,0:T(8,128)S(1)}, f32[264,256]{1,0:T(8,128)S(1)}, u32[]{:S(2)}, u32[]{:S(2)}) collective-permute-start(f32[264,256]{1,0:T(8,128)S(1)} %shard_map.109.own_block.chunk.refs_0_.own), channel_id=1, source_target_pairs={{0,1},{1,2},{2,3},{3,0},{4,5},{5,6},{6,7},{7,4},{8,9},{9,10},{10,1... | collective-permute-start | bytes 811016 | tf_op jit(solution)/shard_map/ppermute | solution.py:343
  23.8 5.4 %collective-permute-start.4 = (f32[264,256]{1,0:T(8,128)S(1)}, f32[264,256]{1,0:T(8,128)S(1)}, u32[]{:S(2)}, u32[]{:S(2)}) collective-permute-start(f32[264,256]{1,0:T(8,128)S(1)} %collective-permute-done.2.high.refs_0_.above), channel_id=1, source_target_pairs={{0,64},{64,0},{1,65},{65,1},{2,66},{66,2},{3,67},{67,3},{4,68},{68... | collective-permute-start | bytes 811016 | tf_op jit(solution)/shard_map/ppermute | solution.py:367
  26.2 3.1 %collective-permute-start.5 = (f32[264,256]{1,0:T(8,128)S(1)}, f32[264,256]{1,0:T(8,128)S(1)}, u32[]{:S(2)}, u32[]{:S(2)}) collective-permute-start(f32[264,256]{1,0:T(8,128)S(1)} %collective-permute-done.3.low.refs_1_.below), channel_id=1, source_target_pairs={{0,64},{64,0},{1,65},{65,1},{2,66},{66,2},{3,67},{67,3},{4,68},{68... | collective-permute-start | bytes 811016 | tf_op jit(solution)/shard_map/ppermute | solution.py:367
  26.3 3.0 %collective-permute-start.6 = (f32[264,256]{1,0:T(8,128)S(1)}, f32[264,256]{1,0:T(8,128)S(1)}, u32[]{:S(2)}, u32[]{:S(2)}) collective-permute-start(f32[264,256]{1,0:T(8,128)S(1)} %collective-permute-done.1.refs_2_), channel_id=1, source_target_pairs={{0,64},{64,0},{1,65},{65,1},{2,66},{66,2},{3,67},{67,3},{4,68},{68... | collective-permute-start | bytes 811016 | tf_op jit(solution)/shard_map/ppermute | solution.py:367
  31.8 17.1 %copy-start.3 = (f32[48,256]{1,0:T(8,128)S(1)}, f32[48,256]{1,0:T(8,128)}, u32[]{:S(2)}) copy-start(f32[48,256]{1,0:T(8,128)} %filters.1) | copy-start | bytes 147460
  65.6 3.3 %collective-permute-start.7 = (f32[1,256,256]{2,1,0:T(8,128)S(1)}, f32[1,256,256]{2,1,0:T(8,128)S(1)}, u32[]{:S(2)}, u32[]{:S(2)}) collective-permute-start(f32[1,256,256]{2,1,0:T(8,128)S(1)} %get-tuple-element.67), channel_id=1, source_target_pairs={{0,64},{64,0},{1,65},{65,1},{2,66},{66,2},{3,67},{67,3},{4,68},{68... | collective-permute-start | bytes 786440 | tf_op jit(solution)/shard_map/ppermute | solution.py:389
  69.5 7.8 %copy-start = (f32[256,256]{1,0:T(8,128)S(1)}, f32[256,256]{1,0:T(8,128)}, u32[]{:S(2)}) copy-start(f32[256,256]{1,0:T(8,128)} %w_msg.1) | copy-start | bytes 786436
  69.5 7.8 %copy-start.1 = (f32[256,256]{1,0:T(8,128)S(1)}, f32[256,256]{1,0:T(8,128)}, u32[]{:S(2)}) copy-start(f32[256,256]{1,0:T(8,128)} %w_one.1) | copy-start | bytes 786436
  69.5 7.8 %copy-start.2 = (f32[256,256]{1,0:T(8,128)S(1)}, f32[256,256]{1,0:T(8,128)}, u32[]{:S(2)}) copy-start(f32[256,256]{1,0:T(8,128)} %w_two.1) | copy-start | bytes 786436
  69.5 7.8 %copy-start.4 = (s32[2,5]{1,0:T(2,128)S(1)}, s32[2,5]{1,0:T(2,128)}, u32[]{:S(2)}) copy-start(s32[2,5]{1,0:T(2,128)} %neighbours.1) | copy-start | bytes 124
  69.5 7.8 %copy-start.5 = (s32[2]{0:T(128)S(1)}, s32[2]{0:T(128)}, u32[]{:S(2)}) copy-start(s32[2]{0:T(128)} %nbr_count.1) | copy-start | bytes 28
  69.5 3.4 %collective-permute-start.9 = (f32[3,256,256]{2,1,0:T(8,128)S(1)}, f32[3,256,256]{2,1,0:T(8,128)S(1)}, u32[]{:S(2)}, u32[]{:S(2)}) collective-permute-start(f32[3,256,256]{2,1,0:T(8,128)S(1)} %shard_map.121), channel_id=1, source_target_pairs={{0,64},{64,0},{1,65},{65,1},{2,66},{66,2},{3,67},{67,3},{4,68},{68... | collective-permute-start | bytes 2359304 | tf_op jit(solution)/shard_map/ppermute | solution.py:394
  70.0 15.5 %collective-permute-start.10 = (f32[256,256]{1,0:T(8,128)S(1)}, f32[256,256]{1,0:T(8,128)S(1)}, u32[]{:S(2)}, u32[]{:S(2)}) collective-permute-start(f32[256,256]{1,0:T(8,128)S(1)} %shard_map.120), channel_id=1, source_target_pairs={{0,2},{1,3},{2,0},{3,1},{4,6},{5,7},{6,4},{7,5},{8,10},{9,11},{10,... | collective-permute-start | bytes 786440 | tf_op jit(solution)/shard_map/ppermute | solution.py:395
  70.7 14.0 %collective-permute-start.8 = (f32[264,256]{1,0:T(8,128)S(1)}, f32[264,256]{1,0:T(8,128)S(1)}, u32[]{:S(2)}, u32[]{:S(2)}) collective-permute-start(f32[264,256]{1,0:T(8,128)S(1)} %shard_map.117), channel_id=1, source_target_pairs={{0,4},{4,8},{8,12},{12,16},{16,20},{20,24},{24,28},{28,32},{32,36}... | collective-permute-start | bytes 811016 | tf_op jit(solution)/shard_map/ppermute | solution.py:398
  74.0 11.5 %collective-permute-start.11 = (f32[256,256]{1,0:T(8,128)S(1)}, f32[256,256]{1,0:T(8,128)S(1)}, u32[]{:S(2)}, u32[]{:S(2)}) collective-permute-start(f32[256,256]{1,0:T(8,128)S(1)} %get-tuple-element.83), channel_id=1, source_target_pairs={{0,1},{1,2},{2,3},{3,0},{4,5},{5,6},{6,7},{7,4},{8,9},{9,10},{10,1... | collective-permute-start | bytes 786440 | tf_op jit(solution)/shard_map/ppermute | solution.py:400
  74.5 11.1 %collective-permute-start.12 = (f32[256,256]{1,0:T(8,128)S(1)}, f32[256,256]{1,0:T(8,128)S(1)}, u32[]{:S(2)}, u32[]{:S(2)}) collective-permute-start(f32[256,256]{1,0:T(8,128)S(1)} %get-tuple-element.84), channel_id=1, source_target_pairs={{0,3},{1,0},{2,1},{3,2},{4,7},{5,4},{6,5},{7,6},{8,11},{9,8},{10,9... | collective-permute-start | bytes 786440 | tf_op jit(solution)/shard_map/ppermute | solution.py:401

commit v14 on v13

--- a/solution.py
+++ b/solution.py
@@ -146,13 +146,13 @@
             right += [vh, vh, vl]
             turns.append(dot(lhs[...], spots(chunk, slots)) if j >= skip else None)
         right = jnp.concatenate(right, axis=0)
-        for part in range(2):
+        for begin, stop in ((0, 10), (10, groups)):
             for j in range(skip, count):
-                for g in range(part * groups // 2, (part + 1) * groups // 2):
+                for g in range(begin, stop):
                     rows = slice(2 * own * g, 2 * own * (g + 1))
                     pieces = split(cos_and_sin(turns[j][g * own : (g + 1) * own]))
                     mh[j - skip, rows], ml[j - skip, rows] = pieces
-            rows = slice(part * own * groups, (part + 1) * own * groups)
+            rows = slice(2 * own * begin, 2 * own * stop)
             pairs_of = [(ready[0][0, rows], ready[1][0, rows])] if first else []
             pairs_of += [(mh[j, rows], ml[j, rows]) for j in range(count - skip)]
             left = [m for high, low in pairs_of for m in (high, low, high)]
@@ -337,11 +337,12 @@
 
     payload = jnp.pad(feats, ((0, 8), (0, 0))) + jnp.pad(positions, ((slots, 5), (0, 0)))
     payload = payload + jnp.pad(kvec, ((slots + 4, 1), (0, width - kvec.shape[1])))
+    kv = call(pack(slots, own_waves, group), floats(group, 8, 128), 1)(payload)
+    kv, payload = lax.optimization_barrier((kv, payload))
     payload = call(stamp(slots, cells), floats(*payload.shape), 2, alias={1: 0})(cell_counts, payload)
     near2 = lax.ppermute(payload, X, shift(X, 2))
     above = lax.ppermute(payload, X, shift(X, -1))
     below = lax.ppermute(payload, X, shift(X, 1))
-    kv = call(pack(slots, own_waves, group), floats(group, 8, 128), 1)(payload)
     kv, again = lax.optimization_barrier((kv, payload))
     swap = shift("rows", 1)
     beside = lax.ppermute(again, "rows", swap)

time: 87.4 us -> 87.6 us (level)
  no operation moved by 1% of the time
where the time goes in v14:
time: 87.6 us; the launch traced here: 87.3 us
  blocking collectives  47.2 us (54%)
  starting transfers between devices  17.4 us (20%)
  Pallas kernels  15.1 us (17%)
  waiting for transfers between devices  5.57 us (6%)
  other arithmetic  1 us (1%)
    all_to_all x1, blocking collectives, shards(): lax.all_to_all(part.reshape(group, 2 * own_waves, width), (Z, Y), 0, 0, t...  17.1 us
    all_to_all x1, blocking collectives, shards(): lax.all_to_all(spread, (Z, Y), 0, 0, tiled=True).reshape(2 * waves, width)  16.1 us
    all_to_all x1, blocking collectives, shards(): kv = lax.all_to_all(kv, (Z, Y), 0, 0, tiled=True)  14.1 us
    pallas_call x3, Pallas kernels, sums(): call(forward(cells, cell, count, own_waves, group, first), (floats(2 * wa...  6.55 us
    ppermute x1, waiting for transfers between devices, shards(): edge = lax.ppermute(passed, ROWS_WAVES, ends)  5.47 us
    ppermute x3, starting transfers between devices, shards(): other = [lax.ppermute(c, 'rows', swap) for c in line]  2.86 us
    ppermute x1, starting transfers between devices, shards(): near2 = lax.ppermute(payload, X, shift(X, 2))  2.83 us
    ppermute x1, starting transfers between devices, shards(): e2 = lax.ppermute(e2, X, shift(X, -1))  2.81 us
  transfers between devices with their start and end apart: 13, of which 2 were waited for; matrix products, arithmetic and copies ran while one was open for 0% of the time, Pallas kernels for 11%

profile of v14, /device:TPU:1, one launch (start us, length us, event | category | flops | bytes accessed | tf_op | source)
XLA Modules:
  0.0 87.3 jit_solution(5884406808290123849)
XLA Ops:
  0.0 1.0 %pad_add_fusion.own_block._ = f32[264,256]{1,0:T(8,128)S(1)} fusion(f32[3,48]{1,0:T(4,128)} %param.16, f32[3,256]{1,0:T(4,128)} %param.12, f32[256,256]{1,0:T(8,128)} %param.11), kind=kLoop, calls=%fused_computation | loop fusion | flops 135168 | bytes 536128 | tf_op jit(solution)/shard_map/add | solution.py:339
  1.0 0.0 copy-start.7
  1.0 0.1 shard_map.109
  1.1 0.7 copy-done.6
  1.8 1.4 %collective-permute-start = (f32[264,256]{1,0:T(8,128)S(1)}, f32[264,256]{1,0:T(8,128)S(1)}, u32[]{:S(2)}, u32[]{:S(2)}) collective-permute-start(f32[264,256]{1,0:T(8,128)S(1)} %shard_map.110.chunk.refs_0_.own), channel_id=1, source_target_pairs={{0,64},{64,0},{1,65},{65,1},{2,66},{66,2},{3,67},{67,3},{4,68},{68... | collective-permute-start | bytes 811016 | tf_op jit(solution)/shard_map/ppermute | solution.py:348
  3.2 2.8 %collective-permute-start.1 = (f32[264,256]{1,0:T(8,128)S(1)}, f32[264,256]{1,0:T(8,128)S(1)}, u32[]{:S(2)}, u32[]{:S(2)}) collective-permute-start(f32[264,256]{1,0:T(8,128)S(1)} %shard_map.110.chunk.refs_0_.own), channel_id=1, source_target_pairs={{0,2},{1,3},{2,0},{3,1},{4,6},{5,7},{6,4},{7,5},{8,10},{9,11},{10,... | collective-permute-start | bytes 811016 | tf_op jit(solution)/shard_map/ppermute | solution.py:343
  6.0 0.9 collective-permute-start.2
  6.9 0.6 collective-permute-start.3
  7.5 14.1 %all_to_all.15.kv = f32[16,8,128]{2,1,0:T(8,128)S(1)} all-to-all(f32[16,8,128]{2,1,0:T(8,128)S(1)} %shard_map.109), channel_id=1, replica_groups=mesh['rows'=2,'waves_0'=4,'waves_1'=4,'waves_2'=4] {'waves_0','waves_1'}, dimensions={0} | all-to-all | bytes 131072 | tf_op jit(solution)/shard_map/all_to_all | solution.py:349
  21.5 0.2 shard_map.111.lhs
  21.8 0.5 shard_map.112
  22.3 1.4 %shard_map.113 = (f32[768,256]{1,0:T(8,128)S(1)}, bf16[1,768,256]{2,1,0:T(8,128)(2,1)S(1)}, bf16[1,768,256]{2,1,0:T(8,128)(2,1)S(1)}) custom-call(bf16[384,48]{1,0:T(8,128)(2,1)S(1)} %shard_map.111.lhs, f32[256,256]{1,0:T(8,128)S(1)} %copy-done.7, f32[264,256]{1,0:T(8,128)S(1)} %shard_map.110.chunk.refs_0_.own, f32[264,256]{1,0:T(8,128)S(1)} %collective-permute-done.refs_1_, ...), custom_call_target="tpu_custom_call" | custom-call | flops 603979776 | bytes 65536 | tf_op jit(solution)/shard_map/pallas_call | solution.py:357
  23.7 0.0 collective-permute-done.2.high.refs_0_.above
  23.7 0.0 collective-permute-done.3.low.refs_1_.below
  23.7 2.4 %collective-permute-start.4 = (f32[264,256]{1,0:T(8,128)S(1)}, f32[264,256]{1,0:T(8,128)S(1)}, u32[]{:S(2)}, u32[]{:S(2)}) collective-permute-start(f32[264,256]{1,0:T(8,128)S(1)} %collective-permute-done.2.high.refs_0_.above), channel_id=1, source_target_pairs={{0,64},{64,0},{1,65},{65,1},{2,66},{66,2},{3,67},{67,3},{4,68},{68... | collective-permute-start | bytes 811016 | tf_op jit(solution)/shard_map/ppermute | solution.py:368
  26.1 0.1 collective-permute-start.5
  26.2 0.4 collective-permute-start.6
  26.6 2.6 %shard_map.115 = (f32[768,256]{1,0:T(8,128)S(1)}, bf16[3,768,256]{2,1,0:T(8,128)(2,1)S(1)}, bf16[3,768,256]{2,1,0:T(8,128)(2,1)S(1)}) custom-call(bf16[384,48]{1,0:T(8,128)(2,1)S(1)} %shard_map.111.lhs, f32[256,256]{1,0:T(8,128)S(1)} %copy-done.7, f32[264,256]{1,0:T(8,128)S(1)} %collective-permute-done.2.high.refs_0_.above, ...), custom_call_target="tpu_custom_call" | custom-call | flops 905969664 | bytes 65536 | tf_op jit(solution)/shard_map/pallas_call | solution.py:357
  29.2 0.0 collective-permute-done.4.refs_0_
  29.2 0.0 collective-permute-done.5.refs_1_
  29.3 2.6 %shard_map.116 = (f32[768,256]{1,0:T(8,128)S(1)}, bf16[3,768,256]{2,1,0:T(8,128)(2,1)S(1)}, bf16[3,768,256]{2,1,0:T(8,128)(2,1)S(1)}) custom-call(bf16[384,48]{1,0:T(8,128)(2,1)S(1)} %shard_map.111.lhs, f32[256,256]{1,0:T(8,128)S(1)} %copy-done.7, f32[264,256]{1,0:T(8,128)S(1)} %collective-permute-done.4.refs_0_, ...), custom_call_target="tpu_custom_call" | custom-call | flops 905969664 | bytes 65536 | tf_op jit(solution)/shard_map/pallas_call | solution.py:357
  31.9 0.0 copy-start.3
  31.9 17.1 %all_to_all.16.parts = f32[16,48,256]{2,1,0:T(8,128)S(1)} all-to-all(f32[16,48,256]{2,1,0:T(8,128)S(1)} %bitcast.3), channel_id=1, replica_groups=mesh['rows'=2,'waves_0'=4,'waves_1'=4,'waves_2'=4] {'waves_0','waves_1'}, dimensions={0} | all-to-all | bytes 1572864 | tf_op jit(solution)/shard_map/all_to_all | solution.py:373
  49.0 0.1 shard_map.118
  49.1 16.1 %all_to_all.17 = f32[16,48,256]{2,1,0:T(8,128)S(1)} all-to-all(f32[16,48,256]{2,1,0:T(8,128)S(1)} %shard_map.118), channel_id=1, replica_groups=mesh['rows'=2,'waves_0'=4,'waves_1'=4,'waves_2'=4] {'waves_0','waves_1'}, dimensions={0} | all-to-all | bytes 1572864 | tf_op jit(solution)/shard_map/all_to_all | solution.py:376
  65.1 0.6 shard_map.119
  65.7 2.2 %collective-permute-start.7 = (f32[1,256,256]{2,1,0:T(8,128)S(1)}, f32[1,256,256]{2,1,0:T(8,128)S(1)}, u32[]{:S(2)}, u32[]{:S(2)}) collective-permute-start(f32[1,256,256]{2,1,0:T(8,128)S(1)} %get-tuple-element.71), channel_id=1, source_target_pairs={{0,64},{64,0},{1,65},{65,1},{2,66},{66,2},{3,67},{67,3},{4,68},{68... | collective-permute-start | bytes 786440 | tf_op jit(solution)/shard_map/ppermute | solution.py:390
  67.9 1.1 %shard_map.121 = f32[3,256,256]{2,1,0:T(8,128)S(1)} custom-call(bf16[256,768]{1,0:T(8,128)(2,1)S(1)} %get-tuple-element.82.fh, bf16[256,768]{1,0:T(8,128)(2,1)S(1)} %get-tuple-element.83.fl, bf16[1,768,256]{2,1,0:T(8,128)(2,1)S(1)} %get-tuple-element.77.mh0, bf16[1,768,256]{2,1,0:T(8,128)(2,1)S(1)} %get-tuple-element.78.ml0, ...), custom_call_target="tpu_custom_call" | custom-call | flops 905969664 | bytes 65536 | tf_op jit(solution)/shard_map/pallas_call | solution.py:384
  69.0 0.1 collective-permute-done.7.refs_0_
  69.1 0.5 shard_map.120
  69.6 0.0 copy-start
  69.6 0.0 copy-start.1
  69.6 0.0 copy-start.2
  69.6 0.0 copy-start.4
  69.6 0.0 copy-start.5
  69.6 0.5 collective-permute-start.9
  70.1 0.8 collective-permute-start.10
  70.9 2.2 %collective-permute-start.8 = (f32[264,256]{1,0:T(8,128)S(1)}, f32[264,256]{1,0:T(8,128)S(1)}, u32[]{:S(2)}, u32[]{:S(2)}) collective-permute-start(f32[264,256]{1,0:T(8,128)S(1)} %shard_map.117), channel_id=1, source_target_pairs={{0,4},{4,8},{8,12},{12,16},{16,20},{20,24},{24,28},{28,32},{32,36}... | collective-permute-start | bytes 811016 | tf_op jit(solution)/shard_map/ppermute | solution.py:399
  73.1 0.0 collective-permute-done.9.refs_0_
  73.1 1.1 %shard_map.123 = (f32[256,256]{1,0:T(8,128)S(1)}, f32[256,256]{1,0:T(8,128)S(1)}, f32[256,256]{1,0:T(8,128)S(1)}) custom-call(bf16[256,768]{1,0:T(8,128)(2,1)S(1)} %get-tuple-element.82.fh, bf16[256,768]{1,0:T(8,128)(2,1)S(1)} %get-tuple-element.83.fl, bf16[1,768,256]{2,1,0:T(8,128)(2,1)S(1)} %get-tuple-element.53.refs_2_.mh0, ...), custom_call_target="tpu_custom_call" | custom-call | flops 905969664 | bytes 65536 | tf_op jit(solution)/shard_map/pallas_call | solution.py:384
  74.2 0.4 collective-permute-start.11
  74.6 2.8 %collective-permute-start.12 = (f32[256,256]{1,0:T(8,128)S(1)}, f32[256,256]{1,0:T(8,128)S(1)}, u32[]{:S(2)}, u32[]{:S(2)}) collective-permute-start(f32[256,256]{1,0:T(8,128)S(1)} %get-tuple-element.88), channel_id=1, source_target_pairs={{0,3},{1,0},{2,1},{3,2},{4,7},{5,4},{6,5},{7,6},{8,11},{9,8},{10,9... | collective-permute-start | bytes 786440 | tf_op jit(solution)/shard_map/ppermute | solution.py:402
  77.4 2.0 %shard_map.114 = (f32[256,256]{1,0:T(8,128)S(1)}, f32[256,128]{1,0:T(8,128)S(1)}, f32[256,8]{1,0:T(8,128)S(1)}, f32[16,128]{1,0:T(8,128)S(1)}, bf16[256,256]{1,0...) custom-call(s32[2,5]{1,0:T(2,128)S(1)} %copy-done.4, ...), custom_call_target="tpu_custom_call" | custom-call | bytes 65536 | tf_op jit(solution)/shard_map/pallas_call | solution.py:408
  79.4 5.5 %collective-permute-done.8.edge = f32[264,256]{1,0:T(8,128)S(1)} collective-permute-done((f32[264,256]{1,0:T(8,128)S(1)}, f32[264,256]{1,0:T(8,128)S(1)}, u32[]{:S(2)}, u32[]{:S(2)}) %collective-permute-start.8) | collective-permute-done | bytes 270368 | tf_op jit(solution)/shard_map/ppermute | solution.py:399
  84.9 0.8 shard_map.122.base
  85.7 0.0 collective-permute-done.10.refs_1_
  85.7 0.0 collective-permute-done.11.b
  85.7 1.6 %shard_map.125 = f32[256,256]{1,0:T(8,128)} custom-call(f32[256,256]{1,0:T(8,128)S(1)} %shard_map.122.base, f32[256,128]{1,0:T(8,128)S(1)} %get-tuple-element.59.mask, f32[256,256]{1,0:T(8,128)S(1)} %shard_map.124.a, f32[256,256]{1,0:T(8,128)S(1)} %collective-permute-done.11.b, f32[256,256]{1,0:T(8,128)S(1)} %collective-permute-done.12.c, ...), custom_call_target="tpu_custom_call" | custom-call | bytes 65536 | tf_op jit(solution)/shard_map/pallas_call | solution.py:415
  (15 shorter events, 0.1 us)
Async XLA Ops:
  1.0 21.3 %copy-start.7 = (f32[256,256]{1,0:T(8,128)S(1)}, f32[256,256]{1,0:T(8,128)}, u32[]{:S(2)}) copy-start(f32[256,256]{1,0:T(8,128)} %w_val.5) | copy-start | bytes 786436
  1.1 0.7 copy-start.6
  1.8 20.6 %collective-permute-start = (f32[264,256]{1,0:T(8,128)S(1)}, f32[264,256]{1,0:T(8,128)S(1)}, u32[]{:S(2)}, u32[]{:S(2)}) collective-permute-start(f32[264,256]{1,0:T(8,128)S(1)} %shard_map.110.chunk.refs_0_.own), channel_id=1, source_target_pairs={{0,64},{64,0},{1,65},{65,1},{2,66},{66,2},{3,67},{67,3},{4,68},{68... | collective-permute-start | bytes 811016 | tf_op jit(solution)/shard_map/ppermute | solution.py:348
  3.2 20.5 %collective-permute-start.1 = (f32[264,256]{1,0:T(8,128)S(1)}, f32[264,256]{1,0:T(8,128)S(1)}, u32[]{:S(2)}, u32[]{:S(2)}) collective-permute-start(f32[264,256]{1,0:T(8,128)S(1)} %shard_map.110.chunk.refs_0_.own), channel_id=1, source_target_pairs={{0,2},{1,3},{2,0},{3,1},{4,6},{5,7},{6,4},{7,5},{8,10},{9,11},{10,... | collective-permute-start | bytes 811016 | tf_op jit(solution)/shard_map/ppermute | solution.py:343
  6.0 17.7 %collective-permute-start.2 = (f32[264,256]{1,0:T(8,128)S(1)}, f32[264,256]{1,0:T(8,128)S(1)}, u32[]{:S(2)}, u32[]{:S(2)}) collective-permute-start(f32[264,256]{1,0:T(8,128)S(1)} %shard_map.110.chunk.refs_0_.own), channel_id=1, source_target_pairs={{0,3},{1,0},{2,1},{3,2},{4,7},{5,4},{6,5},{7,6},{8,11},{9,8},{10,9... | collective-permute-start | bytes 811016 | tf_op jit(solution)/shard_map/ppermute | solution.py:344
  6.9 16.9 %collective-permute-start.3 = (f32[264,256]{1,0:T(8,128)S(1)}, f32[264,256]{1,0:T(8,128)S(1)}, u32[]{:S(2)}, u32[]{:S(2)}) collective-permute-start(f32[264,256]{1,0:T(8,128)S(1)} %shard_map.110.chunk.refs_0_.own), channel_id=1, source_target_pairs={{0,1},{1,2},{2,3},{3,0},{4,5},{5,6},{6,7},{7,4},{8,9},{9,10},{10,1... | collective-permute-start | bytes 811016 | tf_op jit(solution)/shard_map/ppermute | solution.py:345
  23.7 5.5 %collective-permute-start.4 = (f32[264,256]{1,0:T(8,128)S(1)}, f32[264,256]{1,0:T(8,128)S(1)}, u32[]{:S(2)}, u32[]{:S(2)}) collective-permute-start(f32[264,256]{1,0:T(8,128)S(1)} %collective-permute-done.2.high.refs_0_.above), channel_id=1, source_target_pairs={{0,64},{64,0},{1,65},{65,1},{2,66},{66,2},{3,67},{67,3},{4,68},{68... | collective-permute-start | bytes 811016 | tf_op jit(solution)/shard_map/ppermute | solution.py:368
  26.1 3.2 %collective-permute-start.5 = (f32[264,256]{1,0:T(8,128)S(1)}, f32[264,256]{1,0:T(8,128)S(1)}, u32[]{:S(2)}, u32[]{:S(2)}) collective-permute-start(f32[264,256]{1,0:T(8,128)S(1)} %collective-permute-done.3.low.refs_1_.below), channel_id=1, source_target_pairs={{0,64},{64,0},{1,65},{65,1},{2,66},{66,2},{3,67},{67,3},{4,68},{68... | collective-permute-start | bytes 811016 | tf_op jit(solution)/shard_map/ppermute | solution.py:368
  26.2 3.1 %collective-permute-start.6 = (f32[264,256]{1,0:T(8,128)S(1)}, f32[264,256]{1,0:T(8,128)S(1)}, u32[]{:S(2)}, u32[]{:S(2)}) collective-permute-start(f32[264,256]{1,0:T(8,128)S(1)} %collective-permute-done.1.refs_2_), channel_id=1, source_target_pairs={{0,64},{64,0},{1,65},{65,1},{2,66},{66,2},{3,67},{67,3},{4,68},{68... | collective-permute-start | bytes 811016 | tf_op jit(solution)/shard_map/ppermute | solution.py:368
  31.9 17.1 %copy-start.3 = (f32[48,256]{1,0:T(8,128)S(1)}, f32[48,256]{1,0:T(8,128)}, u32[]{:S(2)}) copy-start(f32[48,256]{1,0:T(8,128)} %filters.1) | copy-start | bytes 147460
  65.7 3.3 %collective-permute-start.7 = (f32[1,256,256]{2,1,0:T(8,128)S(1)}, f32[1,256,256]{2,1,0:T(8,128)S(1)}, u32[]{:S(2)}, u32[]{:S(2)}) collective-permute-start(f32[1,256,256]{2,1,0:T(8,128)S(1)} %get-tuple-element.71), channel_id=1, source_target_pairs={{0,64},{64,0},{1,65},{65,1},{2,66},{66,2},{3,67},{67,3},{4,68},{68... | collective-permute-start | bytes 786440 | tf_op jit(solution)/shard_map/ppermute | solution.py:390
  69.6 7.8 %copy-start = (f32[256,256]{1,0:T(8,128)S(1)}, f32[256,256]{1,0:T(8,128)}, u32[]{:S(2)}) copy-start(f32[256,256]{1,0:T(8,128)} %w_msg.1) | copy-start | bytes 786436
  69.6 7.8 %copy-start.1 = (f32[256,256]{1,0:T(8,128)S(1)}, f32[256,256]{1,0:T(8,128)}, u32[]{:S(2)}) copy-start(f32[256,256]{1,0:T(8,128)} %w_one.1) | copy-start | bytes 786436
  69.6 7.8 %copy-start.2 = (f32[256,256]{1,0:T(8,128)S(1)}, f32[256,256]{1,0:T(8,128)}, u32[]{:S(2)}) copy-start(f32[256,256]{1,0:T(8,128)} %w_two.1) | copy-start | bytes 786436
  69.6 7.8 %copy-start.4 = (s32[2,5]{1,0:T(2,128)S(1)}, s32[2,5]{1,0:T(2,128)}, u32[]{:S(2)}) copy-start(s32[2,5]{1,0:T(2,128)} %neighbours.1) | copy-start | bytes 124
  69.6 7.8 %copy-start.5 = (s32[2]{0:T(128)S(1)}, s32[2]{0:T(128)}, u32[]{:S(2)}) copy-start(s32[2]{0:T(128)} %nbr_count.1) | copy-start | bytes 28
  69.6 3.5 %collective-permute-start.9 = (f32[3,256,256]{2,1,0:T(8,128)S(1)}, f32[3,256,256]{2,1,0:T(8,128)S(1)}, u32[]{:S(2)}, u32[]{:S(2)}) collective-permute-start(f32[3,256,256]{2,1,0:T(8,128)S(1)} %shard_map.121), channel_id=1, source_target_pairs={{0,64},{64,0},{1,65},{65,1},{2,66},{66,2},{3,67},{67,3},{4,68},{68... | collective-permute-start | bytes 2359304 | tf_op jit(solution)/shard_map/ppermute | solution.py:395
  70.1 15.6 %collective-permute-start.10 = (f32[256,256]{1,0:T(8,128)S(1)}, f32[256,256]{1,0:T(8,128)S(1)}, u32[]{:S(2)}, u32[]{:S(2)}) collective-permute-start(f32[256,256]{1,0:T(8,128)S(1)} %shard_map.120), channel_id=1, source_target_pairs={{0,2},{1,3},{2,0},{3,1},{4,6},{5,7},{6,4},{7,5},{8,10},{9,11},{10,... | collective-permute-start | bytes 786440 | tf_op jit(solution)/shard_map/ppermute | solution.py:396
  70.9 14.0 %collective-permute-start.8 = (f32[264,256]{1,0:T(8,128)S(1)}, f32[264,256]{1,0:T(8,128)S(1)}, u32[]{:S(2)}, u32[]{:S(2)}) collective-permute-start(f32[264,256]{1,0:T(8,128)S(1)} %shard_map.117), channel_id=1, source_target_pairs={{0,4},{4,8},{8,12},{12,16},{16,20},{20,24},{24,28},{28,32},{32,36}... | collective-permute-start | bytes 811016 | tf_op jit(solution)/shard_map/ppermute | solution.py:399
  74.2 11.5 %collective-permute-start.11 = (f32[256,256]{1,0:T(8,128)S(1)}, f32[256,256]{1,0:T(8,128)S(1)}, u32[]{:S(2)}, u32[]{:S(2)}) collective-permute-start(f32[256,256]{1,0:T(8,128)S(1)} %get-tuple-element.87), channel_id=1, source_target_pairs={{0,1},{1,2},{2,3},{3,0},{4,5},{5,6},{6,7},{7,4},{8,9},{9,10},{10,1... | collective-permute-start | bytes 786440 | tf_op jit(solution)/shard_map/ppermute | solution.py:401
  74.6 11.2 %collective-permute-start.12 = (f32[256,256]{1,0:T(8,128)S(1)}, f32[256,256]{1,0:T(8,128)S(1)}, u32[]{:S(2)}, u32[]{:S(2)}) collective-permute-start(f32[256,256]{1,0:T(8,128)S(1)} %get-tuple-element.88), channel_id=1, source_target_pairs={{0,3},{1,0},{2,1},{3,2},{4,7},{5,4},{6,5},{7,6},{8,11},{9,8},{10,9... | collective-permute-start | bytes 786440 | tf_op jit(solution)/shard_map/ppermute | solution.py:402

commit v15 on v14

--- a/solution.py
+++ b/solution.py
@@ -146,7 +146,7 @@
             right += [vh, vh, vl]
             turns.append(dot(lhs[...], spots(chunk, slots)) if j >= skip else None)
         right = jnp.concatenate(right, axis=0)
-        for begin, stop in ((0, 10), (10, groups)):
+        for begin, stop in ((0, groups // 2), (groups // 2, groups)):
             for j in range(skip, count):
                 for g in range(begin, stop):
                     rows = slice(2 * own * g, 2 * own * (g + 1))

time: 87.6 us -> 87.4 us (level)
  no operation moved by 1% of the time
where the time goes in v15:
time: 87.4 us; the launch traced here: 87.1 us
  blocking collectives  47.2 us (54%)
  starting transfers between devices  17.4 us (20%)
  Pallas kernels  14.9 us (17%)
  waiting for transfers between devices  5.56 us (6%)
  other arithmetic  1 us (1%)
    all_to_all x1, blocking collectives, shards(): lax.all_to_all(part.reshape(group, 2 * own_waves, width), (Z, Y), 0, 0, t...  17.1 us
    all_to_all x1, blocking collectives, shards(): lax.all_to_all(spread, (Z, Y), 0, 0, tiled=True).reshape(2 * waves, width)  16.1 us
    all_to_all x1, blocking collectives, shards(): kv = lax.all_to_all(kv, (Z, Y), 0, 0, tiled=True)  14.1 us
    pallas_call x3, Pallas kernels, sums(): call(forward(cells, cell, count, own_waves, group, first), (floats(2 * wa...  6.37 us
    ppermute x1, waiting for transfers between devices, shards(): edge = lax.ppermute(passed, ROWS_WAVES, ends)  5.46 us
    ppermute x3, starting transfers between devices, shards(): other = [lax.ppermute(c, 'rows', swap) for c in line]  2.85 us
    ppermute x1, starting transfers between devices, shards(): near2 = lax.ppermute(payload, X, shift(X, 2))  2.83 us
    ppermute x1, starting transfers between devices, shards(): e2 = lax.ppermute(e2, X, shift(X, -1))  2.8 us
  transfers between devices with their start and end apart: 13, of which 2 were waited for; matrix products, arithmetic and copies ran while one was open for 0% of the time, Pallas kernels for 11%

profile of v15, /device:TPU:1, one launch (start us, length us, event | category | flops | bytes accessed | tf_op | source)
XLA Modules:
  0.0 87.1 jit_solution(11277345708115577302)
XLA Ops:
  0.0 1.0 %pad_add_fusion.own_block._ = f32[264,256]{1,0:T(8,128)S(1)} fusion(f32[3,48]{1,0:T(4,128)} %param.16, f32[3,256]{1,0:T(4,128)} %param.12, f32[256,256]{1,0:T(8,128)} %param.11), kind=kLoop, calls=%fused_computation | loop fusion | flops 135168 | bytes 536128 | tf_op jit(solution)/shard_map/add | solution.py:339
  1.0 0.0 copy-start.7
  1.0 0.1 shard_map.109
  1.1 0.7 copy-done.6
  1.8 1.4 %collective-permute-start = (f32[264,256]{1,0:T(8,128)S(1)}, f32[264,256]{1,0:T(8,128)S(1)}, u32[]{:S(2)}, u32[]{:S(2)}) collective-permute-start(f32[264,256]{1,0:T(8,128)S(1)} %shard_map.110.chunk.refs_0_.own), channel_id=1, source_target_pairs={{0,64},{64,0},{1,65},{65,1},{2,66},{66,2},{3,67},{67,3},{4,68},{68... | collective-permute-start | bytes 811016 | tf_op jit(solution)/shard_map/ppermute | solution.py:348
  3.2 2.8 %collective-permute-start.1 = (f32[264,256]{1,0:T(8,128)S(1)}, f32[264,256]{1,0:T(8,128)S(1)}, u32[]{:S(2)}, u32[]{:S(2)}) collective-permute-start(f32[264,256]{1,0:T(8,128)S(1)} %shard_map.110.chunk.refs_0_.own), channel_id=1, source_target_pairs={{0,2},{1,3},{2,0},{3,1},{4,6},{5,7},{6,4},{7,5},{8,10},{9,11},{10,... | collective-permute-start | bytes 811016 | tf_op jit(solution)/shard_map/ppermute | solution.py:343
  6.0 0.9 collective-permute-start.2
  6.9 0.6 collective-permute-start.3
  7.5 14.1 %all_to_all.15.kv = f32[16,8,128]{2,1,0:T(8,128)S(1)} all-to-all(f32[16,8,128]{2,1,0:T(8,128)S(1)} %shard_map.109), channel_id=1, replica_groups=mesh['rows'=2,'waves_0'=4,'waves_1'=4,'waves_2'=4] {'waves_0','waves_1'}, dimensions={0} | all-to-all | bytes 131072 | tf_op jit(solution)/shard_map/all_to_all | solution.py:349
  21.5 0.2 shard_map.111.lhs
  21.8 0.5 shard_map.112
  22.3 1.4 %shard_map.113 = (f32[768,256]{1,0:T(8,128)S(1)}, bf16[1,768,256]{2,1,0:T(8,128)(2,1)S(1)}, bf16[1,768,256]{2,1,0:T(8,128)(2,1)S(1)}) custom-call(bf16[384,48]{1,0:T(8,128)(2,1)S(1)} %shard_map.111.lhs, f32[256,256]{1,0:T(8,128)S(1)} %copy-done.7, f32[264,256]{1,0:T(8,128)S(1)} %shard_map.110.chunk.refs_0_.own, f32[264,256]{1,0:T(8,128)S(1)} %collective-permute-done.refs_1_, ...), custom_call_target="tpu_custom_call" | custom-call | flops 603979776 | bytes 65536 | tf_op jit(solution)/shard_map/pallas_call | solution.py:357
  23.7 0.0 collective-permute-done.3.low.refs_1_.below
  23.7 2.3 %collective-permute-start.4 = (f32[264,256]{1,0:T(8,128)S(1)}, f32[264,256]{1,0:T(8,128)S(1)}, u32[]{:S(2)}, u32[]{:S(2)}) collective-permute-start(f32[264,256]{1,0:T(8,128)S(1)} %collective-permute-done.2.high.refs_0_.above), channel_id=1, source_target_pairs={{0,64},{64,0},{1,65},{65,1},{2,66},{66,2},{3,67},{67,3},{4,68},{68... | collective-permute-start | bytes 811016 | tf_op jit(solution)/shard_map/ppermute | solution.py:368
  26.1 0.1 collective-permute-start.5
  26.2 0.4 collective-permute-start.6
  26.6 2.5 %shard_map.115 = (f32[768,256]{1,0:T(8,128)S(1)}, bf16[3,768,256]{2,1,0:T(8,128)(2,1)S(1)}, bf16[3,768,256]{2,1,0:T(8,128)(2,1)S(1)}) custom-call(bf16[384,48]{1,0:T(8,128)(2,1)S(1)} %shard_map.111.lhs, f32[256,256]{1,0:T(8,128)S(1)} %copy-done.7, f32[264,256]{1,0:T(8,128)S(1)} %collective-permute-done.2.high.refs_0_.above, ...), custom_call_target="tpu_custom_call" | custom-call | flops 905969664 | bytes 65536 | tf_op jit(solution)/shard_map/pallas_call | solution.py:357
  29.1 0.0 collective-permute-done.5.refs_1_
  29.2 0.0 collective-permute-done.6.refs_2_
  29.2 2.5 %shard_map.116 = (f32[768,256]{1,0:T(8,128)S(1)}, bf16[3,768,256]{2,1,0:T(8,128)(2,1)S(1)}, bf16[3,768,256]{2,1,0:T(8,128)(2,1)S(1)}) custom-call(bf16[384,48]{1,0:T(8,128)(2,1)S(1)} %shard_map.111.lhs, f32[256,256]{1,0:T(8,128)S(1)} %copy-done.7, f32[264,256]{1,0:T(8,128)S(1)} %collective-permute-done.4.refs_0_, ...), custom_call_target="tpu_custom_call" | custom-call | flops 905969664 | bytes 65536 | tf_op jit(solution)/shard_map/pallas_call | solution.py:357
  31.7 0.0 copy-start.3
  31.7 17.1 %all_to_all.16.parts = f32[16,48,256]{2,1,0:T(8,128)S(1)} all-to-all(f32[16,48,256]{2,1,0:T(8,128)S(1)} %bitcast.3), channel_id=1, replica_groups=mesh['rows'=2,'waves_0'=4,'waves_1'=4,'waves_2'=4] {'waves_0','waves_1'}, dimensions={0} | all-to-all | bytes 1572864 | tf_op jit(solution)/shard_map/all_to_all | solution.py:373
  48.8 0.1 shard_map.118
  48.9 16.1 %all_to_all.17 = f32[16,48,256]{2,1,0:T(8,128)S(1)} all-to-all(f32[16,48,256]{2,1,0:T(8,128)S(1)} %shard_map.118), channel_id=1, replica_groups=mesh['rows'=2,'waves_0'=4,'waves_1'=4,'waves_2'=4] {'waves_0','waves_1'}, dimensions={0} | all-to-all | bytes 1572864 | tf_op jit(solution)/shard_map/all_to_all | solution.py:376
  64.9 0.6 shard_map.119
  65.5 2.2 %collective-permute-start.7 = (f32[1,256,256]{2,1,0:T(8,128)S(1)}, f32[1,256,256]{2,1,0:T(8,128)S(1)}, u32[]{:S(2)}, u32[]{:S(2)}) collective-permute-start(f32[1,256,256]{2,1,0:T(8,128)S(1)} %get-tuple-element.71), channel_id=1, source_target_pairs={{0,64},{64,0},{1,65},{65,1},{2,66},{66,2},{3,67},{67,3},{4,68},{68... | collective-permute-start | bytes 786440 | tf_op jit(solution)/shard_map/ppermute | solution.py:390
  67.7 1.1 %shard_map.121 = f32[3,256,256]{2,1,0:T(8,128)S(1)} custom-call(bf16[256,768]{1,0:T(8,128)(2,1)S(1)} %get-tuple-element.82.fh, bf16[256,768]{1,0:T(8,128)(2,1)S(1)} %get-tuple-element.83.fl, bf16[1,768,256]{2,1,0:T(8,128)(2,1)S(1)} %get-tuple-element.77.mh0, bf16[1,768,256]{2,1,0:T(8,128)(2,1)S(1)} %get-tuple-element.78.ml0, ...), custom_call_target="tpu_custom_call" | custom-call | flops 905969664 | bytes 65536 | tf_op jit(solution)/shard_map/pallas_call | solution.py:384
  68.8 0.1 collective-permute-done.7.refs_0_
  68.9 0.5 shard_map.120
  69.4 0.0 copy-start
  69.4 0.0 copy-start.1
  69.4 0.0 copy-start.2
  69.4 0.0 copy-start.4
  69.4 0.0 copy-start.5
  69.4 0.5 collective-permute-start.9
  69.9 0.8 collective-permute-start.10
  70.7 2.2 %collective-permute-start.8 = (f32[264,256]{1,0:T(8,128)S(1)}, f32[264,256]{1,0:T(8,128)S(1)}, u32[]{:S(2)}, u32[]{:S(2)}) collective-permute-start(f32[264,256]{1,0:T(8,128)S(1)} %shard_map.117), channel_id=1, source_target_pairs={{0,4},{4,8},{8,12},{12,16},{16,20},{20,24},{24,28},{28,32},{32,36}... | collective-permute-start | bytes 811016 | tf_op jit(solution)/shard_map/ppermute | solution.py:399
  72.9 0.0 collective-permute-done.9.refs_0_
  72.9 1.1 %shard_map.123 = (f32[256,256]{1,0:T(8,128)S(1)}, f32[256,256]{1,0:T(8,128)S(1)}, f32[256,256]{1,0:T(8,128)S(1)}) custom-call(bf16[256,768]{1,0:T(8,128)(2,1)S(1)} %get-tuple-element.82.fh, bf16[256,768]{1,0:T(8,128)(2,1)S(1)} %get-tuple-element.83.fl, bf16[1,768,256]{2,1,0:T(8,128)(2,1)S(1)} %get-tuple-element.53.refs_2_.mh0, ...), custom_call_target="tpu_custom_call" | custom-call | flops 905969664 | bytes 65536 | tf_op jit(solution)/shard_map/pallas_call | solution.py:384
  74.0 0.4 collective-permute-start.11
  74.4 2.8 %collective-permute-start.12 = (f32[256,256]{1,0:T(8,128)S(1)}, f32[256,256]{1,0:T(8,128)S(1)}, u32[]{:S(2)}, u32[]{:S(2)}) collective-permute-start(f32[256,256]{1,0:T(8,128)S(1)} %get-tuple-element.88), channel_id=1, source_target_pairs={{0,3},{1,0},{2,1},{3,2},{4,7},{5,4},{6,5},{7,6},{8,11},{9,8},{10,9... | collective-permute-start | bytes 786440 | tf_op jit(solution)/shard_map/ppermute | solution.py:402
  77.2 2.0 %shard_map.114 = (f32[256,256]{1,0:T(8,128)S(1)}, f32[256,128]{1,0:T(8,128)S(1)}, f32[256,8]{1,0:T(8,128)S(1)}, f32[16,128]{1,0:T(8,128)S(1)}, bf16[256,256]{1,0...) custom-call(s32[2,5]{1,0:T(2,128)S(1)} %copy-done.4, ...), custom_call_target="tpu_custom_call" | custom-call | bytes 65536 | tf_op jit(solution)/shard_map/pallas_call | solution.py:408
  79.2 5.5 %collective-permute-done.8.edge = f32[264,256]{1,0:T(8,128)S(1)} collective-permute-done((f32[264,256]{1,0:T(8,128)S(1)}, f32[264,256]{1,0:T(8,128)S(1)}, u32[]{:S(2)}, u32[]{:S(2)}) %collective-permute-start.8) | collective-permute-done | bytes 270368 | tf_op jit(solution)/shard_map/ppermute | solution.py:399
  84.7 0.8 shard_map.122.base
  85.5 0.0 collective-permute-done.10.refs_1_
  85.5 0.0 collective-permute-done.11.b
  85.5 0.0 collective-permute-done.12.c
  85.6 1.6 %shard_map.125 = f32[256,256]{1,0:T(8,128)} custom-call(f32[256,256]{1,0:T(8,128)S(1)} %shard_map.122.base, f32[256,128]{1,0:T(8,128)S(1)} %get-tuple-element.59.mask, f32[256,256]{1,0:T(8,128)S(1)} %shard_map.124.a, f32[256,256]{1,0:T(8,128)S(1)} %collective-permute-done.11.b, f32[256,256]{1,0:T(8,128)S(1)} %collective-permute-done.12.c, ...), custom_call_target="tpu_custom_call" | custom-call | bytes 65536 | tf_op jit(solution)/shard_map/pallas_call | solution.py:415
  (15 shorter events, 0.1 us)
Async XLA Ops:
  1.0 21.3 %copy-start.7 = (f32[256,256]{1,0:T(8,128)S(1)}, f32[256,256]{1,0:T(8,128)}, u32[]{:S(2)}) copy-start(f32[256,256]{1,0:T(8,128)} %w_val.5) | copy-start | bytes 786436
  1.1 0.7 copy-start.6
  1.8 20.6 %collective-permute-start = (f32[264,256]{1,0:T(8,128)S(1)}, f32[264,256]{1,0:T(8,128)S(1)}, u32[]{:S(2)}, u32[]{:S(2)}) collective-permute-start(f32[264,256]{1,0:T(8,128)S(1)} %shard_map.110.chunk.refs_0_.own), channel_id=1, source_target_pairs={{0,64},{64,0},{1,65},{65,1},{2,66},{66,2},{3,67},{67,3},{4,68},{68... | collective-permute-start | bytes 811016 | tf_op jit(solution)/shard_map/ppermute | solution.py:348
  3.2 20.5 %collective-permute-start.1 = (f32[264,256]{1,0:T(8,128)S(1)}, f32[264,256]{1,0:T(8,128)S(1)}, u32[]{:S(2)}, u32[]{:S(2)}) collective-permute-start(f32[264,256]{1,0:T(8,128)S(1)} %shard_map.110.chunk.refs_0_.own), channel_id=1, source_target_pairs={{0,2},{1,3},{2,0},{3,1},{4,6},{5,7},{6,4},{7,5},{8,10},{9,11},{10,... | collective-permute-start | bytes 811016 | tf_op jit(solution)/shard_map/ppermute | solution.py:343
  6.0 17.7 %collective-permute-start.2 = (f32[264,256]{1,0:T(8,128)S(1)}, f32[264,256]{1,0:T(8,128)S(1)}, u32[]{:S(2)}, u32[]{:S(2)}) collective-permute-start(f32[264,256]{1,0:T(8,128)S(1)} %shard_map.110.chunk.refs_0_.own), channel_id=1, source_target_pairs={{0,3},{1,0},{2,1},{3,2},{4,7},{5,4},{6,5},{7,6},{8,11},{9,8},{10,9... | collective-permute-start | bytes 811016 | tf_op jit(solution)/shard_map/ppermute | solution.py:344
  6.9 16.9 %collective-permute-start.3 = (f32[264,256]{1,0:T(8,128)S(1)}, f32[264,256]{1,0:T(8,128)S(1)}, u32[]{:S(2)}, u32[]{:S(2)}) collective-permute-start(f32[264,256]{1,0:T(8,128)S(1)} %shard_map.110.chunk.refs_0_.own), channel_id=1, source_target_pairs={{0,1},{1,2},{2,3},{3,0},{4,5},{5,6},{6,7},{7,4},{8,9},{9,10},{10,1... | collective-permute-start | bytes 811016 | tf_op jit(solution)/shard_map/ppermute | solution.py:345
  23.7 5.4 %collective-permute-start.4 = (f32[264,256]{1,0:T(8,128)S(1)}, f32[264,256]{1,0:T(8,128)S(1)}, u32[]{:S(2)}, u32[]{:S(2)}) collective-permute-start(f32[264,256]{1,0:T(8,128)S(1)} %collective-permute-done.2.high.refs_0_.above), channel_id=1, source_target_pairs={{0,64},{64,0},{1,65},{65,1},{2,66},{66,2},{3,67},{67,3},{4,68},{68... | collective-permute-start | bytes 811016 | tf_op jit(solution)/shard_map/ppermute | solution.py:368
  26.1 3.1 %collective-permute-start.5 = (f32[264,256]{1,0:T(8,128)S(1)}, f32[264,256]{1,0:T(8,128)S(1)}, u32[]{:S(2)}, u32[]{:S(2)}) collective-permute-start(f32[264,256]{1,0:T(8,128)S(1)} %collective-permute-done.3.low.refs_1_.below), channel_id=1, source_target_pairs={{0,64},{64,0},{1,65},{65,1},{2,66},{66,2},{3,67},{67,3},{4,68},{68... | collective-permute-start | bytes 811016 | tf_op jit(solution)/shard_map/ppermute | solution.py:368
  26.2 3.0 %collective-permute-start.6 = (f32[264,256]{1,0:T(8,128)S(1)}, f32[264,256]{1,0:T(8,128)S(1)}, u32[]{:S(2)}, u32[]{:S(2)}) collective-permute-start(f32[264,256]{1,0:T(8,128)S(1)} %collective-permute-done.1.refs_2_), channel_id=1, source_target_pairs={{0,64},{64,0},{1,65},{65,1},{2,66},{66,2},{3,67},{67,3},{4,68},{68... | collective-permute-start | bytes 811016 | tf_op jit(solution)/shard_map/ppermute | solution.py:368
  31.7 17.1 %copy-start.3 = (f32[48,256]{1,0:T(8,128)S(1)}, f32[48,256]{1,0:T(8,128)}, u32[]{:S(2)}) copy-start(f32[48,256]{1,0:T(8,128)} %filters.1) | copy-start | bytes 147460
  65.5 3.3 %collective-permute-start.7 = (f32[1,256,256]{2,1,0:T(8,128)S(1)}, f32[1,256,256]{2,1,0:T(8,128)S(1)}, u32[]{:S(2)}, u32[]{:S(2)}) collective-permute-start(f32[1,256,256]{2,1,0:T(8,128)S(1)} %get-tuple-element.71), channel_id=1, source_target_pairs={{0,64},{64,0},{1,65},{65,1},{2,66},{66,2},{3,67},{67,3},{4,68},{68... | collective-permute-start | bytes 786440 | tf_op jit(solution)/shard_map/ppermute | solution.py:390
  69.4 7.8 %copy-start = (f32[256,256]{1,0:T(8,128)S(1)}, f32[256,256]{1,0:T(8,128)}, u32[]{:S(2)}) copy-start(f32[256,256]{1,0:T(8,128)} %w_msg.1) | copy-start | bytes 786436
  69.4 7.8 %copy-start.1 = (f32[256,256]{1,0:T(8,128)S(1)}, f32[256,256]{1,0:T(8,128)}, u32[]{:S(2)}) copy-start(f32[256,256]{1,0:T(8,128)} %w_one.1) | copy-start | bytes 786436
  69.4 7.8 %copy-start.2 = (f32[256,256]{1,0:T(8,128)S(1)}, f32[256,256]{1,0:T(8,128)}, u32[]{:S(2)}) copy-start(f32[256,256]{1,0:T(8,128)} %w_two.1) | copy-start | bytes 786436
  69.4 7.8 %copy-start.4 = (s32[2,5]{1,0:T(2,128)S(1)}, s32[2,5]{1,0:T(2,128)}, u32[]{:S(2)}) copy-start(s32[2,5]{1,0:T(2,128)} %neighbours.1) | copy-start | bytes 124
  69.4 7.8 %copy-start.5 = (s32[2]{0:T(128)S(1)}, s32[2]{0:T(128)}, u32[]{:S(2)}) copy-start(s32[2]{0:T(128)} %nbr_count.1) | copy-start | bytes 28
  69.4 3.5 %collective-permute-start.9 = (f32[3,256,256]{2,1,0:T(8,128)S(1)}, f32[3,256,256]{2,1,0:T(8,128)S(1)}, u32[]{:S(2)}, u32[]{:S(2)}) collective-permute-start(f32[3,256,256]{2,1,0:T(8,128)S(1)} %shard_map.121), channel_id=1, source_target_pairs={{0,64},{64,0},{1,65},{65,1},{2,66},{66,2},{3,67},{67,3},{4,68},{68... | collective-permute-start | bytes 2359304 | tf_op jit(solution)/shard_map/ppermute | solution.py:395
  69.9 15.6 %collective-permute-start.10 = (f32[256,256]{1,0:T(8,128)S(1)}, f32[256,256]{1,0:T(8,128)S(1)}, u32[]{:S(2)}, u32[]{:S(2)}) collective-permute-start(f32[256,256]{1,0:T(8,128)S(1)} %shard_map.120), channel_id=1, source_target_pairs={{0,2},{1,3},{2,0},{3,1},{4,6},{5,7},{6,4},{7,5},{8,10},{9,11},{10,... | collective-permute-start | bytes 786440 | tf_op jit(solution)/shard_map/ppermute | solution.py:396
  70.7 14.0 %collective-permute-start.8 = (f32[264,256]{1,0:T(8,128)S(1)}, f32[264,256]{1,0:T(8,128)S(1)}, u32[]{:S(2)}, u32[]{:S(2)}) collective-permute-start(f32[264,256]{1,0:T(8,128)S(1)} %shard_map.117), channel_id=1, source_target_pairs={{0,4},{4,8},{8,12},{12,16},{16,20},{20,24},{24,28},{28,32},{32,36}... | collective-permute-start | bytes 811016 | tf_op jit(solution)/shard_map/ppermute | solution.py:399
  74.0 11.5 %collective-permute-start.11 = (f32[256,256]{1,0:T(8,128)S(1)}, f32[256,256]{1,0:T(8,128)S(1)}, u32[]{:S(2)}, u32[]{:S(2)}) collective-permute-start(f32[256,256]{1,0:T(8,128)S(1)} %get-tuple-element.87), channel_id=1, source_target_pairs={{0,1},{1,2},{2,3},{3,0},{4,5},{5,6},{6,7},{7,4},{8,9},{9,10},{10,1... | collective-permute-start | bytes 786440 | tf_op jit(solution)/shard_map/ppermute | solution.py:401
  74.4 11.1 %collective-permute-start.12 = (f32[256,256]{1,0:T(8,128)S(1)}, f32[256,256]{1,0:T(8,128)S(1)}, u32[]{:S(2)}, u32[]{:S(2)}) collective-permute-start(f32[256,256]{1,0:T(8,128)S(1)} %get-tuple-element.88), channel_id=1, source_target_pairs={{0,3},{1,0},{2,1},{3,2},{4,7},{5,4},{6,5},{7,6},{8,11},{9,8},{10,9... | collective-permute-start | bytes 786440 | tf_op jit(solution)/shard_map/ppermute | solution.py:402
